TPU v7x, 128 devices: a whole 4x4x4 slice. The times are simulated.
128 devices in a mesh: dp: 16 (over x_lo, z, core), tensor: 8 (over y, x_hi).
Axes of the slice: x: 4 (x_hi: 2, x_lo: 2; x = x_hi * 2 + x_lo), y: 4, z: 4, core: 2. Of those that a mesh axis runs over, the one named last changes fastest.
Arguments:
- tokens: bfloat16 [16384, 1024], P('dp'), may hold values from -6 to 6
- segment_ids: int32 [16384], P('dp'), may hold values from 0 to 7, as said below
- attn_gain: float32 [1024], replicated, may hold values from 0.25 to 1.75
- w_query: bfloat16 [1024, 1024], P(None, 'tensor'), may hold values from -0.1875 to 0.1875
- w_key: bfloat16 [1024, 512], P(None, 'tensor'), may hold values from -0.1875 to 0.1875
- w_value: bfloat16 [1024, 512], P(None, 'tensor'), may hold values from -0.1875 to 0.1875
- query_gain: float32 [64], replicated, may hold values from 0.25 to 1.75
- key_gain: float32 [64], replicated, may hold values from 0.25 to 1.75
- w_out: bfloat16 [1024, 1024], P('tensor'), may hold values from -1.5 to 1.5
- ffn_gain: float32 [1024], replicated, may hold values from 0.25 to 1.75
- w_gate: bfloat16 [1024, 4608], P(None, 'tensor'), may hold values from -0.1875 to 0.1875
- w_up: bfloat16 [1024, 4608], P(None, 'tensor'), may hold values from -0.1875 to 0.1875
- w_down: bfloat16 [4608, 1024], P('tensor'), may hold values from -0.1875 to 0.1875
- cotangent: bfloat16 [16384, 1024], P('dp'), may hold values from -6 to 6
Outputs:
- output: bfloat16 [16384, 1024], P('dp')
- input_grad: float32 [16384, 1024], P('dp')
- attn_gain_grad: float32 [1024], replicated
- w_query_grad: float32 [1024, 1024], P(None, 'tensor')
- w_key_grad: float32 [1024, 512], P(None, 'tensor')
- w_value_grad: float32 [1024, 512], P(None, 'tensor')
- query_gain_grad: float32 [64], replicated
- key_gain_grad: float32 [64], replicated
- w_out_grad: float32 [1024, 1024], P('tensor')
- ffn_gain_grad: float32 [1024], replicated
- w_gate_grad: float32 [1024, 4608], P(None, 'tensor')
- w_up_grad: float32 [1024, 4608], P(None, 'tensor')
- w_down_grad: float32 [4608, 1024], P('tensor')
Inputs may be any that keep to these rules, and one draw needn't show every extreme that they name: `segment_ids`: within each index of dp's 1024 tokens the ids start at 0 and never fall; a sequence is a run of equal ids and never crosses devices.
All inputs are finite; a program needn't handle non-finite values.
Results may differ from a plain program's by a relative error of at most 0.014.
The roundings to bfloat16 on the way count: a program that leaves them out, or rounds other values in their place, can miss the bound.
Values sent between devices are 32-bit elements; how exact they have to be, the bound alone decides.
No kernel may reach another device: no remote copies, remote signals or barrier semaphores. Data moves between devices by JAX's collectives and lax.ppermute only.
A program may use at most 128 MiB of HBM per device.

v0:
```python
import math

import jax
import jax.numpy as jnp
from jax import lax
from jax.sharding import PartitionSpec as P

EPS = 1e-05
THETA = 1000000.0
TENSOR = ("ty", "tx")


def outer(first_op, second_op):
    return lax.dot_general(
        first_op, second_op, (((0,), (0,)), ((), ())), preferred_element_type=jnp.float32
    )


def inner(first_op, second_op):
    return lax.dot_general(
        first_op, second_op, (((1,), (1,)), ((), ())), preferred_element_type=jnp.float32
    )


def rms_scale(values):
    return lax.rsqrt(jnp.mean(values * values, axis=-1, keepdims=True) + EPS)


def rms_back(upstream, values, inv_rms, gain_vec):
    normed = values * inv_rms
    weighted = upstream * gain_vec
    return inv_rms * (weighted - normed * jnp.mean(weighted * normed, axis=-1, keepdims=True))


def seq_layout(segment):
    length = segment.shape[0]
    ordinal = jnp.arange(length, dtype=jnp.int32)
    same_seq = segment[:, None] == segment[None, :]
    places = jnp.sum((same_seq & (ordinal[None, :] < ordinal[:, None])).astype(jnp.int32), axis=1)
    allowed = same_seq & (ordinal[None, :] <= ordinal[:, None])
    return (places, allowed)


def rope_tables(places, head_size):
    frequency = jnp.exp(
        jnp.arange(head_size // 2, dtype=jnp.float32) * (-2.0 * math.log(THETA) / head_size)
    )
    angles = places.astype(jnp.float32)[:, None] * frequency[None, :]
    angles = jnp.concatenate([angles, angles], axis=1)
    return (jnp.cos(angles), jnp.sin(angles))


def rotate(values, cosine, sine_table):
    half = values.shape[-1] // 2
    turned = jnp.concatenate([-values[..., half:], values[..., :half]], axis=-1)
    return values * cosine[:, None, :] + turned * sine_table[:, None, :]


def unrotate(incoming, cosine, sine_table):
    half = incoming.shape[-1] // 2
    scaled = incoming * sine_table[:, None, :]
    swapped = jnp.concatenate([scaled[..., half:], -scaled[..., :half]], axis=-1)
    return incoming * cosine[:, None, :] + swapped


def score_table(q_rot, k_rot, allowed, factor):
    raw = jnp.einsum("ikgd,jkd->kgij", q_rot, k_rot, preferred_element_type=jnp.float32) * factor
    return jnp.where(allowed[None, None], raw, -1e30)


def ring(size, shift):
    return [(i, (i + shift) % size) for i in range(size)]


def tensor_sum(values, extra=None):
    rows, cols = values.shape
    ny = lax.axis_size("ty")
    nx = lax.axis_size("tx")
    y = lax.axis_index("ty")
    h = lax.axis_index("tx")
    leaf = rows // (2 * ny * nx)
    parts = values.reshape(2, ny, nx, leaf, cols)
    pairs = ring(nx, 1)
    total = extra
    accs = []
    for way, shift in ((0, 1), (1, -1)):
        chunks = parts[way]
        acc = lax.dynamic_index_in_dim(chunks, (y - shift) % ny, 0, keepdims=False)
        passing = extra
        for step in range(1, ny):
            if way == 0 and extra is not None:
                acc, passing = lax.ppermute((acc, passing), "ty", ring(ny, shift))
                total = total + passing
            else:
                acc = lax.ppermute(acc, "ty", ring(ny, shift))
            acc = acc + lax.dynamic_index_in_dim(chunks, (y - shift * (1 + step)) % ny, 0, keepdims=False)
        accs.append(acc)
    acc = jnp.stack(accs)
    keep = lax.dynamic_index_in_dim(acc, h, 1, keepdims=False)
    send = lax.dynamic_index_in_dim(acc, (h + 1) % nx, 1, keepdims=False)
    if extra is not None:
        got, got_total = lax.ppermute((send, total), "tx", pairs)
        total = total + got_total
    else:
        got = lax.ppermute(send, "tx", pairs)
    mine = keep + got
    other = lax.ppermute(mine, "tx", pairs)
    both = jnp.where(h == 0, jnp.stack([mine, other], 1), jnp.stack([other, mine], 1))
    outs = []
    for way, shift in ((0, 1), (1, -1)):
        cur = both[way]
        gathered = jnp.zeros((ny,) + cur.shape, values.dtype)
        gathered = lax.dynamic_update_index_in_dim(gathered, cur, y, 0)
        for step in range(1, ny):
            cur = lax.ppermute(cur, "ty", ring(ny, shift))
            gathered = lax.dynamic_update_index_in_dim(gathered, cur, (y - shift * step) % ny, 0)
        outs.append(gathered)
    result = jnp.stack(outs).reshape(rows, cols)
    if extra is None:
        return result
    return result, total


def small_tensor_sum(values):
    ny = lax.axis_size("ty")
    nx = lax.axis_size("tx")
    dist = 1
    while dist < ny:
        values = values + lax.ppermute(values, "ty", [(i, i ^ dist) for i in range(ny)])
        dist *= 2
    dist = 1
    while dist < nx:
        values = values + lax.ppermute(values, "tx", [(i, i ^ dist) for i in range(nx)])
        dist *= 2
    return values


def per_device(
    tokens,
    segment_ids,
    attn_gain,
    w_query,
    w_key,
    w_value,
    query_gain,
    key_gain,
    w_out,
    ffn_gain,
    w_gate,
    w_up,
    w_down,
    cotangent,
):
    length = tokens.shape[0]
    head_size = query_gain.shape[0]
    q_heads = w_query.shape[1] // head_size
    kv_heads = w_key.shape[1] // head_size
    groups = q_heads // kv_heads
    factor = 1.0 / math.sqrt(head_size)
    places, allowed = seq_layout(segment_ids)
    cosine, sine_table = rope_tables(places, head_size)
    tokens_wide = tokens.astype(jnp.float32)
    scale_one = rms_scale(tokens_wide)
    normed_one = (tokens_wide * scale_one * attn_gain).astype(jnp.bfloat16)
    q_raw = jnp.dot(normed_one, w_query, preferred_element_type=jnp.float32).reshape(
        length, q_heads, head_size
    )
    k_raw = jnp.dot(normed_one, w_key, preferred_element_type=jnp.float32).reshape(
        length, kv_heads, head_size
    )
    v_half = (
        jnp.dot(normed_one, w_value, preferred_element_type=jnp.float32)
        .astype(jnp.bfloat16)
        .reshape(length, kv_heads, head_size)
    )
    q_scale = rms_scale(q_raw)
    k_scale = rms_scale(k_raw)
    q_hat = q_raw * q_scale
    k_hat = k_raw * k_scale
    q_rot = (
        rotate(q_hat * query_gain, cosine, sine_table)
        .astype(jnp.bfloat16)
        .reshape(length, kv_heads, groups, head_size)
    )
    k_rot = rotate(k_hat * key_gain, cosine, sine_table).astype(jnp.bfloat16)
    scores = score_table(q_rot, k_rot, allowed, factor)
    row_peak = jnp.max(scores, axis=-1, keepdims=True)
    log_total = row_peak + jnp.log(jnp.sum(jnp.exp(scores - row_peak), axis=-1, keepdims=True))
    attn_probs = jnp.exp(scores - log_total).astype(jnp.bfloat16)
    attn_mixed = jnp.einsum(
        "kgij,jkd->ikgd", attn_probs, v_half, preferred_element_type=jnp.float32
    )
    attn_mixed = attn_mixed.reshape(length, q_heads * head_size).astype(jnp.bfloat16)
    attn_sum = tensor_sum(jnp.dot(attn_mixed, w_out, preferred_element_type=jnp.float32))
    residual = tokens_wide + attn_sum
    scale_two = rms_scale(residual)
    normed_two = (residual * scale_two * ffn_gain).astype(jnp.bfloat16)
    gate_proj = jnp.dot(normed_two, w_gate, preferred_element_type=jnp.float32)
    up_proj = jnp.dot(normed_two, w_up, preferred_element_type=jnp.float32)
    gate_sigmoid = jax.nn.sigmoid(gate_proj)
    hidden = (gate_proj * gate_sigmoid * up_proj).astype(jnp.bfloat16)
    mlp_sum = tensor_sum(jnp.dot(hidden, w_down, preferred_element_type=jnp.float32))
    output = (residual + mlp_sum).astype(jnp.bfloat16)
    down_grad = outer(hidden, cotangent)
    hidden_grad = inner(cotangent, w_down)
    gate_grad = (
        hidden_grad * up_proj * gate_sigmoid * (1.0 + gate_proj * (1.0 - gate_sigmoid))
    ).astype(jnp.bfloat16)
    up_grad = (hidden_grad * gate_proj * gate_sigmoid).astype(jnp.bfloat16)
    gate_w_grad = outer(normed_two, gate_grad)
    up_w_grad = outer(normed_two, up_grad)
    normed_two_grad = tensor_sum(inner(gate_grad, w_gate) + inner(up_grad, w_up))
    ffn_grad = jnp.sum(normed_two_grad * residual * scale_two, axis=0)
    residual_grad = cotangent.astype(jnp.float32) + rms_back(
        normed_two_grad, residual, scale_two, ffn_gain
    )
    residual_half = residual_grad.astype(jnp.bfloat16)
    out_w_grad = outer(attn_mixed, residual_half)
    mixed_grad = (
        inner(residual_half, w_out)
        .astype(jnp.bfloat16)
        .reshape(length, kv_heads, groups, head_size)
    )
    attn_full = jnp.exp(score_table(q_rot, k_rot, allowed, factor) - log_total)
    probs_half = attn_full.astype(jnp.bfloat16)
    value_grad = jnp.einsum(
        "kgij,ikgd->jkd", probs_half, mixed_grad, preferred_element_type=jnp.float32
    ).astype(jnp.bfloat16)
    prob_grad = jnp.einsum("ikgd,jkd->kgij", mixed_grad, v_half, preferred_element_type=jnp.float32)
    row_delta = jnp.sum(attn_full * prob_grad, axis=-1, keepdims=True)
    score_grad = (attn_full * (prob_grad - row_delta) * factor).astype(jnp.bfloat16)
    q_rot_grad = jnp.einsum(
        "kgij,jkd->ikgd", score_grad, k_rot, preferred_element_type=jnp.float32
    ).reshape(length, q_heads, head_size)
    k_rot_grad = jnp.einsum("kgij,ikgd->jkd", score_grad, q_rot, preferred_element_type=jnp.float32)
    q_norm_grad = unrotate(q_rot_grad, cosine, sine_table)
    k_norm_grad = unrotate(k_rot_grad, cosine, sine_table)
    qgain_grad = jnp.sum(q_norm_grad * q_hat, axis=(0, 1))
    kgain_grad = jnp.sum(k_norm_grad * k_hat, axis=(0, 1))
    q_grad = (
        rms_back(q_norm_grad, q_raw, q_scale, query_gain)
        .astype(jnp.bfloat16)
        .reshape(length, q_heads * head_size)
    )
    k_grad = (
        rms_back(k_norm_grad, k_raw, k_scale, key_gain)
        .astype(jnp.bfloat16)
        .reshape(length, kv_heads * head_size)
    )
    v_grad = value_grad.reshape(length, kv_heads * head_size)
    query_w_grad = outer(normed_one, q_grad)
    key_w_grad = outer(normed_one, k_grad)
    value_w_grad = outer(normed_one, v_grad)
    one_partial = inner(q_grad, w_query) + inner(k_grad, w_key) + inner(v_grad, w_value)
    attn_part = jnp.sum(one_partial * tokens_wide * scale_one, axis=0)
    width = attn_part.shape[0]
    small = jnp.zeros((8, width), jnp.float32)
    small = small.at[0].set(ffn_grad).at[1].set(attn_part)
    small = small.at[2, :head_size].set(qgain_grad).at[2, head_size : 2 * head_size].set(kgain_grad)
    out_rows = out_w_grad.shape[0]
    dp_sums, one_partial = lax.optimization_barrier(
        (
            (
                query_w_grad,
                key_w_grad,
                value_w_grad,
                jnp.concatenate([out_w_grad, small]),
                gate_w_grad,
                up_w_grad,
                down_grad,
            ),
            one_partial,
        )
    )
    (
        query_w_grad,
        key_w_grad,
        value_w_grad,
        out_pack,
        gate_w_grad,
        up_w_grad,
        down_grad,
    ) = lax.psum(dp_sums, "dp")
    normed_one_grad = tensor_sum(one_partial)
    input_grad = residual_grad + rms_back(normed_one_grad, tokens_wide, scale_one, attn_gain)
    out_w_grad = out_pack[:out_rows]
    ffn_grad = out_pack[out_rows]
    gains = small_tensor_sum(out_pack[out_rows + 1 : out_rows + 3])
    attn_grad = gains[0]
    qgain_grad = gains[1, :head_size]
    kgain_grad = gains[1, head_size : 2 * head_size]
    return (
        output,
        input_grad,
        attn_grad,
        query_w_grad,
        key_w_grad,
        value_w_grad,
        qgain_grad,
        kgain_grad,
        out_w_grad,
        ffn_grad,
        gate_w_grad,
        up_w_grad,
        down_grad,
    )


def solution(mesh):
    from jax.sharding import Mesh

    dp_size, tensor_size = mesh.devices.shape
    split = Mesh(mesh.devices.reshape(dp_size, tensor_size // 2, 2), ("dp", "ty", "tx"))
    return jax.shard_map(
        per_device,
        mesh=split,
        in_specs=(
            P("dp", None),
            P("dp"),
            P(),
            P(None, TENSOR),
            P(None, TENSOR),
            P(None, TENSOR),
            P(),
            P(),
            P(TENSOR, None),
            P(),
            P(None, TENSOR),
            P(None, TENSOR),
            P(TENSOR, None),
            P("dp", None),
        ),
        out_specs=(
            P("dp", None),
            P("dp", None),
            P(),
            P(None, TENSOR),
            P(None, TENSOR),
            P(None, TENSOR),
            P(),
            P(),
            P(TENSOR, None),
            P(),
            P(None, TENSOR),
            P(None, TENSOR),
            P(TENSOR, None),
        ),
        check_vma=False,
    )
```

profile of v0, /device:TPU:0, one launch (start us, length us, event | category | flops | bytes accessed | tf_op | source)
XLA Modules:
  0.0 583.5 jit_solution(11373796553550133518)
XLA Ops:
  46.0 9.3 %collective-permute-done.3 = f32[2,64,1024]{2,1,0:T(8,128)} collective-permute-done((f32[2,64,1024]{2,1,0:T(8,128)}, f32[2,64,1024]{2,1,0:T(8,128)}, u32[]{:S(2)}, u32[]{:S(2)}) %collective-permute-start.3) | collective-permute-done | bytes 524320 | tf_op jit(solution)/shard_map/ppermute | solution.py:95
  57.4 3.7 collective-permute-start.4
  63.1 8.6 %collective-permute-done.4 = f32[2,64,1024]{2,1,0:T(8,128)} collective-permute-done((f32[2,64,1024]{2,1,0:T(8,128)}, f32[2,64,1024]{2,1,0:T(8,128)}, u32[]{:S(2)}, u32[]{:S(2)}) %collective-permute-start.4) | collective-permute-done | bytes 524320 | tf_op jit(solution)/shard_map/ppermute | solution.py:95
  73.7 3.7 collective-permute-start.5
  79.5 7.6 %collective-permute-done.5 = f32[2,64,1024]{2,1,0:T(8,128)} collective-permute-done((f32[2,64,1024]{2,1,0:T(8,128)}, f32[2,64,1024]{2,1,0:T(8,128)}, u32[]{:S(2)}, u32[]{:S(2)}) %collective-permute-start.5) | collective-permute-done | bytes 524320 | tf_op jit(solution)/shard_map/ppermute | solution.py:95
  88.4 4.2 collective-permute-done.2
  97.9 9.5 %collective-permute-done.6 = f32[2,64,1024]{2,1,0:T(8,128)} collective-permute-done((f32[2,64,1024]{2,1,0:T(8,128)}, f32[2,64,1024]{2,1,0:T(8,128)}, u32[]{:S(2)}, u32[]{:S(2)}) %collective-permute-start.6) | collective-permute-done | bytes 524320 | tf_op jit(solution)/shard_map/ppermute | solution.py:105
  112.4 8.5 %collective-permute-done.7 = f32[2,64,1024]{2,1,0:T(8,128)} collective-permute-done((f32[2,64,1024]{2,1,0:T(8,128)}, f32[2,64,1024]{2,1,0:T(8,128)}, u32[]{:S(2)}, u32[]{:S(2)}) %collective-permute-start.7) | collective-permute-done | bytes 524320 | tf_op jit(solution)/shard_map/ppermute | solution.py:107
  127.9 9.4 %collective-permute-done.8 = f32[2,64,1024]{2,1,0:T(8,128)} collective-permute-done((f32[2,64,1024]{2,1,0:T(8,128)}, f32[2,64,1024]{2,1,0:T(8,128)}, u32[]{:S(2)}, u32[]{:S(2)}) %collective-permute-start.8) | collective-permute-done | bytes 524320 | tf_op jit(solution)/shard_map/ppermute | solution.py:115
  137.6 3.3 collective-permute-start.12
  142.3 8.9 %collective-permute-done.9 = f32[2,64,1024]{2,1,0:T(8,128)S(1)} collective-permute-done((f32[2,64,1024]{2,1,0:T(8,128)}, f32[2,64,1024]{2,1,0:T(8,128)S(1)}, u32[]{:S(2)}, u32[]{:S(2)}) %collective-permute-start.9) | collective-permute-done | bytes 524320 | tf_op jit(solution)/shard_map/ppermute | solution.py:115
  152.4 3.3 collective-permute-start.13
  155.8 5.9 %collective-permute-done.10 = f32[2,64,1024]{2,1,0:T(8,128)S(1)} collective-permute-done((f32[2,64,1024]{2,1,0:T(8,128)S(1)}, f32[2,64,1024]{2,1,0:T(8,128)S(1)}, u32[]{:S(2)}, u32[]{:S(2)}) %collective-permute-start.10) | collective-permute-done | bytes 524320 | tf_op jit(solution)/shard_map/ppermute | solution.py:115
  178.3 3.8 collective-permute-start.17
  182.1 11.2 %collective-permute-start.14 = (f32[2,64,1024]{2,1,0:T(8,128)S(1)}, f32[2,64,1024]{2,1,0:T(8,128)S(1)}, u32[]{:S(2)}, u32[]{:S(2)}) collective-permute-start(f32[2,64,1024]{2,1,0:T(8,128)S(1)} %dynamic-slice_bitcast_fusion.5), channel_id=1, source_target_pairs={{0,2},{2,4},{4,6},{6,0},{1,3},{3,5},{5,7},{7,1},{8,10},{10,12},{12... | collective-permute-start | bytes 1572872 | tf_op jit(solution)/shard_map/ppermute | solution.py:95
  205.5 4.0 collective-permute-done.14
  209.6 4.7 collective-permute-done.31
  214.4 3.8 collective-permute-start.32
  220.8 4.7 collective-permute-done.18
  225.7 3.8 collective-permute-start.19
  232.1 4.7 collective-permute-done.32
  236.9 3.8 collective-permute-start.33
  243.4 8.7 %collective-permute-done.16 = f32[2,64,1024]{2,1,0:T(8,128)S(1)} collective-permute-done((f32[2,64,1024]{2,1,0:T(8,128)S(1)}, f32[2,64,1024]{2,1,0:T(8,128)S(1)}, u32[]{:S(2)}, u32[]{:S(2)}) %collective-permute-start.16) | collective-permute-done | bytes 524320 | tf_op jit(solution)/shard_map/ppermute | solution.py:95
  261.0 7.7 %collective-permute-done.20 = f32[2,64,1024]{2,1,0:T(8,128)S(1)} collective-permute-done((f32[2,64,1024]{2,1,0:T(8,128)S(1)}, f32[2,64,1024]{2,1,0:T(8,128)S(1)}, u32[]{:S(2)}, u32[]{:S(2)}) %collective-permute-start.20) | collective-permute-done | bytes 524320 | tf_op jit(solution)/shard_map/ppermute | solution.py:105
  274.7 5.3 collective-permute-done.34
  283.1 4.9 collective-permute-done.21
  298.1 6.2 %collective-permute-done.22 = f32[2,64,1024]{2,1,0:T(8,128)S(1)} collective-permute-done((f32[2,64,1024]{2,1,0:T(8,128)S(1)}, f32[2,64,1024]{2,1,0:T(8,128)S(1)}, u32[]{:S(2)}, u32[]{:S(2)}) %collective-permute-start.22) | collective-permute-done | bytes 524320 | tf_op jit(solution)/shard_map/ppermute | solution.py:115
  307.6 8.0 %collective-permute-done.36 = f32[2,64,1024]{2,1,0:T(8,128)S(1)} collective-permute-done((f32[2,64,1024]{2,1,0:T(8,128)S(1)}, f32[2,64,1024]{2,1,0:T(8,128)S(1)}, u32[]{:S(2)}, u32[]{:S(2)}) %collective-permute-start.36) | collective-permute-done | bytes 524320 | tf_op jit(solution)/shard_map/ppermute | solution.py:115
  315.7 3.3 collective-permute-start.40
  319.1 7.7 %collective-permute-done.23 = f32[2,64,1024]{2,1,0:T(8,128)S(1)} collective-permute-done((f32[2,64,1024]{2,1,0:T(8,128)S(1)}, f32[2,64,1024]{2,1,0:T(8,128)S(1)}, u32[]{:S(2)}, u32[]{:S(2)}) %collective-permute-start.23) | collective-permute-done | bytes 524320 | tf_op jit(solution)/shard_map/ppermute | solution.py:115
  330.1 8.0 %collective-permute-done.37 = f32[2,64,1024]{2,1,0:T(8,128)S(1)} collective-permute-done((f32[2,64,1024]{2,1,0:T(8,128)S(1)}, f32[2,64,1024]{2,1,0:T(8,128)S(1)}, u32[]{:S(2)}, u32[]{:S(2)}) %collective-permute-start.37) | collective-permute-done | bytes 524320 | tf_op jit(solution)/shard_map/ppermute | solution.py:115
  338.2 3.7 collective-permute-start.41
  342.0 8.8 %collective-permute-done.38 = f32[2,64,1024]{2,1,0:T(8,128)S(1)} collective-permute-done((f32[2,64,1024]{2,1,0:T(8,128)S(1)}, f32[2,64,1024]{2,1,0:T(8,128)S(1)}, u32[]{:S(2)}, u32[]{:S(2)}) %collective-permute-start.38) | collective-permute-done | bytes 524320 | tf_op jit(solution)/shard_map/ppermute | solution.py:115
  387.9 3.3 collective-permute-start.45
  391.4 11.1 %collective-permute-done.45 = f32[2,64,1024]{2,1,0:T(8,128)S(1)} collective-permute-done((f32[2,64,1024]{2,1,0:T(8,128)S(1)}, f32[2,64,1024]{2,1,0:T(8,128)S(1)}, u32[]{:S(2)}, u32[]{:S(2)}) %collective-permute-start.45) | collective-permute-done | bytes 524320 | tf_op jit(solution)/shard_map/ppermute | solution.py:95
  402.6 3.8 collective-permute-start.46
  406.5 10.3 %collective-permute-done.46 = f32[2,64,1024]{2,1,0:T(8,128)S(1)} collective-permute-done((f32[2,64,1024]{2,1,0:T(8,128)S(1)}, f32[2,64,1024]{2,1,0:T(8,128)S(1)}, u32[]{:S(2)}, u32[]{:S(2)}) %collective-permute-start.46) | collective-permute-done | bytes 524320 | tf_op jit(solution)/shard_map/ppermute | solution.py:95
  416.9 3.8 collective-permute-start.47
  420.8 6.5 %collective-permute-done.47 = f32[2,64,1024]{2,1,0:T(8,128)S(1)} collective-permute-done((f32[2,64,1024]{2,1,0:T(8,128)S(1)}, f32[2,64,1024]{2,1,0:T(8,128)S(1)}, u32[]{:S(2)}, u32[]{:S(2)}) %collective-permute-start.47) | collective-permute-done | bytes 524320 | tf_op jit(solution)/shard_map/ppermute | solution.py:95
  427.4 3.8 collective-permute-done.44
  434.4 17.3 %collective-permute-done.48 = f32[2,64,1024]{2,1,0:T(8,128)S(1)} collective-permute-done((f32[2,64,1024]{2,1,0:T(8,128)S(1)}, f32[2,64,1024]{2,1,0:T(8,128)S(1)}, u32[]{:S(2)}, u32[]{:S(2)}) %collective-permute-start.48) | collective-permute-done | bytes 524320 | tf_op jit(solution)/shard_map/ppermute | solution.py:105
  451.8 3.7 collective-permute-start.49
  455.4 11.5 %collective-permute-done.49 = f32[2,64,1024]{2,1,0:T(8,128)S(1)} collective-permute-done((f32[2,64,1024]{2,1,0:T(8,128)S(1)}, f32[2,64,1024]{2,1,0:T(8,128)S(1)}, u32[]{:S(2)}, u32[]{:S(2)}) %collective-permute-start.49) | collective-permute-done | bytes 524320 | tf_op jit(solution)/shard_map/ppermute | solution.py:107
  470.5 8.8 %collective-permute-done.50 = f32[2,64,1024]{2,1,0:T(8,128)S(1)} collective-permute-done((f32[2,64,1024]{2,1,0:T(8,128)S(1)}, f32[2,64,1024]{2,1,0:T(8,128)S(1)}, u32[]{:S(2)}, u32[]{:S(2)}) %collective-permute-start.50) | collective-permute-done | bytes 524320 | tf_op jit(solution)/shard_map/ppermute | solution.py:115
  483.2 7.2 %collective-permute-done.51 = f32[2,64,1024]{2,1,0:T(8,128)S(1)} collective-permute-done((f32[2,64,1024]{2,1,0:T(8,128)S(1)}, f32[2,64,1024]{2,1,0:T(8,128)S(1)}, u32[]{:S(2)}, u32[]{:S(2)}) %collective-permute-start.51) | collective-permute-done | bytes 524320 | tf_op jit(solution)/shard_map/ppermute | solution.py:115
  493.9 6.9 %collective-permute-done.52 = f32[2,64,1024]{2,1,0:T(8,128)S(1)} collective-permute-done((f32[2,64,1024]{2,1,0:T(8,128)S(1)}, f32[2,64,1024]{2,1,0:T(8,128)S(1)}, u32[]{:S(2)}, u32[]{:S(2)}) %collective-permute-start.52) | collective-permute-done | bytes 524320 | tf_op jit(solution)/shard_map/ppermute | solution.py:115
  503.2 44.2 %all-reduce.4.cloned.1.call-done = (f32[136,1024]{1,0:T(8,128)}, f32[1024,128]{1,0:T(8,128)}, f32[1024,64]{0,1:T(8,128)}, f32[1024,64]{0,1:T(8,128)}, f32[1024,5...) async-done(((f32[136,1024]{1,0:T(8,128)}, f32[1024,128]{1,0:T(8,128)}, f32[1024,64]{0,1:T(8,128)}, f32[1024,64]{0,1:T(8,128)}, f32[1024,576]{0,1:T(8,128)}, ...) | async-done | bytes 8683536 | tf_op jit(solution)/shard_map/psum | solution.py:283
  560.9 4.2 fusion.13
  (387 shorter events, 218.4 us)
Async XLA Ops:
  7.2 540.2 %all-reduce.4.cloned.1.call-start = ((), (), s32[]{:S(2)}) async-start(), calls=%async_computation | async-start | bytes 17367040 | tf_op jit(solution)/shard_map/psum | solution.py:283
  40.7 14.6 %collective-permute-start.3 = (f32[2,64,1024]{2,1,0:T(8,128)}, f32[2,64,1024]{2,1,0:T(8,128)}, u32[]{:S(2)}, u32[]{:S(2)}) collective-permute-start(f32[2,64,1024]{2,1,0:T(8,128)} %dynamic-slice_bitcast_fusion.6), channel_id=1, source_target_pairs={{0,6},{2,0},{4,2},{6,4},{1,7},{3,1},{5,3},{7,5},{8,14},{10,8},{12,... | collective-permute-start | bytes 1572872 | tf_op jit(solution)/shard_map/ppermute | solution.py:95
  45.7 15.4 %collective-permute-start = (f32[2,64,1024]{2,1,0:T(8,128)}, f32[2,64,1024]{2,1,0:T(8,128)}, u32[]{:S(2)}, u32[]{:S(2)}) collective-permute-start(f32[2,64,1024]{2,1,0:T(8,128)} %dynamic-slice_bitcast_fusion.7), channel_id=1, source_target_pairs={{0,2},{2,4},{4,6},{6,0},{1,3},{3,5},{5,7},{7,1},{8,10},{10,12},{12... | collective-permute-start | bytes 1572872 | tf_op jit(solution)/shard_map/ppermute | solution.py:95
  57.4 14.3 %collective-permute-start.4 = (f32[2,64,1024]{2,1,0:T(8,128)}, f32[2,64,1024]{2,1,0:T(8,128)}, u32[]{:S(2)}, u32[]{:S(2)}) collective-permute-start(f32[2,64,1024]{2,1,0:T(8,128)} %bitcast_add_fusion.21), channel_id=1, source_target_pairs={{0,6},{2,0},{4,2},{6,4},{1,7},{3,1},{5,3},{7,5},{8,14},{10,8},{12,... | collective-permute-start | bytes 1572872 | tf_op jit(solution)/shard_map/ppermute | solution.py:95
  63.1 14.3 %collective-permute-start.1 = (f32[2,64,1024]{2,1,0:T(8,128)}, f32[2,64,1024]{2,1,0:T(8,128)}, u32[]{:S(2)}, u32[]{:S(2)}) collective-permute-start(f32[2,64,1024]{2,1,0:T(8,128)} %bitcast_add_fusion.24), channel_id=1, source_target_pairs={{0,2},{2,4},{4,6},{6,0},{1,3},{3,5},{5,7},{7,1},{8,10},{10,12},{12... | collective-permute-start | bytes 1572872 | tf_op jit(solution)/shard_map/ppermute | solution.py:95
  73.7 13.4 %collective-permute-start.5 = (f32[2,64,1024]{2,1,0:T(8,128)}, f32[2,64,1024]{2,1,0:T(8,128)}, u32[]{:S(2)}, u32[]{:S(2)}) collective-permute-start(f32[2,64,1024]{2,1,0:T(8,128)} %bitcast_add_fusion.20), channel_id=1, source_target_pairs={{0,6},{2,0},{4,2},{6,4},{1,7},{3,1},{5,3},{7,5},{8,14},{10,8},{12,... | collective-permute-start | bytes 1572872 | tf_op jit(solution)/shard_map/ppermute | solution.py:95
  79.5 13.1 %collective-permute-start.2 = (f32[2,64,1024]{2,1,0:T(8,128)}, f32[2,64,1024]{2,1,0:T(8,128)}, u32[]{:S(2)}, u32[]{:S(2)}) collective-permute-start(f32[2,64,1024]{2,1,0:T(8,128)} %bitcast_add_fusion.23), channel_id=1, source_target_pairs={{0,2},{2,4},{4,6},{6,0},{1,3},{3,5},{5,7},{7,1},{8,10},{10,12},{12... | collective-permute-start | bytes 1572872 | tf_op jit(solution)/shard_map/ppermute | solution.py:95
  94.9 12.5 %collective-permute-start.6 = (f32[2,64,1024]{2,1,0:T(8,128)}, f32[2,64,1024]{2,1,0:T(8,128)}, u32[]{:S(2)}, u32[]{:S(2)}) collective-permute-start(f32[2,64,1024]{2,1,0:T(8,128)} %fusion.50), channel_id=1, source_target_pairs={{0,1},{1,0},{2,3},{3,2},{4,5},{5,4},{6,7},{7,6},{8,9},{9,8},{10,11... | collective-permute-start | bytes 1572872 | tf_op jit(solution)/shard_map/ppermute | solution.py:105
  124.6 12.7 %collective-permute-start.8 = (f32[2,64,1024]{2,1,0:T(8,128)}, f32[2,64,1024]{2,1,0:T(8,128)}, u32[]{:S(2)}, u32[]{:S(2)}) collective-permute-start(f32[2,64,1024]{2,1,0:T(8,128)} %get-tuple-element.112), channel_id=1, source_target_pairs={{0,2},{2,4},{4,6},{6,0},{1,3},{3,5},{5,7},{7,1},{8,10},{10,12},{12... | collective-permute-start | bytes 1572872 | tf_op jit(solution)/shard_map/ppermute | solution.py:115
  124.6 13.0 %collective-permute-start.11 = (f32[2,64,1024]{2,1,0:T(8,128)}, f32[2,64,1024]{2,1,0:T(8,128)}, u32[]{:S(2)}, u32[]{:S(2)}) collective-permute-start(f32[2,64,1024]{2,1,0:T(8,128)} %get-tuple-element.113), channel_id=1, source_target_pairs={{0,6},{2,0},{4,2},{6,4},{1,7},{3,1},{5,3},{7,5},{8,14},{10,8},{12,... | collective-permute-start | bytes 1572872 | tf_op jit(solution)/shard_map/ppermute | solution.py:115
  137.3 14.0 %collective-permute-start.9 = (f32[2,64,1024]{2,1,0:T(8,128)}, f32[2,64,1024]{2,1,0:T(8,128)S(1)}, u32[]{:S(2)}, u32[]{:S(2)}) collective-permute-start(f32[2,64,1024]{2,1,0:T(8,128)} %collective-permute-done.8), channel_id=1, source_target_pairs={{0,2},{2,4},{4,6},{6,0},{1,3},{3,5},{5,7},{7,1},{8,10},{10,12},{12... | collective-permute-start | bytes 1572872 | tf_op jit(solution)/shard_map/ppermute | solution.py:115
  137.6 14.7 %collective-permute-start.12 = (f32[2,64,1024]{2,1,0:T(8,128)}, f32[2,64,1024]{2,1,0:T(8,128)S(1)}, u32[]{:S(2)}, u32[]{:S(2)}) collective-permute-start(f32[2,64,1024]{2,1,0:T(8,128)} %collective-permute-done.11), channel_id=1, source_target_pairs={{0,6},{2,0},{4,2},{6,4},{1,7},{3,1},{5,3},{7,5},{8,14},{10,8},{12,... | collective-permute-start | bytes 1572872 | tf_op jit(solution)/shard_map/ppermute | solution.py:115
  178.3 23.7 %collective-permute-start.17 = (f32[2,64,1024]{2,1,0:T(8,128)S(1)}, f32[2,64,1024]{2,1,0:T(8,128)S(1)}, u32[]{:S(2)}, u32[]{:S(2)}) collective-permute-start(f32[2,64,1024]{2,1,0:T(8,128)S(1)} %dynamic-slice_bitcast_fusion.4), channel_id=1, source_target_pairs={{0,6},{2,0},{4,2},{6,4},{1,7},{3,1},{5,3},{7,5},{8,14},{10,8},{12,... | collective-permute-start | bytes 1572872 | tf_op jit(solution)/shard_map/ppermute | solution.py:95
  182.1 27.3 %collective-permute-start.14 = (f32[2,64,1024]{2,1,0:T(8,128)S(1)}, f32[2,64,1024]{2,1,0:T(8,128)S(1)}, u32[]{:S(2)}, u32[]{:S(2)}) collective-permute-start(f32[2,64,1024]{2,1,0:T(8,128)S(1)} %dynamic-slice_bitcast_fusion.5), channel_id=1, source_target_pairs={{0,2},{2,4},{4,6},{6,0},{1,3},{3,5},{5,7},{7,1},{8,10},{10,12},{12... | collective-permute-start | bytes 1572872 | tf_op jit(solution)/shard_map/ppermute | solution.py:95
  198.7 15.7 %collective-permute-start.31 = (f32[2,64,1024]{2,1,0:T(8,128)S(1)}, f32[2,64,1024]{2,1,0:T(8,128)S(1)}, u32[]{:S(2)}, u32[]{:S(2)}) collective-permute-start(f32[2,64,1024]{2,1,0:T(8,128)S(1)} %dynamic-slice_bitcast_fusion.2), channel_id=1, source_target_pairs={{0,6},{2,0},{4,2},{6,4},{1,7},{3,1},{5,3},{7,5},{8,14},{10,8},{12,... | collective-permute-start | bytes 1572872 | tf_op jit(solution)/shard_map/ppermute | solution.py:95
  202.0 18.7 %collective-permute-start.28 = (f32[2,64,1024]{2,1,0:T(8,128)S(1)}, f32[2,64,1024]{2,1,0:T(8,128)S(1)}, u32[]{:S(2)}, u32[]{:S(2)}) collective-permute-start(f32[2,64,1024]{2,1,0:T(8,128)S(1)} %dynamic-slice_bitcast_fusion.3), channel_id=1, source_target_pairs={{0,2},{2,4},{4,6},{6,0},{1,3},{3,5},{5,7},{7,1},{8,10},{10,12},{12... | collective-permute-start | bytes 1572872 | tf_op jit(solution)/shard_map/ppermute | solution.py:95
  202.2 23.4 %collective-permute-start.18 = (f32[2,64,1024]{2,1,0:T(8,128)S(1)}, f32[2,64,1024]{2,1,0:T(8,128)S(1)}, u32[]{:S(2)}, u32[]{:S(2)}) collective-permute-start(f32[2,64,1024]{2,1,0:T(8,128)S(1)} %bitcast_add_fusion.15), channel_id=1, source_target_pairs={{0,6},{2,0},{4,2},{6,4},{1,7},{3,1},{5,3},{7,5},{8,14},{10,8},{12,... | collective-permute-start | bytes 1572872 | tf_op jit(solution)/shard_map/ppermute | solution.py:95
  209.5 22.4 %collective-permute-start.15 = (f32[2,64,1024]{2,1,0:T(8,128)S(1)}, f32[2,64,1024]{2,1,0:T(8,128)S(1)}, u32[]{:S(2)}, u32[]{:S(2)}) collective-permute-start(f32[2,64,1024]{2,1,0:T(8,128)S(1)} %bitcast_add_fusion.18), channel_id=1, source_target_pairs={{0,2},{2,4},{4,6},{6,0},{1,3},{3,5},{5,7},{7,1},{8,10},{10,12},{12... | collective-permute-start | bytes 1572872 | tf_op jit(solution)/shard_map/ppermute | solution.py:95
  214.4 22.4 %collective-permute-start.32 = (f32[2,64,1024]{2,1,0:T(8,128)S(1)}, f32[2,64,1024]{2,1,0:T(8,128)S(1)}, u32[]{:S(2)}, u32[]{:S(2)}) collective-permute-start(f32[2,64,1024]{2,1,0:T(8,128)S(1)} %bitcast_add_fusion.9), channel_id=1, source_target_pairs={{0,6},{2,0},{4,2},{6,4},{1,7},{3,1},{5,3},{7,5},{8,14},{10,8},{12,... | collective-permute-start | bytes 1572872 | tf_op jit(solution)/shard_map/ppermute | solution.py:95
  220.8 22.4 %collective-permute-start.29 = (f32[2,64,1024]{2,1,0:T(8,128)S(1)}, f32[2,64,1024]{2,1,0:T(8,128)S(1)}, u32[]{:S(2)}, u32[]{:S(2)}) collective-permute-start(f32[2,64,1024]{2,1,0:T(8,128)S(1)} %bitcast_add_fusion.12), channel_id=1, source_target_pairs={{0,2},{2,4},{4,6},{6,0},{1,3},{3,5},{5,7},{7,1},{8,10},{10,12},{12... | collective-permute-start | bytes 1572872 | tf_op jit(solution)/shard_map/ppermute | solution.py:95
  225.7 17.7 %collective-permute-start.19 = (f32[2,64,1024]{2,1,0:T(8,128)S(1)}, f32[2,64,1024]{2,1,0:T(8,128)S(1)}, u32[]{:S(2)}, u32[]{:S(2)}) collective-permute-start(f32[2,64,1024]{2,1,0:T(8,128)S(1)} %bitcast_add_fusion.14), channel_id=1, source_target_pairs={{0,6},{2,0},{4,2},{6,4},{1,7},{3,1},{5,3},{7,5},{8,14},{10,8},{12,... | collective-permute-start | bytes 1572872 | tf_op jit(solution)/shard_map/ppermute | solution.py:95
  232.0 20.1 %collective-permute-start.16 = (f32[2,64,1024]{2,1,0:T(8,128)S(1)}, f32[2,64,1024]{2,1,0:T(8,128)S(1)}, u32[]{:S(2)}, u32[]{:S(2)}) collective-permute-start(f32[2,64,1024]{2,1,0:T(8,128)S(1)} %bitcast_add_fusion.17), channel_id=1, source_target_pairs={{0,2},{2,4},{4,6},{6,0},{1,3},{3,5},{5,7},{7,1},{8,10},{10,12},{12... | collective-permute-start | bytes 1572872 | tf_op jit(solution)/shard_map/ppermute | solution.py:95
  236.9 18.5 %collective-permute-start.33 = (f32[2,64,1024]{2,1,0:T(8,128)S(1)}, f32[2,64,1024]{2,1,0:T(8,128)S(1)}, u32[]{:S(2)}, u32[]{:S(2)}) collective-permute-start(f32[2,64,1024]{2,1,0:T(8,128)S(1)} %bitcast_add_fusion.8), channel_id=1, source_target_pairs={{0,6},{2,0},{4,2},{6,4},{1,7},{3,1},{5,3},{7,5},{8,14},{10,8},{12,... | collective-permute-start | bytes 1572872 | tf_op jit(solution)/shard_map/ppermute | solution.py:95
  243.2 14.5 %collective-permute-start.30 = (f32[2,64,1024]{2,1,0:T(8,128)S(1)}, f32[2,64,1024]{2,1,0:T(8,128)S(1)}, u32[]{:S(2)}, u32[]{:S(2)}) collective-permute-start(f32[2,64,1024]{2,1,0:T(8,128)S(1)} %bitcast_add_fusion.11), channel_id=1, source_target_pairs={{0,2},{2,4},{4,6},{6,0},{1,3},{3,5},{5,7},{7,1},{8,10},{10,12},{12... | collective-permute-start | bytes 1572872 | tf_op jit(solution)/shard_map/ppermute | solution.py:95
  252.3 16.4 %collective-permute-start.20 = (f32[2,64,1024]{2,1,0:T(8,128)S(1)}, f32[2,64,1024]{2,1,0:T(8,128)S(1)}, u32[]{:S(2)}, u32[]{:S(2)}) collective-permute-start(f32[2,64,1024]{2,1,0:T(8,128)S(1)} %fusion.45), channel_id=1, source_target_pairs={{0,1},{1,0},{2,3},{3,2},{4,5},{5,4},{6,7},{7,6},{8,9},{9,8},{10,11... | collective-permute-start | bytes 1572872 | tf_op jit(solution)/shard_map/ppermute | solution.py:105
  257.9 22.1 %collective-permute-start.34 = (f32[2,64,1024]{2,1,0:T(8,128)S(1)}, f32[2,64,1024]{2,1,0:T(8,128)S(1)}, u32[]{:S(2)}, u32[]{:S(2)}) collective-permute-start(f32[2,64,1024]{2,1,0:T(8,128)S(1)} %fusion.40), channel_id=1, source_target_pairs={{0,1},{1,0},{2,3},{3,2},{4,5},{5,4},{6,7},{7,6},{8,9},{9,8},{10,11... | collective-permute-start | bytes 1572872 | tf_op jit(solution)/shard_map/ppermute | solution.py:105
  268.8 19.2 %collective-permute-start.21 = (f32[2,64,1024]{2,1,0:T(8,128)S(1)}, f32[2,64,1024]{2,1,0:T(8,128)S(1)}, u32[]{:S(2)}, u32[]{:S(2)}) collective-permute-start(f32[2,64,1024]{2,1,0:T(8,128)S(1)} %fusion.48), channel_id=1, source_target_pairs={{0,1},{1,0},{2,3},{3,2},{4,5},{5,4},{6,7},{7,6},{8,9},{9,8},{10,11... | collective-permute-start | bytes 1572872 | tf_op jit(solution)/shard_map/ppermute | solution.py:107
  280.0 13.6 %collective-permute-start.35 = (f32[2,64,1024]{2,1,0:T(8,128)S(1)}, f32[2,64,1024]{2,1,0:T(8,128)S(1)}, u32[]{:S(2)}, u32[]{:S(2)}) collective-permute-start(f32[2,64,1024]{2,1,0:T(8,128)S(1)} %fusion.43), channel_id=1, source_target_pairs={{0,1},{1,0},{2,3},{3,2},{4,5},{5,4},{6,7},{7,6},{8,9},{9,8},{10,11... | collective-permute-start | bytes 1572872 | tf_op jit(solution)/shard_map/ppermute | solution.py:107
  288.2 16.1 %collective-permute-start.22 = (f32[2,64,1024]{2,1,0:T(8,128)S(1)}, f32[2,64,1024]{2,1,0:T(8,128)S(1)}, u32[]{:S(2)}, u32[]{:S(2)}) collective-permute-start(f32[2,64,1024]{2,1,0:T(8,128)S(1)} %get-tuple-element.110), channel_id=1, source_target_pairs={{0,2},{2,4},{4,6},{6,0},{1,3},{3,5},{5,7},{7,1},{8,10},{10,12},{12... | collective-permute-start | bytes 1572872 | tf_op jit(solution)/shard_map/ppermute | solution.py:115
  288.3 16.1 %collective-permute-start.25 = (f32[2,64,1024]{2,1,0:T(8,128)S(1)}, f32[2,64,1024]{2,1,0:T(8,128)S(1)}, u32[]{:S(2)}, u32[]{:S(2)}) collective-permute-start(f32[2,64,1024]{2,1,0:T(8,128)S(1)} %get-tuple-element.111), channel_id=1, source_target_pairs={{0,6},{2,0},{4,2},{6,4},{1,7},{3,1},{5,3},{7,5},{8,14},{10,8},{12,... | collective-permute-start | bytes 1572872 | tf_op jit(solution)/shard_map/ppermute | solution.py:115
  293.8 21.8 %collective-permute-start.36 = (f32[2,64,1024]{2,1,0:T(8,128)S(1)}, f32[2,64,1024]{2,1,0:T(8,128)S(1)}, u32[]{:S(2)}, u32[]{:S(2)}) collective-permute-start(f32[2,64,1024]{2,1,0:T(8,128)S(1)} %get-tuple-element.108), channel_id=1, source_target_pairs={{0,2},{2,4},{4,6},{6,0},{1,3},{3,5},{5,7},{7,1},{8,10},{10,12},{12... | collective-permute-start | bytes 1572872 | tf_op jit(solution)/shard_map/ppermute | solution.py:115
  294.2 21.5 %collective-permute-start.39 = (f32[2,64,1024]{2,1,0:T(8,128)S(1)}, f32[2,64,1024]{2,1,0:T(8,128)S(1)}, u32[]{:S(2)}, u32[]{:S(2)}) collective-permute-start(f32[2,64,1024]{2,1,0:T(8,128)S(1)} %get-tuple-element.109), channel_id=1, source_target_pairs={{0,6},{2,0},{4,2},{6,4},{1,7},{3,1},{5,3},{7,5},{8,14},{10,8},{12,... | collective-permute-start | bytes 1572872 | tf_op jit(solution)/shard_map/ppermute | solution.py:115
  304.4 22.5 %collective-permute-start.23 = (f32[2,64,1024]{2,1,0:T(8,128)S(1)}, f32[2,64,1024]{2,1,0:T(8,128)S(1)}, u32[]{:S(2)}, u32[]{:S(2)}) collective-permute-start(f32[2,64,1024]{2,1,0:T(8,128)S(1)} %collective-permute-done.22), channel_id=1, source_target_pairs={{0,2},{2,4},{4,6},{6,0},{1,3},{3,5},{5,7},{7,1},{8,10},{10,12},{12... | collective-permute-start | bytes 1572872 | tf_op jit(solution)/shard_map/ppermute | solution.py:115
  304.4 22.5 %collective-permute-start.26 = (f32[2,64,1024]{2,1,0:T(8,128)S(1)}, f32[2,64,1024]{2,1,0:T(8,128)S(1)}, u32[]{:S(2)}, u32[]{:S(2)}) collective-permute-start(f32[2,64,1024]{2,1,0:T(8,128)S(1)} %collective-permute-done.25), channel_id=1, source_target_pairs={{0,6},{2,0},{4,2},{6,4},{1,7},{3,1},{5,3},{7,5},{8,14},{10,8},{12,... | collective-permute-start | bytes 1572872 | tf_op jit(solution)/shard_map/ppermute | solution.py:115
  315.6 22.5 %collective-permute-start.37 = (f32[2,64,1024]{2,1,0:T(8,128)S(1)}, f32[2,64,1024]{2,1,0:T(8,128)S(1)}, u32[]{:S(2)}, u32[]{:S(2)}) collective-permute-start(f32[2,64,1024]{2,1,0:T(8,128)S(1)} %collective-permute-done.36), channel_id=1, source_target_pairs={{0,2},{2,4},{4,6},{6,0},{1,3},{3,5},{5,7},{7,1},{8,10},{10,12},{12... | collective-permute-start | bytes 1572872 | tf_op jit(solution)/shard_map/ppermute | solution.py:115
  315.7 22.5 %collective-permute-start.40 = (f32[2,64,1024]{2,1,0:T(8,128)S(1)}, f32[2,64,1024]{2,1,0:T(8,128)S(1)}, u32[]{:S(2)}, u32[]{:S(2)}) collective-permute-start(f32[2,64,1024]{2,1,0:T(8,128)S(1)} %collective-permute-done.39), channel_id=1, source_target_pairs={{0,6},{2,0},{4,2},{6,4},{1,7},{3,1},{5,3},{7,5},{8,14},{10,8},{12,... | collective-permute-start | bytes 1572872 | tf_op jit(solution)/shard_map/ppermute | solution.py:115
  326.8 26.1 %collective-permute-start.24 = (f32[2,64,1024]{2,1,0:T(8,128)S(1)}, f32[2,64,1024]{2,1,0:T(8,128)S(1)}, u32[]{:S(2)}, u32[]{:S(2)}) collective-permute-start(f32[2,64,1024]{2,1,0:T(8,128)S(1)} %collective-permute-done.23), channel_id=1, source_target_pairs={{0,2},{2,4},{4,6},{6,0},{1,3},{3,5},{5,7},{7,1},{8,10},{10,12},{12... | collective-permute-start | bytes 1572872 | tf_op jit(solution)/shard_map/ppermute | solution.py:115
  326.8 26.1 %collective-permute-start.27 = (f32[2,64,1024]{2,1,0:T(8,128)S(1)}, f32[2,64,1024]{2,1,0:T(8,128)S(1)}, u32[]{:S(2)}, u32[]{:S(2)}) collective-permute-start(f32[2,64,1024]{2,1,0:T(8,128)S(1)} %collective-permute-done.26), channel_id=1, source_target_pairs={{0,6},{2,0},{4,2},{6,4},{1,7},{3,1},{5,3},{7,5},{8,14},{10,8},{12,... | collective-permute-start | bytes 1572872 | tf_op jit(solution)/shard_map/ppermute | solution.py:115
  338.1 12.8 %collective-permute-start.38 = (f32[2,64,1024]{2,1,0:T(8,128)S(1)}, f32[2,64,1024]{2,1,0:T(8,128)S(1)}, u32[]{:S(2)}, u32[]{:S(2)}) collective-permute-start(f32[2,64,1024]{2,1,0:T(8,128)S(1)} %collective-permute-done.37), channel_id=1, source_target_pairs={{0,2},{2,4},{4,6},{6,0},{1,3},{3,5},{5,7},{7,1},{8,10},{10,12},{12... | collective-permute-start | bytes 1572872 | tf_op jit(solution)/shard_map/ppermute | solution.py:115
  338.2 12.7 %collective-permute-start.41 = (f32[2,64,1024]{2,1,0:T(8,128)S(1)}, f32[2,64,1024]{2,1,0:T(8,128)S(1)}, u32[]{:S(2)}, u32[]{:S(2)}) collective-permute-start(f32[2,64,1024]{2,1,0:T(8,128)S(1)} %collective-permute-done.40), channel_id=1, source_target_pairs={{0,6},{2,0},{4,2},{6,4},{1,7},{3,1},{5,3},{7,5},{8,14},{10,8},{12,... | collective-permute-start | bytes 1572872 | tf_op jit(solution)/shard_map/ppermute | solution.py:115
  387.9 14.6 %collective-permute-start.45 = (f32[2,64,1024]{2,1,0:T(8,128)S(1)}, f32[2,64,1024]{2,1,0:T(8,128)S(1)}, u32[]{:S(2)}, u32[]{:S(2)}) collective-permute-start(f32[2,64,1024]{2,1,0:T(8,128)S(1)} %dynamic-slice_bitcast_fusion), channel_id=1, source_target_pairs={{0,6},{2,0},{4,2},{6,4},{1,7},{3,1},{5,3},{7,5},{8,14},{10,8},{12,... | collective-permute-start | bytes 1572872 | tf_op jit(solution)/shard_map/ppermute | solution.py:95
  391.3 15.0 %collective-permute-start.42 = (f32[2,64,1024]{2,1,0:T(8,128)S(1)}, f32[2,64,1024]{2,1,0:T(8,128)S(1)}, u32[]{:S(2)}, u32[]{:S(2)}) collective-permute-start(f32[2,64,1024]{2,1,0:T(8,128)S(1)} %dynamic-slice_bitcast_fusion.1), channel_id=1, source_target_pairs={{0,2},{2,4},{4,6},{6,0},{1,3},{3,5},{5,7},{7,1},{8,10},{10,12},{12... | collective-permute-start | bytes 1572872 | tf_op jit(solution)/shard_map/ppermute | solution.py:95
  402.6 14.2 %collective-permute-start.46 = (f32[2,64,1024]{2,1,0:T(8,128)S(1)}, f32[2,64,1024]{2,1,0:T(8,128)S(1)}, u32[]{:S(2)}, u32[]{:S(2)}) collective-permute-start(f32[2,64,1024]{2,1,0:T(8,128)S(1)} %bitcast_add_fusion.3), channel_id=1, source_target_pairs={{0,6},{2,0},{4,2},{6,4},{1,7},{3,1},{5,3},{7,5},{8,14},{10,8},{12,... | collective-permute-start | bytes 1572872 | tf_op jit(solution)/shard_map/ppermute | solution.py:95
  406.4 14.2 %collective-permute-start.43 = (f32[2,64,1024]{2,1,0:T(8,128)S(1)}, f32[2,64,1024]{2,1,0:T(8,128)S(1)}, u32[]{:S(2)}, u32[]{:S(2)}) collective-permute-start(f32[2,64,1024]{2,1,0:T(8,128)S(1)} %bitcast_add_fusion.6), channel_id=1, source_target_pairs={{0,2},{2,4},{4,6},{6,0},{1,3},{3,5},{5,7},{7,1},{8,10},{10,12},{12... | collective-permute-start | bytes 1572872 | tf_op jit(solution)/shard_map/ppermute | solution.py:95
  431.3 20.4 %collective-permute-start.48 = (f32[2,64,1024]{2,1,0:T(8,128)S(1)}, f32[2,64,1024]{2,1,0:T(8,128)S(1)}, u32[]{:S(2)}, u32[]{:S(2)}) collective-permute-start(f32[2,64,1024]{2,1,0:T(8,128)S(1)} %fusion.35), channel_id=1, source_target_pairs={{0,1},{1,0},{2,3},{3,2},{4,5},{5,4},{6,7},{7,6},{8,9},{9,8},{10,11... | collective-permute-start | bytes 1572872 | tf_op jit(solution)/shard_map/ppermute | solution.py:105
  451.8 15.1 %collective-permute-start.49 = (f32[2,64,1024]{2,1,0:T(8,128)S(1)}, f32[2,64,1024]{2,1,0:T(8,128)S(1)}, u32[]{:S(2)}, u32[]{:S(2)}) collective-permute-start(f32[2,64,1024]{2,1,0:T(8,128)S(1)} %fusion.38), channel_id=1, source_target_pairs={{0,1},{1,0},{2,3},{3,2},{4,5},{5,4},{6,7},{7,6},{8,9},{9,8},{10,11... | collective-permute-start | bytes 1572872 | tf_op jit(solution)/shard_map/ppermute | solution.py:107
  467.2 12.1 %collective-permute-start.50 = (f32[2,64,1024]{2,1,0:T(8,128)S(1)}, f32[2,64,1024]{2,1,0:T(8,128)S(1)}, u32[]{:S(2)}, u32[]{:S(2)}) collective-permute-start(f32[2,64,1024]{2,1,0:T(8,128)S(1)} %get-tuple-element.106), channel_id=1, source_target_pairs={{0,2},{2,4},{4,6},{6,0},{1,3},{3,5},{5,7},{7,1},{8,10},{10,12},{12... | collective-permute-start | bytes 1572872 | tf_op jit(solution)/shard_map/ppermute | solution.py:115
  467.2 12.3 %collective-permute-start.53 = (f32[2,64,1024]{2,1,0:T(8,128)S(1)}, f32[2,64,1024]{2,1,0:T(8,128)S(1)}, u32[]{:S(2)}, u32[]{:S(2)}) collective-permute-start(f32[2,64,1024]{2,1,0:T(8,128)S(1)} %get-tuple-element.107), channel_id=1, source_target_pairs={{0,6},{2,0},{4,2},{6,4},{1,7},{3,1},{5,3},{7,5},{8,14},{10,8},{12,... | collective-permute-start | bytes 1572872 | tf_op jit(solution)/shard_map/ppermute | solution.py:115
  (78 other events, 561.4 us)
Sparse Core Ops, SparseCore 0:
  385.3 162.0 all-reduce.3
where the time goes:
time: 587 us; the launch traced here: 583 us
  waiting for transfers between devices  298 us (51%)
  starting transfers between devices  127 us (22%)
  other arithmetic  57 us (10%)
  matrix products  45.7 us (8%)
  local copies, waits for them, and re-layouts  39.7 us (7%)
  between operations  15.9 us (3%)
    ppermute x24, waiting for transfers between devices, tensor_sum(): acc = lax.ppermute(acc, 'ty', ring(ny, shift))  98.2 us
    ppermute x24, waiting for transfers between devices, tensor_sum(): cur = lax.ppermute(cur, 'ty', ring(ny, shift))  86.5 us
    ppermute x24, starting transfers between devices, tensor_sum(): acc = lax.ppermute(acc, 'ty', ring(ny, shift))  55 us
    psum x1, waiting for transfers between devices, per_device(): lax.psum(dp_sums, 'dp')  44.2 us
    ppermute x24, starting transfers between devices, tensor_sum(): cur = lax.ppermute(cur, 'ty', ring(ny, shift))  39.9 us
    ppermute x4, waiting for transfers between devices, tensor_sum(): got = lax.ppermute(send, 'tx', pairs)  39.8 us
    ppermute x4, waiting for transfers between devices, tensor_sum(): other = lax.ppermute(mine, 'tx', pairs)  26.7 us
    unnamed x138, local copies, waits for them, and re-layouts  17.1 us
  transfers between devices with their start and end apart: 60, of which 39 were waited for; matrix products, arithmetic and copies ran while one was open for 7% of the time, Pallas kernels for 0%

commit v1 on v0

--- a/solution.py
+++ b/solution.py
@@ -121,6 +121,11 @@
     return result, total
 
 
+def split_tensor_sum(values, pieces=2):
+    blocks = jnp.split(values, pieces, axis=0)
+    return jnp.concatenate([tensor_sum(block) for block in blocks], axis=0)
+
+
 def small_tensor_sum(values):
     ny = lax.axis_size("ty")
     nx = lax.axis_size("tx")
@@ -191,7 +196,7 @@
         "kgij,jkd->ikgd", attn_probs, v_half, preferred_element_type=jnp.float32
     )
     attn_mixed = attn_mixed.reshape(length, q_heads * head_size).astype(jnp.bfloat16)
-    attn_sum = tensor_sum(jnp.dot(attn_mixed, w_out, preferred_element_type=jnp.float32))
+    attn_sum = split_tensor_sum(jnp.dot(attn_mixed, w_out, preferred_element_type=jnp.float32))
     residual = tokens_wide + attn_sum
     scale_two = rms_scale(residual)
     normed_two = (residual * scale_two * ffn_gain).astype(jnp.bfloat16)
@@ -199,7 +204,7 @@
     up_proj = jnp.dot(normed_two, w_up, preferred_element_type=jnp.float32)
     gate_sigmoid = jax.nn.sigmoid(gate_proj)
     hidden = (gate_proj * gate_sigmoid * up_proj).astype(jnp.bfloat16)
-    mlp_sum = tensor_sum(jnp.dot(hidden, w_down, preferred_element_type=jnp.float32))
+    mlp_sum = split_tensor_sum(jnp.dot(hidden, w_down, preferred_element_type=jnp.float32))
     output = (residual + mlp_sum).astype(jnp.bfloat16)
     down_grad = outer(hidden, cotangent)
     hidden_grad = inner(cotangent, w_down)
@@ -209,7 +214,7 @@
     up_grad = (hidden_grad * gate_proj * gate_sigmoid).astype(jnp.bfloat16)
     gate_w_grad = outer(normed_two, gate_grad)
     up_w_grad = outer(normed_two, up_grad)
-    normed_two_grad = tensor_sum(inner(gate_grad, w_gate) + inner(up_grad, w_up))
+    normed_two_grad = split_tensor_sum(inner(gate_grad, w_gate) + inner(up_grad, w_up))
     ffn_grad = jnp.sum(normed_two_grad * residual * scale_two, axis=0)
     residual_grad = cotangent.astype(jnp.float32) + rms_back(
         normed_two_grad, residual, scale_two, ffn_gain
@@ -281,7 +286,7 @@
         up_w_grad,
         down_grad,
     ) = lax.psum(dp_sums, "dp")
-    normed_one_grad = tensor_sum(one_partial)
+    normed_one_grad = split_tensor_sum(one_partial)
     input_grad = residual_grad + rms_back(normed_one_grad, tokens_wide, scale_one, attn_gain)
     out_w_grad = out_pack[:out_rows]
     ffn_grad = out_pack[out_rows]

time: 587 us -> 582 us (level)
  waiting for transfers between devices: 298 us -> 233 us
  starting transfers between devices: 127 us -> 174 us
    ppermute x24 -> x48, waiting for transfers between devices: 98.2 us -> 60.9 us  [tensor_sum(): acc = lax.ppermute(acc, 'ty', ring(ny, shift))]
    psum x1, waiting for transfers between devices: 44.2 us -> 73 us  [per_device(): lax.psum(dp_sums, 'dp')]
    ppermute x24 -> x48, starting transfers between devices: 39.9 us -> 66.9 us  [tensor_sum(): cur = lax.ppermute(cur, 'ty', ring(ny, shift))]
    ppermute x24 -> x48, waiting for transfers between devices: 86.5 us -> 62.4 us  [tensor_sum(): cur = lax.ppermute(cur, 'ty', ring(ny, shift))]
    ppermute x4 -> x8, waiting for transfers between devices: 26.7 us -> 9.57 us  [tensor_sum(): other = lax.ppermute(mine, 'tx', pairs)]
    ppermute x4 -> x8, waiting for transfers between devices: 39.8 us -> 24.8 us  [tensor_sum(): got = lax.ppermute(send, 'tx', pairs)]
    ppermute x4 -> x8, starting transfers between devices: 12.9 us -> 24.8 us  [tensor_sum(): other = lax.ppermute(mine, 'tx', pairs)]
    ppermute x4 -> x8, starting transfers between devices: 12.3 us -> 20.8 us  [tensor_sum(): got = lax.ppermute(send, 'tx', pairs)]
  transfers between devices with their start and end apart: 60 -> 116, of which waited for: 39 -> 67; matrix products, arithmetic and copies ran while one was open for 7% -> 7% of each run, Pallas kernels for 0% -> 0%
where the time goes in v1:
time: 582 us; the launch traced here: 573 us
  waiting for transfers between devices  233 us (40%)
  starting transfers between devices  174 us (30%)
  other arithmetic  61.6 us (11%)
  matrix products  47.6 us (8%)
  local copies, waits for them, and re-layouts  40.1 us (7%)
  between operations  16.5 us (3%)
    psum x1, waiting for transfers between devices, per_device(): lax.psum(dp_sums, 'dp')  73 us
    ppermute x48, starting transfers between devices, tensor_sum(): cur = lax.ppermute(cur, 'ty', ring(ny, shift))  66.9 us
    ppermute x48, waiting for transfers between devices, tensor_sum(): cur = lax.ppermute(cur, 'ty', ring(ny, shift))  62.4 us
    ppermute x48, waiting for transfers between devices, tensor_sum(): acc = lax.ppermute(acc, 'ty', ring(ny, shift))  60.9 us
    ppermute x48, starting transfers between devices, tensor_sum(): acc = lax.ppermute(acc, 'ty', ring(ny, shift))  54.3 us
    ppermute x8, waiting for transfers between devices, tensor_sum(): got = lax.ppermute(send, 'tx', pairs)  24.8 us
    ppermute x8, starting transfers between devices, tensor_sum(): other = lax.ppermute(mine, 'tx', pairs)  24.8 us
    ppermute x8, starting transfers between devices, tensor_sum(): got = lax.ppermute(send, 'tx', pairs)  20.8 us
  transfers between devices with their start and end apart: 116, of which 67 were waited for; matrix products, arithmetic and copies ran while one was open for 7% of the time, Pallas kernels for 0%

profile of v1, /device:TPU:0, one launch (start us, length us, event | category | flops | bytes accessed | tf_op | source)
XLA Modules:
  0.0 572.7 jit_solution(14372634924874406004)
XLA Ops:
  46.7 3.7 collective-permute-start.17
  53.3 3.3 collective-permute-start.4
  68.5 3.8 collective-permute-start.19
  75.2 4.0 collective-permute-done.2
  91.5 3.6 collective-permute-done.20
  106.1 3.3 collective-permute-start.25
  112.6 3.3 collective-permute-start.12
  118.2 3.3 collective-permute-start.26
  123.8 3.3 collective-permute-start.13
  129.4 3.5 collective-permute-start.27
  133.7 3.3 collective-permute-done.24
  167.2 3.3 collective-permute-start.59
  170.7 3.3 collective-permute-start.73
  174.2 3.3 collective-permute-start.32
  177.6 3.5 collective-permute-done.56
  183.3 3.4 collective-permute-done.70
  188.9 3.4 collective-permute-done.29
  194.5 3.4 collective-permute-done.43
  200.1 3.4 collective-permute-done.57
  205.7 3.4 collective-permute-done.71
  211.3 3.4 collective-permute-done.30
  265.1 3.5 collective-permute-done.50
  270.7 3.5 collective-permute-done.64
  276.3 3.5 collective-permute-done.78
  282.0 3.5 collective-permute-done.37
  287.6 3.5 collective-permute-done.51
  293.2 3.5 collective-permute-done.65
  298.8 3.5 collective-permute-done.79
  302.3 3.5 collective-permute-start.69
  305.9 8.2 %collective-permute-done.66 = f32[2,32,1024]{2,1,0:T(8,128)S(1)} collective-permute-done((f32[2,32,1024]{2,1,0:T(8,128)S(1)}, f32[2,32,1024]{2,1,0:T(8,128)S(1)}, u32[]{:S(2)}, u32[]{:S(2)}) %collective-permute-start.66) | collective-permute-done | bytes 262176 | tf_op jit(solution)/shard_map/ppermute | solution.py:115
  314.1 3.3 collective-permute-start.83
  317.7 4.0 collective-permute-done.80
  324.5 3.5 collective-permute-done.55
  329.5 5.3 multiply_add_fusion
  336.9 5.0 fusion
  345.7 5.5 fusion.18
  376.8 4.8 collective-permute-done.87
  395.8 3.3 collective-permute-start.103
  399.2 4.1 collective-permute-done.86
  409.9 7.1 %collective-permute-done.90 = f32[2,32,1024]{2,1,0:T(8,128)S(1)} collective-permute-done((f32[2,32,1024]{2,1,0:T(8,128)S(1)}, f32[2,32,1024]{2,1,0:T(8,128)S(1)}, u32[]{:S(2)}, u32[]{:S(2)}) %collective-permute-start.90) | collective-permute-done | bytes 262176 | tf_op jit(solution)/shard_map/ppermute | solution.py:105
  420.2 4.1 collective-permute-done.104
  436.3 3.3 collective-permute-start.109
  440.5 3.3 collective-permute-start.96
  446.6 3.4 collective-permute-start.110
  450.2 3.3 collective-permute-start.97
  454.2 3.4 collective-permute-start.111
  463.3 73.0 %all-reduce.4.cloned.1.call-done = (f32[136,1024]{1,0:T(8,128)}, f32[1024,128]{1,0:T(8,128)}, f32[1024,64]{0,1:T(8,128)}, f32[1024,64]{0,1:T(8,128)}, f32[1024,5...) async-done(((f32[136,1024]{1,0:T(8,128)}, f32[1024,128]{1,0:T(8,128)}, f32[1024,64]{0,1:T(8,128)}, f32[1024,64]{0,1:T(8,128)}, f32[1024,576]{0,1:T(8,128)}, ...) | async-done | bytes 8683536 | tf_op jit(solution)/shard_map/psum | solution.py:288
  550.6 3.8 fusion.13
  (599 shorter events, 304.4 us)
Async XLA Ops:
  7.2 529.1 %all-reduce.4.cloned.1.call-start = ((), (), s32[]{:S(2)}) async-start(), calls=%async_computation | async-start | bytes 17367040 | tf_op jit(solution)/shard_map/psum | solution.py:288
  68.5 13.9 %collective-permute-start.19 = (f32[2,32,1024]{2,1,0:T(8,128)S(1)}, f32[2,32,1024]{2,1,0:T(8,128)S(1)}, u32[]{:S(2)}, u32[]{:S(2)}) collective-permute-start(f32[2,32,1024]{2,1,0:T(8,128)S(1)} %bitcast_add_fusion.37), channel_id=1, source_target_pairs={{0,6},{2,0},{4,2},{6,4},{1,7},{3,1},{5,3},{7,5},{8,14},{10,8},{12,... | collective-permute-start | bytes 786440 | tf_op jit(solution)/shard_map/ppermute | solution.py:95
  88.4 12.3 %collective-permute-start.7 = (f32[2,32,1024]{2,1,0:T(8,128)}, f32[2,32,1024]{2,1,0:T(8,128)}, u32[]{:S(2)}, u32[]{:S(2)}) collective-permute-start(f32[2,32,1024]{2,1,0:T(8,128)} %fusion.72), channel_id=1, source_target_pairs={{0,1},{1,0},{2,3},{3,2},{4,5},{5,4},{6,7},{7,6},{8,9},{9,8},{10,11... | collective-permute-start | bytes 786440 | tf_op jit(solution)/shard_map/ppermute | solution.py:107
  105.9 12.3 %collective-permute-start.22 = (f32[2,32,1024]{2,1,0:T(8,128)S(1)}, f32[2,32,1024]{2,1,0:T(8,128)S(1)}, u32[]{:S(2)}, u32[]{:S(2)}) collective-permute-start(f32[2,32,1024]{2,1,0:T(8,128)S(1)} %get-tuple-element.131), channel_id=1, source_target_pairs={{0,2},{2,4},{4,6},{6,0},{1,3},{3,5},{5,7},{7,1},{8,10},{10,12},{12... | collective-permute-start | bytes 786440 | tf_op jit(solution)/shard_map/ppermute | solution.py:115
  106.1 12.1 %collective-permute-start.25 = (f32[2,32,1024]{2,1,0:T(8,128)S(1)}, f32[2,32,1024]{2,1,0:T(8,128)S(1)}, u32[]{:S(2)}, u32[]{:S(2)}) collective-permute-start(f32[2,32,1024]{2,1,0:T(8,128)S(1)} %get-tuple-element.132), channel_id=1, source_target_pairs={{0,6},{2,0},{4,2},{6,4},{1,7},{3,1},{5,3},{7,5},{8,14},{10,8},{12,... | collective-permute-start | bytes 786440 | tf_op jit(solution)/shard_map/ppermute | solution.py:115
  155.8 14.8 %collective-permute-start.31 = (f32[2,32,1024]{2,1,0:T(8,128)S(1)}, f32[2,32,1024]{2,1,0:T(8,128)S(1)}, u32[]{:S(2)}, u32[]{:S(2)}) collective-permute-start(f32[2,32,1024]{2,1,0:T(8,128)S(1)} %dynamic-slice_bitcast_fusion.10), channel_id=1, source_target_pairs={{0,6},{2,0},{4,2},{6,4},{1,7},{3,1},{5,3},{7,5},{8,14},{10,8},{12,... | collective-permute-start | bytes 786440 | tf_op jit(solution)/shard_map/ppermute | solution.py:95
  158.0 12.6 %collective-permute-start.28 = (f32[2,32,1024]{2,1,0:T(8,128)S(1)}, f32[2,32,1024]{2,1,0:T(8,128)S(1)}, u32[]{:S(2)}, u32[]{:S(2)}) collective-permute-start(f32[2,32,1024]{2,1,0:T(8,128)S(1)} %dynamic-slice_bitcast_fusion.11), channel_id=1, source_target_pairs={{0,2},{2,4},{4,6},{6,0},{1,3},{3,5},{5,7},{7,1},{8,10},{10,12},{12... | collective-permute-start | bytes 786440 | tf_op jit(solution)/shard_map/ppermute | solution.py:95
  158.6 15.4 %collective-permute-start.45 = (f32[2,32,1024]{2,1,0:T(8,128)S(1)}, f32[2,32,1024]{2,1,0:T(8,128)S(1)}, u32[]{:S(2)}, u32[]{:S(2)}) collective-permute-start(f32[2,32,1024]{2,1,0:T(8,128)S(1)} %dynamic-slice_bitcast_fusion.8), channel_id=1, source_target_pairs={{0,6},{2,0},{4,2},{6,4},{1,7},{3,1},{5,3},{7,5},{8,14},{10,8},{12,... | collective-permute-start | bytes 786440 | tf_op jit(solution)/shard_map/ppermute | solution.py:95
  161.9 12.3 %collective-permute-start.42 = (f32[2,32,1024]{2,1,0:T(8,128)S(1)}, f32[2,32,1024]{2,1,0:T(8,128)S(1)}, u32[]{:S(2)}, u32[]{:S(2)}) collective-permute-start(f32[2,32,1024]{2,1,0:T(8,128)S(1)} %dynamic-slice_bitcast_fusion.9), channel_id=1, source_target_pairs={{0,2},{2,4},{4,6},{6,0},{1,3},{3,5},{5,7},{7,1},{8,10},{10,12},{12... | collective-permute-start | bytes 786440 | tf_op jit(solution)/shard_map/ppermute | solution.py:95
  170.7 12.1 %collective-permute-start.73 = (f32[2,32,1024]{2,1,0:T(8,128)S(1)}, f32[2,32,1024]{2,1,0:T(8,128)S(1)}, u32[]{:S(2)}, u32[]{:S(2)}) collective-permute-start(f32[2,32,1024]{2,1,0:T(8,128)S(1)} %dynamic-slice_bitcast_fusion.4), channel_id=1, source_target_pairs={{0,6},{2,0},{4,2},{6,4},{1,7},{3,1},{5,3},{7,5},{8,14},{10,8},{12,... | collective-permute-start | bytes 786440 | tf_op jit(solution)/shard_map/ppermute | solution.py:95
  174.0 12.7 %collective-permute-start.70 = (f32[2,32,1024]{2,1,0:T(8,128)S(1)}, f32[2,32,1024]{2,1,0:T(8,128)S(1)}, u32[]{:S(2)}, u32[]{:S(2)}) collective-permute-start(f32[2,32,1024]{2,1,0:T(8,128)S(1)} %dynamic-slice_bitcast_fusion.5), channel_id=1, source_target_pairs={{0,2},{2,4},{4,6},{6,0},{1,3},{3,5},{5,7},{7,1},{8,10},{10,12},{12... | collective-permute-start | bytes 786440 | tf_op jit(solution)/shard_map/ppermute | solution.py:95
  174.2 14.3 %collective-permute-start.32 = (f32[2,32,1024]{2,1,0:T(8,128)S(1)}, f32[2,32,1024]{2,1,0:T(8,128)S(1)}, u32[]{:S(2)}, u32[]{:S(2)}) collective-permute-start(f32[2,32,1024]{2,1,0:T(8,128)S(1)} %bitcast_add_fusion.32), channel_id=1, source_target_pairs={{0,6},{2,0},{4,2},{6,4},{1,7},{3,1},{5,3},{7,5},{8,14},{10,8},{12,... | collective-permute-start | bytes 786440 | tf_op jit(solution)/shard_map/ppermute | solution.py:95
  177.5 14.8 %collective-permute-start.29 = (f32[2,32,1024]{2,1,0:T(8,128)S(1)}, f32[2,32,1024]{2,1,0:T(8,128)S(1)}, u32[]{:S(2)}, u32[]{:S(2)}) collective-permute-start(f32[2,32,1024]{2,1,0:T(8,128)S(1)} %bitcast_add_fusion.35), channel_id=1, source_target_pairs={{0,2},{2,4},{4,6},{6,0},{1,3},{3,5},{5,7},{7,1},{8,10},{10,12},{12... | collective-permute-start | bytes 786440 | tf_op jit(solution)/shard_map/ppermute | solution.py:95
  181.1 13.0 %collective-permute-start.46 = (f32[2,32,1024]{2,1,0:T(8,128)S(1)}, f32[2,32,1024]{2,1,0:T(8,128)S(1)}, u32[]{:S(2)}, u32[]{:S(2)}) collective-permute-start(f32[2,32,1024]{2,1,0:T(8,128)S(1)} %bitcast_add_fusion.26), channel_id=1, source_target_pairs={{0,6},{2,0},{4,2},{6,4},{1,7},{3,1},{5,3},{7,5},{8,14},{10,8},{12,... | collective-permute-start | bytes 786440 | tf_op jit(solution)/shard_map/ppermute | solution.py:95
  182.8 15.1 %collective-permute-start.43 = (f32[2,32,1024]{2,1,0:T(8,128)S(1)}, f32[2,32,1024]{2,1,0:T(8,128)S(1)}, u32[]{:S(2)}, u32[]{:S(2)}) collective-permute-start(f32[2,32,1024]{2,1,0:T(8,128)S(1)} %bitcast_add_fusion.29), channel_id=1, source_target_pairs={{0,2},{2,4},{4,6},{6,0},{1,3},{3,5},{5,7},{7,1},{8,10},{10,12},{12... | collective-permute-start | bytes 786440 | tf_op jit(solution)/shard_map/ppermute | solution.py:95
  186.7 13.0 %collective-permute-start.60 = (f32[2,32,1024]{2,1,0:T(8,128)S(1)}, f32[2,32,1024]{2,1,0:T(8,128)S(1)}, u32[]{:S(2)}, u32[]{:S(2)}) collective-permute-start(f32[2,32,1024]{2,1,0:T(8,128)S(1)} %bitcast_add_fusion.20), channel_id=1, source_target_pairs={{0,6},{2,0},{4,2},{6,4},{1,7},{3,1},{5,3},{7,5},{8,14},{10,8},{12,... | collective-permute-start | bytes 786440 | tf_op jit(solution)/shard_map/ppermute | solution.py:95
  188.5 15.1 %collective-permute-start.57 = (f32[2,32,1024]{2,1,0:T(8,128)S(1)}, f32[2,32,1024]{2,1,0:T(8,128)S(1)}, u32[]{:S(2)}, u32[]{:S(2)}) collective-permute-start(f32[2,32,1024]{2,1,0:T(8,128)S(1)} %bitcast_add_fusion.23), channel_id=1, source_target_pairs={{0,2},{2,4},{4,6},{6,0},{1,3},{3,5},{5,7},{7,1},{8,10},{10,12},{12... | collective-permute-start | bytes 786440 | tf_op jit(solution)/shard_map/ppermute | solution.py:95
  192.3 13.0 %collective-permute-start.74 = (f32[2,32,1024]{2,1,0:T(8,128)S(1)}, f32[2,32,1024]{2,1,0:T(8,128)S(1)}, u32[]{:S(2)}, u32[]{:S(2)}) collective-permute-start(f32[2,32,1024]{2,1,0:T(8,128)S(1)} %bitcast_add_fusion.14), channel_id=1, source_target_pairs={{0,6},{2,0},{4,2},{6,4},{1,7},{3,1},{5,3},{7,5},{8,14},{10,8},{12,... | collective-permute-start | bytes 786440 | tf_op jit(solution)/shard_map/ppermute | solution.py:95
  194.1 15.1 %collective-permute-start.71 = (f32[2,32,1024]{2,1,0:T(8,128)S(1)}, f32[2,32,1024]{2,1,0:T(8,128)S(1)}, u32[]{:S(2)}, u32[]{:S(2)}) collective-permute-start(f32[2,32,1024]{2,1,0:T(8,128)S(1)} %bitcast_add_fusion.17), channel_id=1, source_target_pairs={{0,2},{2,4},{4,6},{6,0},{1,3},{3,5},{5,7},{7,1},{8,10},{10,12},{12... | collective-permute-start | bytes 786440 | tf_op jit(solution)/shard_map/ppermute | solution.py:95
  197.9 13.0 %collective-permute-start.33 = (f32[2,32,1024]{2,1,0:T(8,128)S(1)}, f32[2,32,1024]{2,1,0:T(8,128)S(1)}, u32[]{:S(2)}, u32[]{:S(2)}) collective-permute-start(f32[2,32,1024]{2,1,0:T(8,128)S(1)} %bitcast_add_fusion.31), channel_id=1, source_target_pairs={{0,6},{2,0},{4,2},{6,4},{1,7},{3,1},{5,3},{7,5},{8,14},{10,8},{12,... | collective-permute-start | bytes 786440 | tf_op jit(solution)/shard_map/ppermute | solution.py:95
  199.7 15.1 %collective-permute-start.30 = (f32[2,32,1024]{2,1,0:T(8,128)S(1)}, f32[2,32,1024]{2,1,0:T(8,128)S(1)}, u32[]{:S(2)}, u32[]{:S(2)}) collective-permute-start(f32[2,32,1024]{2,1,0:T(8,128)S(1)} %bitcast_add_fusion.34), channel_id=1, source_target_pairs={{0,2},{2,4},{4,6},{6,0},{1,3},{3,5},{5,7},{7,1},{8,10},{10,12},{12... | collective-permute-start | bytes 786440 | tf_op jit(solution)/shard_map/ppermute | solution.py:95
  203.5 12.7 %collective-permute-start.47 = (f32[2,32,1024]{2,1,0:T(8,128)S(1)}, f32[2,32,1024]{2,1,0:T(8,128)S(1)}, u32[]{:S(2)}, u32[]{:S(2)}) collective-permute-start(f32[2,32,1024]{2,1,0:T(8,128)S(1)} %bitcast_add_fusion.25), channel_id=1, source_target_pairs={{0,6},{2,0},{4,2},{6,4},{1,7},{3,1},{5,3},{7,5},{8,14},{10,8},{12,... | collective-permute-start | bytes 786440 | tf_op jit(solution)/shard_map/ppermute | solution.py:95
  205.3 14.8 %collective-permute-start.44 = (f32[2,32,1024]{2,1,0:T(8,128)S(1)}, f32[2,32,1024]{2,1,0:T(8,128)S(1)}, u32[]{:S(2)}, u32[]{:S(2)}) collective-permute-start(f32[2,32,1024]{2,1,0:T(8,128)S(1)} %bitcast_add_fusion.28), channel_id=1, source_target_pairs={{0,2},{2,4},{4,6},{6,0},{1,3},{3,5},{5,7},{7,1},{8,10},{10,12},{12... | collective-permute-start | bytes 786440 | tf_op jit(solution)/shard_map/ppermute | solution.py:95
  209.2 14.0 %collective-permute-start.61 = (f32[2,32,1024]{2,1,0:T(8,128)S(1)}, f32[2,32,1024]{2,1,0:T(8,128)S(1)}, u32[]{:S(2)}, u32[]{:S(2)}) collective-permute-start(f32[2,32,1024]{2,1,0:T(8,128)S(1)} %bitcast_add_fusion.19), channel_id=1, source_target_pairs={{0,6},{2,0},{4,2},{6,4},{1,7},{3,1},{5,3},{7,5},{8,14},{10,8},{12,... | collective-permute-start | bytes 786440 | tf_op jit(solution)/shard_map/ppermute | solution.py:95
  210.9 12.9 %collective-permute-start.58 = (f32[2,32,1024]{2,1,0:T(8,128)S(1)}, f32[2,32,1024]{2,1,0:T(8,128)S(1)}, u32[]{:S(2)}, u32[]{:S(2)}) collective-permute-start(f32[2,32,1024]{2,1,0:T(8,128)S(1)} %bitcast_add_fusion.22), channel_id=1, source_target_pairs={{0,2},{2,4},{4,6},{6,0},{1,3},{3,5},{5,7},{7,1},{8,10},{10,12},{12... | collective-permute-start | bytes 786440 | tf_op jit(solution)/shard_map/ppermute | solution.py:95
  214.8 12.2 %collective-permute-start.75 = (f32[2,32,1024]{2,1,0:T(8,128)S(1)}, f32[2,32,1024]{2,1,0:T(8,128)S(1)}, u32[]{:S(2)}, u32[]{:S(2)}) collective-permute-start(f32[2,32,1024]{2,1,0:T(8,128)S(1)} %bitcast_add_fusion.13), channel_id=1, source_target_pairs={{0,6},{2,0},{4,2},{6,4},{1,7},{3,1},{5,3},{7,5},{8,14},{10,8},{12,... | collective-permute-start | bytes 786440 | tf_op jit(solution)/shard_map/ppermute | solution.py:95
  223.2 13.2 %collective-permute-start.48 = (f32[2,32,1024]{2,1,0:T(8,128)S(1)}, f32[2,32,1024]{2,1,0:T(8,128)S(1)}, u32[]{:S(2)}, u32[]{:S(2)}) collective-permute-start(f32[2,32,1024]{2,1,0:T(8,128)S(1)} %fusion.54), channel_id=1, source_target_pairs={{0,1},{1,0},{2,3},{3,2},{4,5},{5,4},{6,7},{7,6},{8,9},{9,8},{10,11... | collective-permute-start | bytes 786440 | tf_op jit(solution)/shard_map/ppermute | solution.py:105
  223.9 18.1 %collective-permute-start.62 = (f32[2,32,1024]{2,1,0:T(8,128)S(1)}, f32[2,32,1024]{2,1,0:T(8,128)S(1)}, u32[]{:S(2)}, u32[]{:S(2)}) collective-permute-start(f32[2,32,1024]{2,1,0:T(8,128)S(1)} %fusion.49), channel_id=1, source_target_pairs={{0,1},{1,0},{2,3},{3,2},{4,5},{5,4},{6,7},{7,6},{8,9},{9,8},{10,11... | collective-permute-start | bytes 786440 | tf_op jit(solution)/shard_map/ppermute | solution.py:105
  227.1 20.5 %collective-permute-start.76 = (f32[2,32,1024]{2,1,0:T(8,128)S(1)}, f32[2,32,1024]{2,1,0:T(8,128)S(1)}, u32[]{:S(2)}, u32[]{:S(2)}) collective-permute-start(f32[2,32,1024]{2,1,0:T(8,128)S(1)} %fusion.44), channel_id=1, source_target_pairs={{0,1},{1,0},{2,3},{3,2},{4,5},{5,4},{6,7},{7,6},{8,9},{9,8},{10,11... | collective-permute-start | bytes 786440 | tf_op jit(solution)/shard_map/ppermute | solution.py:105
  230.8 21.4 %collective-permute-start.35 = (f32[2,32,1024]{2,1,0:T(8,128)S(1)}, f32[2,32,1024]{2,1,0:T(8,128)S(1)}, u32[]{:S(2)}, u32[]{:S(2)}) collective-permute-start(f32[2,32,1024]{2,1,0:T(8,128)S(1)} %fusion.62), channel_id=1, source_target_pairs={{0,1},{1,0},{2,3},{3,2},{4,5},{5,4},{6,7},{7,6},{8,9},{9,8},{10,11... | collective-permute-start | bytes 786440 | tf_op jit(solution)/shard_map/ppermute | solution.py:107
  236.4 19.5 %collective-permute-start.49 = (f32[2,32,1024]{2,1,0:T(8,128)S(1)}, f32[2,32,1024]{2,1,0:T(8,128)S(1)}, u32[]{:S(2)}, u32[]{:S(2)}) collective-permute-start(f32[2,32,1024]{2,1,0:T(8,128)S(1)} %fusion.57), channel_id=1, source_target_pairs={{0,1},{1,0},{2,3},{3,2},{4,5},{5,4},{6,7},{7,6},{8,9},{9,8},{10,11... | collective-permute-start | bytes 786440 | tf_op jit(solution)/shard_map/ppermute | solution.py:107
  242.0 15.8 %collective-permute-start.63 = (f32[2,32,1024]{2,1,0:T(8,128)S(1)}, f32[2,32,1024]{2,1,0:T(8,128)S(1)}, u32[]{:S(2)}, u32[]{:S(2)}) collective-permute-start(f32[2,32,1024]{2,1,0:T(8,128)S(1)} %fusion.52), channel_id=1, source_target_pairs={{0,1},{1,0},{2,3},{3,2},{4,5},{5,4},{6,7},{7,6},{8,9},{9,8},{10,11... | collective-permute-start | bytes 786440 | tf_op jit(solution)/shard_map/ppermute | solution.py:107
  247.7 13.0 %collective-permute-start.77 = (f32[2,32,1024]{2,1,0:T(8,128)S(1)}, f32[2,32,1024]{2,1,0:T(8,128)S(1)}, u32[]{:S(2)}, u32[]{:S(2)}) collective-permute-start(f32[2,32,1024]{2,1,0:T(8,128)S(1)} %fusion.47), channel_id=1, source_target_pairs={{0,1},{1,0},{2,3},{3,2},{4,5},{5,4},{6,7},{7,6},{8,9},{9,8},{10,11... | collective-permute-start | bytes 786440 | tf_op jit(solution)/shard_map/ppermute | solution.py:107
  256.1 12.4 %collective-permute-start.50 = (f32[2,32,1024]{2,1,0:T(8,128)S(1)}, f32[2,32,1024]{2,1,0:T(8,128)S(1)}, u32[]{:S(2)}, u32[]{:S(2)}) collective-permute-start(f32[2,32,1024]{2,1,0:T(8,128)S(1)} %get-tuple-element.127), channel_id=1, source_target_pairs={{0,2},{2,4},{4,6},{6,0},{1,3},{3,5},{5,7},{7,1},{8,10},{10,12},{12... | collective-permute-start | bytes 786440 | tf_op jit(solution)/shard_map/ppermute | solution.py:115
  260.6 13.6 %collective-permute-start.64 = (f32[2,32,1024]{2,1,0:T(8,128)S(1)}, f32[2,32,1024]{2,1,0:T(8,128)S(1)}, u32[]{:S(2)}, u32[]{:S(2)}) collective-permute-start(f32[2,32,1024]{2,1,0:T(8,128)S(1)} %get-tuple-element.121), channel_id=1, source_target_pairs={{0,2},{2,4},{4,6},{6,0},{1,3},{3,5},{5,7},{7,1},{8,10},{10,12},{12... | collective-permute-start | bytes 786440 | tf_op jit(solution)/shard_map/ppermute | solution.py:115
  264.4 15.5 %collective-permute-start.78 = (f32[2,32,1024]{2,1,0:T(8,128)S(1)}, f32[2,32,1024]{2,1,0:T(8,128)S(1)}, u32[]{:S(2)}, u32[]{:S(2)}) collective-permute-start(f32[2,32,1024]{2,1,0:T(8,128)S(1)} %get-tuple-element.123), channel_id=1, source_target_pairs={{0,2},{2,4},{4,6},{6,0},{1,3},{3,5},{5,7},{7,1},{8,10},{10,12},{12... | collective-permute-start | bytes 786440 | tf_op jit(solution)/shard_map/ppermute | solution.py:115
  268.6 16.8 %collective-permute-start.37 = (f32[2,32,1024]{2,1,0:T(8,128)S(1)}, f32[2,32,1024]{2,1,0:T(8,128)S(1)}, u32[]{:S(2)}, u32[]{:S(2)}) collective-permute-start(f32[2,32,1024]{2,1,0:T(8,128)S(1)} %collective-permute-done.36), channel_id=1, source_target_pairs={{0,2},{2,4},{4,6},{6,0},{1,3},{3,5},{5,7},{7,1},{8,10},{10,12},{12... | collective-permute-start | bytes 786440 | tf_op jit(solution)/shard_map/ppermute | solution.py:115
  274.2 16.8 %collective-permute-start.51 = (f32[2,32,1024]{2,1,0:T(8,128)S(1)}, f32[2,32,1024]{2,1,0:T(8,128)S(1)}, u32[]{:S(2)}, u32[]{:S(2)}) collective-permute-start(f32[2,32,1024]{2,1,0:T(8,128)S(1)} %collective-permute-done.50), channel_id=1, source_target_pairs={{0,2},{2,4},{4,6},{6,0},{1,3},{3,5},{5,7},{7,1},{8,10},{10,12},{12... | collective-permute-start | bytes 786440 | tf_op jit(solution)/shard_map/ppermute | solution.py:115
  279.9 16.8 %collective-permute-start.65 = (f32[2,32,1024]{2,1,0:T(8,128)S(1)}, f32[2,32,1024]{2,1,0:T(8,128)S(1)}, u32[]{:S(2)}, u32[]{:S(2)}) collective-permute-start(f32[2,32,1024]{2,1,0:T(8,128)S(1)} %collective-permute-done.64), channel_id=1, source_target_pairs={{0,2},{2,4},{4,6},{6,0},{1,3},{3,5},{5,7},{7,1},{8,10},{10,12},{12... | collective-permute-start | bytes 786440 | tf_op jit(solution)/shard_map/ppermute | solution.py:115
  285.5 16.8 %collective-permute-start.79 = (f32[2,32,1024]{2,1,0:T(8,128)S(1)}, f32[2,32,1024]{2,1,0:T(8,128)S(1)}, u32[]{:S(2)}, u32[]{:S(2)}) collective-permute-start(f32[2,32,1024]{2,1,0:T(8,128)S(1)} %collective-permute-done.78), channel_id=1, source_target_pairs={{0,2},{2,4},{4,6},{6,0},{1,3},{3,5},{5,7},{7,1},{8,10},{10,12},{12... | collective-permute-start | bytes 786440 | tf_op jit(solution)/shard_map/ppermute | solution.py:115
  291.1 33.0 %collective-permute-start.38 = (f32[2,32,1024]{2,1,0:T(8,128)S(1)}, f32[2,32,1024]{2,1,0:T(8,128)S(1)}, u32[]{:S(2)}, u32[]{:S(2)}) collective-permute-start(f32[2,32,1024]{2,1,0:T(8,128)S(1)} %collective-permute-done.37), channel_id=1, source_target_pairs={{0,2},{2,4},{4,6},{6,0},{1,3},{3,5},{5,7},{7,1},{8,10},{10,12},{12... | collective-permute-start | bytes 786440 | tf_op jit(solution)/shard_map/ppermute | solution.py:115
  296.7 27.5 %collective-permute-start.41 = (f32[2,32,1024]{2,1,0:T(8,128)S(1)}, f32[2,32,1024]{2,1,0:T(8,128)S(1)}, u32[]{:S(2)}, u32[]{:S(2)}) collective-permute-start(f32[2,32,1024]{2,1,0:T(8,128)S(1)} %collective-permute-done.40), channel_id=1, source_target_pairs={{0,6},{2,0},{4,2},{6,4},{1,7},{3,1},{5,3},{7,5},{8,14},{10,8},{12,... | collective-permute-start | bytes 786440 | tf_op jit(solution)/shard_map/ppermute | solution.py:115
  296.7 27.7 %collective-permute-start.52 = (f32[2,32,1024]{2,1,0:T(8,128)S(1)}, f32[2,32,1024]{2,1,0:T(8,128)S(1)}, u32[]{:S(2)}, u32[]{:S(2)}) collective-permute-start(f32[2,32,1024]{2,1,0:T(8,128)S(1)} %collective-permute-done.51), channel_id=1, source_target_pairs={{0,2},{2,4},{4,6},{6,0},{1,3},{3,5},{5,7},{7,1},{8,10},{10,12},{12... | collective-permute-start | bytes 786440 | tf_op jit(solution)/shard_map/ppermute | solution.py:115
  374.2 12.9 %collective-permute-start.101 = (f32[2,32,1024]{2,1,0:T(8,128)S(1)}, f32[2,32,1024]{2,1,0:T(8,128)S(1)}, u32[]{:S(2)}, u32[]{:S(2)}) collective-permute-start(f32[2,32,1024]{2,1,0:T(8,128)S(1)} %dynamic-slice_bitcast_fusion), channel_id=1, source_target_pairs={{0,6},{2,0},{4,2},{6,4},{1,7},{3,1},{5,3},{7,5},{8,14},{10,8},{12,... | collective-permute-start | bytes 786440 | tf_op jit(solution)/shard_map/ppermute | solution.py:95
  376.7 12.7 %collective-permute-start.98 = (f32[2,32,1024]{2,1,0:T(8,128)S(1)}, f32[2,32,1024]{2,1,0:T(8,128)S(1)}, u32[]{:S(2)}, u32[]{:S(2)}) collective-permute-start(f32[2,32,1024]{2,1,0:T(8,128)S(1)} %dynamic-slice_bitcast_fusion.1), channel_id=1, source_target_pairs={{0,2},{2,4},{4,6},{6,0},{1,3},{3,5},{5,7},{7,1},{8,10},{10,12},{12... | collective-permute-start | bytes 786440 | tf_op jit(solution)/shard_map/ppermute | solution.py:95
  403.4 13.7 %collective-permute-start.90 = (f32[2,32,1024]{2,1,0:T(8,128)S(1)}, f32[2,32,1024]{2,1,0:T(8,128)S(1)}, u32[]{:S(2)}, u32[]{:S(2)}) collective-permute-start(f32[2,32,1024]{2,1,0:T(8,128)S(1)} %fusion.39), channel_id=1, source_target_pairs={{0,1},{1,0},{2,3},{3,2},{4,5},{5,4},{6,7},{7,6},{8,9},{9,8},{10,11... | collective-permute-start | bytes 786440 | tf_op jit(solution)/shard_map/ppermute | solution.py:105
  406.8 17.4 %collective-permute-start.104 = (f32[2,32,1024]{2,1,0:T(8,128)S(1)}, f32[2,32,1024]{2,1,0:T(8,128)S(1)}, u32[]{:S(2)}, u32[]{:S(2)}) collective-permute-start(f32[2,32,1024]{2,1,0:T(8,128)S(1)} %fusion.34), channel_id=1, source_target_pairs={{0,1},{1,0},{2,3},{3,2},{4,5},{5,4},{6,7},{7,6},{8,9},{9,8},{10,11... | collective-permute-start | bytes 786440 | tf_op jit(solution)/shard_map/ppermute | solution.py:105
  417.1 12.8 %collective-permute-start.91 = (f32[2,32,1024]{2,1,0:T(8,128)S(1)}, f32[2,32,1024]{2,1,0:T(8,128)S(1)}, u32[]{:S(2)}, u32[]{:S(2)}) collective-permute-start(f32[2,32,1024]{2,1,0:T(8,128)S(1)} %fusion.42), channel_id=1, source_target_pairs={{0,1},{1,0},{2,3},{3,2},{4,5},{5,4},{6,7},{7,6},{8,9},{9,8},{10,11... | collective-permute-start | bytes 786440 | tf_op jit(solution)/shard_map/ppermute | solution.py:107
  (138 other events, 1224.6 us)
Sparse Core Ops, SparseCore 0:
  374.2 162.0 all-reduce.3

commit v2 on v1

--- a/solution.py
+++ b/solution.py
@@ -214,7 +214,11 @@
     up_grad = (hidden_grad * gate_proj * gate_sigmoid).astype(jnp.bfloat16)
     gate_w_grad = outer(normed_two, gate_grad)
     up_w_grad = outer(normed_two, up_grad)
-    normed_two_grad = split_tensor_sum(inner(gate_grad, w_gate) + inner(up_grad, w_up))
+    ffn_w_grads, two_partial = lax.optimization_barrier(
+        ((down_grad, gate_w_grad, up_w_grad), inner(gate_grad, w_gate) + inner(up_grad, w_up))
+    )
+    ffn_w_grads = lax.psum(ffn_w_grads, "dp")
+    normed_two_grad = split_tensor_sum(two_partial)
     ffn_grad = jnp.sum(normed_two_grad * residual * scale_two, axis=0)
     residual_grad = cotangent.astype(jnp.float32) + rms_back(
         normed_two_grad, residual, scale_two, ffn_gain
@@ -263,29 +267,15 @@
     small = small.at[0].set(ffn_grad).at[1].set(attn_part)
     small = small.at[2, :head_size].set(qgain_grad).at[2, head_size : 2 * head_size].set(kgain_grad)
     out_rows = out_w_grad.shape[0]
-    dp_sums, one_partial = lax.optimization_barrier(
+    ffn_w_grads, dp_sums, one_partial = lax.optimization_barrier(
         (
-            (
-                query_w_grad,
-                key_w_grad,
-                value_w_grad,
-                jnp.concatenate([out_w_grad, small]),
-                gate_w_grad,
-                up_w_grad,
-                down_grad,
-            ),
+            ffn_w_grads,
+            (query_w_grad, key_w_grad, value_w_grad, jnp.concatenate([out_w_grad, small])),
             one_partial,
         )
     )
-    (
-        query_w_grad,
-        key_w_grad,
-        value_w_grad,
-        out_pack,
-        gate_w_grad,
-        up_w_grad,
-        down_grad,
-    ) = lax.psum(dp_sums, "dp")
+    query_w_grad, key_w_grad, value_w_grad, out_pack = lax.psum(dp_sums, "dp")
+    down_grad, gate_w_grad, up_w_grad = ffn_w_grads
     normed_one_grad = split_tensor_sum(one_partial)
     input_grad = residual_grad + rms_back(normed_one_grad, tokens_wide, scale_one, attn_gain)
     out_w_grad = out_pack[:out_rows]

time: 582 us -> 620 us (1.065)
  local copies, waits for them, and re-layouts: 40.1 us -> 59 us
  waiting for transfers between devices: 233 us -> 250 us
    psum x1 -> x2, waiting for transfers between devices: 73 us -> 95.6 us  [the longest x1 95.6 us: per_device(): query_w_grad, key_w_grad, value_w_grad, out_pack = lax.psum(dp_sums, 'dp')]
    ppermute x48, waiting for transfers between devices: 60.9 us -> 47.4 us  [tensor_sum(): acc = lax.ppermute(acc, 'ty', ring(ny, shift))]
    ppermute x48, starting transfers between devices: 54.3 us -> 66.3 us  [tensor_sum(): acc = lax.ppermute(acc, 'ty', ring(ny, shift))]
    ppermute x8, waiting for transfers between devices: 24.8 us -> 31.9 us  [tensor_sum(): got = lax.ppermute(send, 'tx', pairs)]
    ppermute x48, starting transfers between devices: 66.9 us -> 60.5 us  [tensor_sum(): cur = lax.ppermute(cur, 'ty', ring(ny, shift))]
    unnamed x146 -> x194, local copies, waits for them, and re-layouts: 17.3 us -> 22.4 us
  transfers between devices with their start and end apart: 116 -> 117, of which waited for: 67 -> 65; matrix products, arithmetic and copies ran while one was open for 7% -> 15% of each run, Pallas kernels for 0% -> 0%
where the time goes in v2:
time: 620 us; the launch traced here: 610 us
  waiting for transfers between devices  250 us (40%)
  starting transfers between devices  177 us (29%)
  local copies, waits for them, and re-layouts  59 us (10%)
  other arithmetic  55.9 us (9%)
  matrix products  52 us (8%)
  between operations  16.9 us (3%)
    psum x1, waiting for transfers between devices, per_device(): query_w_grad, key_w_grad, value_w_grad, out_pack = lax.psum(dp_sums, 'dp')  95.6 us
    ppermute x48, starting transfers between devices, tensor_sum(): acc = lax.ppermute(acc, 'ty', ring(ny, shift))  66.3 us
    ppermute x48, starting transfers between devices, tensor_sum(): cur = lax.ppermute(cur, 'ty', ring(ny, shift))  60.5 us
    ppermute x48, waiting for transfers between devices, tensor_sum(): cur = lax.ppermute(cur, 'ty', ring(ny, shift))  59.6 us
    ppermute x48, waiting for transfers between devices, tensor_sum(): acc = lax.ppermute(acc, 'ty', ring(ny, shift))  47.4 us
    ppermute x8, waiting for transfers between devices, tensor_sum(): got = lax.ppermute(send, 'tx', pairs)  31.9 us
    ppermute x8, starting transfers between devices, tensor_sum(): other = lax.ppermute(mine, 'tx', pairs)  23 us
    unnamed x194, local copies, waits for them, and re-layouts  22.4 us
  transfers between devices with their start and end apart: 117, of which 65 were waited for; matrix products, arithmetic and copies ran while one was open for 15% of the time, Pallas kernels for 0%

profile of v2, /device:TPU:0, one launch (start us, length us, event | category | flops | bytes accessed | tf_op | source)
XLA Modules:
  0.0 610.0 jit_solution(15404982917206247764)
XLA Ops:
  46.7 3.4 collective-permute-start.17
  53.0 3.3 collective-permute-start.4
  58.5 3.3 collective-permute-start.18
  63.9 3.3 collective-permute-start.5
  68.2 3.8 collective-permute-start.19
  74.9 4.0 collective-permute-done.2
  91.2 3.6 collective-permute-done.20
  101.8 3.2 collective-permute-start.11
  105.8 3.3 collective-permute-start.25
  112.3 3.3 collective-permute-start.12
  117.9 3.3 collective-permute-start.26
  123.5 3.3 collective-permute-start.13
  129.1 3.7 collective-permute-start.27
  133.3 3.4 collective-permute-done.24
  146.5 3.9 fusion.121
  169.9 4.8 convolution_add_fusion
  176.0 3.2 collective-permute-start.59
  205.6 3.4 collective-permute-done.43
  211.2 3.4 collective-permute-done.57
  216.8 3.4 collective-permute-done.71
  222.5 3.4 collective-permute-done.30
  228.3 3.2 collective-permute-done.44
  240.4 4.8 collective-permute-done.34
  248.3 5.3 collective-permute-done.48
  256.7 5.3 collective-permute-done.62
  265.1 5.3 collective-permute-done.76
  272.8 3.9 collective-permute-done.35
  287.9 3.3 collective-permute-start.67
  294.8 3.5 collective-permute-done.64
  300.4 3.5 collective-permute-done.78
  306.0 3.5 collective-permute-done.37
  311.6 3.5 collective-permute-done.51
  317.2 3.5 collective-permute-done.65
  322.9 3.5 collective-permute-done.79
  326.8 3.2 collective-permute-start.69
  330.1 9.0 %collective-permute-done.66 = f32[2,32,1024]{2,1,0:T(8,128)S(1)} collective-permute-done((f32[2,32,1024]{2,1,0:T(8,128)S(1)}, f32[2,32,1024]{2,1,0:T(8,128)S(1)}, u32[]{:S(2)}, u32[]{:S(2)}) %collective-permute-start.66) | collective-permute-done | bytes 262176 | tf_op jit(solution)/shard_map/ppermute | solution.py:115
  339.1 3.3 collective-permute-start.83
  342.6 4.1 collective-permute-done.80
  353.2 4.7 multiply_add_fusion
  376.5 3.3 fusion.17
  395.7 4.3 collective-permute-done.87
  429.4 4.0 collective-permute-done.90
  442.0 3.2 collective-permute-start.95
  451.7 3.3 collective-permute-start.109
  455.1 3.3 collective-permute-start.96
  458.4 95.6 %all-reduce.6.cloned.1.call-done = (f32[136,1024]{1,0:T(8,128)}, f32[1024,128]{1,0:T(8,128)}, f32[1024,64]{0,1:T(8,128)}, f32[1024,64]{0,1:T(8,128)}) async-done(((f32[136,1024]{1,0:T(8,128)}, f32[1024,128]{1,0:T(8,128)}, f32[1024,64]{0,1:T(8,128)}, f32[1024,64]{0,1:T(8,128)}), (f32[136,1024]{1,0:T(8,128)}, f32[1024,128]{1,0:T(8,128)}, f32[1024,64]{0,1:T(8,128)}, ...) | async-done | bytes 1605648 | tf_op jit(solution)/shard_map/psum | solution.py:277
  573.3 3.3 collective-permute-start.97
  577.4 3.5 collective-permute-start.111
  (650 shorter events, 319.2 us)
Async XLA Ops:
  7.2 380.7 %all-reduce.8.cloned.1.call-start = ((), (), s32[]{:S(2)}) async-start(), calls=%async_computation.1 | async-start | bytes 14155776 | tf_op jit(solution)/shard_map/psum | solution.py:220
  68.2 13.9 %collective-permute-start.19 = (f32[2,32,1024]{2,1,0:T(8,128)S(1)}, f32[2,32,1024]{2,1,0:T(8,128)S(1)}, u32[]{:S(2)}, u32[]{:S(2)}) collective-permute-start(f32[2,32,1024]{2,1,0:T(8,128)S(1)} %bitcast_add_fusion.37), channel_id=1, source_target_pairs={{0,6},{2,0},{4,2},{6,4},{1,7},{3,1},{5,3},{7,5},{8,14},{10,8},{12,... | collective-permute-start | bytes 786440 | tf_op jit(solution)/shard_map/ppermute | solution.py:95
  159.2 22.4 %collective-permute-start.31 = (f32[2,32,1024]{2,1,0:T(8,128)}, f32[2,32,1024]{2,1,0:T(8,128)}, u32[]{:S(2)}, u32[]{:S(2)}) collective-permute-start(f32[2,32,1024]{2,1,0:T(8,128)} %dynamic-slice_bitcast_fusion.10), channel_id=1, source_target_pairs={{0,6},{2,0},{4,2},{6,4},{1,7},{3,1},{5,3},{7,5},{8,14},{10,8},{12,... | collective-permute-start | bytes 786440 | tf_op jit(solution)/shard_map/ppermute | solution.py:95
  162.2 20.6 %collective-permute-start.28 = (f32[2,32,1024]{2,1,0:T(8,128)}, f32[2,32,1024]{2,1,0:T(8,128)}, u32[]{:S(2)}, u32[]{:S(2)}) collective-permute-start(f32[2,32,1024]{2,1,0:T(8,128)} %dynamic-slice_bitcast_fusion.11), channel_id=1, source_target_pairs={{0,2},{2,4},{4,6},{6,0},{1,3},{3,5},{5,7},{7,1},{8,10},{10,12},{12... | collective-permute-start | bytes 786440 | tf_op jit(solution)/shard_map/ppermute | solution.py:95
  163.1 23.9 %collective-permute-start.45 = (f32[2,32,1024]{2,1,0:T(8,128)}, f32[2,32,1024]{2,1,0:T(8,128)}, u32[]{:S(2)}, u32[]{:S(2)}) collective-permute-start(f32[2,32,1024]{2,1,0:T(8,128)} %dynamic-slice_bitcast_fusion.8), channel_id=1, source_target_pairs={{0,6},{2,0},{4,2},{6,4},{1,7},{3,1},{5,3},{7,5},{8,14},{10,8},{12,... | collective-permute-start | bytes 786440 | tf_op jit(solution)/shard_map/ppermute | solution.py:95
  167.1 21.3 %collective-permute-start.42 = (f32[2,32,1024]{2,1,0:T(8,128)}, f32[2,32,1024]{2,1,0:T(8,128)}, u32[]{:S(2)}, u32[]{:S(2)}) collective-permute-start(f32[2,32,1024]{2,1,0:T(8,128)} %dynamic-slice_bitcast_fusion.9), channel_id=1, source_target_pairs={{0,2},{2,4},{4,6},{6,0},{1,3},{3,5},{5,7},{7,1},{8,10},{10,12},{12... | collective-permute-start | bytes 786440 | tf_op jit(solution)/shard_map/ppermute | solution.py:95
  176.0 16.5 %collective-permute-start.59 = (f32[2,32,1024]{2,1,0:T(8,128)}, f32[2,32,1024]{2,1,0:T(8,128)}, u32[]{:S(2)}, u32[]{:S(2)}) collective-permute-start(f32[2,32,1024]{2,1,0:T(8,128)} %dynamic-slice_bitcast_fusion.6), channel_id=1, source_target_pairs={{0,6},{2,0},{4,2},{6,4},{1,7},{3,1},{5,3},{7,5},{8,14},{10,8},{12,... | collective-permute-start | bytes 786440 | tf_op jit(solution)/shard_map/ppermute | solution.py:95
  181.5 372.5 %all-reduce.6.cloned.1.call-start = ((), (), s32[]{:S(2)}) async-start(), calls=%async_computation | async-start | bytes 3211264 | tf_op jit(solution)/shard_map/psum | solution.py:277
  182.9 14.2 %collective-permute-start.73 = (f32[2,32,1024]{2,1,0:T(8,128)}, f32[2,32,1024]{2,1,0:T(8,128)S(1)}, u32[]{:S(2)}, u32[]{:S(2)}) collective-permute-start(f32[2,32,1024]{2,1,0:T(8,128)} %dynamic-slice_bitcast_fusion.4), channel_id=1, source_target_pairs={{0,6},{2,0},{4,2},{6,4},{1,7},{3,1},{5,3},{7,5},{8,14},{10,8},{12,... | collective-permute-start | bytes 786440 | tf_op jit(solution)/shard_map/ppermute | solution.py:95
  200.5 14.1 %collective-permute-start.57 = (f32[2,32,1024]{2,1,0:T(8,128)S(1)}, f32[2,32,1024]{2,1,0:T(8,128)S(1)}, u32[]{:S(2)}, u32[]{:S(2)}) collective-permute-start(f32[2,32,1024]{2,1,0:T(8,128)S(1)} %bitcast_add_fusion.23), channel_id=1, source_target_pairs={{0,2},{2,4},{4,6},{6,0},{1,3},{3,5},{5,7},{7,1},{8,10},{10,12},{12... | collective-permute-start | bytes 786440 | tf_op jit(solution)/shard_map/ppermute | solution.py:95
  204.0 16.3 %collective-permute-start.71 = (f32[2,32,1024]{2,1,0:T(8,128)S(1)}, f32[2,32,1024]{2,1,0:T(8,128)S(1)}, u32[]{:S(2)}, u32[]{:S(2)}) collective-permute-start(f32[2,32,1024]{2,1,0:T(8,128)S(1)} %bitcast_add_fusion.17), channel_id=1, source_target_pairs={{0,2},{2,4},{4,6},{6,0},{1,3},{3,5},{5,7},{7,1},{8,10},{10,12},{12... | collective-permute-start | bytes 786440 | tf_op jit(solution)/shard_map/ppermute | solution.py:95
  209.5 16.4 %collective-permute-start.30 = (f32[2,32,1024]{2,1,0:T(8,128)S(1)}, f32[2,32,1024]{2,1,0:T(8,128)S(1)}, u32[]{:S(2)}, u32[]{:S(2)}) collective-permute-start(f32[2,32,1024]{2,1,0:T(8,128)S(1)} %bitcast_add_fusion.34), channel_id=1, source_target_pairs={{0,2},{2,4},{4,6},{6,0},{1,3},{3,5},{5,7},{7,1},{8,10},{10,12},{12... | collective-permute-start | bytes 786440 | tf_op jit(solution)/shard_map/ppermute | solution.py:95
  215.2 16.4 %collective-permute-start.44 = (f32[2,32,1024]{2,1,0:T(8,128)S(1)}, f32[2,32,1024]{2,1,0:T(8,128)S(1)}, u32[]{:S(2)}, u32[]{:S(2)}) collective-permute-start(f32[2,32,1024]{2,1,0:T(8,128)S(1)} %bitcast_add_fusion.28), channel_id=1, source_target_pairs={{0,2},{2,4},{4,6},{6,0},{1,3},{3,5},{5,7},{7,1},{8,10},{10,12},{12... | collective-permute-start | bytes 786440 | tf_op jit(solution)/shard_map/ppermute | solution.py:95
  220.3 14.3 %collective-permute-start.61 = (f32[2,32,1024]{2,1,0:T(8,128)S(1)}, f32[2,32,1024]{2,1,0:T(8,128)S(1)}, u32[]{:S(2)}, u32[]{:S(2)}) collective-permute-start(f32[2,32,1024]{2,1,0:T(8,128)S(1)} %bitcast_add_fusion.19), channel_id=1, source_target_pairs={{0,6},{2,0},{4,2},{6,4},{1,7},{3,1},{5,3},{7,5},{8,14},{10,8},{12,... | collective-permute-start | bytes 786440 | tf_op jit(solution)/shard_map/ppermute | solution.py:95
  220.8 14.5 %collective-permute-start.58 = (f32[2,32,1024]{2,1,0:T(8,128)S(1)}, f32[2,32,1024]{2,1,0:T(8,128)S(1)}, u32[]{:S(2)}, u32[]{:S(2)}) collective-permute-start(f32[2,32,1024]{2,1,0:T(8,128)S(1)} %bitcast_add_fusion.22), channel_id=1, source_target_pairs={{0,2},{2,4},{4,6},{6,0},{1,3},{3,5},{5,7},{7,1},{8,10},{10,12},{12... | collective-permute-start | bytes 786440 | tf_op jit(solution)/shard_map/ppermute | solution.py:95
  225.9 12.5 %collective-permute-start.75 = (f32[2,32,1024]{2,1,0:T(8,128)S(1)}, f32[2,32,1024]{2,1,0:T(8,128)S(1)}, u32[]{:S(2)}, u32[]{:S(2)}) collective-permute-start(f32[2,32,1024]{2,1,0:T(8,128)S(1)} %bitcast_add_fusion.13), channel_id=1, source_target_pairs={{0,6},{2,0},{4,2},{6,4},{1,7},{3,1},{5,3},{7,5},{8,14},{10,8},{12,... | collective-permute-start | bytes 786440 | tf_op jit(solution)/shard_map/ppermute | solution.py:95
  231.5 13.6 %collective-permute-start.34 = (f32[2,32,1024]{2,1,0:T(8,128)S(1)}, f32[2,32,1024]{2,1,0:T(8,128)S(1)}, u32[]{:S(2)}, u32[]{:S(2)}) collective-permute-start(f32[2,32,1024]{2,1,0:T(8,128)S(1)} %fusion.59), channel_id=1, source_target_pairs={{0,1},{1,0},{2,3},{3,2},{4,5},{5,4},{6,7},{7,6},{8,9},{9,8},{10,11... | collective-permute-start | bytes 786440 | tf_op jit(solution)/shard_map/ppermute | solution.py:105
  234.6 18.9 %collective-permute-start.48 = (f32[2,32,1024]{2,1,0:T(8,128)S(1)}, f32[2,32,1024]{2,1,0:T(8,128)S(1)}, u32[]{:S(2)}, u32[]{:S(2)}) collective-permute-start(f32[2,32,1024]{2,1,0:T(8,128)S(1)} %fusion.54), channel_id=1, source_target_pairs={{0,1},{1,0},{2,3},{3,2},{4,5},{5,4},{6,7},{7,6},{8,9},{9,8},{10,11... | collective-permute-start | bytes 786440 | tf_op jit(solution)/shard_map/ppermute | solution.py:105
  235.3 26.7 %collective-permute-start.62 = (f32[2,32,1024]{2,1,0:T(8,128)S(1)}, f32[2,32,1024]{2,1,0:T(8,128)S(1)}, u32[]{:S(2)}, u32[]{:S(2)}) collective-permute-start(f32[2,32,1024]{2,1,0:T(8,128)S(1)} %fusion.49), channel_id=1, source_target_pairs={{0,1},{1,0},{2,3},{3,2},{4,5},{5,4},{6,7},{7,6},{8,9},{9,8},{10,11... | collective-permute-start | bytes 786440 | tf_op jit(solution)/shard_map/ppermute | solution.py:105
  238.6 31.9 %collective-permute-start.76 = (f32[2,32,1024]{2,1,0:T(8,128)S(1)}, f32[2,32,1024]{2,1,0:T(8,128)S(1)}, u32[]{:S(2)}, u32[]{:S(2)}) collective-permute-start(f32[2,32,1024]{2,1,0:T(8,128)S(1)} %fusion.44), channel_id=1, source_target_pairs={{0,1},{1,0},{2,3},{3,2},{4,5},{5,4},{6,7},{7,6},{8,9},{9,8},{10,11... | collective-permute-start | bytes 786440 | tf_op jit(solution)/shard_map/ppermute | solution.py:105
  245.2 31.5 %collective-permute-start.35 = (f32[2,32,1024]{2,1,0:T(8,128)S(1)}, f32[2,32,1024]{2,1,0:T(8,128)S(1)}, u32[]{:S(2)}, u32[]{:S(2)}) collective-permute-start(f32[2,32,1024]{2,1,0:T(8,128)S(1)} %fusion.62), channel_id=1, source_target_pairs={{0,1},{1,0},{2,3},{3,2},{4,5},{5,4},{6,7},{7,6},{8,9},{9,8},{10,11... | collective-permute-start | bytes 786440 | tf_op jit(solution)/shard_map/ppermute | solution.py:107
  253.6 28.2 %collective-permute-start.49 = (f32[2,32,1024]{2,1,0:T(8,128)S(1)}, f32[2,32,1024]{2,1,0:T(8,128)S(1)}, u32[]{:S(2)}, u32[]{:S(2)}) collective-permute-start(f32[2,32,1024]{2,1,0:T(8,128)S(1)} %fusion.57), channel_id=1, source_target_pairs={{0,1},{1,0},{2,3},{3,2},{4,5},{5,4},{6,7},{7,6},{8,9},{9,8},{10,11... | collective-permute-start | bytes 786440 | tf_op jit(solution)/shard_map/ppermute | solution.py:107
  262.0 22.6 %collective-permute-start.63 = (f32[2,32,1024]{2,1,0:T(8,128)S(1)}, f32[2,32,1024]{2,1,0:T(8,128)S(1)}, u32[]{:S(2)}, u32[]{:S(2)}) collective-permute-start(f32[2,32,1024]{2,1,0:T(8,128)S(1)} %fusion.52), channel_id=1, source_target_pairs={{0,1},{1,0},{2,3},{3,2},{4,5},{5,4},{6,7},{7,6},{8,9},{9,8},{10,11... | collective-permute-start | bytes 786440 | tf_op jit(solution)/shard_map/ppermute | solution.py:107
  270.5 17.0 %collective-permute-start.77 = (f32[2,32,1024]{2,1,0:T(8,128)S(1)}, f32[2,32,1024]{2,1,0:T(8,128)S(1)}, u32[]{:S(2)}, u32[]{:S(2)}) collective-permute-start(f32[2,32,1024]{2,1,0:T(8,128)S(1)} %fusion.47), channel_id=1, source_target_pairs={{0,1},{1,0},{2,3},{3,2},{4,5},{5,4},{6,7},{7,6},{8,9},{9,8},{10,11... | collective-permute-start | bytes 786440 | tf_op jit(solution)/shard_map/ppermute | solution.py:107
  277.6 13.6 %collective-permute-start.39 = (f32[2,32,1024]{2,1,0:T(8,128)S(1)}, f32[2,32,1024]{2,1,0:T(8,128)S(1)}, u32[]{:S(2)}, u32[]{:S(2)}) collective-permute-start(f32[2,32,1024]{2,1,0:T(8,128)S(1)} %get-tuple-element.134), channel_id=1, source_target_pairs={{0,6},{2,0},{4,2},{6,4},{1,7},{3,1},{5,3},{7,5},{8,14},{10,8},{12,... | collective-permute-start | bytes 786440 | tf_op jit(solution)/shard_map/ppermute | solution.py:115
  291.2 12.6 %collective-permute-start.78 = (f32[2,32,1024]{2,1,0:T(8,128)S(1)}, f32[2,32,1024]{2,1,0:T(8,128)S(1)}, u32[]{:S(2)}, u32[]{:S(2)}) collective-permute-start(f32[2,32,1024]{2,1,0:T(8,128)S(1)} %get-tuple-element.131), channel_id=1, source_target_pairs={{0,2},{2,4},{4,6},{6,0},{1,3},{3,5},{5,7},{7,1},{8,10},{10,12},{12... | collective-permute-start | bytes 786440 | tf_op jit(solution)/shard_map/ppermute | solution.py:115
  292.6 12.4 %collective-permute-start.81 = (f32[2,32,1024]{2,1,0:T(8,128)S(1)}, f32[2,32,1024]{2,1,0:T(8,128)S(1)}, u32[]{:S(2)}, u32[]{:S(2)}) collective-permute-start(f32[2,32,1024]{2,1,0:T(8,128)S(1)} %get-tuple-element.132), channel_id=1, source_target_pairs={{0,6},{2,0},{4,2},{6,4},{1,7},{3,1},{5,3},{7,5},{8,14},{10,8},{12,... | collective-permute-start | bytes 786440 | tf_op jit(solution)/shard_map/ppermute | solution.py:115
  294.7 14.8 %collective-permute-start.37 = (f32[2,32,1024]{2,1,0:T(8,128)S(1)}, f32[2,32,1024]{2,1,0:T(8,128)S(1)}, u32[]{:S(2)}, u32[]{:S(2)}) collective-permute-start(f32[2,32,1024]{2,1,0:T(8,128)S(1)} %collective-permute-done.36), channel_id=1, source_target_pairs={{0,2},{2,4},{4,6},{6,0},{1,3},{3,5},{5,7},{7,1},{8,10},{10,12},{12... | collective-permute-start | bytes 786440 | tf_op jit(solution)/shard_map/ppermute | solution.py:115
  298.2 12.4 %collective-permute-start.40 = (f32[2,32,1024]{2,1,0:T(8,128)S(1)}, f32[2,32,1024]{2,1,0:T(8,128)S(1)}, u32[]{:S(2)}, u32[]{:S(2)}) collective-permute-start(f32[2,32,1024]{2,1,0:T(8,128)S(1)} %collective-permute-done.39), channel_id=1, source_target_pairs={{0,6},{2,0},{4,2},{6,4},{1,7},{3,1},{5,3},{7,5},{8,14},{10,8},{12,... | collective-permute-start | bytes 786440 | tf_op jit(solution)/shard_map/ppermute | solution.py:115
  299.4 15.7 %collective-permute-start.51 = (f32[2,32,1024]{2,1,0:T(8,128)S(1)}, f32[2,32,1024]{2,1,0:T(8,128)S(1)}, u32[]{:S(2)}, u32[]{:S(2)}) collective-permute-start(f32[2,32,1024]{2,1,0:T(8,128)S(1)} %collective-permute-done.50), channel_id=1, source_target_pairs={{0,2},{2,4},{4,6},{6,0},{1,3},{3,5},{5,7},{7,1},{8,10},{10,12},{12... | collective-permute-start | bytes 786440 | tf_op jit(solution)/shard_map/ppermute | solution.py:115
  303.8 12.4 %collective-permute-start.54 = (f32[2,32,1024]{2,1,0:T(8,128)S(1)}, f32[2,32,1024]{2,1,0:T(8,128)S(1)}, u32[]{:S(2)}, u32[]{:S(2)}) collective-permute-start(f32[2,32,1024]{2,1,0:T(8,128)S(1)} %collective-permute-done.53), channel_id=1, source_target_pairs={{0,6},{2,0},{4,2},{6,4},{1,7},{3,1},{5,3},{7,5},{8,14},{10,8},{12,... | collective-permute-start | bytes 786440 | tf_op jit(solution)/shard_map/ppermute | solution.py:115
  305.0 15.7 %collective-permute-start.65 = (f32[2,32,1024]{2,1,0:T(8,128)S(1)}, f32[2,32,1024]{2,1,0:T(8,128)S(1)}, u32[]{:S(2)}, u32[]{:S(2)}) collective-permute-start(f32[2,32,1024]{2,1,0:T(8,128)S(1)} %collective-permute-done.64), channel_id=1, source_target_pairs={{0,2},{2,4},{4,6},{6,0},{1,3},{3,5},{5,7},{7,1},{8,10},{10,12},{12... | collective-permute-start | bytes 786440 | tf_op jit(solution)/shard_map/ppermute | solution.py:115
  310.6 15.7 %collective-permute-start.79 = (f32[2,32,1024]{2,1,0:T(8,128)S(1)}, f32[2,32,1024]{2,1,0:T(8,128)S(1)}, u32[]{:S(2)}, u32[]{:S(2)}) collective-permute-start(f32[2,32,1024]{2,1,0:T(8,128)S(1)} %collective-permute-done.78), channel_id=1, source_target_pairs={{0,2},{2,4},{4,6},{6,0},{1,3},{3,5},{5,7},{7,1},{8,10},{10,12},{12... | collective-permute-start | bytes 786440 | tf_op jit(solution)/shard_map/ppermute | solution.py:115
  316.3 34.8 %collective-permute-start.38 = (f32[2,32,1024]{2,1,0:T(8,128)S(1)}, f32[2,32,1024]{2,1,0:T(8,128)S(1)}, u32[]{:S(2)}, u32[]{:S(2)}) collective-permute-start(f32[2,32,1024]{2,1,0:T(8,128)S(1)} %collective-permute-done.37), channel_id=1, source_target_pairs={{0,2},{2,4},{4,6},{6,0},{1,3},{3,5},{5,7},{7,1},{8,10},{10,12},{12... | collective-permute-start | bytes 786440 | tf_op jit(solution)/shard_map/ppermute | solution.py:115
  320.7 30.4 %collective-permute-start.41 = (f32[2,32,1024]{2,1,0:T(8,128)S(1)}, f32[2,32,1024]{2,1,0:T(8,128)S(1)}, u32[]{:S(2)}, u32[]{:S(2)}) collective-permute-start(f32[2,32,1024]{2,1,0:T(8,128)S(1)} %collective-permute-done.40), channel_id=1, source_target_pairs={{0,6},{2,0},{4,2},{6,4},{1,7},{3,1},{5,3},{7,5},{8,14},{10,8},{12,... | collective-permute-start | bytes 786440 | tf_op jit(solution)/shard_map/ppermute | solution.py:115
  321.7 29.7 %collective-permute-start.52 = (f32[2,32,1024]{2,1,0:T(8,128)S(1)}, f32[2,32,1024]{2,1,0:T(8,128)S(1)}, u32[]{:S(2)}, u32[]{:S(2)}) collective-permute-start(f32[2,32,1024]{2,1,0:T(8,128)S(1)} %collective-permute-done.51), channel_id=1, source_target_pairs={{0,2},{2,4},{4,6},{6,0},{1,3},{3,5},{5,7},{7,1},{8,10},{10,12},{12... | collective-permute-start | bytes 786440 | tf_op jit(solution)/shard_map/ppermute | solution.py:115
  326.3 12.8 %collective-permute-start.66 = (f32[2,32,1024]{2,1,0:T(8,128)S(1)}, f32[2,32,1024]{2,1,0:T(8,128)S(1)}, u32[]{:S(2)}, u32[]{:S(2)}) collective-permute-start(f32[2,32,1024]{2,1,0:T(8,128)S(1)} %collective-permute-done.65), channel_id=1, source_target_pairs={{0,2},{2,4},{4,6},{6,0},{1,3},{3,5},{5,7},{7,1},{8,10},{10,12},{12... | collective-permute-start | bytes 786440 | tf_op jit(solution)/shard_map/ppermute | solution.py:115
  326.8 12.3 %collective-permute-start.69 = (f32[2,32,1024]{2,1,0:T(8,128)S(1)}, f32[2,32,1024]{2,1,0:T(8,128)S(1)}, u32[]{:S(2)}, u32[]{:S(2)}) collective-permute-start(f32[2,32,1024]{2,1,0:T(8,128)S(1)} %collective-permute-done.68), channel_id=1, source_target_pairs={{0,6},{2,0},{4,2},{6,4},{1,7},{3,1},{5,3},{7,5},{8,14},{10,8},{12,... | collective-permute-start | bytes 786440 | tf_op jit(solution)/shard_map/ppermute | solution.py:115
  393.1 12.5 %collective-permute-start.101 = (f32[2,32,1024]{2,1,0:T(8,128)S(1)}, f32[2,32,1024]{2,1,0:T(8,128)S(1)}, u32[]{:S(2)}, u32[]{:S(2)}) collective-permute-start(f32[2,32,1024]{2,1,0:T(8,128)S(1)} %dynamic-slice_bitcast_fusion), channel_id=1, source_target_pairs={{0,6},{2,0},{4,2},{6,4},{1,7},{3,1},{5,3},{7,5},{8,14},{10,8},{12,... | collective-permute-start | bytes 786440 | tf_op jit(solution)/shard_map/ppermute | solution.py:95
  395.6 12.5 %collective-permute-start.98 = (f32[2,32,1024]{2,1,0:T(8,128)S(1)}, f32[2,32,1024]{2,1,0:T(8,128)S(1)}, u32[]{:S(2)}, u32[]{:S(2)}) collective-permute-start(f32[2,32,1024]{2,1,0:T(8,128)S(1)} %dynamic-slice_bitcast_fusion.1), channel_id=1, source_target_pairs={{0,2},{2,4},{4,6},{6,0},{1,3},{3,5},{5,7},{7,1},{8,10},{10,12},{12... | collective-permute-start | bytes 786440 | tf_op jit(solution)/shard_map/ppermute | solution.py:95
  441.9 13.2 %collective-permute-start.92 = (f32[2,32,1024]{2,1,0:T(8,128)S(1)}, f32[2,32,1024]{2,1,0:T(8,128)S(1)}, u32[]{:S(2)}, u32[]{:S(2)}) collective-permute-start(f32[2,32,1024]{2,1,0:T(8,128)S(1)} %get-tuple-element.122), channel_id=1, source_target_pairs={{0,2},{2,4},{4,6},{6,0},{1,3},{3,5},{5,7},{7,1},{8,10},{10,12},{12... | collective-permute-start | bytes 786440 | tf_op jit(solution)/shard_map/ppermute | solution.py:115
  442.0 13.1 %collective-permute-start.95 = (f32[2,32,1024]{2,1,0:T(8,128)S(1)}, f32[2,32,1024]{2,1,0:T(8,128)S(1)}, u32[]{:S(2)}, u32[]{:S(2)}) collective-permute-start(f32[2,32,1024]{2,1,0:T(8,128)S(1)} %get-tuple-element.123), channel_id=1, source_target_pairs={{0,6},{2,0},{4,2},{6,4},{1,7},{3,1},{5,3},{7,5},{8,14},{10,8},{12,... | collective-permute-start | bytes 786440 | tf_op jit(solution)/shard_map/ppermute | solution.py:115
  451.6 105.3 %collective-permute-start.106 = (f32[2,32,1024]{2,1,0:T(8,128)}, f32[2,32,1024]{2,1,0:T(8,128)}, u32[]{:S(2)}, u32[]{:S(2)}) collective-permute-start(f32[2,32,1024]{2,1,0:T(8,128)} %get-tuple-element.124), channel_id=1, source_target_pairs={{0,2},{2,4},{4,6},{6,0},{1,3},{3,5},{5,7},{7,1},{8,10},{10,12},{12... | collective-permute-start | bytes 786440 | tf_op jit(solution)/shard_map/ppermute | solution.py:115
  451.7 112.1 %collective-permute-start.109 = (f32[2,32,1024]{2,1,0:T(8,128)}, f32[2,32,1024]{2,1,0:T(8,128)S(1)}, u32[]{:S(2)}, u32[]{:S(2)}) collective-permute-start(f32[2,32,1024]{2,1,0:T(8,128)} %get-tuple-element.125), channel_id=1, source_target_pairs={{0,6},{2,0},{4,2},{6,4},{1,7},{3,1},{5,3},{7,5},{8,14},{10,8},{12,... | collective-permute-start | bytes 786440 | tf_op jit(solution)/shard_map/ppermute | solution.py:115
  455.1 118.2 %collective-permute-start.93 = (f32[2,32,1024]{2,1,0:T(8,128)S(1)}, f32[2,32,1024]{2,1,0:T(8,128)S(1)}, u32[]{:S(2)}, u32[]{:S(2)}) collective-permute-start(f32[2,32,1024]{2,1,0:T(8,128)S(1)} %collective-permute-done.92), channel_id=1, source_target_pairs={{0,2},{2,4},{4,6},{6,0},{1,3},{3,5},{5,7},{7,1},{8,10},{10,12},{12... | collective-permute-start | bytes 786440 | tf_op jit(solution)/shard_map/ppermute | solution.py:115
  455.1 118.2 %collective-permute-start.96 = (f32[2,32,1024]{2,1,0:T(8,128)S(1)}, f32[2,32,1024]{2,1,0:T(8,128)S(1)}, u32[]{:S(2)}, u32[]{:S(2)}) collective-permute-start(f32[2,32,1024]{2,1,0:T(8,128)S(1)} %collective-permute-done.95), channel_id=1, source_target_pairs={{0,6},{2,0},{4,2},{6,4},{1,7},{3,1},{5,3},{7,5},{8,14},{10,8},{12,... | collective-permute-start | bytes 786440 | tf_op jit(solution)/shard_map/ppermute | solution.py:115
  556.9 20.4 %collective-permute-start.107 = (f32[2,32,1024]{2,1,0:T(8,128)}, f32[2,32,1024]{2,1,0:T(8,128)S(1)}, u32[]{:S(2)}, u32[]{:S(2)}) collective-permute-start(f32[2,32,1024]{2,1,0:T(8,128)} %collective-permute-done.106), channel_id=1, source_target_pairs={{0,2},{2,4},{4,6},{6,0},{1,3},{3,5},{5,7},{7,1},{8,10},{10,12},{12... | collective-permute-start | bytes 786440 | tf_op jit(solution)/shard_map/ppermute | solution.py:115
  563.8 13.6 %collective-permute-start.110 = (f32[2,32,1024]{2,1,0:T(8,128)S(1)}, f32[2,32,1024]{2,1,0:T(8,128)S(1)}, u32[]{:S(2)}, u32[]{:S(2)}) collective-permute-start(f32[2,32,1024]{2,1,0:T(8,128)S(1)} %collective-permute-done.109), channel_id=1, source_target_pairs={{0,6},{2,0},{4,2},{6,4},{1,7},{3,1},{5,3},{7,5},{8,14},{10,8},{12,... | collective-permute-start | bytes 786440 | tf_op jit(solution)/shard_map/ppermute | solution.py:115
  (163 other events, 1253.4 us)
Sparse Core Ops, SparseCore 0:
  181.6 160.7 all-reduce.7
  436.2 117.7 all-reduce.5

commit v3 on v2

--- a/solution.py
+++ b/solution.py
@@ -8,6 +8,7 @@
 EPS = 1e-05
 THETA = 1000000.0
 TENSOR = ("ty", "tx")
+DP = ("dx", "dz", "dc")
 
 
 def outer(first_op, second_op):
@@ -126,6 +127,44 @@
     return jnp.concatenate([tensor_sum(block) for block in blocks], axis=0)
 
 
+def ring_sum(values, ring_axis, pair_axes):
+    rows, cols = values.shape
+    size = lax.axis_size(ring_axis)
+    here = lax.axis_index(ring_axis)
+    parts = values.reshape(2, size, rows // (2 * size), cols)
+    accs = []
+    for way, shift in ((0, 1), (1, -1)):
+        chunks = parts[way]
+        acc = lax.dynamic_index_in_dim(chunks, (here - shift) % size, 0, keepdims=False)
+        for step in range(1, size):
+            acc = lax.ppermute(acc, ring_axis, ring(size, shift))
+            acc = acc + lax.dynamic_index_in_dim(chunks, (here - shift * (1 + step)) % size, 0, keepdims=False)
+        accs.append(acc)
+    acc = jnp.stack(accs)
+    sides = []
+    for axis in pair_axes:
+        side = lax.axis_index(axis)
+        halves = acc.reshape(2, 2, acc.shape[1] // 2, cols)
+        keep = lax.dynamic_index_in_dim(halves, side, 1, keepdims=False)
+        send = lax.dynamic_index_in_dim(halves, 1 - side, 1, keepdims=False)
+        acc = keep + lax.ppermute(send, axis, [(0, 1), (1, 0)])
+        sides.append(side)
+    for axis, side in zip(pair_axes[::-1], sides[::-1]):
+        other = lax.ppermute(acc, axis, [(0, 1), (1, 0)])
+        both = jnp.where(side == 0, jnp.stack([acc, other], 1), jnp.stack([other, acc], 1))
+        acc = both.reshape(2, 2 * acc.shape[1], cols)
+    outs = []
+    for way, shift in ((0, 1), (1, -1)):
+        cur = acc[way]
+        gathered = jnp.zeros((size,) + cur.shape, values.dtype)
+        gathered = lax.dynamic_update_index_in_dim(gathered, cur, here, 0)
+        for step in range(1, size):
+            cur = lax.ppermute(cur, ring_axis, ring(size, shift))
+            gathered = lax.dynamic_update_index_in_dim(gathered, cur, (here - shift * step) % size, 0)
+        outs.append(gathered)
+    return jnp.stack(outs).reshape(rows, cols)
+
+
 def small_tensor_sum(values):
     ny = lax.axis_size("ty")
     nx = lax.axis_size("tx")
@@ -217,7 +256,7 @@
     ffn_w_grads, two_partial = lax.optimization_barrier(
         ((down_grad, gate_w_grad, up_w_grad), inner(gate_grad, w_gate) + inner(up_grad, w_up))
     )
-    ffn_w_grads = lax.psum(ffn_w_grads, "dp")
+    ffn_w_grads = lax.psum(ffn_w_grads, DP)
     normed_two_grad = split_tensor_sum(two_partial)
     ffn_grad = jnp.sum(normed_two_grad * residual * scale_two, axis=0)
     residual_grad = cotangent.astype(jnp.float32) + rms_back(
@@ -274,7 +313,21 @@
             one_partial,
         )
     )
-    query_w_grad, key_w_grad, value_w_grad, out_pack = lax.psum(dp_sums, "dp")
+    query_w_grad, key_w_grad, value_w_grad, out_pack = dp_sums
+    q_cols = query_w_grad.shape[1]
+    k_cols = key_w_grad.shape[1]
+    width = out_pack.shape[1]
+    flat = jnp.concatenate([query_w_grad, key_w_grad, value_w_grad], axis=1).reshape(-1, width)
+    flat_rows = flat.shape[0]
+    packed = jnp.concatenate([flat, out_pack], axis=0)
+    padded_rows = -(-packed.shape[0] // 256) * 256
+    packed = jnp.pad(packed, ((0, padded_rows - packed.shape[0]), (0, 0)))
+    packed = ring_sum(packed, "dz", ("dc", "dx"))
+    flat = packed[:flat_rows].reshape(query_w_grad.shape[0], -1)
+    query_w_grad = flat[:, :q_cols]
+    key_w_grad = flat[:, q_cols : q_cols + k_cols]
+    value_w_grad = flat[:, q_cols + k_cols :]
+    out_pack = packed[flat_rows : flat_rows + out_pack.shape[0]]
     down_grad, gate_w_grad, up_w_grad = ffn_w_grads
     normed_one_grad = split_tensor_sum(one_partial)
     input_grad = residual_grad + rms_back(normed_one_grad, tokens_wide, scale_one, attn_gain)
@@ -305,13 +358,15 @@
     from jax.sharding import Mesh
 
     dp_size, tensor_size = mesh.devices.shape
-    split = Mesh(mesh.devices.reshape(dp_size, tensor_size // 2, 2), ("dp", "ty", "tx"))
+    split = Mesh(
+        mesh.devices.reshape(2, dp_size // 4, 2, tensor_size // 2, 2), DP + TENSOR
+    )
     return jax.shard_map(
         per_device,
         mesh=split,
         in_specs=(
-            P("dp", None),
-            P("dp"),
+            P(DP, None),
+            P(DP),
             P(),
             P(None, TENSOR),
             P(None, TENSOR),
@@ -323,11 +378,11 @@
             P(None, TENSOR),
             P(None, TENSOR),
             P(TENSOR, None),
-            P("dp", None),
+            P(DP, None),
         ),
         out_specs=(
-            P("dp", None),
-            P("dp", None),
+            P(DP, None),
+            P(DP, None),
             P(),
             P(None, TENSOR),
             P(None, TENSOR),

time: 620 us -> 550 us (0.89)
  waiting for transfers between devices: 250 us -> 187 us
  local copies, waits for them, and re-layouts: 59 us -> 48.2 us
    psum x2 -> x1, waiting for transfers between devices: 95.6 us -> 0.01 us  [per_device(): ffn_w_grads = lax.psum(ffn_w_grads, DP)]
    ppermute x0 -> x16, waiting for transfers between devices: none -> 23.5 us  [the longest x6 7.64 us: ring_sum(): acc = lax.ppermute(acc, ring_axis, ring(size, shift))]
    ppermute x48, waiting for transfers between devices: 59.6 us -> 78.8 us  [tensor_sum(): cur = lax.ppermute(cur, 'ty', ring(ny, shift))]
    ppermute x0 -> x16, starting transfers between devices: none -> 16.2 us  [the longest x6 7.05 us: ring_sum(): cur = lax.ppermute(cur, ring_axis, ring(size, shift))]
    ppermute x48, waiting for transfers between devices: 47.4 us -> 40.9 us  [tensor_sum(): acc = lax.ppermute(acc, 'ty', ring(ny, shift))]
    unnamed x194 -> x179, local copies, waits for them, and re-layouts: 22.4 us -> 18.3 us
  transfers between devices with their start and end apart: 117 -> 132, of which waited for: 65 -> 78; matrix products, arithmetic and copies ran while one was open for 15% -> 16% of each run, Pallas kernels for 0% -> 0%
where the time goes in v3:
time: 550 us; the launch traced here: 541 us
  waiting for transfers between devices  187 us (34%)
  starting transfers between devices  178 us (32%)
  other arithmetic  59.3 us (11%)
  matrix products  50.6 us (9%)
  local copies, waits for them, and re-layouts  48.2 us (9%)
  between operations  17.3 us (3%)
    ppermute x48, waiting for transfers between devices, tensor_sum(): cur = lax.ppermute(cur, 'ty', ring(ny, shift))  78.8 us
    ppermute x48, starting transfers between devices, tensor_sum(): acc = lax.ppermute(acc, 'ty', ring(ny, shift))  64.6 us
    ppermute x48, starting transfers between devices, tensor_sum(): cur = lax.ppermute(cur, 'ty', ring(ny, shift))  55.3 us
    ppermute x48, waiting for transfers between devices, tensor_sum(): acc = lax.ppermute(acc, 'ty', ring(ny, shift))  40.9 us
    ppermute x8, waiting for transfers between devices, tensor_sum(): got = lax.ppermute(send, 'tx', pairs)  29.7 us
    ppermute x8, starting transfers between devices, tensor_sum(): other = lax.ppermute(mine, 'tx', pairs)  21.5 us
    unnamed x179, local copies, waits for them, and re-layouts  18.3 us
    dot_general x7, matrix products, inner(): lax.dot_general(first_op, second_op, (((1,), (1,)), ((), ())), preferred_...  16.5 us
  transfers between devices with their start and end apart: 132, of which 78 were waited for; matrix products, arithmetic and copies ran while one was open for 16% of the time, Pallas kernels for 0%

profile of v3, /device:TPU:0, one launch (start us, length us, event | category | flops | bytes accessed | tf_op | source)
XLA Modules:
  0.0 540.6 jit_solution(9635205750514043744)
XLA Ops:
  46.7 3.4 collective-permute-start.17
  53.0 3.3 collective-permute-start.4
  58.6 3.3 collective-permute-start.18
  63.9 3.3 collective-permute-start.5
  68.2 3.8 collective-permute-start.19
  75.0 4.0 collective-permute-done.2
  91.2 3.7 collective-permute-done.20
  105.9 3.3 collective-permute-start.25
  112.3 3.3 collective-permute-start.12
  118.0 3.3 collective-permute-start.26
  123.6 3.3 collective-permute-start.13
  129.2 3.7 collective-permute-start.27
  133.4 3.4 collective-permute-done.24
  146.6 3.9 fusion.129
  170.1 4.8 convolution_add_fusion
  176.2 3.2 collective-permute-start.59
  205.8 3.4 collective-permute-done.43
  211.4 3.4 collective-permute-done.57
  217.0 3.4 collective-permute-done.71
  222.6 3.4 collective-permute-done.30
  240.5 4.8 collective-permute-done.34
  248.4 5.3 collective-permute-done.48
  256.9 5.3 collective-permute-done.62
  265.3 5.3 collective-permute-done.76
  273.0 3.8 collective-permute-done.35
  288.0 3.3 collective-permute-start.67
  294.9 3.5 collective-permute-done.64
  300.5 3.5 collective-permute-done.78
  306.1 3.5 collective-permute-done.37
  311.8 3.5 collective-permute-done.51
  317.4 3.5 collective-permute-done.65
  323.0 3.5 collective-permute-done.79
  326.9 3.2 collective-permute-start.69
  330.2 9.0 %collective-permute-done.66 = f32[2,32,1024]{2,1,0:T(8,128)S(1)} collective-permute-done((f32[2,32,1024]{2,1,0:T(8,128)S(1)}, f32[2,32,1024]{2,1,0:T(8,128)S(1)}, u32[]{:S(2)}, u32[]{:S(2)}) %collective-permute-start.66) | collective-permute-done | bytes 262176 | tf_op jit(solution)/shard_map/ppermute | solution.py:116
  339.3 3.3 collective-permute-start.83
  342.8 4.0 collective-permute-done.80
  353.4 4.8 multiply_add_fusion
  377.2 3.3 fusion.17
  436.0 4.7 collective-permute-done.90
  440.8 6.7 %collective-permute-done.119 = f32[2,16,1024]{2,1,0:T(8,128)S(1)} collective-permute-done((f32[2,16,1024]{2,1,0:T(8,128)S(1)}, f32[2,16,1024]{2,1,0:T(8,128)S(1)}, u32[]{:S(2)}, u32[]{:S(2)}) %collective-permute-start.119) | collective-permute-done | bytes 131104 | tf_op jit(solution)/shard_map/ppermute | solution.py:150
  447.8 3.6 collective-permute-start.105
  451.4 4.5 collective-permute-done.120
  476.7 3.3 collective-permute-done.93
  486.3 4.1 collective-permute-done.94
  501.4 4.2 collective-permute-done.124
  506.6 3.6 collective-permute-done.128
  515.4 3.2 collective-permute-start.130
  525.9 3.5 copy.133
  (698 shorter events, 335.2 us)
Async XLA Ops:
  7.2 380.2 %all-reduce.5.cloned.1.call-start = ((), (), s32[]{:S(2)}) async-start(), calls=%async_computation | async-start | bytes 14155776 | tf_op jit(solution)/shard_map/psum | solution.py:259
  68.2 13.9 %collective-permute-start.19 = (f32[2,32,1024]{2,1,0:T(8,128)S(1)}, f32[2,32,1024]{2,1,0:T(8,128)S(1)}, u32[]{:S(2)}, u32[]{:S(2)}) collective-permute-start(f32[2,32,1024]{2,1,0:T(8,128)S(1)} %bitcast_add_fusion.43), channel_id=1, source_target_pairs={{0,6},{2,0},{4,2},{6,4},{1,7},{3,1},{5,3},{7,5},{8,14},{10,8},{12,... | collective-permute-start | bytes 786440 | tf_op jit(solution)/shard_map/ppermute | solution.py:96
  88.2 12.3 %collective-permute-start.7 = (f32[2,32,1024]{2,1,0:T(8,128)}, f32[2,32,1024]{2,1,0:T(8,128)}, u32[]{:S(2)}, u32[]{:S(2)}) collective-permute-start(f32[2,32,1024]{2,1,0:T(8,128)} %fusion.78), channel_id=1, source_target_pairs={{0,1},{1,0},{2,3},{3,2},{4,5},{5,4},{6,7},{7,6},{8,9},{9,8},{10,11... | collective-permute-start | bytes 786440 | tf_op jit(solution)/shard_map/ppermute | solution.py:108
  105.6 12.3 %collective-permute-start.22 = (f32[2,32,1024]{2,1,0:T(8,128)S(1)}, f32[2,32,1024]{2,1,0:T(8,128)S(1)}, u32[]{:S(2)}, u32[]{:S(2)}) collective-permute-start(f32[2,32,1024]{2,1,0:T(8,128)S(1)} %get-tuple-element.178), channel_id=1, source_target_pairs={{0,2},{2,4},{4,6},{6,0},{1,3},{3,5},{5,7},{7,1},{8,10},{10,12},{12... | collective-permute-start | bytes 786440 | tf_op jit(solution)/shard_map/ppermute | solution.py:116
  159.3 22.4 %collective-permute-start.31 = (f32[2,32,1024]{2,1,0:T(8,128)}, f32[2,32,1024]{2,1,0:T(8,128)}, u32[]{:S(2)}, u32[]{:S(2)}) collective-permute-start(f32[2,32,1024]{2,1,0:T(8,128)} %dynamic-slice_bitcast_fusion.12), channel_id=1, source_target_pairs={{0,6},{2,0},{4,2},{6,4},{1,7},{3,1},{5,3},{7,5},{8,14},{10,8},{12,... | collective-permute-start | bytes 786440 | tf_op jit(solution)/shard_map/ppermute | solution.py:96
  162.4 20.6 %collective-permute-start.28 = (f32[2,32,1024]{2,1,0:T(8,128)}, f32[2,32,1024]{2,1,0:T(8,128)}, u32[]{:S(2)}, u32[]{:S(2)}) collective-permute-start(f32[2,32,1024]{2,1,0:T(8,128)} %dynamic-slice_bitcast_fusion.13), channel_id=1, source_target_pairs={{0,2},{2,4},{4,6},{6,0},{1,3},{3,5},{5,7},{7,1},{8,10},{10,12},{12... | collective-permute-start | bytes 786440 | tf_op jit(solution)/shard_map/ppermute | solution.py:96
  163.3 23.9 %collective-permute-start.45 = (f32[2,32,1024]{2,1,0:T(8,128)}, f32[2,32,1024]{2,1,0:T(8,128)}, u32[]{:S(2)}, u32[]{:S(2)}) collective-permute-start(f32[2,32,1024]{2,1,0:T(8,128)} %dynamic-slice_bitcast_fusion.10), channel_id=1, source_target_pairs={{0,6},{2,0},{4,2},{6,4},{1,7},{3,1},{5,3},{7,5},{8,14},{10,8},{12,... | collective-permute-start | bytes 786440 | tf_op jit(solution)/shard_map/ppermute | solution.py:96
  167.3 21.2 %collective-permute-start.42 = (f32[2,32,1024]{2,1,0:T(8,128)}, f32[2,32,1024]{2,1,0:T(8,128)}, u32[]{:S(2)}, u32[]{:S(2)}) collective-permute-start(f32[2,32,1024]{2,1,0:T(8,128)} %dynamic-slice_bitcast_fusion.11), channel_id=1, source_target_pairs={{0,2},{2,4},{4,6},{6,0},{1,3},{3,5},{5,7},{7,1},{8,10},{10,12},{12... | collective-permute-start | bytes 786440 | tf_op jit(solution)/shard_map/ppermute | solution.py:96
  176.2 16.5 %collective-permute-start.59 = (f32[2,32,1024]{2,1,0:T(8,128)}, f32[2,32,1024]{2,1,0:T(8,128)}, u32[]{:S(2)}, u32[]{:S(2)}) collective-permute-start(f32[2,32,1024]{2,1,0:T(8,128)} %dynamic-slice_bitcast_fusion.8), channel_id=1, source_target_pairs={{0,6},{2,0},{4,2},{6,4},{1,7},{3,1},{5,3},{7,5},{8,14},{10,8},{12,... | collective-permute-start | bytes 786440 | tf_op jit(solution)/shard_map/ppermute | solution.py:96
  181.7 12.2 %collective-permute-start.56 = (f32[2,32,1024]{2,1,0:T(8,128)}, f32[2,32,1024]{2,1,0:T(8,128)S(1)}, u32[]{:S(2)}, u32[]{:S(2)}) collective-permute-start(f32[2,32,1024]{2,1,0:T(8,128)} %dynamic-slice_bitcast_fusion.9), channel_id=1, source_target_pairs={{0,2},{2,4},{4,6},{6,0},{1,3},{3,5},{5,7},{7,1},{8,10},{10,12},{12... | collective-permute-start | bytes 786440 | tf_op jit(solution)/shard_map/ppermute | solution.py:96
  183.0 14.2 %collective-permute-start.73 = (f32[2,32,1024]{2,1,0:T(8,128)}, f32[2,32,1024]{2,1,0:T(8,128)S(1)}, u32[]{:S(2)}, u32[]{:S(2)}) collective-permute-start(f32[2,32,1024]{2,1,0:T(8,128)} %dynamic-slice_bitcast_fusion.6), channel_id=1, source_target_pairs={{0,6},{2,0},{4,2},{6,4},{1,7},{3,1},{5,3},{7,5},{8,14},{10,8},{12,... | collective-permute-start | bytes 786440 | tf_op jit(solution)/shard_map/ppermute | solution.py:96
  188.5 12.2 %collective-permute-start.32 = (f32[2,32,1024]{2,1,0:T(8,128)S(1)}, f32[2,32,1024]{2,1,0:T(8,128)S(1)}, u32[]{:S(2)}, u32[]{:S(2)}) collective-permute-start(f32[2,32,1024]{2,1,0:T(8,128)S(1)} %bitcast_add_fusion.38), channel_id=1, source_target_pairs={{0,6},{2,0},{4,2},{6,4},{1,7},{3,1},{5,3},{7,5},{8,14},{10,8},{12,... | collective-permute-start | bytes 786440 | tf_op jit(solution)/shard_map/ppermute | solution.py:96
  200.7 14.1 %collective-permute-start.57 = (f32[2,32,1024]{2,1,0:T(8,128)S(1)}, f32[2,32,1024]{2,1,0:T(8,128)S(1)}, u32[]{:S(2)}, u32[]{:S(2)}) collective-permute-start(f32[2,32,1024]{2,1,0:T(8,128)S(1)} %bitcast_add_fusion.29), channel_id=1, source_target_pairs={{0,2},{2,4},{4,6},{6,0},{1,3},{3,5},{5,7},{7,1},{8,10},{10,12},{12... | collective-permute-start | bytes 786440 | tf_op jit(solution)/shard_map/ppermute | solution.py:96
  204.2 16.3 %collective-permute-start.71 = (f32[2,32,1024]{2,1,0:T(8,128)S(1)}, f32[2,32,1024]{2,1,0:T(8,128)S(1)}, u32[]{:S(2)}, u32[]{:S(2)}) collective-permute-start(f32[2,32,1024]{2,1,0:T(8,128)S(1)} %bitcast_add_fusion.23), channel_id=1, source_target_pairs={{0,2},{2,4},{4,6},{6,0},{1,3},{3,5},{5,7},{7,1},{8,10},{10,12},{12... | collective-permute-start | bytes 786440 | tf_op jit(solution)/shard_map/ppermute | solution.py:96
  209.7 16.4 %collective-permute-start.30 = (f32[2,32,1024]{2,1,0:T(8,128)S(1)}, f32[2,32,1024]{2,1,0:T(8,128)S(1)}, u32[]{:S(2)}, u32[]{:S(2)}) collective-permute-start(f32[2,32,1024]{2,1,0:T(8,128)S(1)} %bitcast_add_fusion.40), channel_id=1, source_target_pairs={{0,2},{2,4},{4,6},{6,0},{1,3},{3,5},{5,7},{7,1},{8,10},{10,12},{12... | collective-permute-start | bytes 786440 | tf_op jit(solution)/shard_map/ppermute | solution.py:96
  215.3 16.4 %collective-permute-start.44 = (f32[2,32,1024]{2,1,0:T(8,128)S(1)}, f32[2,32,1024]{2,1,0:T(8,128)S(1)}, u32[]{:S(2)}, u32[]{:S(2)}) collective-permute-start(f32[2,32,1024]{2,1,0:T(8,128)S(1)} %bitcast_add_fusion.34), channel_id=1, source_target_pairs={{0,2},{2,4},{4,6},{6,0},{1,3},{3,5},{5,7},{7,1},{8,10},{10,12},{12... | collective-permute-start | bytes 786440 | tf_op jit(solution)/shard_map/ppermute | solution.py:96
  220.5 14.3 %collective-permute-start.61 = (f32[2,32,1024]{2,1,0:T(8,128)S(1)}, f32[2,32,1024]{2,1,0:T(8,128)S(1)}, u32[]{:S(2)}, u32[]{:S(2)}) collective-permute-start(f32[2,32,1024]{2,1,0:T(8,128)S(1)} %bitcast_add_fusion.25), channel_id=1, source_target_pairs={{0,6},{2,0},{4,2},{6,4},{1,7},{3,1},{5,3},{7,5},{8,14},{10,8},{12,... | collective-permute-start | bytes 786440 | tf_op jit(solution)/shard_map/ppermute | solution.py:96
  220.9 14.5 %collective-permute-start.58 = (f32[2,32,1024]{2,1,0:T(8,128)S(1)}, f32[2,32,1024]{2,1,0:T(8,128)S(1)}, u32[]{:S(2)}, u32[]{:S(2)}) collective-permute-start(f32[2,32,1024]{2,1,0:T(8,128)S(1)} %bitcast_add_fusion.28), channel_id=1, source_target_pairs={{0,2},{2,4},{4,6},{6,0},{1,3},{3,5},{5,7},{7,1},{8,10},{10,12},{12... | collective-permute-start | bytes 786440 | tf_op jit(solution)/shard_map/ppermute | solution.py:96
  226.1 12.5 %collective-permute-start.75 = (f32[2,32,1024]{2,1,0:T(8,128)S(1)}, f32[2,32,1024]{2,1,0:T(8,128)S(1)}, u32[]{:S(2)}, u32[]{:S(2)}) collective-permute-start(f32[2,32,1024]{2,1,0:T(8,128)S(1)} %bitcast_add_fusion.19), channel_id=1, source_target_pairs={{0,6},{2,0},{4,2},{6,4},{1,7},{3,1},{5,3},{7,5},{8,14},{10,8},{12,... | collective-permute-start | bytes 786440 | tf_op jit(solution)/shard_map/ppermute | solution.py:96
  231.7 13.6 %collective-permute-start.34 = (f32[2,32,1024]{2,1,0:T(8,128)S(1)}, f32[2,32,1024]{2,1,0:T(8,128)S(1)}, u32[]{:S(2)}, u32[]{:S(2)}) collective-permute-start(f32[2,32,1024]{2,1,0:T(8,128)S(1)} %fusion.65), channel_id=1, source_target_pairs={{0,1},{1,0},{2,3},{3,2},{4,5},{5,4},{6,7},{7,6},{8,9},{9,8},{10,11... | collective-permute-start | bytes 786440 | tf_op jit(solution)/shard_map/ppermute | solution.py:106
  234.8 18.9 %collective-permute-start.48 = (f32[2,32,1024]{2,1,0:T(8,128)S(1)}, f32[2,32,1024]{2,1,0:T(8,128)S(1)}, u32[]{:S(2)}, u32[]{:S(2)}) collective-permute-start(f32[2,32,1024]{2,1,0:T(8,128)S(1)} %fusion.60), channel_id=1, source_target_pairs={{0,1},{1,0},{2,3},{3,2},{4,5},{5,4},{6,7},{7,6},{8,9},{9,8},{10,11... | collective-permute-start | bytes 786440 | tf_op jit(solution)/shard_map/ppermute | solution.py:106
  235.5 26.7 %collective-permute-start.62 = (f32[2,32,1024]{2,1,0:T(8,128)S(1)}, f32[2,32,1024]{2,1,0:T(8,128)S(1)}, u32[]{:S(2)}, u32[]{:S(2)}) collective-permute-start(f32[2,32,1024]{2,1,0:T(8,128)S(1)} %fusion.55), channel_id=1, source_target_pairs={{0,1},{1,0},{2,3},{3,2},{4,5},{5,4},{6,7},{7,6},{8,9},{9,8},{10,11... | collective-permute-start | bytes 786440 | tf_op jit(solution)/shard_map/ppermute | solution.py:106
  238.7 31.9 %collective-permute-start.76 = (f32[2,32,1024]{2,1,0:T(8,128)S(1)}, f32[2,32,1024]{2,1,0:T(8,128)S(1)}, u32[]{:S(2)}, u32[]{:S(2)}) collective-permute-start(f32[2,32,1024]{2,1,0:T(8,128)S(1)} %fusion.50), channel_id=1, source_target_pairs={{0,1},{1,0},{2,3},{3,2},{4,5},{5,4},{6,7},{7,6},{8,9},{9,8},{10,11... | collective-permute-start | bytes 786440 | tf_op jit(solution)/shard_map/ppermute | solution.py:106
  245.3 31.5 %collective-permute-start.35 = (f32[2,32,1024]{2,1,0:T(8,128)S(1)}, f32[2,32,1024]{2,1,0:T(8,128)S(1)}, u32[]{:S(2)}, u32[]{:S(2)}) collective-permute-start(f32[2,32,1024]{2,1,0:T(8,128)S(1)} %fusion.68), channel_id=1, source_target_pairs={{0,1},{1,0},{2,3},{3,2},{4,5},{5,4},{6,7},{7,6},{8,9},{9,8},{10,11... | collective-permute-start | bytes 786440 | tf_op jit(solution)/shard_map/ppermute | solution.py:108
  253.8 28.2 %collective-permute-start.49 = (f32[2,32,1024]{2,1,0:T(8,128)S(1)}, f32[2,32,1024]{2,1,0:T(8,128)S(1)}, u32[]{:S(2)}, u32[]{:S(2)}) collective-permute-start(f32[2,32,1024]{2,1,0:T(8,128)S(1)} %fusion.63), channel_id=1, source_target_pairs={{0,1},{1,0},{2,3},{3,2},{4,5},{5,4},{6,7},{7,6},{8,9},{9,8},{10,11... | collective-permute-start | bytes 786440 | tf_op jit(solution)/shard_map/ppermute | solution.py:108
  262.2 22.6 %collective-permute-start.63 = (f32[2,32,1024]{2,1,0:T(8,128)S(1)}, f32[2,32,1024]{2,1,0:T(8,128)S(1)}, u32[]{:S(2)}, u32[]{:S(2)}) collective-permute-start(f32[2,32,1024]{2,1,0:T(8,128)S(1)} %fusion.58), channel_id=1, source_target_pairs={{0,1},{1,0},{2,3},{3,2},{4,5},{5,4},{6,7},{7,6},{8,9},{9,8},{10,11... | collective-permute-start | bytes 786440 | tf_op jit(solution)/shard_map/ppermute | solution.py:108
  270.6 17.0 %collective-permute-start.77 = (f32[2,32,1024]{2,1,0:T(8,128)S(1)}, f32[2,32,1024]{2,1,0:T(8,128)S(1)}, u32[]{:S(2)}, u32[]{:S(2)}) collective-permute-start(f32[2,32,1024]{2,1,0:T(8,128)S(1)} %fusion.53), channel_id=1, source_target_pairs={{0,1},{1,0},{2,3},{3,2},{4,5},{5,4},{6,7},{7,6},{8,9},{9,8},{10,11... | collective-permute-start | bytes 786440 | tf_op jit(solution)/shard_map/ppermute | solution.py:108
  277.7 13.6 %collective-permute-start.39 = (f32[2,32,1024]{2,1,0:T(8,128)S(1)}, f32[2,32,1024]{2,1,0:T(8,128)S(1)}, u32[]{:S(2)}, u32[]{:S(2)}) collective-permute-start(f32[2,32,1024]{2,1,0:T(8,128)S(1)} %get-tuple-element.173), channel_id=1, source_target_pairs={{0,6},{2,0},{4,2},{6,4},{1,7},{3,1},{5,3},{7,5},{8,14},{10,8},{12,... | collective-permute-start | bytes 786440 | tf_op jit(solution)/shard_map/ppermute | solution.py:116
  291.3 12.6 %collective-permute-start.78 = (f32[2,32,1024]{2,1,0:T(8,128)S(1)}, f32[2,32,1024]{2,1,0:T(8,128)S(1)}, u32[]{:S(2)}, u32[]{:S(2)}) collective-permute-start(f32[2,32,1024]{2,1,0:T(8,128)S(1)} %get-tuple-element.170), channel_id=1, source_target_pairs={{0,2},{2,4},{4,6},{6,0},{1,3},{3,5},{5,7},{7,1},{8,10},{10,12},{12... | collective-permute-start | bytes 786440 | tf_op jit(solution)/shard_map/ppermute | solution.py:116
  292.7 12.4 %collective-permute-start.81 = (f32[2,32,1024]{2,1,0:T(8,128)S(1)}, f32[2,32,1024]{2,1,0:T(8,128)S(1)}, u32[]{:S(2)}, u32[]{:S(2)}) collective-permute-start(f32[2,32,1024]{2,1,0:T(8,128)S(1)} %get-tuple-element.171), channel_id=1, source_target_pairs={{0,6},{2,0},{4,2},{6,4},{1,7},{3,1},{5,3},{7,5},{8,14},{10,8},{12,... | collective-permute-start | bytes 786440 | tf_op jit(solution)/shard_map/ppermute | solution.py:116
  294.8 14.8 %collective-permute-start.37 = (f32[2,32,1024]{2,1,0:T(8,128)S(1)}, f32[2,32,1024]{2,1,0:T(8,128)S(1)}, u32[]{:S(2)}, u32[]{:S(2)}) collective-permute-start(f32[2,32,1024]{2,1,0:T(8,128)S(1)} %collective-permute-done.36), channel_id=1, source_target_pairs={{0,2},{2,4},{4,6},{6,0},{1,3},{3,5},{5,7},{7,1},{8,10},{10,12},{12... | collective-permute-start | bytes 786440 | tf_op jit(solution)/shard_map/ppermute | solution.py:116
  298.4 12.4 %collective-permute-start.40 = (f32[2,32,1024]{2,1,0:T(8,128)S(1)}, f32[2,32,1024]{2,1,0:T(8,128)S(1)}, u32[]{:S(2)}, u32[]{:S(2)}) collective-permute-start(f32[2,32,1024]{2,1,0:T(8,128)S(1)} %collective-permute-done.39), channel_id=1, source_target_pairs={{0,6},{2,0},{4,2},{6,4},{1,7},{3,1},{5,3},{7,5},{8,14},{10,8},{12,... | collective-permute-start | bytes 786440 | tf_op jit(solution)/shard_map/ppermute | solution.py:116
  299.5 15.7 %collective-permute-start.51 = (f32[2,32,1024]{2,1,0:T(8,128)S(1)}, f32[2,32,1024]{2,1,0:T(8,128)S(1)}, u32[]{:S(2)}, u32[]{:S(2)}) collective-permute-start(f32[2,32,1024]{2,1,0:T(8,128)S(1)} %collective-permute-done.50), channel_id=1, source_target_pairs={{0,2},{2,4},{4,6},{6,0},{1,3},{3,5},{5,7},{7,1},{8,10},{10,12},{12... | collective-permute-start | bytes 786440 | tf_op jit(solution)/shard_map/ppermute | solution.py:116
  304.0 12.4 %collective-permute-start.54 = (f32[2,32,1024]{2,1,0:T(8,128)S(1)}, f32[2,32,1024]{2,1,0:T(8,128)S(1)}, u32[]{:S(2)}, u32[]{:S(2)}) collective-permute-start(f32[2,32,1024]{2,1,0:T(8,128)S(1)} %collective-permute-done.53), channel_id=1, source_target_pairs={{0,6},{2,0},{4,2},{6,4},{1,7},{3,1},{5,3},{7,5},{8,14},{10,8},{12,... | collective-permute-start | bytes 786440 | tf_op jit(solution)/shard_map/ppermute | solution.py:116
  305.2 15.7 %collective-permute-start.65 = (f32[2,32,1024]{2,1,0:T(8,128)S(1)}, f32[2,32,1024]{2,1,0:T(8,128)S(1)}, u32[]{:S(2)}, u32[]{:S(2)}) collective-permute-start(f32[2,32,1024]{2,1,0:T(8,128)S(1)} %collective-permute-done.64), channel_id=1, source_target_pairs={{0,2},{2,4},{4,6},{6,0},{1,3},{3,5},{5,7},{7,1},{8,10},{10,12},{12... | collective-permute-start | bytes 786440 | tf_op jit(solution)/shard_map/ppermute | solution.py:116
  310.8 15.7 %collective-permute-start.79 = (f32[2,32,1024]{2,1,0:T(8,128)S(1)}, f32[2,32,1024]{2,1,0:T(8,128)S(1)}, u32[]{:S(2)}, u32[]{:S(2)}) collective-permute-start(f32[2,32,1024]{2,1,0:T(8,128)S(1)} %collective-permute-done.78), channel_id=1, source_target_pairs={{0,2},{2,4},{4,6},{6,0},{1,3},{3,5},{5,7},{7,1},{8,10},{10,12},{12... | collective-permute-start | bytes 786440 | tf_op jit(solution)/shard_map/ppermute | solution.py:116
  316.4 34.8 %collective-permute-start.38 = (f32[2,32,1024]{2,1,0:T(8,128)S(1)}, f32[2,32,1024]{2,1,0:T(8,128)S(1)}, u32[]{:S(2)}, u32[]{:S(2)}) collective-permute-start(f32[2,32,1024]{2,1,0:T(8,128)S(1)} %collective-permute-done.37), channel_id=1, source_target_pairs={{0,2},{2,4},{4,6},{6,0},{1,3},{3,5},{5,7},{7,1},{8,10},{10,12},{12... | collective-permute-start | bytes 786440 | tf_op jit(solution)/shard_map/ppermute | solution.py:116
  320.8 30.4 %collective-permute-start.41 = (f32[2,32,1024]{2,1,0:T(8,128)S(1)}, f32[2,32,1024]{2,1,0:T(8,128)S(1)}, u32[]{:S(2)}, u32[]{:S(2)}) collective-permute-start(f32[2,32,1024]{2,1,0:T(8,128)S(1)} %collective-permute-done.40), channel_id=1, source_target_pairs={{0,6},{2,0},{4,2},{6,4},{1,7},{3,1},{5,3},{7,5},{8,14},{10,8},{12,... | collective-permute-start | bytes 786440 | tf_op jit(solution)/shard_map/ppermute | solution.py:116
  321.8 29.7 %collective-permute-start.52 = (f32[2,32,1024]{2,1,0:T(8,128)S(1)}, f32[2,32,1024]{2,1,0:T(8,128)S(1)}, u32[]{:S(2)}, u32[]{:S(2)}) collective-permute-start(f32[2,32,1024]{2,1,0:T(8,128)S(1)} %collective-permute-done.51), channel_id=1, source_target_pairs={{0,2},{2,4},{4,6},{6,0},{1,3},{3,5},{5,7},{7,1},{8,10},{10,12},{12... | collective-permute-start | bytes 786440 | tf_op jit(solution)/shard_map/ppermute | solution.py:116
  326.4 12.8 %collective-permute-start.66 = (f32[2,32,1024]{2,1,0:T(8,128)S(1)}, f32[2,32,1024]{2,1,0:T(8,128)S(1)}, u32[]{:S(2)}, u32[]{:S(2)}) collective-permute-start(f32[2,32,1024]{2,1,0:T(8,128)S(1)} %collective-permute-done.65), channel_id=1, source_target_pairs={{0,2},{2,4},{4,6},{6,0},{1,3},{3,5},{5,7},{7,1},{8,10},{10,12},{12... | collective-permute-start | bytes 786440 | tf_op jit(solution)/shard_map/ppermute | solution.py:116
  326.9 12.3 %collective-permute-start.69 = (f32[2,32,1024]{2,1,0:T(8,128)S(1)}, f32[2,32,1024]{2,1,0:T(8,128)S(1)}, u32[]{:S(2)}, u32[]{:S(2)}) collective-permute-start(f32[2,32,1024]{2,1,0:T(8,128)S(1)} %collective-permute-done.68), channel_id=1, source_target_pairs={{0,6},{2,0},{4,2},{6,4},{1,7},{3,1},{5,3},{7,5},{8,14},{10,8},{12,... | collective-permute-start | bytes 786440 | tf_op jit(solution)/shard_map/ppermute | solution.py:116
  433.3 14.4 %collective-permute-start.104 = (f32[2,32,1024]{2,1,0:T(8,128)S(1)}, f32[2,32,1024]{2,1,0:T(8,128)S(1)}, u32[]{:S(2)}, u32[]{:S(2)}) collective-permute-start(f32[2,32,1024]{2,1,0:T(8,128)S(1)} %fusion.40), channel_id=1, source_target_pairs={{0,1},{1,0},{2,3},{3,2},{4,5},{5,4},{6,7},{7,6},{8,9},{9,8},{10,11... | collective-permute-start | bytes 786440 | tf_op jit(solution)/shard_map/ppermute | solution.py:106
  434.0 13.5 %collective-permute-start.119 = (f32[2,16,1024]{2,1,0:T(8,128)S(1)}, f32[2,16,1024]{2,1,0:T(8,128)S(1)}, u32[]{:S(2)}, u32[]{:S(2)}) collective-permute-start(f32[2,16,1024]{2,1,0:T(8,128)S(1)} %dynamic-slice_bitcast_fusion.18), channel_id=1, source_target_pairs={{0,64},{64,0},{1,65},{65,1},{2,66},{66,2},{3,67},{67,3},{4,68},{68... | collective-permute-start | bytes 393224 | tf_op jit(solution)/shard_map/ppermute | solution.py:150
  440.7 15.2 %collective-permute-start.91 = (f32[2,32,1024]{2,1,0:T(8,128)S(1)}, f32[2,32,1024]{2,1,0:T(8,128)S(1)}, u32[]{:S(2)}, u32[]{:S(2)}) collective-permute-start(f32[2,32,1024]{2,1,0:T(8,128)S(1)} %fusion.48), channel_id=1, source_target_pairs={{0,1},{1,0},{2,3},{3,2},{4,5},{5,4},{6,7},{7,6},{8,9},{9,8},{10,11... | collective-permute-start | bytes 786440 | tf_op jit(solution)/shard_map/ppermute | solution.py:108
  456.3 13.2 %collective-permute-start.95 = (f32[2,32,1024]{2,1,0:T(8,128)S(1)}, f32[2,32,1024]{2,1,0:T(8,128)S(1)}, u32[]{:S(2)}, u32[]{:S(2)}) collective-permute-start(f32[2,32,1024]{2,1,0:T(8,128)S(1)} %get-tuple-element.162), channel_id=1, source_target_pairs={{0,6},{2,0},{4,2},{6,4},{1,7},{3,1},{5,3},{7,5},{8,14},{10,8},{12,... | collective-permute-start | bytes 786440 | tf_op jit(solution)/shard_map/ppermute | solution.py:116
  460.0 12.9 %collective-permute-start.109 = (f32[2,32,1024]{2,1,0:T(8,128)S(1)}, f32[2,32,1024]{2,1,0:T(8,128)S(1)}, u32[]{:S(2)}, u32[]{:S(2)}) collective-permute-start(f32[2,32,1024]{2,1,0:T(8,128)S(1)} %get-tuple-element.164), channel_id=1, source_target_pairs={{0,6},{2,0},{4,2},{6,4},{1,7},{3,1},{5,3},{7,5},{8,14},{10,8},{12,... | collective-permute-start | bytes 786440 | tf_op jit(solution)/shard_map/ppermute | solution.py:116
  476.6 21.4 %collective-permute-start.123 = (f32[64,1024]{1,0:T(8,128)S(1)}, f32[64,1024]{1,0:T(8,128)S(1)}, u32[]{:S(2)}, u32[]{:S(2)}) collective-permute-start(f32[64,1024]{1,0:T(8,128)S(1)} %collective-permute-done.122), channel_id=1, source_target_pairs={{0,16},{16,32},{32,48},{48,0},{1,17},{17,33},{33,49},{49,1},{2,18}... | collective-permute-start | bytes 786440 | tf_op jit(solution)/shard_map/ppermute | solution.py:162
  480.0 19.7 %collective-permute-start.126 = (f32[64,1024]{1,0:T(8,128)S(1)}, f32[64,1024]{1,0:T(8,128)S(1)}, u32[]{:S(2)}, u32[]{:S(2)}) collective-permute-start(f32[64,1024]{1,0:T(8,128)S(1)} %collective-permute-done.125), channel_id=1, source_target_pairs={{0,48},{16,0},{32,16},{48,32},{1,49},{17,1},{33,17},{49,33},{2,50}... | collective-permute-start | bytes 786440 | tf_op jit(solution)/shard_map/ppermute | solution.py:162
  (171 other events, 1341.1 us)
Sparse Core Ops, SparseCore 0:
  181.8 160.6 all-reduce.4

commit v4 on v3

--- a/solution.py
+++ b/solution.py
@@ -243,7 +243,7 @@
     up_proj = jnp.dot(normed_two, w_up, preferred_element_type=jnp.float32)
     gate_sigmoid = jax.nn.sigmoid(gate_proj)
     hidden = (gate_proj * gate_sigmoid * up_proj).astype(jnp.bfloat16)
-    mlp_sum = split_tensor_sum(jnp.dot(hidden, w_down, preferred_element_type=jnp.float32))
+    mlp_sum = tensor_sum(jnp.dot(hidden, w_down, preferred_element_type=jnp.float32))
     output = (residual + mlp_sum).astype(jnp.bfloat16)
     down_grad = outer(hidden, cotangent)
     hidden_grad = inner(cotangent, w_down)
@@ -257,7 +257,7 @@
         ((down_grad, gate_w_grad, up_w_grad), inner(gate_grad, w_gate) + inner(up_grad, w_up))
     )
     ffn_w_grads = lax.psum(ffn_w_grads, DP)
-    normed_two_grad = split_tensor_sum(two_partial)
+    normed_two_grad = tensor_sum(two_partial)
     ffn_grad = jnp.sum(normed_two_grad * residual * scale_two, axis=0)
     residual_grad = cotangent.astype(jnp.float32) + rms_back(
         normed_two_grad, residual, scale_two, ffn_gain
@@ -329,7 +329,7 @@
     value_w_grad = flat[:, q_cols + k_cols :]
     out_pack = packed[flat_rows : flat_rows + out_pack.shape[0]]
     down_grad, gate_w_grad, up_w_grad = ffn_w_grads
-    normed_one_grad = split_tensor_sum(one_partial)
+    normed_one_grad = tensor_sum(one_partial)
     input_grad = residual_grad + rms_back(normed_one_grad, tokens_wide, scale_one, attn_gain)
     out_w_grad = out_pack[:out_rows]
     ffn_grad = out_pack[out_rows]

time: 550 us -> 577 us (1.049)
  waiting for transfers between devices: 187 us -> 232 us
  starting transfers between devices: 178 us -> 154 us
    ppermute x48 -> x30, waiting for transfers between devices: 40.9 us -> 67.3 us  [tensor_sum(): acc = lax.ppermute(acc, 'ty', ring(ny, shift))]
    psum x1, waiting for transfers between devices: 0.01 us -> 18.5 us  [per_device(): ffn_w_grads = lax.psum(ffn_w_grads, DP)]
    ppermute x48 -> x30, starting transfers between devices: 64.6 us -> 54 us  [tensor_sum(): acc = lax.ppermute(acc, 'ty', ring(ny, shift))]
    ppermute x48 -> x30, starting transfers between devices: 55.3 us -> 46.5 us  [tensor_sum(): cur = lax.ppermute(cur, 'ty', ring(ny, shift))]
    ppermute x8 -> x5, waiting for transfers between devices: 10.5 us -> 17.9 us  [tensor_sum(): other = lax.ppermute(mine, 'tx', pairs)]
    ppermute x48 -> x30, waiting for transfers between devices: 78.8 us -> 71.8 us  [tensor_sum(): cur = lax.ppermute(cur, 'ty', ring(ny, shift))]
    ppermute x6, waiting for transfers between devices: 7.64 us -> 14.5 us  [ring_sum(): acc = lax.ppermute(acc, ring_axis, ring(size, shift))]
    ppermute x2, waiting for transfers between devices: 6.66 us -> 0.01 us  [ring_sum(): acc = keep + lax.ppermute(send, axis, [(0, 1), (1, 0)])]
  transfers between devices with their start and end apart: 132 -> 90, of which waited for: 78 -> 53; matrix products, arithmetic and copies ran while one was open for 16% -> 15% of each run, Pallas kernels for 0% -> 0%
where the time goes in v4:
time: 577 us; the launch traced here: 567 us
  waiting for transfers between devices  232 us (40%)
  starting transfers between devices  154 us (27%)
  other arithmetic  60.1 us (10%)
  local copies, waits for them, and re-layouts  53.8 us (9%)
  matrix products  50.3 us (9%)
  between operations  16.8 us (3%)
    ppermute x30, waiting for transfers between devices, tensor_sum(): cur = lax.ppermute(cur, 'ty', ring(ny, shift))  71.8 us
    ppermute x30, waiting for transfers between devices, tensor_sum(): acc = lax.ppermute(acc, 'ty', ring(ny, shift))  67.3 us
    ppermute x30, starting transfers between devices, tensor_sum(): acc = lax.ppermute(acc, 'ty', ring(ny, shift))  54 us
    ppermute x30, starting transfers between devices, tensor_sum(): cur = lax.ppermute(cur, 'ty', ring(ny, shift))  46.5 us
    ppermute x5, waiting for transfers between devices, tensor_sum(): got = lax.ppermute(send, 'tx', pairs)  24.9 us
    unnamed x173, local copies, waits for them, and re-layouts  22.2 us
    psum x1, waiting for transfers between devices, per_device(): ffn_w_grads = lax.psum(ffn_w_grads, DP)  18.5 us
    ppermute x5, waiting for transfers between devices, tensor_sum(): other = lax.ppermute(mine, 'tx', pairs)  17.9 us
  transfers between devices with their start and end apart: 90, of which 53 were waited for; matrix products, arithmetic and copies ran while one was open for 15% of the time, Pallas kernels for 0%

profile of v4, /device:TPU:0, one launch (start us, length us, event | category | flops | bytes accessed | tf_op | source)
XLA Modules:
  0.0 566.8 jit_solution(3399605917658459796)
XLA Ops:
  46.8 3.7 collective-permute-start.17
  53.4 3.3 collective-permute-start.4
  69.0 3.8 collective-permute-start.19
  74.6 4.7 collective-permute-done.2
  91.6 3.5 collective-permute-done.20
  112.6 3.3 collective-permute-start.12
  118.2 3.3 collective-permute-start.26
  123.9 3.3 collective-permute-start.13
  129.5 3.5 collective-permute-start.27
  133.7 3.4 collective-permute-done.24
  146.9 3.9 fusion.110
  159.8 3.5 collective-permute-start.31
  167.1 4.4 convolution_add_fusion
  181.2 6.6 %collective-permute-done.45 = f32[2,64,1024]{2,1,0:T(8,128)S(1)} collective-permute-done((f32[2,64,1024]{2,1,0:T(8,128)S(1)}, f32[2,64,1024]{2,1,0:T(8,128)S(1)}, u32[]{:S(2)}, u32[]{:S(2)}) %collective-permute-start.45) | collective-permute-done | bytes 524320 | tf_op jit(solution)/shard_map/ppermute | solution.py:96
  187.9 3.8 collective-permute-start.46
  191.8 7.2 %collective-permute-done.32 = f32[2,64,1024]{2,1,0:T(8,128)S(1)} collective-permute-done((f32[2,64,1024]{2,1,0:T(8,128)S(1)}, f32[2,64,1024]{2,1,0:T(8,128)S(1)}, u32[]{:S(2)}, u32[]{:S(2)}) %collective-permute-start.32) | collective-permute-done | bytes 524320 | tf_op jit(solution)/shard_map/ppermute | solution.py:96
  199.1 3.8 collective-permute-start.33
  203.1 7.2 %collective-permute-done.46 = f32[2,64,1024]{2,1,0:T(8,128)S(1)} collective-permute-done((f32[2,64,1024]{2,1,0:T(8,128)S(1)}, f32[2,64,1024]{2,1,0:T(8,128)S(1)}, u32[]{:S(2)}, u32[]{:S(2)}) %collective-permute-start.46) | collective-permute-done | bytes 524320 | tf_op jit(solution)/shard_map/ppermute | solution.py:96
  210.4 3.8 collective-permute-start.47
  214.3 6.4 %collective-permute-done.33 = f32[2,64,1024]{2,1,0:T(8,128)S(1)} collective-permute-done((f32[2,64,1024]{2,1,0:T(8,128)S(1)}, f32[2,64,1024]{2,1,0:T(8,128)S(1)}, u32[]{:S(2)}, u32[]{:S(2)}) %collective-permute-start.33) | collective-permute-done | bytes 524320 | tf_op jit(solution)/shard_map/ppermute | solution.py:96
  220.8 4.6 collective-permute-done.30
  235.0 6.6 %collective-permute-done.34 = f32[2,64,1024]{2,1,0:T(8,128)S(1)} collective-permute-done((f32[2,64,1024]{2,1,0:T(8,128)S(1)}, f32[2,64,1024]{2,1,0:T(8,128)S(1)}, u32[]{:S(2)}, u32[]{:S(2)}) %collective-permute-start.34) | collective-permute-done | bytes 524320 | tf_op jit(solution)/shard_map/ppermute | solution.py:106
  245.5 7.4 %collective-permute-done.48 = f32[2,64,1024]{2,1,0:T(8,128)} collective-permute-done((f32[2,64,1024]{2,1,0:T(8,128)}, f32[2,64,1024]{2,1,0:T(8,128)}, u32[]{:S(2)}, u32[]{:S(2)}) %collective-permute-start.48) | collective-permute-done | bytes 524320 | tf_op jit(solution)/shard_map/ppermute | solution.py:106
  257.2 11.3 %collective-permute-done.35 = f32[2,64,1024]{2,1,0:T(8,128)} collective-permute-done((f32[2,64,1024]{2,1,0:T(8,128)}, f32[2,64,1024]{2,1,0:T(8,128)}, u32[]{:S(2)}, u32[]{:S(2)}) %collective-permute-start.35) | collective-permute-done | bytes 524320 | tf_op jit(solution)/shard_map/ppermute | solution.py:108
  274.0 3.8 collective-permute-done.49
  282.2 4.3 collective-permute-done.36
  290.1 7.6 %collective-permute-done.50 = f32[2,64,1024]{2,1,0:T(8,128)S(1)} collective-permute-done((f32[2,64,1024]{2,1,0:T(8,128)S(1)}, f32[2,64,1024]{2,1,0:T(8,128)S(1)}, u32[]{:S(2)}, u32[]{:S(2)}) %collective-permute-start.50) | collective-permute-done | bytes 524320 | tf_op jit(solution)/shard_map/ppermute | solution.py:116
  297.9 3.3 collective-permute-start.54
  301.3 7.7 %collective-permute-done.37 = f32[2,64,1024]{2,1,0:T(8,128)S(1)} collective-permute-done((f32[2,64,1024]{2,1,0:T(8,128)S(1)}, f32[2,64,1024]{2,1,0:T(8,128)S(1)}, u32[]{:S(2)}, u32[]{:S(2)}) %collective-permute-start.37) | collective-permute-done | bytes 524320 | tf_op jit(solution)/shard_map/ppermute | solution.py:116
  312.2 8.0 %collective-permute-done.51 = f32[2,64,1024]{2,1,0:T(8,128)S(1)} collective-permute-done((f32[2,64,1024]{2,1,0:T(8,128)S(1)}, f32[2,64,1024]{2,1,0:T(8,128)S(1)}, u32[]{:S(2)}, u32[]{:S(2)}) %collective-permute-start.51) | collective-permute-done | bytes 524320 | tf_op jit(solution)/shard_map/ppermute | solution.py:116
  320.3 3.3 collective-permute-start.55
  323.7 11.3 %collective-permute-done.52 = f32[2,64,1024]{2,1,0:T(8,128)S(1)} collective-permute-done((f32[2,64,1024]{2,1,0:T(8,128)S(1)}, f32[2,64,1024]{2,1,0:T(8,128)S(1)}, u32[]{:S(2)}, u32[]{:S(2)}) %collective-permute-start.52) | collective-permute-done | bytes 524320 | tf_op jit(solution)/shard_map/ppermute | solution.py:116
  372.9 18.5 %all-reduce.5.cloned.1.call-done = (f32[576,1024]{1,0:T(8,128)}, f32[1024,576]{0,1:T(8,128)}, f32[1024,576]{0,1:T(8,128)}) async-done(((f32[576,1024]{1,0:T(8,128)}, f32[1024,576]{0,1:T(8,128)}, f32[1024,576]{0,1:T(8,128)}), (f32[576,1024]{1,0:T(8,128)}, f32[1024,576]{0,1:T(8,128)}, f32[1024,576]{0,1:T(8,128)})) %all-reduce.5.cloned.1.call-update) | async-done | bytes 7077904 | tf_op jit(solution)/shard_map/psum | solution.py:259
  397.3 4.3 collective-permute-done.73
  411.1 3.8 collective-permute-start.75
  420.8 3.9 collective-permute-done.72
  430.5 3.7 collective-permute-start.60
  434.8 5.7 %collective-permute-done.56 = f32[2,64,1024]{2,1,0:T(8,128)S(1)} collective-permute-done((f32[2,64,1024]{2,1,0:T(8,128)S(1)}, f32[2,64,1024]{2,1,0:T(8,128)S(1)}, u32[]{:S(2)}, u32[]{:S(2)}) %collective-permute-start.56) | collective-permute-done | bytes 524320 | tf_op jit(solution)/shard_map/ppermute | solution.py:96
  442.3 4.4 collective-permute-done.78
  451.2 5.3 collective-permute-done.57
  464.1 7.4 %collective-permute-done.58 = f32[2,64,1024]{2,1,0:T(8,128)S(1)} collective-permute-done((f32[2,64,1024]{2,1,0:T(8,128)S(1)}, f32[2,64,1024]{2,1,0:T(8,128)S(1)}, u32[]{:S(2)}, u32[]{:S(2)}) %collective-permute-start.58) | collective-permute-done | bytes 524320 | tf_op jit(solution)/shard_map/ppermute | solution.py:96
  478.4 6.6 %collective-permute-done.62 = f32[2,64,1024]{2,1,0:T(8,128)S(1)} collective-permute-done((f32[2,64,1024]{2,1,0:T(8,128)S(1)}, f32[2,64,1024]{2,1,0:T(8,128)S(1)}, u32[]{:S(2)}, u32[]{:S(2)}) %collective-permute-start.62) | collective-permute-done | bytes 524320 | tf_op jit(solution)/shard_map/ppermute | solution.py:106
  488.1 3.3 collective-permute-start.85
  491.4 4.2 collective-permute-done.82
  500.0 8.0 %collective-permute-done.87 = f32[2,1024]{1,0:T(2,128)S(1)} collective-permute-done((f32[2,1024]{1,0:T(2,128)S(1)}, f32[2,1024]{1,0:T(2,128)S(1)}, u32[]{:S(2)}, u32[]{:S(2)}) %collective-permute-start.87) | collective-permute-done | bytes 8224 | tf_op jit(solution)/shard_map/ppermute | solution.py:173
  525.4 6.0 %collective-permute-done.65 = f32[2,64,1024]{2,1,0:T(8,128)S(1)} collective-permute-done((f32[2,64,1024]{2,1,0:T(8,128)}, f32[2,64,1024]{2,1,0:T(8,128)S(1)}, u32[]{:S(2)}, u32[]{:S(2)}) %collective-permute-start.65) | collective-permute-done | bytes 524320 | tf_op jit(solution)/shard_map/ppermute | solution.py:116
  538.3 3.8 collective-permute-done.66
  542.2 4.1 collective-permute-done.69
  (540 shorter events, 291.6 us)
Async XLA Ops:
  7.2 384.2 %all-reduce.5.cloned.1.call-start = ((), (), s32[]{:S(2)}) async-start(), calls=%async_computation | async-start | bytes 14155776 | tf_op jit(solution)/shard_map/psum | solution.py:259
  69.0 13.5 %collective-permute-start.19 = (f32[2,32,1024]{2,1,0:T(8,128)S(1)}, f32[2,32,1024]{2,1,0:T(8,128)S(1)}, u32[]{:S(2)}, u32[]{:S(2)}) collective-permute-start(f32[2,32,1024]{2,1,0:T(8,128)S(1)} %bitcast_add_fusion.26), channel_id=1, source_target_pairs={{0,6},{2,0},{4,2},{6,4},{1,7},{3,1},{5,3},{7,5},{8,14},{10,8},{12,... | collective-permute-start | bytes 786440 | tf_op jit(solution)/shard_map/ppermute | solution.py:96
  88.6 12.1 %collective-permute-start.7 = (f32[2,32,1024]{2,1,0:T(8,128)}, f32[2,32,1024]{2,1,0:T(8,128)}, u32[]{:S(2)}, u32[]{:S(2)}) collective-permute-start(f32[2,32,1024]{2,1,0:T(8,128)} %fusion.71), channel_id=1, source_target_pairs={{0,1},{1,0},{2,3},{3,2},{4,5},{5,4},{6,7},{7,6},{8,9},{9,8},{10,11... | collective-permute-start | bytes 786440 | tf_op jit(solution)/shard_map/ppermute | solution.py:108
  105.9 12.3 %collective-permute-start.22 = (f32[2,32,1024]{2,1,0:T(8,128)S(1)}, f32[2,32,1024]{2,1,0:T(8,128)S(1)}, u32[]{:S(2)}, u32[]{:S(2)}) collective-permute-start(f32[2,32,1024]{2,1,0:T(8,128)S(1)} %get-tuple-element.166), channel_id=1, source_target_pairs={{0,2},{2,4},{4,6},{6,0},{1,3},{3,5},{5,7},{7,1},{8,10},{10,12},{12... | collective-permute-start | bytes 786440 | tf_op jit(solution)/shard_map/ppermute | solution.py:116
  159.8 15.8 %collective-permute-start.31 = (f32[2,64,1024]{2,1,0:T(8,128)}, f32[2,64,1024]{2,1,0:T(8,128)}, u32[]{:S(2)}, u32[]{:S(2)}) collective-permute-start(f32[2,64,1024]{2,1,0:T(8,128)} %dynamic-slice_bitcast_fusion.4), channel_id=1, source_target_pairs={{0,6},{2,0},{4,2},{6,4},{1,7},{3,1},{5,3},{7,5},{8,14},{10,8},{12,... | collective-permute-start | bytes 1572872 | tf_op jit(solution)/shard_map/ppermute | solution.py:96
  164.1 15.9 %collective-permute-start.28 = (f32[2,64,1024]{2,1,0:T(8,128)}, f32[2,64,1024]{2,1,0:T(8,128)}, u32[]{:S(2)}, u32[]{:S(2)}) collective-permute-start(f32[2,64,1024]{2,1,0:T(8,128)} %dynamic-slice_bitcast_fusion.5), channel_id=1, source_target_pairs={{0,2},{2,4},{4,6},{6,0},{1,3},{3,5},{5,7},{7,1},{8,10},{10,12},{12... | collective-permute-start | bytes 1572872 | tf_op jit(solution)/shard_map/ppermute | solution.py:96
  172.2 15.7 %collective-permute-start.45 = (f32[2,64,1024]{2,1,0:T(8,128)S(1)}, f32[2,64,1024]{2,1,0:T(8,128)S(1)}, u32[]{:S(2)}, u32[]{:S(2)}) collective-permute-start(f32[2,64,1024]{2,1,0:T(8,128)S(1)} %dynamic-slice_bitcast_fusion.2), channel_id=1, source_target_pairs={{0,6},{2,0},{4,2},{6,4},{1,7},{3,1},{5,3},{7,5},{8,14},{10,8},{12,... | collective-permute-start | bytes 1572872 | tf_op jit(solution)/shard_map/ppermute | solution.py:96
  175.5 16.2 %collective-permute-start.42 = (f32[2,64,1024]{2,1,0:T(8,128)S(1)}, f32[2,64,1024]{2,1,0:T(8,128)S(1)}, u32[]{:S(2)}, u32[]{:S(2)}) collective-permute-start(f32[2,64,1024]{2,1,0:T(8,128)S(1)} %dynamic-slice_bitcast_fusion.3), channel_id=1, source_target_pairs={{0,2},{2,4},{4,6},{6,0},{1,3},{3,5},{5,7},{7,1},{8,10},{10,12},{12... | collective-permute-start | bytes 1572872 | tf_op jit(solution)/shard_map/ppermute | solution.py:96
  176.7 22.4 %collective-permute-start.32 = (f32[2,64,1024]{2,1,0:T(8,128)S(1)}, f32[2,64,1024]{2,1,0:T(8,128)S(1)}, u32[]{:S(2)}, u32[]{:S(2)}) collective-permute-start(f32[2,64,1024]{2,1,0:T(8,128)S(1)} %bitcast_add_fusion.15), channel_id=1, source_target_pairs={{0,6},{2,0},{4,2},{6,4},{1,7},{3,1},{5,3},{7,5},{8,14},{10,8},{12,... | collective-permute-start | bytes 1572872 | tf_op jit(solution)/shard_map/ppermute | solution.py:96
  181.1 21.8 %collective-permute-start.29 = (f32[2,64,1024]{2,1,0:T(8,128)S(1)}, f32[2,64,1024]{2,1,0:T(8,128)S(1)}, u32[]{:S(2)}, u32[]{:S(2)}) collective-permute-start(f32[2,64,1024]{2,1,0:T(8,128)S(1)} %bitcast_add_fusion.18), channel_id=1, source_target_pairs={{0,2},{2,4},{4,6},{6,0},{1,3},{3,5},{5,7},{7,1},{8,10},{10,12},{12... | collective-permute-start | bytes 1572872 | tf_op jit(solution)/shard_map/ppermute | solution.py:96
  187.9 22.4 %collective-permute-start.46 = (f32[2,64,1024]{2,1,0:T(8,128)S(1)}, f32[2,64,1024]{2,1,0:T(8,128)S(1)}, u32[]{:S(2)}, u32[]{:S(2)}) collective-permute-start(f32[2,64,1024]{2,1,0:T(8,128)S(1)} %bitcast_add_fusion.9), channel_id=1, source_target_pairs={{0,6},{2,0},{4,2},{6,4},{1,7},{3,1},{5,3},{7,5},{8,14},{10,8},{12,... | collective-permute-start | bytes 1572872 | tf_op jit(solution)/shard_map/ppermute | solution.py:96
  191.7 22.4 %collective-permute-start.43 = (f32[2,64,1024]{2,1,0:T(8,128)S(1)}, f32[2,64,1024]{2,1,0:T(8,128)S(1)}, u32[]{:S(2)}, u32[]{:S(2)}) collective-permute-start(f32[2,64,1024]{2,1,0:T(8,128)S(1)} %bitcast_add_fusion.12), channel_id=1, source_target_pairs={{0,2},{2,4},{4,6},{6,0},{1,3},{3,5},{5,7},{7,1},{8,10},{10,12},{12... | collective-permute-start | bytes 1572872 | tf_op jit(solution)/shard_map/ppermute | solution.py:96
  199.1 21.5 %collective-permute-start.33 = (f32[2,64,1024]{2,1,0:T(8,128)S(1)}, f32[2,64,1024]{2,1,0:T(8,128)S(1)}, u32[]{:S(2)}, u32[]{:S(2)}) collective-permute-start(f32[2,64,1024]{2,1,0:T(8,128)S(1)} %bitcast_add_fusion.14), channel_id=1, source_target_pairs={{0,6},{2,0},{4,2},{6,4},{1,7},{3,1},{5,3},{7,5},{8,14},{10,8},{12,... | collective-permute-start | bytes 1572872 | tf_op jit(solution)/shard_map/ppermute | solution.py:96
  203.0 22.4 %collective-permute-start.30 = (f32[2,64,1024]{2,1,0:T(8,128)S(1)}, f32[2,64,1024]{2,1,0:T(8,128)S(1)}, u32[]{:S(2)}, u32[]{:S(2)}) collective-permute-start(f32[2,64,1024]{2,1,0:T(8,128)S(1)} %bitcast_add_fusion.17), channel_id=1, source_target_pairs={{0,2},{2,4},{4,6},{6,0},{1,3},{3,5},{5,7},{7,1},{8,10},{10,12},{12... | collective-permute-start | bytes 1572872 | tf_op jit(solution)/shard_map/ppermute | solution.py:96
  210.4 18.2 %collective-permute-start.47 = (f32[2,64,1024]{2,1,0:T(8,128)S(1)}, f32[2,64,1024]{2,1,0:T(8,128)S(1)}, u32[]{:S(2)}, u32[]{:S(2)}) collective-permute-start(f32[2,64,1024]{2,1,0:T(8,128)S(1)} %bitcast_add_fusion.8), channel_id=1, source_target_pairs={{0,6},{2,0},{4,2},{6,4},{1,7},{3,1},{5,3},{7,5},{8,14},{10,8},{12,... | collective-permute-start | bytes 1572872 | tf_op jit(solution)/shard_map/ppermute | solution.py:96
  214.2 16.8 %collective-permute-start.44 = (f32[2,64,1024]{2,1,0:T(8,128)S(1)}, f32[2,64,1024]{2,1,0:T(8,128)S(1)}, u32[]{:S(2)}, u32[]{:S(2)}) collective-permute-start(f32[2,64,1024]{2,1,0:T(8,128)S(1)} %bitcast_add_fusion.11), channel_id=1, source_target_pairs={{0,2},{2,4},{4,6},{6,0},{1,3},{3,5},{5,7},{7,1},{8,10},{10,12},{12... | collective-permute-start | bytes 1572872 | tf_op jit(solution)/shard_map/ppermute | solution.py:96
  225.5 16.1 %collective-permute-start.34 = (f32[2,64,1024]{2,1,0:T(8,128)S(1)}, f32[2,64,1024]{2,1,0:T(8,128)S(1)}, u32[]{:S(2)}, u32[]{:S(2)}) collective-permute-start(f32[2,64,1024]{2,1,0:T(8,128)S(1)} %fusion.46), channel_id=1, source_target_pairs={{0,1},{1,0},{2,3},{3,2},{4,5},{5,4},{6,7},{7,6},{8,9},{9,8},{10,11... | collective-permute-start | bytes 1572872 | tf_op jit(solution)/shard_map/ppermute | solution.py:106
  232.0 21.0 %collective-permute-start.48 = (f32[2,64,1024]{2,1,0:T(8,128)}, f32[2,64,1024]{2,1,0:T(8,128)}, u32[]{:S(2)}, u32[]{:S(2)}) collective-permute-start(f32[2,64,1024]{2,1,0:T(8,128)} %fusion.41), channel_id=1, source_target_pairs={{0,1},{1,0},{2,3},{3,2},{4,5},{5,4},{6,7},{7,6},{8,9},{9,8},{10,11... | collective-permute-start | bytes 1572872 | tf_op jit(solution)/shard_map/ppermute | solution.py:106
  242.5 26.0 %collective-permute-start.35 = (f32[2,64,1024]{2,1,0:T(8,128)}, f32[2,64,1024]{2,1,0:T(8,128)}, u32[]{:S(2)}, u32[]{:S(2)}) collective-permute-start(f32[2,64,1024]{2,1,0:T(8,128)} %fusion.49), channel_id=1, source_target_pairs={{0,1},{1,0},{2,3},{3,2},{4,5},{5,4},{6,7},{7,6},{8,9},{9,8},{10,11... | collective-permute-start | bytes 1572872 | tf_op jit(solution)/shard_map/ppermute | solution.py:108
  254.1 23.6 %collective-permute-start.49 = (f32[2,64,1024]{2,1,0:T(8,128)S(1)}, f32[2,64,1024]{2,1,0:T(8,128)S(1)}, u32[]{:S(2)}, u32[]{:S(2)}) collective-permute-start(f32[2,64,1024]{2,1,0:T(8,128)S(1)} %fusion.44), channel_id=1, source_target_pairs={{0,1},{1,0},{2,3},{3,2},{4,5},{5,4},{6,7},{7,6},{8,9},{9,8},{10,11... | collective-permute-start | bytes 1572872 | tf_op jit(solution)/shard_map/ppermute | solution.py:108
  270.4 16.1 %collective-permute-start.36 = (f32[2,64,1024]{2,1,0:T(8,128)S(1)}, f32[2,64,1024]{2,1,0:T(8,128)S(1)}, u32[]{:S(2)}, u32[]{:S(2)}) collective-permute-start(f32[2,64,1024]{2,1,0:T(8,128)S(1)} %get-tuple-element.157), channel_id=1, source_target_pairs={{0,2},{2,4},{4,6},{6,0},{1,3},{3,5},{5,7},{7,1},{8,10},{10,12},{12... | collective-permute-start | bytes 1572872 | tf_op jit(solution)/shard_map/ppermute | solution.py:116
  270.4 16.5 %collective-permute-start.39 = (f32[2,64,1024]{2,1,0:T(8,128)S(1)}, f32[2,64,1024]{2,1,0:T(8,128)S(1)}, u32[]{:S(2)}, u32[]{:S(2)}) collective-permute-start(f32[2,64,1024]{2,1,0:T(8,128)S(1)} %get-tuple-element.158), channel_id=1, source_target_pairs={{0,6},{2,0},{4,2},{6,4},{1,7},{3,1},{5,3},{7,5},{8,14},{10,8},{12,... | collective-permute-start | bytes 1572872 | tf_op jit(solution)/shard_map/ppermute | solution.py:116
  277.9 19.8 %collective-permute-start.50 = (f32[2,64,1024]{2,1,0:T(8,128)S(1)}, f32[2,64,1024]{2,1,0:T(8,128)S(1)}, u32[]{:S(2)}, u32[]{:S(2)}) collective-permute-start(f32[2,64,1024]{2,1,0:T(8,128)S(1)} %get-tuple-element.155), channel_id=1, source_target_pairs={{0,2},{2,4},{4,6},{6,0},{1,3},{3,5},{5,7},{7,1},{8,10},{10,12},{12... | collective-permute-start | bytes 1572872 | tf_op jit(solution)/shard_map/ppermute | solution.py:116
  278.3 19.6 %collective-permute-start.53 = (f32[2,64,1024]{2,1,0:T(8,128)S(1)}, f32[2,64,1024]{2,1,0:T(8,128)S(1)}, u32[]{:S(2)}, u32[]{:S(2)}) collective-permute-start(f32[2,64,1024]{2,1,0:T(8,128)S(1)} %get-tuple-element.156), channel_id=1, source_target_pairs={{0,6},{2,0},{4,2},{6,4},{1,7},{3,1},{5,3},{7,5},{8,14},{10,8},{12,... | collective-permute-start | bytes 1572872 | tf_op jit(solution)/shard_map/ppermute | solution.py:116
  286.5 22.5 %collective-permute-start.37 = (f32[2,64,1024]{2,1,0:T(8,128)S(1)}, f32[2,64,1024]{2,1,0:T(8,128)S(1)}, u32[]{:S(2)}, u32[]{:S(2)}) collective-permute-start(f32[2,64,1024]{2,1,0:T(8,128)S(1)} %collective-permute-done.36), channel_id=1, source_target_pairs={{0,2},{2,4},{4,6},{6,0},{1,3},{3,5},{5,7},{7,1},{8,10},{10,12},{12... | collective-permute-start | bytes 1572872 | tf_op jit(solution)/shard_map/ppermute | solution.py:116
  286.9 22.1 %collective-permute-start.40 = (f32[2,64,1024]{2,1,0:T(8,128)S(1)}, f32[2,64,1024]{2,1,0:T(8,128)S(1)}, u32[]{:S(2)}, u32[]{:S(2)}) collective-permute-start(f32[2,64,1024]{2,1,0:T(8,128)S(1)} %collective-permute-done.39), channel_id=1, source_target_pairs={{0,6},{2,0},{4,2},{6,4},{1,7},{3,1},{5,3},{7,5},{8,14},{10,8},{12,... | collective-permute-start | bytes 1572872 | tf_op jit(solution)/shard_map/ppermute | solution.py:116
  297.7 22.5 %collective-permute-start.51 = (f32[2,64,1024]{2,1,0:T(8,128)S(1)}, f32[2,64,1024]{2,1,0:T(8,128)S(1)}, u32[]{:S(2)}, u32[]{:S(2)}) collective-permute-start(f32[2,64,1024]{2,1,0:T(8,128)S(1)} %collective-permute-done.50), channel_id=1, source_target_pairs={{0,2},{2,4},{4,6},{6,0},{1,3},{3,5},{5,7},{7,1},{8,10},{10,12},{12... | collective-permute-start | bytes 1572872 | tf_op jit(solution)/shard_map/ppermute | solution.py:116
  297.9 22.5 %collective-permute-start.54 = (f32[2,64,1024]{2,1,0:T(8,128)S(1)}, f32[2,64,1024]{2,1,0:T(8,128)S(1)}, u32[]{:S(2)}, u32[]{:S(2)}) collective-permute-start(f32[2,64,1024]{2,1,0:T(8,128)S(1)} %collective-permute-done.53), channel_id=1, source_target_pairs={{0,6},{2,0},{4,2},{6,4},{1,7},{3,1},{5,3},{7,5},{8,14},{10,8},{12,... | collective-permute-start | bytes 1572872 | tf_op jit(solution)/shard_map/ppermute | solution.py:116
  309.0 29.8 %collective-permute-start.38 = (f32[2,64,1024]{2,1,0:T(8,128)S(1)}, f32[2,64,1024]{2,1,0:T(8,128)S(1)}, u32[]{:S(2)}, u32[]{:S(2)}) collective-permute-start(f32[2,64,1024]{2,1,0:T(8,128)S(1)} %collective-permute-done.37), channel_id=1, source_target_pairs={{0,2},{2,4},{4,6},{6,0},{1,3},{3,5},{5,7},{7,1},{8,10},{10,12},{12... | collective-permute-start | bytes 1572872 | tf_op jit(solution)/shard_map/ppermute | solution.py:116
  309.0 29.8 %collective-permute-start.41 = (f32[2,64,1024]{2,1,0:T(8,128)S(1)}, f32[2,64,1024]{2,1,0:T(8,128)S(1)}, u32[]{:S(2)}, u32[]{:S(2)}) collective-permute-start(f32[2,64,1024]{2,1,0:T(8,128)S(1)} %collective-permute-done.40), channel_id=1, source_target_pairs={{0,6},{2,0},{4,2},{6,4},{1,7},{3,1},{5,3},{7,5},{8,14},{10,8},{12,... | collective-permute-start | bytes 1572872 | tf_op jit(solution)/shard_map/ppermute | solution.py:116
  320.2 14.8 %collective-permute-start.52 = (f32[2,64,1024]{2,1,0:T(8,128)S(1)}, f32[2,64,1024]{2,1,0:T(8,128)S(1)}, u32[]{:S(2)}, u32[]{:S(2)}) collective-permute-start(f32[2,64,1024]{2,1,0:T(8,128)S(1)} %collective-permute-done.51), channel_id=1, source_target_pairs={{0,2},{2,4},{4,6},{6,0},{1,3},{3,5},{5,7},{7,1},{8,10},{10,12},{12... | collective-permute-start | bytes 1572872 | tf_op jit(solution)/shard_map/ppermute | solution.py:116
  320.3 14.8 %collective-permute-start.55 = (f32[2,64,1024]{2,1,0:T(8,128)S(1)}, f32[2,64,1024]{2,1,0:T(8,128)S(1)}, u32[]{:S(2)}, u32[]{:S(2)}) collective-permute-start(f32[2,64,1024]{2,1,0:T(8,128)S(1)} %collective-permute-done.54), channel_id=1, source_target_pairs={{0,6},{2,0},{4,2},{6,4},{1,7},{3,1},{5,3},{7,5},{8,14},{10,8},{12,... | collective-permute-start | bytes 1572872 | tf_op jit(solution)/shard_map/ppermute | solution.py:116
  415.8 13.8 %collective-permute-start.59 = (f32[2,64,1024]{2,1,0:T(8,128)S(1)}, f32[2,64,1024]{2,1,0:T(8,128)S(1)}, u32[]{:S(2)}, u32[]{:S(2)}) collective-permute-start(f32[2,64,1024]{2,1,0:T(8,128)S(1)} %dynamic-slice_bitcast_fusion), channel_id=1, source_target_pairs={{0,6},{2,0},{4,2},{6,4},{1,7},{3,1},{5,3},{7,5},{8,14},{10,8},{12,... | collective-permute-start | bytes 1572872 | tf_op jit(solution)/shard_map/ppermute | solution.py:96
  425.0 15.6 %collective-permute-start.56 = (f32[2,64,1024]{2,1,0:T(8,128)S(1)}, f32[2,64,1024]{2,1,0:T(8,128)S(1)}, u32[]{:S(2)}, u32[]{:S(2)}) collective-permute-start(f32[2,64,1024]{2,1,0:T(8,128)S(1)} %dynamic-slice_bitcast_fusion.1), channel_id=1, source_target_pairs={{0,2},{2,4},{4,6},{6,0},{1,3},{3,5},{5,7},{7,1},{8,10},{10,12},{12... | collective-permute-start | bytes 1572872 | tf_op jit(solution)/shard_map/ppermute | solution.py:96
  430.5 16.4 %collective-permute-start.60 = (f32[2,64,1024]{2,1,0:T(8,128)}, f32[2,64,1024]{2,1,0:T(8,128)}, u32[]{:S(2)}, u32[]{:S(2)}) collective-permute-start(f32[2,64,1024]{2,1,0:T(8,128)} %bitcast_add_fusion.3), channel_id=1, source_target_pairs={{0,6},{2,0},{4,2},{6,4},{1,7},{3,1},{5,3},{7,5},{8,14},{10,8},{12,... | collective-permute-start | bytes 1572872 | tf_op jit(solution)/shard_map/ppermute | solution.py:96
  441.4 15.1 %collective-permute-start.57 = (f32[2,64,1024]{2,1,0:T(8,128)}, f32[2,64,1024]{2,1,0:T(8,128)}, u32[]{:S(2)}, u32[]{:S(2)}) collective-permute-start(f32[2,64,1024]{2,1,0:T(8,128)} %bitcast_add_fusion.6), channel_id=1, source_target_pairs={{0,2},{2,4},{4,6},{6,0},{1,3},{3,5},{5,7},{7,1},{8,10},{10,12},{12... | collective-permute-start | bytes 1572872 | tf_op jit(solution)/shard_map/ppermute | solution.py:96
  448.1 14.9 %collective-permute-start.61 = (f32[2,64,1024]{2,1,0:T(8,128)S(1)}, f32[2,64,1024]{2,1,0:T(8,128)S(1)}, u32[]{:S(2)}, u32[]{:S(2)}) collective-permute-start(f32[2,64,1024]{2,1,0:T(8,128)S(1)} %bitcast_add_fusion.2), channel_id=1, source_target_pairs={{0,6},{2,0},{4,2},{6,4},{1,7},{3,1},{5,3},{7,5},{8,14},{10,8},{12,... | collective-permute-start | bytes 1572872 | tf_op jit(solution)/shard_map/ppermute | solution.py:96
  457.6 13.9 %collective-permute-start.58 = (f32[2,64,1024]{2,1,0:T(8,128)S(1)}, f32[2,64,1024]{2,1,0:T(8,128)S(1)}, u32[]{:S(2)}, u32[]{:S(2)}) collective-permute-start(f32[2,64,1024]{2,1,0:T(8,128)S(1)} %bitcast_add_fusion.5), channel_id=1, source_target_pairs={{0,2},{2,4},{4,6},{6,0},{1,3},{3,5},{5,7},{7,1},{8,10},{10,12},{12... | collective-permute-start | bytes 1572872 | tf_op jit(solution)/shard_map/ppermute | solution.py:96
  457.8 17.2 %collective-permute-start.80 = (f32[64,1024]{1,0:T(8,128)S(1)}, f32[64,1024]{1,0:T(8,128)S(1)}, u32[]{:S(2)}, u32[]{:S(2)}) collective-permute-start(f32[64,1024]{1,0:T(8,128)S(1)} %bitcast.617), channel_id=1, source_target_pairs={{0,16},{16,32},{32,48},{48,0},{1,17},{17,33},{33,49},{49,1},{2,18}... | collective-permute-start | bytes 786440 | tf_op jit(solution)/shard_map/ppermute | solution.py:162
  457.8 17.2 %collective-permute-start.83 = (f32[64,1024]{1,0:T(8,128)S(1)}, f32[64,1024]{1,0:T(8,128)S(1)}, u32[]{:S(2)}, u32[]{:S(2)}) collective-permute-start(f32[64,1024]{1,0:T(8,128)S(1)} %bitcast.615), channel_id=1, source_target_pairs={{0,48},{16,0},{32,16},{48,32},{1,49},{17,1},{33,17},{49,33},{2,50}... | collective-permute-start | bytes 786440 | tf_op jit(solution)/shard_map/ppermute | solution.py:162
  471.6 13.3 %collective-permute-start.62 = (f32[2,64,1024]{2,1,0:T(8,128)S(1)}, f32[2,64,1024]{2,1,0:T(8,128)S(1)}, u32[]{:S(2)}, u32[]{:S(2)}) collective-permute-start(f32[2,64,1024]{2,1,0:T(8,128)S(1)} %fusion.36), channel_id=1, source_target_pairs={{0,1},{1,0},{2,3},{3,2},{4,5},{5,4},{6,7},{7,6},{8,9},{9,8},{10,11... | collective-permute-start | bytes 1572872 | tf_op jit(solution)/shard_map/ppermute | solution.py:106
  475.0 13.1 %collective-permute-start.81 = (f32[64,1024]{1,0:T(8,128)S(1)}, f32[64,1024]{1,0:T(8,128)S(1)}, u32[]{:S(2)}, u32[]{:S(2)}) collective-permute-start(f32[64,1024]{1,0:T(8,128)S(1)} %collective-permute-done.80), channel_id=1, source_target_pairs={{0,16},{16,32},{32,48},{48,0},{1,17},{17,33},{33,49},{49,1},{2,18}... | collective-permute-start | bytes 786440 | tf_op jit(solution)/shard_map/ppermute | solution.py:162
  475.1 13.0 %collective-permute-start.84 = (f32[64,1024]{1,0:T(8,128)S(1)}, f32[64,1024]{1,0:T(8,128)S(1)}, u32[]{:S(2)}, u32[]{:S(2)}) collective-permute-start(f32[64,1024]{1,0:T(8,128)S(1)} %collective-permute-done.83), channel_id=1, source_target_pairs={{0,48},{16,0},{32,16},{48,32},{1,49},{17,1},{33,17},{49,33},{2,50}... | collective-permute-start | bytes 786440 | tf_op jit(solution)/shard_map/ppermute | solution.py:162
  485.0 12.4 %collective-permute-start.63 = (f32[2,64,1024]{2,1,0:T(8,128)S(1)}, f32[2,64,1024]{2,1,0:T(8,128)S(1)}, u32[]{:S(2)}, u32[]{:S(2)}) collective-permute-start(f32[2,64,1024]{2,1,0:T(8,128)S(1)} %fusion.39), channel_id=1, source_target_pairs={{0,1},{1,0},{2,3},{3,2},{4,5},{5,4},{6,7},{7,6},{8,9},{9,8},{10,11... | collective-permute-start | bytes 1572872 | tf_op jit(solution)/shard_map/ppermute | solution.py:108
  498.6 19.8 %collective-permute-start.64 = (f32[2,64,1024]{2,1,0:T(8,128)}, f32[2,64,1024]{2,1,0:T(8,128)}, u32[]{:S(2)}, u32[]{:S(2)}) collective-permute-start(f32[2,64,1024]{2,1,0:T(8,128)} %get-tuple-element.153), channel_id=1, source_target_pairs={{0,2},{2,4},{4,6},{6,0},{1,3},{3,5},{5,7},{7,1},{8,10},{10,12},{12... | collective-permute-start | bytes 1572872 | tf_op jit(solution)/shard_map/ppermute | solution.py:116
  511.2 12.5 %collective-permute-start.67 = (f32[2,64,1024]{2,1,0:T(8,128)}, f32[2,64,1024]{2,1,0:T(8,128)}, u32[]{:S(2)}, u32[]{:S(2)}) collective-permute-start(f32[2,64,1024]{2,1,0:T(8,128)} %get-tuple-element.154), channel_id=1, source_target_pairs={{0,6},{2,0},{4,2},{6,4},{1,7},{3,1},{5,3},{7,5},{8,14},{10,8},{12,... | collective-permute-start | bytes 1572872 | tf_op jit(solution)/shard_map/ppermute | solution.py:116
  518.4 13.1 %collective-permute-start.65 = (f32[2,64,1024]{2,1,0:T(8,128)}, f32[2,64,1024]{2,1,0:T(8,128)S(1)}, u32[]{:S(2)}, u32[]{:S(2)}) collective-permute-start(f32[2,64,1024]{2,1,0:T(8,128)} %collective-permute-done.64), channel_id=1, source_target_pairs={{0,2},{2,4},{4,6},{6,0},{1,3},{3,5},{5,7},{7,1},{8,10},{10,12},{12... | collective-permute-start | bytes 1572872 | tf_op jit(solution)/shard_map/ppermute | solution.py:116
  523.6 13.5 %collective-permute-start.68 = (f32[2,64,1024]{2,1,0:T(8,128)}, f32[2,64,1024]{2,1,0:T(8,128)S(1)}, u32[]{:S(2)}, u32[]{:S(2)}) collective-permute-start(f32[2,64,1024]{2,1,0:T(8,128)} %collective-permute-done.67), channel_id=1, source_target_pairs={{0,6},{2,0},{4,2},{6,4},{1,7},{3,1},{5,3},{7,5},{8,14},{10,8},{12,... | collective-permute-start | bytes 1572872 | tf_op jit(solution)/shard_map/ppermute | solution.py:116
  (126 other events, 837.5 us)
Sparse Core Ops, SparseCore 0:
  245.7 145.6 all-reduce.4

commit v5 on v3

--- a/solution.py
+++ b/solution.py
@@ -243,8 +243,7 @@
     up_proj = jnp.dot(normed_two, w_up, preferred_element_type=jnp.float32)
     gate_sigmoid = jax.nn.sigmoid(gate_proj)
     hidden = (gate_proj * gate_sigmoid * up_proj).astype(jnp.bfloat16)
-    mlp_sum = split_tensor_sum(jnp.dot(hidden, w_down, preferred_element_type=jnp.float32))
-    output = (residual + mlp_sum).astype(jnp.bfloat16)
+    mlp_partial = jnp.dot(hidden, w_down, preferred_element_type=jnp.float32)
     down_grad = outer(hidden, cotangent)
     hidden_grad = inner(cotangent, w_down)
     gate_grad = (
@@ -258,6 +257,9 @@
     )
     ffn_w_grads = lax.psum(ffn_w_grads, DP)
     normed_two_grad = split_tensor_sum(two_partial)
+    mlp_partial, normed_two_grad = lax.optimization_barrier((mlp_partial, normed_two_grad))
+    mlp_sum = tensor_sum(mlp_partial)
+    output = (residual + mlp_sum).astype(jnp.bfloat16)
     ffn_grad = jnp.sum(normed_two_grad * residual * scale_two, axis=0)
     residual_grad = cotangent.astype(jnp.float32) + rms_back(
         normed_two_grad, residual, scale_two, ffn_gain

time: 550 us -> 614 us (1.12)
  waiting for transfers between devices: 187 us -> 247 us
  starting transfers between devices: 178 us -> 187 us
    psum x1, waiting for transfers between devices: 0.01 us -> 58.4 us  [per_device(): ffn_w_grads = lax.psum(ffn_w_grads, DP)]
    ppermute x48 -> x42, waiting for transfers between devices: 40.9 us -> 71.1 us  [tensor_sum(): acc = lax.ppermute(acc, 'ty', ring(ny, shift))]
    ppermute x48 -> x42, waiting for transfers between devices: 78.8 us -> 66.3 us  [tensor_sum(): cur = lax.ppermute(cur, 'ty', ring(ny, shift))]
    ppermute x8 -> x7, waiting for transfers between devices: 29.7 us -> 20.3 us  [tensor_sum(): got = lax.ppermute(send, 'tx', pairs)]
    ppermute x48 -> x42, starting transfers between devices: 55.3 us -> 62.8 us  [tensor_sum(): cur = lax.ppermute(cur, 'ty', ring(ny, shift))]
    ppermute x6, waiting for transfers between devices: 7.64 us -> 0.72 us  [ring_sum(): acc = lax.ppermute(acc, ring_axis, ring(size, shift))]
    squeeze x16 -> x14, local copies, waits for them, and re-layouts: 12.8 us -> 6.93 us  [tensor_sum(): acc = lax.dynamic_index_in_dim(chunks, (y - shift) % ny, 0, keepdims=False)]
    ppermute x8 -> x7, starting transfers between devices: 15.3 us -> 21.1 us  [tensor_sum(): got = lax.ppermute(send, 'tx', pairs)]
  transfers between devices with their start and end apart: 132 -> 118, of which waited for: 78 -> 68; matrix products, arithmetic and copies ran while one was open for 16% -> 12% of each run, Pallas kernels for 0% -> 0%
where the time goes in v5:
time: 614 us; the launch traced here: 604 us
  waiting for transfers between devices  247 us (40%)
  starting transfers between devices  187 us (30%)
  other arithmetic  58.7 us (10%)
  matrix products  48 us (8%)
  local copies, waits for them, and re-layouts  46.5 us (8%)
  between operations  17 us (3%)
    ppermute x42, waiting for transfers between devices, tensor_sum(): acc = lax.ppermute(acc, 'ty', ring(ny, shift))  71.1 us
    ppermute x42, starting transfers between devices, tensor_sum(): acc = lax.ppermute(acc, 'ty', ring(ny, shift))  66.6 us
    ppermute x42, waiting for transfers between devices, tensor_sum(): cur = lax.ppermute(cur, 'ty', ring(ny, shift))  66.3 us
    ppermute x42, starting transfers between devices, tensor_sum(): cur = lax.ppermute(cur, 'ty', ring(ny, shift))  62.8 us
    psum x1, waiting for transfers between devices, per_device(): ffn_w_grads = lax.psum(ffn_w_grads, DP)  58.4 us
    ppermute x7, starting transfers between devices, tensor_sum(): got = lax.ppermute(send, 'tx', pairs)  21.1 us
    unnamed x159, local copies, waits for them, and re-layouts  20.6 us
    ppermute x7, waiting for transfers between devices, tensor_sum(): got = lax.ppermute(send, 'tx', pairs)  20.3 us
  transfers between devices with their start and end apart: 118, of which 68 were waited for; matrix products, arithmetic and copies ran while one was open for 12% of the time, Pallas kernels for 0%

profile of v5, /device:TPU:0, one launch (start us, length us, event | category | flops | bytes accessed | tf_op | source)
XLA Modules:
  0.0 604.1 jit_solution(13422387104010542256)
XLA Ops:
  46.7 3.4 collective-permute-start.17
  53.0 3.3 collective-permute-start.4
  68.2 3.8 collective-permute-start.19
  75.0 4.0 collective-permute-done.2
  91.3 3.5 collective-permute-done.20
  105.8 3.3 collective-permute-start.25
  112.3 3.3 collective-permute-start.12
  117.9 3.3 collective-permute-start.26
  123.5 3.3 collective-permute-start.13
  129.2 3.7 collective-permute-start.27
  133.4 3.3 collective-permute-done.24
  154.0 4.0 convolution_add_fusion
  169.5 3.3 collective-permute-done.31
  172.9 3.6 collective-permute-start.32
  178.5 3.6 collective-permute-start.46
  184.1 3.6 collective-permute-start.33
  189.3 3.8 collective-permute-start.47
  224.3 3.3 collective-permute-start.40
  230.2 3.4 collective-permute-start.54
  252.4 3.8 collective-permute-start.59
  256.3 10.6 %collective-permute-done.59 = f32[2,64,1024]{2,1,0:T(8,128)S(1)} collective-permute-done((f32[2,64,1024]{2,1,0:T(8,128)S(1)}, f32[2,64,1024]{2,1,0:T(8,128)S(1)}, u32[]{:S(2)}, u32[]{:S(2)}) %collective-permute-start.59) | collective-permute-done | bytes 524320 | tf_op jit(solution)/shard_map/ppermute | solution.py:96
  267.0 3.8 collective-permute-start.60
  270.9 9.6 %collective-permute-done.60 = f32[2,64,1024]{2,1,0:T(8,128)S(1)} collective-permute-done((f32[2,64,1024]{2,1,0:T(8,128)S(1)}, f32[2,64,1024]{2,1,0:T(8,128)S(1)}, u32[]{:S(2)}, u32[]{:S(2)}) %collective-permute-start.60) | collective-permute-done | bytes 524320 | tf_op jit(solution)/shard_map/ppermute | solution.py:96
  280.6 3.8 collective-permute-start.61
  284.6 6.5 %collective-permute-done.61 = f32[2,64,1024]{2,1,0:T(8,128)S(1)} collective-permute-done((f32[2,64,1024]{2,1,0:T(8,128)S(1)}, f32[2,64,1024]{2,1,0:T(8,128)S(1)}, u32[]{:S(2)}, u32[]{:S(2)}) %collective-permute-start.61) | collective-permute-done | bytes 524320 | tf_op jit(solution)/shard_map/ppermute | solution.py:96
  291.2 3.8 collective-permute-done.58
  295.1 3.5 collective-permute-start.62
  298.6 9.7 %collective-permute-done.62 = f32[2,64,1024]{2,1,0:T(8,128)S(1)} collective-permute-done((f32[2,64,1024]{2,1,0:T(8,128)S(1)}, f32[2,64,1024]{2,1,0:T(8,128)S(1)}, u32[]{:S(2)}, u32[]{:S(2)}) %collective-permute-start.62) | collective-permute-done | bytes 524320 | tf_op jit(solution)/shard_map/ppermute | solution.py:106
  312.5 7.6 %collective-permute-done.63 = f32[2,64,1024]{2,1,0:T(8,128)S(1)} collective-permute-done((f32[2,64,1024]{2,1,0:T(8,128)}, f32[2,64,1024]{2,1,0:T(8,128)S(1)}, u32[]{:S(2)}, u32[]{:S(2)}) %collective-permute-start.63) | collective-permute-done | bytes 524320 | tf_op jit(solution)/shard_map/ppermute | solution.py:108
  326.1 3.6 multiply_reduce_fusion
  330.4 5.1 collective-permute-done.64
  335.8 3.3 collective-permute-start.68
  339.4 6.4 %collective-permute-done.65 = f32[2,64,1024]{2,1,0:T(8,128)S(1)} collective-permute-done((f32[2,64,1024]{2,1,0:T(8,128)S(1)}, f32[2,64,1024]{2,1,0:T(8,128)S(1)}, u32[]{:S(2)}, u32[]{:S(2)}) %collective-permute-start.65) | collective-permute-done | bytes 524320 | tf_op jit(solution)/shard_map/ppermute | solution.py:116
  345.9 3.9 collective-permute-start.69
  350.0 6.3 %collective-permute-done.66 = f32[2,64,1024]{2,1,0:T(8,128)S(1)} collective-permute-done((f32[2,64,1024]{2,1,0:T(8,128)S(1)}, f32[2,64,1024]{2,1,0:T(8,128)S(1)}, u32[]{:S(2)}, u32[]{:S(2)}) %collective-permute-start.66) | collective-permute-done | bytes 524320 | tf_op jit(solution)/shard_map/ppermute | solution.py:116
  380.8 3.4 fusion.17
  391.1 58.4 %all-reduce.5.cloned.1.call-done = (f32[576,1024]{1,0:T(8,128)}, f32[1024,576]{0,1:T(8,128)}, f32[1024,576]{0,1:T(8,128)}) async-done(((f32[576,1024]{1,0:T(8,128)}, f32[1024,576]{0,1:T(8,128)}, f32[1024,576]{0,1:T(8,128)}), (f32[576,1024]{1,0:T(8,128)}, f32[1024,576]{0,1:T(8,128)}, f32[1024,576]{0,1:T(8,128)})) %all-reduce.5.cloned.1.call-update) | async-done | bytes 7077904 | tf_op jit(solution)/shard_map/psum | solution.py:258
  466.6 3.7 collective-permute-done.70
  479.4 3.7 collective-permute-done.71
  491.6 3.7 collective-permute-done.72
  502.3 3.7 collective-permute-done.76
  506.6 5.6 collective-permute-done.105
  516.7 3.9 collective-permute-done.106
  533.3 3.8 collective-permute-done.92
  551.1 4.2 collective-permute-done.80
  566.3 4.2 collective-permute-done.110
  571.0 3.6 collective-permute-done.114
  589.4 3.5 copy.125
  (628 shorter events, 323.4 us)
Async XLA Ops:
  7.2 442.3 %all-reduce.5.cloned.1.call-start = ((), (), s32[]{:S(2)}) async-start(), calls=%async_computation | async-start | bytes 14155776 | tf_op jit(solution)/shard_map/psum | solution.py:258
  40.3 11.6 %collective-permute-start.3 = (f32[2,32,1024]{2,1,0:T(8,128)}, f32[2,32,1024]{2,1,0:T(8,128)}, u32[]{:S(2)}, u32[]{:S(2)}) collective-permute-start(f32[2,32,1024]{2,1,0:T(8,128)} %dynamic-slice_bitcast_fusion.14), channel_id=1, source_target_pairs={{0,6},{2,0},{4,2},{6,4},{1,7},{3,1},{5,3},{7,5},{8,14},{10,8},{12,... | collective-permute-start | bytes 786440 | tf_op jit(solution)/shard_map/ppermute | solution.py:96
  45.0 11.3 %collective-permute-start = (f32[2,32,1024]{2,1,0:T(8,128)}, f32[2,32,1024]{2,1,0:T(8,128)}, u32[]{:S(2)}, u32[]{:S(2)}) collective-permute-start(f32[2,32,1024]{2,1,0:T(8,128)} %dynamic-slice_bitcast_fusion.15), channel_id=1, source_target_pairs={{0,2},{2,4},{4,6},{6,0},{1,3},{3,5},{5,7},{7,1},{8,10},{10,12},{12... | collective-permute-start | bytes 786440 | tf_op jit(solution)/shard_map/ppermute | solution.py:96
  46.7 10.8 %collective-permute-start.17 = (f32[2,32,1024]{2,1,0:T(8,128)}, f32[2,32,1024]{2,1,0:T(8,128)}, u32[]{:S(2)}, u32[]{:S(2)}) collective-permute-start(f32[2,32,1024]{2,1,0:T(8,128)} %dynamic-slice_bitcast_fusion.12), channel_id=1, source_target_pairs={{0,6},{2,0},{4,2},{6,4},{1,7},{3,1},{5,3},{7,5},{8,14},{10,8},{12,... | collective-permute-start | bytes 786440 | tf_op jit(solution)/shard_map/ppermute | solution.py:96
  67.5 11.5 %collective-permute-start.2 = (f32[2,32,1024]{2,1,0:T(8,128)S(1)}, f32[2,32,1024]{2,1,0:T(8,128)S(1)}, u32[]{:S(2)}, u32[]{:S(2)}) collective-permute-start(f32[2,32,1024]{2,1,0:T(8,128)S(1)} %bitcast_add_fusion.47), channel_id=1, source_target_pairs={{0,2},{2,4},{4,6},{6,0},{1,3},{3,5},{5,7},{7,1},{8,10},{10,12},{12... | collective-permute-start | bytes 786440 | tf_op jit(solution)/shard_map/ppermute | solution.py:96
  68.2 13.9 %collective-permute-start.19 = (f32[2,32,1024]{2,1,0:T(8,128)S(1)}, f32[2,32,1024]{2,1,0:T(8,128)S(1)}, u32[]{:S(2)}, u32[]{:S(2)}) collective-permute-start(f32[2,32,1024]{2,1,0:T(8,128)S(1)} %bitcast_add_fusion.38), channel_id=1, source_target_pairs={{0,6},{2,0},{4,2},{6,4},{1,7},{3,1},{5,3},{7,5},{8,14},{10,8},{12,... | collective-permute-start | bytes 786440 | tf_op jit(solution)/shard_map/ppermute | solution.py:96
  83.7 11.1 %collective-permute-start.20 = (f32[2,32,1024]{2,1,0:T(8,128)}, f32[2,32,1024]{2,1,0:T(8,128)}, u32[]{:S(2)}, u32[]{:S(2)}) collective-permute-start(f32[2,32,1024]{2,1,0:T(8,128)} %fusion.67), channel_id=1, source_target_pairs={{0,1},{1,0},{2,3},{3,2},{4,5},{5,4},{6,7},{7,6},{8,9},{9,8},{10,11... | collective-permute-start | bytes 786440 | tf_op jit(solution)/shard_map/ppermute | solution.py:106
  88.2 12.2 %collective-permute-start.7 = (f32[2,32,1024]{2,1,0:T(8,128)}, f32[2,32,1024]{2,1,0:T(8,128)}, u32[]{:S(2)}, u32[]{:S(2)}) collective-permute-start(f32[2,32,1024]{2,1,0:T(8,128)} %fusion.75), channel_id=1, source_target_pairs={{0,1},{1,0},{2,3},{3,2},{4,5},{5,4},{6,7},{7,6},{8,9},{9,8},{10,11... | collective-permute-start | bytes 786440 | tf_op jit(solution)/shard_map/ppermute | solution.py:108
  105.6 12.3 %collective-permute-start.22 = (f32[2,32,1024]{2,1,0:T(8,128)S(1)}, f32[2,32,1024]{2,1,0:T(8,128)S(1)}, u32[]{:S(2)}, u32[]{:S(2)}) collective-permute-start(f32[2,32,1024]{2,1,0:T(8,128)S(1)} %get-tuple-element.178), channel_id=1, source_target_pairs={{0,2},{2,4},{4,6},{6,0},{1,3},{3,5},{5,7},{7,1},{8,10},{10,12},{12... | collective-permute-start | bytes 786440 | tf_op jit(solution)/shard_map/ppermute | solution.py:116
  105.8 12.1 %collective-permute-start.25 = (f32[2,32,1024]{2,1,0:T(8,128)S(1)}, f32[2,32,1024]{2,1,0:T(8,128)S(1)}, u32[]{:S(2)}, u32[]{:S(2)}) collective-permute-start(f32[2,32,1024]{2,1,0:T(8,128)S(1)} %get-tuple-element.179), channel_id=1, source_target_pairs={{0,6},{2,0},{4,2},{6,4},{1,7},{3,1},{5,3},{7,5},{8,14},{10,8},{12,... | collective-permute-start | bytes 786440 | tf_op jit(solution)/shard_map/ppermute | solution.py:116
  112.3 11.2 %collective-permute-start.9 = (f32[2,32,1024]{2,1,0:T(8,128)S(1)}, f32[2,32,1024]{2,1,0:T(8,128)S(1)}, u32[]{:S(2)}, u32[]{:S(2)}) collective-permute-start(f32[2,32,1024]{2,1,0:T(8,128)S(1)} %collective-permute-done.8), channel_id=1, source_target_pairs={{0,2},{2,4},{4,6},{6,0},{1,3},{3,5},{5,7},{7,1},{8,10},{10,12},{12... | collective-permute-start | bytes 786440 | tf_op jit(solution)/shard_map/ppermute | solution.py:116
  112.3 11.2 %collective-permute-start.12 = (f32[2,32,1024]{2,1,0:T(8,128)S(1)}, f32[2,32,1024]{2,1,0:T(8,128)S(1)}, u32[]{:S(2)}, u32[]{:S(2)}) collective-permute-start(f32[2,32,1024]{2,1,0:T(8,128)S(1)} %collective-permute-done.11), channel_id=1, source_target_pairs={{0,6},{2,0},{4,2},{6,4},{1,7},{3,1},{5,3},{7,5},{8,14},{10,8},{12,... | collective-permute-start | bytes 786440 | tf_op jit(solution)/shard_map/ppermute | solution.py:116
  117.9 11.2 %collective-permute-start.23 = (f32[2,32,1024]{2,1,0:T(8,128)S(1)}, f32[2,32,1024]{2,1,0:T(8,128)S(1)}, u32[]{:S(2)}, u32[]{:S(2)}) collective-permute-start(f32[2,32,1024]{2,1,0:T(8,128)S(1)} %collective-permute-done.22), channel_id=1, source_target_pairs={{0,2},{2,4},{4,6},{6,0},{1,3},{3,5},{5,7},{7,1},{8,10},{10,12},{12... | collective-permute-start | bytes 786440 | tf_op jit(solution)/shard_map/ppermute | solution.py:116
  117.9 11.2 %collective-permute-start.26 = (f32[2,32,1024]{2,1,0:T(8,128)S(1)}, f32[2,32,1024]{2,1,0:T(8,128)S(1)}, u32[]{:S(2)}, u32[]{:S(2)}) collective-permute-start(f32[2,32,1024]{2,1,0:T(8,128)S(1)} %collective-permute-done.25), channel_id=1, source_target_pairs={{0,6},{2,0},{4,2},{6,4},{1,7},{3,1},{5,3},{7,5},{8,14},{10,8},{12,... | collective-permute-start | bytes 786440 | tf_op jit(solution)/shard_map/ppermute | solution.py:116
  166.1 12.3 %collective-permute-start.45 = (f32[2,32,1024]{2,1,0:T(8,128)S(1)}, f32[2,32,1024]{2,1,0:T(8,128)S(1)}, u32[]{:S(2)}, u32[]{:S(2)}) collective-permute-start(f32[2,32,1024]{2,1,0:T(8,128)S(1)} %dynamic-slice_bitcast_fusion.8), channel_id=1, source_target_pairs={{0,6},{2,0},{4,2},{6,4},{1,7},{3,1},{5,3},{7,5},{8,14},{10,8},{12,... | collective-permute-start | bytes 786440 | tf_op jit(solution)/shard_map/ppermute | solution.py:96
  169.4 12.7 %collective-permute-start.42 = (f32[2,32,1024]{2,1,0:T(8,128)S(1)}, f32[2,32,1024]{2,1,0:T(8,128)S(1)}, u32[]{:S(2)}, u32[]{:S(2)}) collective-permute-start(f32[2,32,1024]{2,1,0:T(8,128)S(1)} %dynamic-slice_bitcast_fusion.9), channel_id=1, source_target_pairs={{0,2},{2,4},{4,6},{6,0},{1,3},{3,5},{5,7},{7,1},{8,10},{10,12},{12... | collective-permute-start | bytes 786440 | tf_op jit(solution)/shard_map/ppermute | solution.py:96
  172.9 11.2 %collective-permute-start.32 = (f32[2,32,1024]{2,1,0:T(8,128)S(1)}, f32[2,32,1024]{2,1,0:T(8,128)S(1)}, u32[]{:S(2)}, u32[]{:S(2)}) collective-permute-start(f32[2,32,1024]{2,1,0:T(8,128)S(1)} %bitcast_add_fusion.33), channel_id=1, source_target_pairs={{0,6},{2,0},{4,2},{6,4},{1,7},{3,1},{5,3},{7,5},{8,14},{10,8},{12,... | collective-permute-start | bytes 786440 | tf_op jit(solution)/shard_map/ppermute | solution.py:96
  176.5 11.2 %collective-permute-start.29 = (f32[2,32,1024]{2,1,0:T(8,128)S(1)}, f32[2,32,1024]{2,1,0:T(8,128)S(1)}, u32[]{:S(2)}, u32[]{:S(2)}) collective-permute-start(f32[2,32,1024]{2,1,0:T(8,128)S(1)} %bitcast_add_fusion.36), channel_id=1, source_target_pairs={{0,2},{2,4},{4,6},{6,0},{1,3},{3,5},{5,7},{7,1},{8,10},{10,12},{12... | collective-permute-start | bytes 786440 | tf_op jit(solution)/shard_map/ppermute | solution.py:96
  178.5 10.8 %collective-permute-start.46 = (f32[2,32,1024]{2,1,0:T(8,128)S(1)}, f32[2,32,1024]{2,1,0:T(8,128)S(1)}, u32[]{:S(2)}, u32[]{:S(2)}) collective-permute-start(f32[2,32,1024]{2,1,0:T(8,128)S(1)} %bitcast_add_fusion.27), channel_id=1, source_target_pairs={{0,6},{2,0},{4,2},{6,4},{1,7},{3,1},{5,3},{7,5},{8,14},{10,8},{12,... | collective-permute-start | bytes 786440 | tf_op jit(solution)/shard_map/ppermute | solution.py:96
  182.1 10.9 %collective-permute-start.43 = (f32[2,32,1024]{2,1,0:T(8,128)S(1)}, f32[2,32,1024]{2,1,0:T(8,128)S(1)}, u32[]{:S(2)}, u32[]{:S(2)}) collective-permute-start(f32[2,32,1024]{2,1,0:T(8,128)S(1)} %bitcast_add_fusion.30), channel_id=1, source_target_pairs={{0,2},{2,4},{4,6},{6,0},{1,3},{3,5},{5,7},{7,1},{8,10},{10,12},{12... | collective-permute-start | bytes 786440 | tf_op jit(solution)/shard_map/ppermute | solution.py:96
  195.7 10.8 %collective-permute-start.34 = (f32[2,32,1024]{2,1,0:T(8,128)S(1)}, f32[2,32,1024]{2,1,0:T(8,128)S(1)}, u32[]{:S(2)}, u32[]{:S(2)}) collective-permute-start(f32[2,32,1024]{2,1,0:T(8,128)S(1)} %fusion.62), channel_id=1, source_target_pairs={{0,1},{1,0},{2,3},{3,2},{4,5},{5,4},{6,7},{7,6},{8,9},{9,8},{10,11... | collective-permute-start | bytes 786440 | tf_op jit(solution)/shard_map/ppermute | solution.py:106
  224.2 11.5 %collective-permute-start.37 = (f32[2,32,1024]{2,1,0:T(8,128)S(1)}, f32[2,32,1024]{2,1,0:T(8,128)S(1)}, u32[]{:S(2)}, u32[]{:S(2)}) collective-permute-start(f32[2,32,1024]{2,1,0:T(8,128)S(1)} %collective-permute-done.36), channel_id=1, source_target_pairs={{0,2},{2,4},{4,6},{6,0},{1,3},{3,5},{5,7},{7,1},{8,10},{10,12},{12... | collective-permute-start | bytes 786440 | tf_op jit(solution)/shard_map/ppermute | solution.py:116
  224.3 11.7 %collective-permute-start.40 = (f32[2,32,1024]{2,1,0:T(8,128)S(1)}, f32[2,32,1024]{2,1,0:T(8,128)S(1)}, u32[]{:S(2)}, u32[]{:S(2)}) collective-permute-start(f32[2,32,1024]{2,1,0:T(8,128)S(1)} %collective-permute-done.39), channel_id=1, source_target_pairs={{0,6},{2,0},{4,2},{6,4},{1,7},{3,1},{5,3},{7,5},{8,14},{10,8},{12,... | collective-permute-start | bytes 786440 | tf_op jit(solution)/shard_map/ppermute | solution.py:116
  252.4 14.5 %collective-permute-start.59 = (f32[2,64,1024]{2,1,0:T(8,128)S(1)}, f32[2,64,1024]{2,1,0:T(8,128)S(1)}, u32[]{:S(2)}, u32[]{:S(2)}) collective-permute-start(f32[2,64,1024]{2,1,0:T(8,128)S(1)} %dynamic-slice_bitcast_fusion), channel_id=1, source_target_pairs={{0,6},{2,0},{4,2},{6,4},{1,7},{3,1},{5,3},{7,5},{8,14},{10,8},{12,... | collective-permute-start | bytes 1572872 | tf_op jit(solution)/shard_map/ppermute | solution.py:96
  256.2 14.5 %collective-permute-start.56 = (f32[2,64,1024]{2,1,0:T(8,128)S(1)}, f32[2,64,1024]{2,1,0:T(8,128)S(1)}, u32[]{:S(2)}, u32[]{:S(2)}) collective-permute-start(f32[2,64,1024]{2,1,0:T(8,128)S(1)} %dynamic-slice_bitcast_fusion.1), channel_id=1, source_target_pairs={{0,2},{2,4},{4,6},{6,0},{1,3},{3,5},{5,7},{7,1},{8,10},{10,12},{12... | collective-permute-start | bytes 1572872 | tf_op jit(solution)/shard_map/ppermute | solution.py:96
  267.0 13.6 %collective-permute-start.60 = (f32[2,64,1024]{2,1,0:T(8,128)S(1)}, f32[2,64,1024]{2,1,0:T(8,128)S(1)}, u32[]{:S(2)}, u32[]{:S(2)}) collective-permute-start(f32[2,64,1024]{2,1,0:T(8,128)S(1)} %bitcast_add_fusion.3), channel_id=1, source_target_pairs={{0,6},{2,0},{4,2},{6,4},{1,7},{3,1},{5,3},{7,5},{8,14},{10,8},{12,... | collective-permute-start | bytes 1572872 | tf_op jit(solution)/shard_map/ppermute | solution.py:96
  270.8 13.6 %collective-permute-start.57 = (f32[2,64,1024]{2,1,0:T(8,128)S(1)}, f32[2,64,1024]{2,1,0:T(8,128)S(1)}, u32[]{:S(2)}, u32[]{:S(2)}) collective-permute-start(f32[2,64,1024]{2,1,0:T(8,128)S(1)} %bitcast_add_fusion.6), channel_id=1, source_target_pairs={{0,2},{2,4},{4,6},{6,0},{1,3},{3,5},{5,7},{7,1},{8,10},{10,12},{12... | collective-permute-start | bytes 1572872 | tf_op jit(solution)/shard_map/ppermute | solution.py:96
  295.1 13.3 %collective-permute-start.62 = (f32[2,64,1024]{2,1,0:T(8,128)S(1)}, f32[2,64,1024]{2,1,0:T(8,128)S(1)}, u32[]{:S(2)}, u32[]{:S(2)}) collective-permute-start(f32[2,64,1024]{2,1,0:T(8,128)S(1)} %fusion.34), channel_id=1, source_target_pairs={{0,1},{1,0},{2,3},{3,2},{4,5},{5,4},{6,7},{7,6},{8,9},{9,8},{10,11... | collective-permute-start | bytes 1572872 | tf_op jit(solution)/shard_map/ppermute | solution.py:106
  309.2 10.9 %collective-permute-start.63 = (f32[2,64,1024]{2,1,0:T(8,128)}, f32[2,64,1024]{2,1,0:T(8,128)S(1)}, u32[]{:S(2)}, u32[]{:S(2)}) collective-permute-start(f32[2,64,1024]{2,1,0:T(8,128)} %fusion.37), channel_id=1, source_target_pairs={{0,1},{1,0},{2,3},{3,2},{4,5},{5,4},{6,7},{7,6},{8,9},{9,8},{10,11... | collective-permute-start | bytes 1572872 | tf_op jit(solution)/shard_map/ppermute | solution.py:108
  322.8 12.6 %collective-permute-start.64 = (f32[2,64,1024]{2,1,0:T(8,128)S(1)}, f32[2,64,1024]{2,1,0:T(8,128)S(1)}, u32[]{:S(2)}, u32[]{:S(2)}) collective-permute-start(f32[2,64,1024]{2,1,0:T(8,128)S(1)} %get-tuple-element.161), channel_id=1, source_target_pairs={{0,2},{2,4},{4,6},{6,0},{1,3},{3,5},{5,7},{7,1},{8,10},{10,12},{12... | collective-permute-start | bytes 1572872 | tf_op jit(solution)/shard_map/ppermute | solution.py:116
  322.9 12.9 %collective-permute-start.67 = (f32[2,64,1024]{2,1,0:T(8,128)S(1)}, f32[2,64,1024]{2,1,0:T(8,128)S(1)}, u32[]{:S(2)}, u32[]{:S(2)}) collective-permute-start(f32[2,64,1024]{2,1,0:T(8,128)S(1)} %get-tuple-element.162), channel_id=1, source_target_pairs={{0,6},{2,0},{4,2},{6,4},{1,7},{3,1},{5,3},{7,5},{8,14},{10,8},{12,... | collective-permute-start | bytes 1572872 | tf_op jit(solution)/shard_map/ppermute | solution.py:116
  460.0 12.1 %collective-permute-start.87 = (f32[2,32,1024]{2,1,0:T(8,128)S(1)}, f32[2,32,1024]{2,1,0:T(8,128)S(1)}, u32[]{:S(2)}, u32[]{:S(2)}) collective-permute-start(f32[2,32,1024]{2,1,0:T(8,128)S(1)} %dynamic-slice_bitcast_fusion.4), channel_id=1, source_target_pairs={{0,6},{2,0},{4,2},{6,4},{1,7},{3,1},{5,3},{7,5},{8,14},{10,8},{12,... | collective-permute-start | bytes 786440 | tf_op jit(solution)/shard_map/ppermute | solution.py:96
  463.3 11.6 %collective-permute-start.84 = (f32[2,32,1024]{2,1,0:T(8,128)S(1)}, f32[2,32,1024]{2,1,0:T(8,128)S(1)}, u32[]{:S(2)}, u32[]{:S(2)}) collective-permute-start(f32[2,32,1024]{2,1,0:T(8,128)S(1)} %dynamic-slice_bitcast_fusion.5), channel_id=1, source_target_pairs={{0,2},{2,4},{4,6},{6,0},{1,3},{3,5},{5,7},{7,1},{8,10},{10,12},{12... | collective-permute-start | bytes 786440 | tf_op jit(solution)/shard_map/ppermute | solution.py:96
  464.1 11.8 %collective-permute-start.102 = (f32[64,1024]{1,0:T(8,128)S(1)}, f32[64,1024]{1,0:T(8,128)S(1)}, u32[]{:S(2)}, u32[]{:S(2)}) collective-permute-start(f32[64,1024]{1,0:T(8,128)S(1)} %bitcast_add_fusion.9), channel_id=1, source_target_pairs={{0,48},{16,0},{32,16},{48,32},{1,49},{17,1},{33,17},{49,33},{2,50}... | collective-permute-start | bytes 786440 | tf_op jit(solution)/shard_map/ppermute | solution.py:140
  472.1 10.9 %collective-permute-start.71 = (f32[2,32,1024]{2,1,0:T(8,128)S(1)}, f32[2,32,1024]{2,1,0:T(8,128)S(1)}, u32[]{:S(2)}, u32[]{:S(2)}) collective-permute-start(f32[2,32,1024]{2,1,0:T(8,128)S(1)} %bitcast_add_fusion.24), channel_id=1, source_target_pairs={{0,2},{2,4},{4,6},{6,0},{1,3},{3,5},{5,7},{7,1},{8,10},{10,12},{12... | collective-permute-start | bytes 786440 | tf_op jit(solution)/shard_map/ppermute | solution.py:96
  477.1 11.5 %collective-permute-start.103 = (f32[64,1024]{1,0:T(8,128)S(1)}, f32[64,1024]{1,0:T(8,128)S(1)}, u32[]{:S(2)}, u32[]{:S(2)}) collective-permute-start(f32[64,1024]{1,0:T(8,128)S(1)} %bitcast_add_fusion.8), channel_id=1, source_target_pairs={{0,48},{16,0},{32,16},{48,32},{1,49},{17,1},{33,17},{49,33},{2,50}... | collective-permute-start | bytes 786440 | tf_op jit(solution)/shard_map/ppermute | solution.py:140
  486.6 10.8 %collective-permute-start.89 = (f32[2,32,1024]{2,1,0:T(8,128)S(1)}, f32[2,32,1024]{2,1,0:T(8,128)S(1)}, u32[]{:S(2)}, u32[]{:S(2)}) collective-permute-start(f32[2,32,1024]{2,1,0:T(8,128)S(1)} %bitcast_add_fusion.14), channel_id=1, source_target_pairs={{0,6},{2,0},{4,2},{6,4},{1,7},{3,1},{5,3},{7,5},{8,14},{10,8},{12,... | collective-permute-start | bytes 786440 | tf_op jit(solution)/shard_map/ppermute | solution.py:96
  488.9 12.7 %collective-permute-start.104 = (f32[2,32,1024]{2,1,0:T(8,128)S(1)}, f32[2,32,1024]{2,1,0:T(8,128)S(1)}, u32[]{:S(2)}, u32[]{:S(2)}) collective-permute-start(f32[2,32,1024]{2,1,0:T(8,128)S(1)} %fusion.42), channel_id=1, source_target_pairs={{0,8},{8,0},{1,9},{9,1},{2,10},{10,2},{3,11},{11,3},{4,12},{12,4},... | collective-permute-start | bytes 786440 | tf_op jit(solution)/shard_map/ppermute | solution.py:150
  498.3 15.4 %collective-permute-start.90 = (f32[2,32,1024]{2,1,0:T(8,128)S(1)}, f32[2,32,1024]{2,1,0:T(8,128)S(1)}, u32[]{:S(2)}, u32[]{:S(2)}) collective-permute-start(f32[2,32,1024]{2,1,0:T(8,128)S(1)} %fusion.47), channel_id=1, source_target_pairs={{0,1},{1,0},{2,3},{3,2},{4,5},{5,4},{6,7},{7,6},{8,9},{9,8},{10,11... | collective-permute-start | bytes 786440 | tf_op jit(solution)/shard_map/ppermute | solution.py:106
  506.1 14.7 %collective-permute-start.77 = (f32[2,32,1024]{2,1,0:T(8,128)S(1)}, f32[2,32,1024]{2,1,0:T(8,128)S(1)}, u32[]{:S(2)}, u32[]{:S(2)}) collective-permute-start(f32[2,32,1024]{2,1,0:T(8,128)S(1)} %fusion.55), channel_id=1, source_target_pairs={{0,1},{1,0},{2,3},{3,2},{4,5},{5,4},{6,7},{7,6},{8,9},{9,8},{10,11... | collective-permute-start | bytes 786440 | tf_op jit(solution)/shard_map/ppermute | solution.py:108
  513.7 12.2 %collective-permute-start.91 = (f32[2,32,1024]{2,1,0:T(8,128)S(1)}, f32[2,32,1024]{2,1,0:T(8,128)S(1)}, u32[]{:S(2)}, u32[]{:S(2)}) collective-permute-start(f32[2,32,1024]{2,1,0:T(8,128)S(1)} %fusion.50), channel_id=1, source_target_pairs={{0,1},{1,0},{2,3},{3,2},{4,5},{5,4},{6,7},{7,6},{8,9},{9,8},{10,11... | collective-permute-start | bytes 786440 | tf_op jit(solution)/shard_map/ppermute | solution.py:108
  521.1 12.0 %collective-permute-start.81 = (f32[2,32,1024]{2,1,0:T(8,128)S(1)}, f32[2,32,1024]{2,1,0:T(8,128)S(1)}, u32[]{:S(2)}, u32[]{:S(2)}) collective-permute-start(f32[2,32,1024]{2,1,0:T(8,128)S(1)} %get-tuple-element.166), channel_id=1, source_target_pairs={{0,6},{2,0},{4,2},{6,4},{1,7},{3,1},{5,3},{7,5},{8,14},{10,8},{12,... | collective-permute-start | bytes 786440 | tf_op jit(solution)/shard_map/ppermute | solution.py:116
  526.1 10.9 %collective-permute-start.92 = (f32[2,32,1024]{2,1,0:T(8,128)S(1)}, f32[2,32,1024]{2,1,0:T(8,128)S(1)}, u32[]{:S(2)}, u32[]{:S(2)}) collective-permute-start(f32[2,32,1024]{2,1,0:T(8,128)S(1)} %get-tuple-element.167), channel_id=1, source_target_pairs={{0,2},{2,4},{4,6},{6,0},{1,3},{3,5},{5,7},{7,1},{8,10},{10,12},{12... | collective-permute-start | bytes 786440 | tf_op jit(solution)/shard_map/ppermute | solution.py:116
  526.2 11.4 %collective-permute-start.95 = (f32[2,32,1024]{2,1,0:T(8,128)S(1)}, f32[2,32,1024]{2,1,0:T(8,128)S(1)}, u32[]{:S(2)}, u32[]{:S(2)}) collective-permute-start(f32[2,32,1024]{2,1,0:T(8,128)S(1)} %get-tuple-element.168), channel_id=1, source_target_pairs={{0,6},{2,0},{4,2},{6,4},{1,7},{3,1},{5,3},{7,5},{8,14},{10,8},{12,... | collective-permute-start | bytes 786440 | tf_op jit(solution)/shard_map/ppermute | solution.py:116
  537.9 11.0 %collective-permute-start.93 = (f32[2,32,1024]{2,1,0:T(8,128)S(1)}, f32[2,32,1024]{2,1,0:T(8,128)S(1)}, u32[]{:S(2)}, u32[]{:S(2)}) collective-permute-start(f32[2,32,1024]{2,1,0:T(8,128)S(1)} %collective-permute-done.92), channel_id=1, source_target_pairs={{0,2},{2,4},{4,6},{6,0},{1,3},{3,5},{5,7},{7,1},{8,10},{10,12},{12... | collective-permute-start | bytes 786440 | tf_op jit(solution)/shard_map/ppermute | solution.py:116
  539.5 11.6 %collective-permute-start.96 = (f32[2,32,1024]{2,1,0:T(8,128)S(1)}, f32[2,32,1024]{2,1,0:T(8,128)S(1)}, u32[]{:S(2)}, u32[]{:S(2)}) collective-permute-start(f32[2,32,1024]{2,1,0:T(8,128)S(1)} %collective-permute-done.95), channel_id=1, source_target_pairs={{0,6},{2,0},{4,2},{6,4},{1,7},{3,1},{5,3},{7,5},{8,14},{10,8},{12,... | collective-permute-start | bytes 786440 | tf_op jit(solution)/shard_map/ppermute | solution.py:116
  541.3 21.6 %collective-permute-start.109 = (f32[64,1024]{1,0:T(8,128)S(1)}, f32[64,1024]{1,0:T(8,128)S(1)}, u32[]{:S(2)}, u32[]{:S(2)}) collective-permute-start(f32[64,1024]{1,0:T(8,128)S(1)} %collective-permute-done.108), channel_id=1, source_target_pairs={{0,16},{16,32},{32,48},{48,0},{1,17},{17,33},{33,49},{49,1},{2,18}... | collective-permute-start | bytes 786440 | tf_op jit(solution)/shard_map/ppermute | solution.py:162
  543.6 19.4 %collective-permute-start.112 = (f32[64,1024]{1,0:T(8,128)S(1)}, f32[64,1024]{1,0:T(8,128)S(1)}, u32[]{:S(2)}, u32[]{:S(2)}) collective-permute-start(f32[64,1024]{1,0:T(8,128)S(1)} %collective-permute-done.111), channel_id=1, source_target_pairs={{0,48},{16,0},{32,16},{48,32},{1,49},{17,1},{33,17},{49,33},{2,50}... | collective-permute-start | bytes 786440 | tf_op jit(solution)/shard_map/ppermute | solution.py:162
  (147 other events, 1072.5 us)
Sparse Core Ops, SparseCore 0:
  312.6 136.8 all-reduce.4

commit v6 on v3

--- a/solution.py
+++ b/solution.py
@@ -227,15 +227,28 @@
         .reshape(length, kv_heads, groups, head_size)
     )
     k_rot = rotate(k_hat * key_gain, cosine, sine_table).astype(jnp.bfloat16)
-    scores = score_table(q_rot, k_rot, allowed, factor)
-    row_peak = jnp.max(scores, axis=-1, keepdims=True)
-    log_total = row_peak + jnp.log(jnp.sum(jnp.exp(scores - row_peak), axis=-1, keepdims=True))
-    attn_probs = jnp.exp(scores - log_total).astype(jnp.bfloat16)
-    attn_mixed = jnp.einsum(
-        "kgij,jkd->ikgd", attn_probs, v_half, preferred_element_type=jnp.float32
-    )
-    attn_mixed = attn_mixed.reshape(length, q_heads * head_size).astype(jnp.bfloat16)
-    attn_sum = split_tensor_sum(jnp.dot(attn_mixed, w_out, preferred_element_type=jnp.float32))
+    block = length // 2
+    log_blocks, mixed_blocks, sum_blocks = [], [], []
+    for first in range(0, length, block):
+        seen = first + block
+        scores = score_table(
+            q_rot[first:seen], k_rot[:seen], allowed[first:seen, :seen], factor
+        )
+        row_peak = jnp.max(scores, axis=-1, keepdims=True)
+        log_block = row_peak + jnp.log(
+            jnp.sum(jnp.exp(scores - row_peak), axis=-1, keepdims=True)
+        )
+        attn_probs = jnp.exp(scores - log_block).astype(jnp.bfloat16)
+        mixed = jnp.einsum(
+            "kgij,jkd->ikgd", attn_probs, v_half[:seen], preferred_element_type=jnp.float32
+        )
+        mixed = mixed.reshape(block, q_heads * head_size).astype(jnp.bfloat16)
+        log_blocks.append(log_block)
+        mixed_blocks.append(mixed)
+        sum_blocks.append(tensor_sum(jnp.dot(mixed, w_out, preferred_element_type=jnp.float32)))
+    log_total = jnp.concatenate(log_blocks, axis=2)
+    attn_mixed = jnp.concatenate(mixed_blocks, axis=0)
+    attn_sum = jnp.concatenate(sum_blocks, axis=0)
     residual = tokens_wide + attn_sum
     scale_two = rms_scale(residual)
     normed_two = (residual * scale_two * ffn_gain).astype(jnp.bfloat16)

time: 550 us -> 551 us (level)
  matrix products: 50.6 us -> 56.3 us
    dot_general x1 -> x3, matrix products: 1.86 us -> 8.06 us  [score_table(): jnp.einsum('ikgd,jkd->kgij', q_rot, k_rot, preferred_element_type=jnp.flo...]
    unnamed x179 -> x189, local copies, waits for them, and re-layouts: 18.3 us -> 17.9 us
  transfers between devices with their start and end apart: 132 -> 132, of which waited for: 78 -> 74; matrix products, arithmetic and copies ran while one was open for 16% -> 18% of each run, Pallas kernels for 0% -> 0%
where the time goes in v6:
time: 551 us; the launch traced here: 541 us
  waiting for transfers between devices  189 us (34%)
  starting transfers between devices  177 us (32%)
  matrix products  56.3 us (10%)
  other arithmetic  54 us (10%)
  local copies, waits for them, and re-layouts  47.7 us (9%)
  between operations  17.4 us (3%)
    ppermute x48, waiting for transfers between devices, tensor_sum(): cur = lax.ppermute(cur, 'ty', ring(ny, shift))  78.8 us
    ppermute x48, starting transfers between devices, tensor_sum(): acc = lax.ppermute(acc, 'ty', ring(ny, shift))  64.6 us
    ppermute x48, starting transfers between devices, tensor_sum(): cur = lax.ppermute(cur, 'ty', ring(ny, shift))  55.4 us
    ppermute x48, waiting for transfers between devices, tensor_sum(): acc = lax.ppermute(acc, 'ty', ring(ny, shift))  42.1 us
    ppermute x8, waiting for transfers between devices, tensor_sum(): got = lax.ppermute(send, 'tx', pairs)  29.9 us
    ppermute x8, starting transfers between devices, tensor_sum(): other = lax.ppermute(mine, 'tx', pairs)  21.6 us
    unnamed x189, local copies, waits for them, and re-layouts  17.9 us
    dot_general x7, matrix products, inner(): lax.dot_general(first_op, second_op, (((1,), (1,)), ((), ())), preferred_...  16.5 us
  transfers between devices with their start and end apart: 132, of which 74 were waited for; matrix products, arithmetic and copies ran while one was open for 18% of the time, Pallas kernels for 0%

profile of v6, /device:TPU:0, one launch (start us, length us, event | category | flops | bytes accessed | tf_op | source)
XLA Modules:
  0.0 541.4 jit_solution(18017540552269914861)
XLA Ops:
  39.4 3.2 collective-permute-start.17
  46.8 5.5 %fusion.139 = f32[1024,1024,2]{1,0,2:T(8,128)} fusion(bf16[1024,2,64]{0,2,1:T(8,128)(2,1)S(1)} %bitcast.862, bf16[1024,64]{0,1:T(8,128)(2,1)} %copy-done.49), kind=kOutput, calls=%fused_computation.410 | convolution fusion | flops 268435456 | bytes 8781824 | tf_op jit(solution)/shard_map/ikgd,jkd->kgij/dot_general | solution.py:68
  53.6 3.3 collective-permute-start.4
  59.1 3.3 collective-permute-start.18
  63.6 3.3 collective-permute-start.5
  69.2 3.8 collective-permute-start.19
  74.8 4.8 collective-permute-done.2
  102.7 3.2 collective-permute-start.11
  106.7 3.3 collective-permute-start.25
  113.1 3.3 collective-permute-start.12
  118.8 3.3 collective-permute-start.26
  124.4 3.3 collective-permute-start.13
  130.0 3.7 collective-permute-start.27
  134.1 3.5 collective-permute-done.24
  147.4 3.9 fusion.168
  170.9 4.8 convolution_add_fusion
  177.1 3.2 collective-permute-start.59
  206.6 3.4 collective-permute-done.43
  212.2 3.4 collective-permute-done.57
  217.8 3.4 collective-permute-done.71
  223.4 3.4 collective-permute-done.30
  241.3 4.8 collective-permute-done.34
  249.3 5.3 collective-permute-done.48
  257.7 5.3 collective-permute-done.62
  266.1 5.3 collective-permute-done.76
  273.8 3.8 collective-permute-done.35
  288.8 3.3 collective-permute-start.67
  295.7 3.5 collective-permute-done.64
  301.3 3.5 collective-permute-done.78
  306.9 3.5 collective-permute-done.37
  312.5 3.5 collective-permute-done.51
  318.1 3.5 collective-permute-done.65
  323.8 3.5 collective-permute-done.79
  327.7 3.2 collective-permute-start.69
  331.0 9.0 %collective-permute-done.66 = f32[2,32,1024]{2,1,0:T(8,128)S(1)} collective-permute-done((f32[2,32,1024]{2,1,0:T(8,128)S(1)}, f32[2,32,1024]{2,1,0:T(8,128)S(1)}, u32[]{:S(2)}, u32[]{:S(2)}) %collective-permute-start.66) | collective-permute-done | bytes 262176 | tf_op jit(solution)/shard_map/ppermute | solution.py:116
  340.0 3.3 collective-permute-start.83
  343.6 4.0 collective-permute-done.80
  354.2 4.8 multiply_add_fusion
  378.0 3.3 fusion.18
  436.8 4.8 collective-permute-done.90
  441.7 6.6 %collective-permute-done.119 = f32[2,16,1024]{2,1,0:T(8,128)S(1)} collective-permute-done((f32[2,16,1024]{2,1,0:T(8,128)S(1)}, f32[2,16,1024]{2,1,0:T(8,128)S(1)}, u32[]{:S(2)}, u32[]{:S(2)}) %collective-permute-start.119) | collective-permute-done | bytes 131104 | tf_op jit(solution)/shard_map/ppermute | solution.py:150
  448.5 3.7 collective-permute-start.105
  452.3 4.4 collective-permute-done.120
  477.7 3.3 collective-permute-done.93
  487.0 4.6 collective-permute-done.94
  502.6 4.2 collective-permute-done.124
  507.7 3.6 collective-permute-done.128
  526.7 3.5 copy.137
  (718 shorter events, 332.8 us)
Async XLA Ops:
  7.2 381.1 %all-reduce.5.cloned.1.call-start = ((), (), s32[]{:S(2)}) async-start(), calls=%async_computation | async-start | bytes 14155776 | tf_op jit(solution)/shard_map/psum | solution.py:272
  27.0 25.3 %collective-permute-start.3 = (f32[2,32,1024]{2,1,0:T(8,128)}, f32[2,32,1024]{2,1,0:T(8,128)}, u32[]{:S(2)}, u32[]{:S(2)}) collective-permute-start(f32[2,32,1024]{2,1,0:T(8,128)} %dynamic-slice_bitcast_fusion.16), channel_id=1, source_target_pairs={{0,6},{2,0},{4,2},{6,4},{1,7},{3,1},{5,3},{7,5},{8,14},{10,8},{12,... | collective-permute-start | bytes 786440 | tf_op jit(solution)/shard_map/ppermute | solution.py:96
  31.8 25.1 %collective-permute-start = (f32[2,32,1024]{2,1,0:T(8,128)}, f32[2,32,1024]{2,1,0:T(8,128)}, u32[]{:S(2)}, u32[]{:S(2)}) collective-permute-start(f32[2,32,1024]{2,1,0:T(8,128)} %dynamic-slice_bitcast_fusion.17), channel_id=1, source_target_pairs={{0,2},{2,4},{4,6},{6,0},{1,3},{3,5},{5,7},{7,1},{8,10},{10,12},{12... | collective-permute-start | bytes 786440 | tf_op jit(solution)/shard_map/ppermute | solution.py:96
  39.4 18.7 %collective-permute-start.17 = (f32[2,32,1024]{2,1,0:T(8,128)}, f32[2,32,1024]{2,1,0:T(8,128)}, u32[]{:S(2)}, u32[]{:S(2)}) collective-permute-start(f32[2,32,1024]{2,1,0:T(8,128)} %dynamic-slice_bitcast_fusion.14), channel_id=1, source_target_pairs={{0,6},{2,0},{4,2},{6,4},{1,7},{3,1},{5,3},{7,5},{8,14},{10,8},{12,... | collective-permute-start | bytes 786440 | tf_op jit(solution)/shard_map/ppermute | solution.py:96
  43.3 19.1 %collective-permute-start.14 = (f32[2,32,1024]{2,1,0:T(8,128)}, f32[2,32,1024]{2,1,0:T(8,128)}, u32[]{:S(2)}, u32[]{:S(2)}) collective-permute-start(f32[2,32,1024]{2,1,0:T(8,128)} %dynamic-slice_bitcast_fusion.15), channel_id=1, source_target_pairs={{0,2},{2,4},{4,6},{6,0},{1,3},{3,5},{5,7},{7,1},{8,10},{10,12},{12... | collective-permute-start | bytes 786440 | tf_op jit(solution)/shard_map/ppermute | solution.py:96
  66.9 12.7 %collective-permute-start.2 = (f32[2,32,1024]{2,1,0:T(8,128)S(1)}, f32[2,32,1024]{2,1,0:T(8,128)S(1)}, u32[]{:S(2)}, u32[]{:S(2)}) collective-permute-start(f32[2,32,1024]{2,1,0:T(8,128)S(1)} %bitcast_add_fusion.52), channel_id=1, source_target_pairs={{0,2},{2,4},{4,6},{6,0},{1,3},{3,5},{5,7},{7,1},{8,10},{10,12},{12... | collective-permute-start | bytes 786440 | tf_op jit(solution)/shard_map/ppermute | solution.py:96
  69.2 13.6 %collective-permute-start.19 = (f32[2,32,1024]{2,1,0:T(8,128)S(1)}, f32[2,32,1024]{2,1,0:T(8,128)S(1)}, u32[]{:S(2)}, u32[]{:S(2)}) collective-permute-start(f32[2,32,1024]{2,1,0:T(8,128)S(1)} %bitcast_add_fusion.43), channel_id=1, source_target_pairs={{0,6},{2,0},{4,2},{6,4},{1,7},{3,1},{5,3},{7,5},{8,14},{10,8},{12,... | collective-permute-start | bytes 786440 | tf_op jit(solution)/shard_map/ppermute | solution.py:96
  160.1 22.4 %collective-permute-start.31 = (f32[2,32,1024]{2,1,0:T(8,128)}, f32[2,32,1024]{2,1,0:T(8,128)}, u32[]{:S(2)}, u32[]{:S(2)}) collective-permute-start(f32[2,32,1024]{2,1,0:T(8,128)} %dynamic-slice_bitcast_fusion.12), channel_id=1, source_target_pairs={{0,6},{2,0},{4,2},{6,4},{1,7},{3,1},{5,3},{7,5},{8,14},{10,8},{12,... | collective-permute-start | bytes 786440 | tf_op jit(solution)/shard_map/ppermute | solution.py:96
  163.2 20.6 %collective-permute-start.28 = (f32[2,32,1024]{2,1,0:T(8,128)}, f32[2,32,1024]{2,1,0:T(8,128)}, u32[]{:S(2)}, u32[]{:S(2)}) collective-permute-start(f32[2,32,1024]{2,1,0:T(8,128)} %dynamic-slice_bitcast_fusion.13), channel_id=1, source_target_pairs={{0,2},{2,4},{4,6},{6,0},{1,3},{3,5},{5,7},{7,1},{8,10},{10,12},{12... | collective-permute-start | bytes 786440 | tf_op jit(solution)/shard_map/ppermute | solution.py:96
  164.2 23.9 %collective-permute-start.45 = (f32[2,32,1024]{2,1,0:T(8,128)}, f32[2,32,1024]{2,1,0:T(8,128)}, u32[]{:S(2)}, u32[]{:S(2)}) collective-permute-start(f32[2,32,1024]{2,1,0:T(8,128)} %dynamic-slice_bitcast_fusion.10), channel_id=1, source_target_pairs={{0,6},{2,0},{4,2},{6,4},{1,7},{3,1},{5,3},{7,5},{8,14},{10,8},{12,... | collective-permute-start | bytes 786440 | tf_op jit(solution)/shard_map/ppermute | solution.py:96
  168.1 21.2 %collective-permute-start.42 = (f32[2,32,1024]{2,1,0:T(8,128)}, f32[2,32,1024]{2,1,0:T(8,128)}, u32[]{:S(2)}, u32[]{:S(2)}) collective-permute-start(f32[2,32,1024]{2,1,0:T(8,128)} %dynamic-slice_bitcast_fusion.11), channel_id=1, source_target_pairs={{0,2},{2,4},{4,6},{6,0},{1,3},{3,5},{5,7},{7,1},{8,10},{10,12},{12... | collective-permute-start | bytes 786440 | tf_op jit(solution)/shard_map/ppermute | solution.py:96
  177.1 16.5 %collective-permute-start.59 = (f32[2,32,1024]{2,1,0:T(8,128)}, f32[2,32,1024]{2,1,0:T(8,128)}, u32[]{:S(2)}, u32[]{:S(2)}) collective-permute-start(f32[2,32,1024]{2,1,0:T(8,128)} %dynamic-slice_bitcast_fusion.8), channel_id=1, source_target_pairs={{0,6},{2,0},{4,2},{6,4},{1,7},{3,1},{5,3},{7,5},{8,14},{10,8},{12,... | collective-permute-start | bytes 786440 | tf_op jit(solution)/shard_map/ppermute | solution.py:96
  183.8 14.2 %collective-permute-start.73 = (f32[2,32,1024]{2,1,0:T(8,128)}, f32[2,32,1024]{2,1,0:T(8,128)S(1)}, u32[]{:S(2)}, u32[]{:S(2)}) collective-permute-start(f32[2,32,1024]{2,1,0:T(8,128)} %dynamic-slice_bitcast_fusion.6), channel_id=1, source_target_pairs={{0,6},{2,0},{4,2},{6,4},{1,7},{3,1},{5,3},{7,5},{8,14},{10,8},{12,... | collective-permute-start | bytes 786440 | tf_op jit(solution)/shard_map/ppermute | solution.py:96
  201.5 14.1 %collective-permute-start.57 = (f32[2,32,1024]{2,1,0:T(8,128)S(1)}, f32[2,32,1024]{2,1,0:T(8,128)S(1)}, u32[]{:S(2)}, u32[]{:S(2)}) collective-permute-start(f32[2,32,1024]{2,1,0:T(8,128)S(1)} %bitcast_add_fusion.29), channel_id=1, source_target_pairs={{0,2},{2,4},{4,6},{6,0},{1,3},{3,5},{5,7},{7,1},{8,10},{10,12},{12... | collective-permute-start | bytes 786440 | tf_op jit(solution)/shard_map/ppermute | solution.py:96
  205.0 16.3 %collective-permute-start.71 = (f32[2,32,1024]{2,1,0:T(8,128)S(1)}, f32[2,32,1024]{2,1,0:T(8,128)S(1)}, u32[]{:S(2)}, u32[]{:S(2)}) collective-permute-start(f32[2,32,1024]{2,1,0:T(8,128)S(1)} %bitcast_add_fusion.23), channel_id=1, source_target_pairs={{0,2},{2,4},{4,6},{6,0},{1,3},{3,5},{5,7},{7,1},{8,10},{10,12},{12... | collective-permute-start | bytes 786440 | tf_op jit(solution)/shard_map/ppermute | solution.py:96
  210.5 16.4 %collective-permute-start.30 = (f32[2,32,1024]{2,1,0:T(8,128)S(1)}, f32[2,32,1024]{2,1,0:T(8,128)S(1)}, u32[]{:S(2)}, u32[]{:S(2)}) collective-permute-start(f32[2,32,1024]{2,1,0:T(8,128)S(1)} %bitcast_add_fusion.40), channel_id=1, source_target_pairs={{0,2},{2,4},{4,6},{6,0},{1,3},{3,5},{5,7},{7,1},{8,10},{10,12},{12... | collective-permute-start | bytes 786440 | tf_op jit(solution)/shard_map/ppermute | solution.py:96
  216.1 16.4 %collective-permute-start.44 = (f32[2,32,1024]{2,1,0:T(8,128)S(1)}, f32[2,32,1024]{2,1,0:T(8,128)S(1)}, u32[]{:S(2)}, u32[]{:S(2)}) collective-permute-start(f32[2,32,1024]{2,1,0:T(8,128)S(1)} %bitcast_add_fusion.34), channel_id=1, source_target_pairs={{0,2},{2,4},{4,6},{6,0},{1,3},{3,5},{5,7},{7,1},{8,10},{10,12},{12... | collective-permute-start | bytes 786440 | tf_op jit(solution)/shard_map/ppermute | solution.py:96
  221.3 14.3 %collective-permute-start.61 = (f32[2,32,1024]{2,1,0:T(8,128)S(1)}, f32[2,32,1024]{2,1,0:T(8,128)S(1)}, u32[]{:S(2)}, u32[]{:S(2)}) collective-permute-start(f32[2,32,1024]{2,1,0:T(8,128)S(1)} %bitcast_add_fusion.25), channel_id=1, source_target_pairs={{0,6},{2,0},{4,2},{6,4},{1,7},{3,1},{5,3},{7,5},{8,14},{10,8},{12,... | collective-permute-start | bytes 786440 | tf_op jit(solution)/shard_map/ppermute | solution.py:96
  221.7 14.5 %collective-permute-start.58 = (f32[2,32,1024]{2,1,0:T(8,128)S(1)}, f32[2,32,1024]{2,1,0:T(8,128)S(1)}, u32[]{:S(2)}, u32[]{:S(2)}) collective-permute-start(f32[2,32,1024]{2,1,0:T(8,128)S(1)} %bitcast_add_fusion.28), channel_id=1, source_target_pairs={{0,2},{2,4},{4,6},{6,0},{1,3},{3,5},{5,7},{7,1},{8,10},{10,12},{12... | collective-permute-start | bytes 786440 | tf_op jit(solution)/shard_map/ppermute | solution.py:96
  226.9 12.5 %collective-permute-start.75 = (f32[2,32,1024]{2,1,0:T(8,128)S(1)}, f32[2,32,1024]{2,1,0:T(8,128)S(1)}, u32[]{:S(2)}, u32[]{:S(2)}) collective-permute-start(f32[2,32,1024]{2,1,0:T(8,128)S(1)} %bitcast_add_fusion.19), channel_id=1, source_target_pairs={{0,6},{2,0},{4,2},{6,4},{1,7},{3,1},{5,3},{7,5},{8,14},{10,8},{12,... | collective-permute-start | bytes 786440 | tf_op jit(solution)/shard_map/ppermute | solution.py:96
  232.5 13.6 %collective-permute-start.34 = (f32[2,32,1024]{2,1,0:T(8,128)S(1)}, f32[2,32,1024]{2,1,0:T(8,128)S(1)}, u32[]{:S(2)}, u32[]{:S(2)}) collective-permute-start(f32[2,32,1024]{2,1,0:T(8,128)S(1)} %fusion.86), channel_id=1, source_target_pairs={{0,1},{1,0},{2,3},{3,2},{4,5},{5,4},{6,7},{7,6},{8,9},{9,8},{10,11... | collective-permute-start | bytes 786440 | tf_op jit(solution)/shard_map/ppermute | solution.py:106
  235.6 18.9 %collective-permute-start.48 = (f32[2,32,1024]{2,1,0:T(8,128)S(1)}, f32[2,32,1024]{2,1,0:T(8,128)S(1)}, u32[]{:S(2)}, u32[]{:S(2)}) collective-permute-start(f32[2,32,1024]{2,1,0:T(8,128)S(1)} %fusion.81), channel_id=1, source_target_pairs={{0,1},{1,0},{2,3},{3,2},{4,5},{5,4},{6,7},{7,6},{8,9},{9,8},{10,11... | collective-permute-start | bytes 786440 | tf_op jit(solution)/shard_map/ppermute | solution.py:106
  236.3 26.7 %collective-permute-start.62 = (f32[2,32,1024]{2,1,0:T(8,128)S(1)}, f32[2,32,1024]{2,1,0:T(8,128)S(1)}, u32[]{:S(2)}, u32[]{:S(2)}) collective-permute-start(f32[2,32,1024]{2,1,0:T(8,128)S(1)} %fusion.76), channel_id=1, source_target_pairs={{0,1},{1,0},{2,3},{3,2},{4,5},{5,4},{6,7},{7,6},{8,9},{9,8},{10,11... | collective-permute-start | bytes 786440 | tf_op jit(solution)/shard_map/ppermute | solution.py:106
  239.5 31.9 %collective-permute-start.76 = (f32[2,32,1024]{2,1,0:T(8,128)S(1)}, f32[2,32,1024]{2,1,0:T(8,128)S(1)}, u32[]{:S(2)}, u32[]{:S(2)}) collective-permute-start(f32[2,32,1024]{2,1,0:T(8,128)S(1)} %fusion.71), channel_id=1, source_target_pairs={{0,1},{1,0},{2,3},{3,2},{4,5},{5,4},{6,7},{7,6},{8,9},{9,8},{10,11... | collective-permute-start | bytes 786440 | tf_op jit(solution)/shard_map/ppermute | solution.py:106
  246.1 31.4 %collective-permute-start.35 = (f32[2,32,1024]{2,1,0:T(8,128)S(1)}, f32[2,32,1024]{2,1,0:T(8,128)S(1)}, u32[]{:S(2)}, u32[]{:S(2)}) collective-permute-start(f32[2,32,1024]{2,1,0:T(8,128)S(1)} %fusion.89), channel_id=1, source_target_pairs={{0,1},{1,0},{2,3},{3,2},{4,5},{5,4},{6,7},{7,6},{8,9},{9,8},{10,11... | collective-permute-start | bytes 786440 | tf_op jit(solution)/shard_map/ppermute | solution.py:108
  254.6 28.2 %collective-permute-start.49 = (f32[2,32,1024]{2,1,0:T(8,128)S(1)}, f32[2,32,1024]{2,1,0:T(8,128)S(1)}, u32[]{:S(2)}, u32[]{:S(2)}) collective-permute-start(f32[2,32,1024]{2,1,0:T(8,128)S(1)} %fusion.84), channel_id=1, source_target_pairs={{0,1},{1,0},{2,3},{3,2},{4,5},{5,4},{6,7},{7,6},{8,9},{9,8},{10,11... | collective-permute-start | bytes 786440 | tf_op jit(solution)/shard_map/ppermute | solution.py:108
  263.0 22.6 %collective-permute-start.63 = (f32[2,32,1024]{2,1,0:T(8,128)S(1)}, f32[2,32,1024]{2,1,0:T(8,128)S(1)}, u32[]{:S(2)}, u32[]{:S(2)}) collective-permute-start(f32[2,32,1024]{2,1,0:T(8,128)S(1)} %fusion.79), channel_id=1, source_target_pairs={{0,1},{1,0},{2,3},{3,2},{4,5},{5,4},{6,7},{7,6},{8,9},{9,8},{10,11... | collective-permute-start | bytes 786440 | tf_op jit(solution)/shard_map/ppermute | solution.py:108
  271.4 17.0 %collective-permute-start.77 = (f32[2,32,1024]{2,1,0:T(8,128)S(1)}, f32[2,32,1024]{2,1,0:T(8,128)S(1)}, u32[]{:S(2)}, u32[]{:S(2)}) collective-permute-start(f32[2,32,1024]{2,1,0:T(8,128)S(1)} %fusion.74), channel_id=1, source_target_pairs={{0,1},{1,0},{2,3},{3,2},{4,5},{5,4},{6,7},{7,6},{8,9},{9,8},{10,11... | collective-permute-start | bytes 786440 | tf_op jit(solution)/shard_map/ppermute | solution.py:108
  278.5 13.6 %collective-permute-start.39 = (f32[2,32,1024]{2,1,0:T(8,128)S(1)}, f32[2,32,1024]{2,1,0:T(8,128)S(1)}, u32[]{:S(2)}, u32[]{:S(2)}) collective-permute-start(f32[2,32,1024]{2,1,0:T(8,128)S(1)} %get-tuple-element.175), channel_id=1, source_target_pairs={{0,6},{2,0},{4,2},{6,4},{1,7},{3,1},{5,3},{7,5},{8,14},{10,8},{12,... | collective-permute-start | bytes 786440 | tf_op jit(solution)/shard_map/ppermute | solution.py:116
  292.1 12.6 %collective-permute-start.78 = (f32[2,32,1024]{2,1,0:T(8,128)S(1)}, f32[2,32,1024]{2,1,0:T(8,128)S(1)}, u32[]{:S(2)}, u32[]{:S(2)}) collective-permute-start(f32[2,32,1024]{2,1,0:T(8,128)S(1)} %get-tuple-element.172), channel_id=1, source_target_pairs={{0,2},{2,4},{4,6},{6,0},{1,3},{3,5},{5,7},{7,1},{8,10},{10,12},{12... | collective-permute-start | bytes 786440 | tf_op jit(solution)/shard_map/ppermute | solution.py:116
  293.5 12.4 %collective-permute-start.81 = (f32[2,32,1024]{2,1,0:T(8,128)S(1)}, f32[2,32,1024]{2,1,0:T(8,128)S(1)}, u32[]{:S(2)}, u32[]{:S(2)}) collective-permute-start(f32[2,32,1024]{2,1,0:T(8,128)S(1)} %get-tuple-element.173), channel_id=1, source_target_pairs={{0,6},{2,0},{4,2},{6,4},{1,7},{3,1},{5,3},{7,5},{8,14},{10,8},{12,... | collective-permute-start | bytes 786440 | tf_op jit(solution)/shard_map/ppermute | solution.py:116
  295.6 14.8 %collective-permute-start.37 = (f32[2,32,1024]{2,1,0:T(8,128)S(1)}, f32[2,32,1024]{2,1,0:T(8,128)S(1)}, u32[]{:S(2)}, u32[]{:S(2)}) collective-permute-start(f32[2,32,1024]{2,1,0:T(8,128)S(1)} %collective-permute-done.36), channel_id=1, source_target_pairs={{0,2},{2,4},{4,6},{6,0},{1,3},{3,5},{5,7},{7,1},{8,10},{10,12},{12... | collective-permute-start | bytes 786440 | tf_op jit(solution)/shard_map/ppermute | solution.py:116
  299.1 12.4 %collective-permute-start.40 = (f32[2,32,1024]{2,1,0:T(8,128)S(1)}, f32[2,32,1024]{2,1,0:T(8,128)S(1)}, u32[]{:S(2)}, u32[]{:S(2)}) collective-permute-start(f32[2,32,1024]{2,1,0:T(8,128)S(1)} %collective-permute-done.39), channel_id=1, source_target_pairs={{0,6},{2,0},{4,2},{6,4},{1,7},{3,1},{5,3},{7,5},{8,14},{10,8},{12,... | collective-permute-start | bytes 786440 | tf_op jit(solution)/shard_map/ppermute | solution.py:116
  300.3 15.7 %collective-permute-start.51 = (f32[2,32,1024]{2,1,0:T(8,128)S(1)}, f32[2,32,1024]{2,1,0:T(8,128)S(1)}, u32[]{:S(2)}, u32[]{:S(2)}) collective-permute-start(f32[2,32,1024]{2,1,0:T(8,128)S(1)} %collective-permute-done.50), channel_id=1, source_target_pairs={{0,2},{2,4},{4,6},{6,0},{1,3},{3,5},{5,7},{7,1},{8,10},{10,12},{12... | collective-permute-start | bytes 786440 | tf_op jit(solution)/shard_map/ppermute | solution.py:116
  304.8 12.4 %collective-permute-start.54 = (f32[2,32,1024]{2,1,0:T(8,128)S(1)}, f32[2,32,1024]{2,1,0:T(8,128)S(1)}, u32[]{:S(2)}, u32[]{:S(2)}) collective-permute-start(f32[2,32,1024]{2,1,0:T(8,128)S(1)} %collective-permute-done.53), channel_id=1, source_target_pairs={{0,6},{2,0},{4,2},{6,4},{1,7},{3,1},{5,3},{7,5},{8,14},{10,8},{12,... | collective-permute-start | bytes 786440 | tf_op jit(solution)/shard_map/ppermute | solution.py:116
  305.9 15.7 %collective-permute-start.65 = (f32[2,32,1024]{2,1,0:T(8,128)S(1)}, f32[2,32,1024]{2,1,0:T(8,128)S(1)}, u32[]{:S(2)}, u32[]{:S(2)}) collective-permute-start(f32[2,32,1024]{2,1,0:T(8,128)S(1)} %collective-permute-done.64), channel_id=1, source_target_pairs={{0,2},{2,4},{4,6},{6,0},{1,3},{3,5},{5,7},{7,1},{8,10},{10,12},{12... | collective-permute-start | bytes 786440 | tf_op jit(solution)/shard_map/ppermute | solution.py:116
  311.6 15.7 %collective-permute-start.79 = (f32[2,32,1024]{2,1,0:T(8,128)S(1)}, f32[2,32,1024]{2,1,0:T(8,128)S(1)}, u32[]{:S(2)}, u32[]{:S(2)}) collective-permute-start(f32[2,32,1024]{2,1,0:T(8,128)S(1)} %collective-permute-done.78), channel_id=1, source_target_pairs={{0,2},{2,4},{4,6},{6,0},{1,3},{3,5},{5,7},{7,1},{8,10},{10,12},{12... | collective-permute-start | bytes 786440 | tf_op jit(solution)/shard_map/ppermute | solution.py:116
  317.2 34.8 %collective-permute-start.38 = (f32[2,32,1024]{2,1,0:T(8,128)S(1)}, f32[2,32,1024]{2,1,0:T(8,128)S(1)}, u32[]{:S(2)}, u32[]{:S(2)}) collective-permute-start(f32[2,32,1024]{2,1,0:T(8,128)S(1)} %collective-permute-done.37), channel_id=1, source_target_pairs={{0,2},{2,4},{4,6},{6,0},{1,3},{3,5},{5,7},{7,1},{8,10},{10,12},{12... | collective-permute-start | bytes 786440 | tf_op jit(solution)/shard_map/ppermute | solution.py:116
  321.6 30.4 %collective-permute-start.41 = (f32[2,32,1024]{2,1,0:T(8,128)S(1)}, f32[2,32,1024]{2,1,0:T(8,128)S(1)}, u32[]{:S(2)}, u32[]{:S(2)}) collective-permute-start(f32[2,32,1024]{2,1,0:T(8,128)S(1)} %collective-permute-done.40), channel_id=1, source_target_pairs={{0,6},{2,0},{4,2},{6,4},{1,7},{3,1},{5,3},{7,5},{8,14},{10,8},{12,... | collective-permute-start | bytes 786440 | tf_op jit(solution)/shard_map/ppermute | solution.py:116
  322.6 29.7 %collective-permute-start.52 = (f32[2,32,1024]{2,1,0:T(8,128)S(1)}, f32[2,32,1024]{2,1,0:T(8,128)S(1)}, u32[]{:S(2)}, u32[]{:S(2)}) collective-permute-start(f32[2,32,1024]{2,1,0:T(8,128)S(1)} %collective-permute-done.51), channel_id=1, source_target_pairs={{0,2},{2,4},{4,6},{6,0},{1,3},{3,5},{5,7},{7,1},{8,10},{10,12},{12... | collective-permute-start | bytes 786440 | tf_op jit(solution)/shard_map/ppermute | solution.py:116
  327.2 12.8 %collective-permute-start.66 = (f32[2,32,1024]{2,1,0:T(8,128)S(1)}, f32[2,32,1024]{2,1,0:T(8,128)S(1)}, u32[]{:S(2)}, u32[]{:S(2)}) collective-permute-start(f32[2,32,1024]{2,1,0:T(8,128)S(1)} %collective-permute-done.65), channel_id=1, source_target_pairs={{0,2},{2,4},{4,6},{6,0},{1,3},{3,5},{5,7},{7,1},{8,10},{10,12},{12... | collective-permute-start | bytes 786440 | tf_op jit(solution)/shard_map/ppermute | solution.py:116
  434.2 14.3 %collective-permute-start.104 = (f32[2,32,1024]{2,1,0:T(8,128)S(1)}, f32[2,32,1024]{2,1,0:T(8,128)S(1)}, u32[]{:S(2)}, u32[]{:S(2)}) collective-permute-start(f32[2,32,1024]{2,1,0:T(8,128)S(1)} %fusion.61), channel_id=1, source_target_pairs={{0,1},{1,0},{2,3},{3,2},{4,5},{5,4},{6,7},{7,6},{8,9},{9,8},{10,11... | collective-permute-start | bytes 786440 | tf_op jit(solution)/shard_map/ppermute | solution.py:106
  434.9 13.5 %collective-permute-start.119 = (f32[2,16,1024]{2,1,0:T(8,128)S(1)}, f32[2,16,1024]{2,1,0:T(8,128)S(1)}, u32[]{:S(2)}, u32[]{:S(2)}) collective-permute-start(f32[2,16,1024]{2,1,0:T(8,128)S(1)} %dynamic-slice_bitcast_fusion.18), channel_id=1, source_target_pairs={{0,64},{64,0},{1,65},{65,1},{2,66},{66,2},{3,67},{67,3},{4,68},{68... | collective-permute-start | bytes 393224 | tf_op jit(solution)/shard_map/ppermute | solution.py:150
  441.6 15.1 %collective-permute-start.91 = (f32[2,32,1024]{2,1,0:T(8,128)S(1)}, f32[2,32,1024]{2,1,0:T(8,128)S(1)}, u32[]{:S(2)}, u32[]{:S(2)}) collective-permute-start(f32[2,32,1024]{2,1,0:T(8,128)S(1)} %fusion.69), channel_id=1, source_target_pairs={{0,1},{1,0},{2,3},{3,2},{4,5},{5,4},{6,7},{7,6},{8,9},{9,8},{10,11... | collective-permute-start | bytes 786440 | tf_op jit(solution)/shard_map/ppermute | solution.py:108
  457.1 13.3 %collective-permute-start.95 = (f32[2,32,1024]{2,1,0:T(8,128)S(1)}, f32[2,32,1024]{2,1,0:T(8,128)S(1)}, u32[]{:S(2)}, u32[]{:S(2)}) collective-permute-start(f32[2,32,1024]{2,1,0:T(8,128)S(1)} %get-tuple-element.164), channel_id=1, source_target_pairs={{0,6},{2,0},{4,2},{6,4},{1,7},{3,1},{5,3},{7,5},{8,14},{10,8},{12,... | collective-permute-start | bytes 786440 | tf_op jit(solution)/shard_map/ppermute | solution.py:116
  460.9 13.0 %collective-permute-start.109 = (f32[2,32,1024]{2,1,0:T(8,128)S(1)}, f32[2,32,1024]{2,1,0:T(8,128)S(1)}, u32[]{:S(2)}, u32[]{:S(2)}) collective-permute-start(f32[2,32,1024]{2,1,0:T(8,128)S(1)} %get-tuple-element.166), channel_id=1, source_target_pairs={{0,6},{2,0},{4,2},{6,4},{1,7},{3,1},{5,3},{7,5},{8,14},{10,8},{12,... | collective-permute-start | bytes 786440 | tf_op jit(solution)/shard_map/ppermute | solution.py:116
  477.6 21.6 %collective-permute-start.123 = (f32[64,1024]{1,0:T(8,128)S(1)}, f32[64,1024]{1,0:T(8,128)S(1)}, u32[]{:S(2)}, u32[]{:S(2)}) collective-permute-start(f32[64,1024]{1,0:T(8,128)S(1)} %collective-permute-done.122), channel_id=1, source_target_pairs={{0,16},{16,32},{32,48},{48,0},{1,17},{17,33},{33,49},{49,1},{2,18}... | collective-permute-start | bytes 786440 | tf_op jit(solution)/shard_map/ppermute | solution.py:162
  481.0 19.9 %collective-permute-start.126 = (f32[64,1024]{1,0:T(8,128)S(1)}, f32[64,1024]{1,0:T(8,128)S(1)}, u32[]{:S(2)}, u32[]{:S(2)}) collective-permute-start(f32[64,1024]{1,0:T(8,128)S(1)} %collective-permute-done.125), channel_id=1, source_target_pairs={{0,48},{16,0},{32,16},{48,32},{1,49},{17,1},{33,17},{49,33},{2,50}... | collective-permute-start | bytes 786440 | tf_op jit(solution)/shard_map/ppermute | solution.py:162
  (176 other events, 1401.5 us)
Sparse Core Ops, SparseCore 0:
  182.6 160.5 all-reduce.4

commit v7 on v3

--- a/solution.py
+++ b/solution.py
@@ -329,7 +329,7 @@
     value_w_grad = flat[:, q_cols + k_cols :]
     out_pack = packed[flat_rows : flat_rows + out_pack.shape[0]]
     down_grad, gate_w_grad, up_w_grad = ffn_w_grads
-    normed_one_grad = split_tensor_sum(one_partial)
+    normed_one_grad = tensor_sum(one_partial)
     input_grad = residual_grad + rms_back(normed_one_grad, tokens_wide, scale_one, attn_gain)
     out_w_grad = out_pack[:out_rows]
     ffn_grad = out_pack[out_rows]

time: 550 us -> 571 us (1.038)
  waiting for transfers between devices: 187 us -> 210 us
  starting transfers between devices: 178 us -> 164 us
  local copies, waits for them, and re-layouts: 48.2 us -> 55.2 us
    ppermute x48 -> x42, waiting for transfers between devices: 40.9 us -> 54.7 us  [tensor_sum(): acc = lax.ppermute(acc, 'ty', ring(ny, shift))]
    ppermute x6, waiting for transfers between devices: 7.64 us -> 15.2 us  [ring_sum(): acc = lax.ppermute(acc, ring_axis, ring(size, shift))]
    ppermute x48 -> x42, starting transfers between devices: 55.3 us -> 48.1 us  [tensor_sum(): cur = lax.ppermute(cur, 'ty', ring(ny, shift))]
    ppermute x2, waiting for transfers between devices: 6.66 us -> 0.01 us  [ring_sum(): acc = keep + lax.ppermute(send, axis, [(0, 1), (1, 0)])]
    ppermute x48 -> x42, starting transfers between devices: 64.6 us -> 58.6 us  [tensor_sum(): acc = lax.ppermute(acc, 'ty', ring(ny, shift))]
    ppermute x8 -> x7, waiting for transfers between devices: 29.7 us -> 34.1 us  [tensor_sum(): got = lax.ppermute(send, 'tx', pairs)]
    ppermute x8 -> x7, waiting for transfers between devices: 10.5 us -> 14.6 us  [tensor_sum(): other = lax.ppermute(mine, 'tx', pairs)]
    add x32 -> x28, other arithmetic: 11.6 us -> 15.4 us  [tensor_sum(): acc + lax.dynamic_index_in_dim(chunks, (y - shift * (1 + step)) % ny, 0,...]
  transfers between devices with their start and end apart: 132 -> 118, of which waited for: 78 -> 71; matrix products, arithmetic and copies ran while one was open for 16% -> 17% of each run, Pallas kernels for 0% -> 0%
where the time goes in v7:
time: 571 us; the launch traced here: 560 us
  waiting for transfers between devices  210 us (37%)
  starting transfers between devices  164 us (29%)
  other arithmetic  63.1 us (11%)
  local copies, waits for them, and re-layouts  55.2 us (10%)
  matrix products  50.5 us (9%)
  between operations  17.3 us (3%)
    ppermute x42, waiting for transfers between devices, tensor_sum(): cur = lax.ppermute(cur, 'ty', ring(ny, shift))  75.4 us
    ppermute x42, starting transfers between devices, tensor_sum(): acc = lax.ppermute(acc, 'ty', ring(ny, shift))  58.6 us
    ppermute x42, waiting for transfers between devices, tensor_sum(): acc = lax.ppermute(acc, 'ty', ring(ny, shift))  54.7 us
    ppermute x42, starting transfers between devices, tensor_sum(): cur = lax.ppermute(cur, 'ty', ring(ny, shift))  48.1 us
    ppermute x7, waiting for transfers between devices, tensor_sum(): got = lax.ppermute(send, 'tx', pairs)  34.1 us
    unnamed x187, local copies, waits for them, and re-layouts  19.6 us
    ppermute x7, starting transfers between devices, tensor_sum(): other = lax.ppermute(mine, 'tx', pairs)  18.3 us
    dot_general x7, matrix products, inner(): lax.dot_general(first_op, second_op, (((1,), (1,)), ((), ())), preferred_...  16.5 us
  transfers between devices with their start and end apart: 118, of which 71 were waited for; matrix products, arithmetic and copies ran while one was open for 17% of the time, Pallas kernels for 0%

profile of v7, /device:TPU:0, one launch (start us, length us, event | category | flops | bytes accessed | tf_op | source)
XLA Modules:
  0.0 560.3 jit_solution(5703001485551822042)
XLA Ops:
  46.7 3.4 collective-permute-start.17
  53.0 3.3 collective-permute-start.4
  68.2 3.8 collective-permute-start.19
  74.9 4.0 collective-permute-done.2
  91.2 3.7 collective-permute-done.20
  112.3 3.3 collective-permute-start.12
  117.9 3.3 collective-permute-start.26
  123.5 3.3 collective-permute-start.13
  129.2 3.7 collective-permute-start.27
  133.3 3.4 collective-permute-done.24
  146.5 3.9 fusion.122
  170.0 4.8 convolution_add_fusion
  205.7 3.4 collective-permute-done.43
  211.3 3.4 collective-permute-done.57
  216.9 3.4 collective-permute-done.71
  222.5 3.4 collective-permute-done.30
  240.4 4.8 collective-permute-done.34
  248.3 5.3 collective-permute-done.48
  256.8 5.3 collective-permute-done.62
  265.2 5.3 collective-permute-done.76
  272.8 3.9 collective-permute-done.35
  287.9 3.3 collective-permute-start.67
  294.8 3.5 collective-permute-done.64
  300.4 3.5 collective-permute-done.78
  306.1 3.5 collective-permute-done.37
  311.7 3.5 collective-permute-done.51
  317.3 3.5 collective-permute-done.65
  322.9 3.5 collective-permute-done.79
  330.1 9.0 %collective-permute-done.66 = f32[2,32,1024]{2,1,0:T(8,128)S(1)} collective-permute-done((f32[2,32,1024]{2,1,0:T(8,128)S(1)}, f32[2,32,1024]{2,1,0:T(8,128)S(1)}, u32[]{:S(2)}, u32[]{:S(2)}) %collective-permute-start.66) | collective-permute-done | bytes 262176 | tf_op jit(solution)/shard_map/ppermute | solution.py:116
  339.2 3.3 collective-permute-start.83
  342.8 4.0 collective-permute-done.80
  353.3 4.8 multiply_add_fusion
  393.7 5.3 collective-permute-done.101
  405.8 3.4 collective-permute-done.102
  409.2 3.8 collective-permute-start.103
  416.9 4.1 collective-permute-done.100
  427.1 9.7 %collective-permute-done.84 = f32[2,64,1024]{2,1,0:T(8,128)S(1)} collective-permute-done((f32[2,64,1024]{2,1,0:T(8,128)S(1)}, f32[2,64,1024]{2,1,0:T(8,128)S(1)}, u32[]{:S(2)}, u32[]{:S(2)}) %collective-permute-start.84) | collective-permute-done | bytes 524320 | tf_op jit(solution)/shard_map/ppermute | solution.py:96
  438.7 4.2 collective-permute-done.106
  447.4 5.3 collective-permute-done.85
  460.4 7.4 %collective-permute-done.86 = f32[2,64,1024]{2,1,0:T(8,128)S(1)} collective-permute-done((f32[2,64,1024]{2,1,0:T(8,128)S(1)}, f32[2,64,1024]{2,1,0:T(8,128)S(1)}, u32[]{:S(2)}, u32[]{:S(2)}) %collective-permute-start.86) | collective-permute-done | bytes 524320 | tf_op jit(solution)/shard_map/ppermute | solution.py:96
  472.0 9.2 %collective-permute-done.90 = f32[2,64,1024]{2,1,0:T(8,128)S(1)} collective-permute-done((f32[2,64,1024]{2,1,0:T(8,128)S(1)}, f32[2,64,1024]{2,1,0:T(8,128)S(1)}, u32[]{:S(2)}, u32[]{:S(2)}) %collective-permute-start.90) | collective-permute-done | bytes 524320 | tf_op jit(solution)/shard_map/ppermute | solution.py:106
  481.7 3.3 collective-permute-start.113
  485.1 4.2 collective-permute-done.110
  489.6 4.0 collective-permute-done.91
  496.2 7.9 %collective-permute-done.115 = f32[2,1024]{1,0:T(2,128)S(1)} collective-permute-done((f32[2,1024]{1,0:T(2,128)S(1)}, f32[2,1024]{1,0:T(2,128)S(1)}, u32[]{:S(2)}, u32[]{:S(2)}) %collective-permute-start.115) | collective-permute-done | bytes 8224 | tf_op jit(solution)/shard_map/ppermute | solution.py:173
  519.2 6.0 %collective-permute-done.93 = f32[2,64,1024]{2,1,0:T(8,128)S(1)} collective-permute-done((f32[2,64,1024]{2,1,0:T(8,128)}, f32[2,64,1024]{2,1,0:T(8,128)S(1)}, u32[]{:S(2)}, u32[]{:S(2)}) %collective-permute-start.93) | collective-permute-done | bytes 524320 | tf_op jit(solution)/shard_map/ppermute | solution.py:116
  532.2 3.8 collective-permute-done.94
  536.0 3.8 collective-permute-done.97
  (656 shorter events, 330.5 us)
Async XLA Ops:
  7.2 379.9 %all-reduce.5.cloned.1.call-start = ((), (), s32[]{:S(2)}) async-start(), calls=%async_computation | async-start | bytes 14155776 | tf_op jit(solution)/shard_map/psum | solution.py:259
  68.2 13.9 %collective-permute-start.19 = (f32[2,32,1024]{2,1,0:T(8,128)S(1)}, f32[2,32,1024]{2,1,0:T(8,128)S(1)}, u32[]{:S(2)}, u32[]{:S(2)}) collective-permute-start(f32[2,32,1024]{2,1,0:T(8,128)S(1)} %bitcast_add_fusion.37), channel_id=1, source_target_pairs={{0,6},{2,0},{4,2},{6,4},{1,7},{3,1},{5,3},{7,5},{8,14},{10,8},{12,... | collective-permute-start | bytes 786440 | tf_op jit(solution)/shard_map/ppermute | solution.py:96
  159.2 22.4 %collective-permute-start.31 = (f32[2,32,1024]{2,1,0:T(8,128)}, f32[2,32,1024]{2,1,0:T(8,128)}, u32[]{:S(2)}, u32[]{:S(2)}) collective-permute-start(f32[2,32,1024]{2,1,0:T(8,128)} %dynamic-slice_bitcast_fusion.10), channel_id=1, source_target_pairs={{0,6},{2,0},{4,2},{6,4},{1,7},{3,1},{5,3},{7,5},{8,14},{10,8},{12,... | collective-permute-start | bytes 786440 | tf_op jit(solution)/shard_map/ppermute | solution.py:96
  162.3 20.6 %collective-permute-start.28 = (f32[2,32,1024]{2,1,0:T(8,128)}, f32[2,32,1024]{2,1,0:T(8,128)}, u32[]{:S(2)}, u32[]{:S(2)}) collective-permute-start(f32[2,32,1024]{2,1,0:T(8,128)} %dynamic-slice_bitcast_fusion.11), channel_id=1, source_target_pairs={{0,2},{2,4},{4,6},{6,0},{1,3},{3,5},{5,7},{7,1},{8,10},{10,12},{12... | collective-permute-start | bytes 786440 | tf_op jit(solution)/shard_map/ppermute | solution.py:96
  163.2 23.9 %collective-permute-start.45 = (f32[2,32,1024]{2,1,0:T(8,128)}, f32[2,32,1024]{2,1,0:T(8,128)}, u32[]{:S(2)}, u32[]{:S(2)}) collective-permute-start(f32[2,32,1024]{2,1,0:T(8,128)} %dynamic-slice_bitcast_fusion.8), channel_id=1, source_target_pairs={{0,6},{2,0},{4,2},{6,4},{1,7},{3,1},{5,3},{7,5},{8,14},{10,8},{12,... | collective-permute-start | bytes 786440 | tf_op jit(solution)/shard_map/ppermute | solution.py:96
  167.2 21.2 %collective-permute-start.42 = (f32[2,32,1024]{2,1,0:T(8,128)}, f32[2,32,1024]{2,1,0:T(8,128)}, u32[]{:S(2)}, u32[]{:S(2)}) collective-permute-start(f32[2,32,1024]{2,1,0:T(8,128)} %dynamic-slice_bitcast_fusion.9), channel_id=1, source_target_pairs={{0,2},{2,4},{4,6},{6,0},{1,3},{3,5},{5,7},{7,1},{8,10},{10,12},{12... | collective-permute-start | bytes 786440 | tf_op jit(solution)/shard_map/ppermute | solution.py:96
  176.1 16.5 %collective-permute-start.59 = (f32[2,32,1024]{2,1,0:T(8,128)}, f32[2,32,1024]{2,1,0:T(8,128)}, u32[]{:S(2)}, u32[]{:S(2)}) collective-permute-start(f32[2,32,1024]{2,1,0:T(8,128)} %dynamic-slice_bitcast_fusion.6), channel_id=1, source_target_pairs={{0,6},{2,0},{4,2},{6,4},{1,7},{3,1},{5,3},{7,5},{8,14},{10,8},{12,... | collective-permute-start | bytes 786440 | tf_op jit(solution)/shard_map/ppermute | solution.py:96
  182.9 14.2 %collective-permute-start.73 = (f32[2,32,1024]{2,1,0:T(8,128)}, f32[2,32,1024]{2,1,0:T(8,128)S(1)}, u32[]{:S(2)}, u32[]{:S(2)}) collective-permute-start(f32[2,32,1024]{2,1,0:T(8,128)} %dynamic-slice_bitcast_fusion.4), channel_id=1, source_target_pairs={{0,6},{2,0},{4,2},{6,4},{1,7},{3,1},{5,3},{7,5},{8,14},{10,8},{12,... | collective-permute-start | bytes 786440 | tf_op jit(solution)/shard_map/ppermute | solution.py:96
  200.6 14.1 %collective-permute-start.57 = (f32[2,32,1024]{2,1,0:T(8,128)S(1)}, f32[2,32,1024]{2,1,0:T(8,128)S(1)}, u32[]{:S(2)}, u32[]{:S(2)}) collective-permute-start(f32[2,32,1024]{2,1,0:T(8,128)S(1)} %bitcast_add_fusion.23), channel_id=1, source_target_pairs={{0,2},{2,4},{4,6},{6,0},{1,3},{3,5},{5,7},{7,1},{8,10},{10,12},{12... | collective-permute-start | bytes 786440 | tf_op jit(solution)/shard_map/ppermute | solution.py:96
  204.0 16.3 %collective-permute-start.71 = (f32[2,32,1024]{2,1,0:T(8,128)S(1)}, f32[2,32,1024]{2,1,0:T(8,128)S(1)}, u32[]{:S(2)}, u32[]{:S(2)}) collective-permute-start(f32[2,32,1024]{2,1,0:T(8,128)S(1)} %bitcast_add_fusion.17), channel_id=1, source_target_pairs={{0,2},{2,4},{4,6},{6,0},{1,3},{3,5},{5,7},{7,1},{8,10},{10,12},{12... | collective-permute-start | bytes 786440 | tf_op jit(solution)/shard_map/ppermute | solution.py:96
  209.6 16.4 %collective-permute-start.30 = (f32[2,32,1024]{2,1,0:T(8,128)S(1)}, f32[2,32,1024]{2,1,0:T(8,128)S(1)}, u32[]{:S(2)}, u32[]{:S(2)}) collective-permute-start(f32[2,32,1024]{2,1,0:T(8,128)S(1)} %bitcast_add_fusion.34), channel_id=1, source_target_pairs={{0,2},{2,4},{4,6},{6,0},{1,3},{3,5},{5,7},{7,1},{8,10},{10,12},{12... | collective-permute-start | bytes 786440 | tf_op jit(solution)/shard_map/ppermute | solution.py:96
  215.2 16.4 %collective-permute-start.44 = (f32[2,32,1024]{2,1,0:T(8,128)S(1)}, f32[2,32,1024]{2,1,0:T(8,128)S(1)}, u32[]{:S(2)}, u32[]{:S(2)}) collective-permute-start(f32[2,32,1024]{2,1,0:T(8,128)S(1)} %bitcast_add_fusion.28), channel_id=1, source_target_pairs={{0,2},{2,4},{4,6},{6,0},{1,3},{3,5},{5,7},{7,1},{8,10},{10,12},{12... | collective-permute-start | bytes 786440 | tf_op jit(solution)/shard_map/ppermute | solution.py:96
  220.3 14.3 %collective-permute-start.61 = (f32[2,32,1024]{2,1,0:T(8,128)S(1)}, f32[2,32,1024]{2,1,0:T(8,128)S(1)}, u32[]{:S(2)}, u32[]{:S(2)}) collective-permute-start(f32[2,32,1024]{2,1,0:T(8,128)S(1)} %bitcast_add_fusion.19), channel_id=1, source_target_pairs={{0,6},{2,0},{4,2},{6,4},{1,7},{3,1},{5,3},{7,5},{8,14},{10,8},{12,... | collective-permute-start | bytes 786440 | tf_op jit(solution)/shard_map/ppermute | solution.py:96
  220.8 14.5 %collective-permute-start.58 = (f32[2,32,1024]{2,1,0:T(8,128)S(1)}, f32[2,32,1024]{2,1,0:T(8,128)S(1)}, u32[]{:S(2)}, u32[]{:S(2)}) collective-permute-start(f32[2,32,1024]{2,1,0:T(8,128)S(1)} %bitcast_add_fusion.22), channel_id=1, source_target_pairs={{0,2},{2,4},{4,6},{6,0},{1,3},{3,5},{5,7},{7,1},{8,10},{10,12},{12... | collective-permute-start | bytes 786440 | tf_op jit(solution)/shard_map/ppermute | solution.py:96
  226.0 12.5 %collective-permute-start.75 = (f32[2,32,1024]{2,1,0:T(8,128)S(1)}, f32[2,32,1024]{2,1,0:T(8,128)S(1)}, u32[]{:S(2)}, u32[]{:S(2)}) collective-permute-start(f32[2,32,1024]{2,1,0:T(8,128)S(1)} %bitcast_add_fusion.13), channel_id=1, source_target_pairs={{0,6},{2,0},{4,2},{6,4},{1,7},{3,1},{5,3},{7,5},{8,14},{10,8},{12,... | collective-permute-start | bytes 786440 | tf_op jit(solution)/shard_map/ppermute | solution.py:96
  231.6 13.6 %collective-permute-start.34 = (f32[2,32,1024]{2,1,0:T(8,128)S(1)}, f32[2,32,1024]{2,1,0:T(8,128)S(1)}, u32[]{:S(2)}, u32[]{:S(2)}) collective-permute-start(f32[2,32,1024]{2,1,0:T(8,128)S(1)} %fusion.62), channel_id=1, source_target_pairs={{0,1},{1,0},{2,3},{3,2},{4,5},{5,4},{6,7},{7,6},{8,9},{9,8},{10,11... | collective-permute-start | bytes 786440 | tf_op jit(solution)/shard_map/ppermute | solution.py:106
  234.7 18.9 %collective-permute-start.48 = (f32[2,32,1024]{2,1,0:T(8,128)S(1)}, f32[2,32,1024]{2,1,0:T(8,128)S(1)}, u32[]{:S(2)}, u32[]{:S(2)}) collective-permute-start(f32[2,32,1024]{2,1,0:T(8,128)S(1)} %fusion.57), channel_id=1, source_target_pairs={{0,1},{1,0},{2,3},{3,2},{4,5},{5,4},{6,7},{7,6},{8,9},{9,8},{10,11... | collective-permute-start | bytes 786440 | tf_op jit(solution)/shard_map/ppermute | solution.py:106
  235.4 26.7 %collective-permute-start.62 = (f32[2,32,1024]{2,1,0:T(8,128)S(1)}, f32[2,32,1024]{2,1,0:T(8,128)S(1)}, u32[]{:S(2)}, u32[]{:S(2)}) collective-permute-start(f32[2,32,1024]{2,1,0:T(8,128)S(1)} %fusion.52), channel_id=1, source_target_pairs={{0,1},{1,0},{2,3},{3,2},{4,5},{5,4},{6,7},{7,6},{8,9},{9,8},{10,11... | collective-permute-start | bytes 786440 | tf_op jit(solution)/shard_map/ppermute | solution.py:106
  238.6 31.9 %collective-permute-start.76 = (f32[2,32,1024]{2,1,0:T(8,128)S(1)}, f32[2,32,1024]{2,1,0:T(8,128)S(1)}, u32[]{:S(2)}, u32[]{:S(2)}) collective-permute-start(f32[2,32,1024]{2,1,0:T(8,128)S(1)} %fusion.47), channel_id=1, source_target_pairs={{0,1},{1,0},{2,3},{3,2},{4,5},{5,4},{6,7},{7,6},{8,9},{9,8},{10,11... | collective-permute-start | bytes 786440 | tf_op jit(solution)/shard_map/ppermute | solution.py:106
  245.2 31.5 %collective-permute-start.35 = (f32[2,32,1024]{2,1,0:T(8,128)S(1)}, f32[2,32,1024]{2,1,0:T(8,128)S(1)}, u32[]{:S(2)}, u32[]{:S(2)}) collective-permute-start(f32[2,32,1024]{2,1,0:T(8,128)S(1)} %fusion.65), channel_id=1, source_target_pairs={{0,1},{1,0},{2,3},{3,2},{4,5},{5,4},{6,7},{7,6},{8,9},{9,8},{10,11... | collective-permute-start | bytes 786440 | tf_op jit(solution)/shard_map/ppermute | solution.py:108
  253.7 28.2 %collective-permute-start.49 = (f32[2,32,1024]{2,1,0:T(8,128)S(1)}, f32[2,32,1024]{2,1,0:T(8,128)S(1)}, u32[]{:S(2)}, u32[]{:S(2)}) collective-permute-start(f32[2,32,1024]{2,1,0:T(8,128)S(1)} %fusion.60), channel_id=1, source_target_pairs={{0,1},{1,0},{2,3},{3,2},{4,5},{5,4},{6,7},{7,6},{8,9},{9,8},{10,11... | collective-permute-start | bytes 786440 | tf_op jit(solution)/shard_map/ppermute | solution.py:108
  262.1 22.6 %collective-permute-start.63 = (f32[2,32,1024]{2,1,0:T(8,128)S(1)}, f32[2,32,1024]{2,1,0:T(8,128)S(1)}, u32[]{:S(2)}, u32[]{:S(2)}) collective-permute-start(f32[2,32,1024]{2,1,0:T(8,128)S(1)} %fusion.55), channel_id=1, source_target_pairs={{0,1},{1,0},{2,3},{3,2},{4,5},{5,4},{6,7},{7,6},{8,9},{9,8},{10,11... | collective-permute-start | bytes 786440 | tf_op jit(solution)/shard_map/ppermute | solution.py:108
  270.5 17.0 %collective-permute-start.77 = (f32[2,32,1024]{2,1,0:T(8,128)S(1)}, f32[2,32,1024]{2,1,0:T(8,128)S(1)}, u32[]{:S(2)}, u32[]{:S(2)}) collective-permute-start(f32[2,32,1024]{2,1,0:T(8,128)S(1)} %fusion.50), channel_id=1, source_target_pairs={{0,1},{1,0},{2,3},{3,2},{4,5},{5,4},{6,7},{7,6},{8,9},{9,8},{10,11... | collective-permute-start | bytes 786440 | tf_op jit(solution)/shard_map/ppermute | solution.py:108
  277.6 13.7 %collective-permute-start.39 = (f32[2,32,1024]{2,1,0:T(8,128)S(1)}, f32[2,32,1024]{2,1,0:T(8,128)S(1)}, u32[]{:S(2)}, u32[]{:S(2)}) collective-permute-start(f32[2,32,1024]{2,1,0:T(8,128)S(1)} %get-tuple-element.169), channel_id=1, source_target_pairs={{0,6},{2,0},{4,2},{6,4},{1,7},{3,1},{5,3},{7,5},{8,14},{10,8},{12,... | collective-permute-start | bytes 786440 | tf_op jit(solution)/shard_map/ppermute | solution.py:116
  291.3 12.6 %collective-permute-start.78 = (f32[2,32,1024]{2,1,0:T(8,128)S(1)}, f32[2,32,1024]{2,1,0:T(8,128)S(1)}, u32[]{:S(2)}, u32[]{:S(2)}) collective-permute-start(f32[2,32,1024]{2,1,0:T(8,128)S(1)} %get-tuple-element.166), channel_id=1, source_target_pairs={{0,2},{2,4},{4,6},{6,0},{1,3},{3,5},{5,7},{7,1},{8,10},{10,12},{12... | collective-permute-start | bytes 786440 | tf_op jit(solution)/shard_map/ppermute | solution.py:116
  292.7 12.4 %collective-permute-start.81 = (f32[2,32,1024]{2,1,0:T(8,128)S(1)}, f32[2,32,1024]{2,1,0:T(8,128)S(1)}, u32[]{:S(2)}, u32[]{:S(2)}) collective-permute-start(f32[2,32,1024]{2,1,0:T(8,128)S(1)} %get-tuple-element.167), channel_id=1, source_target_pairs={{0,6},{2,0},{4,2},{6,4},{1,7},{3,1},{5,3},{7,5},{8,14},{10,8},{12,... | collective-permute-start | bytes 786440 | tf_op jit(solution)/shard_map/ppermute | solution.py:116
  294.7 14.8 %collective-permute-start.37 = (f32[2,32,1024]{2,1,0:T(8,128)S(1)}, f32[2,32,1024]{2,1,0:T(8,128)S(1)}, u32[]{:S(2)}, u32[]{:S(2)}) collective-permute-start(f32[2,32,1024]{2,1,0:T(8,128)S(1)} %collective-permute-done.36), channel_id=1, source_target_pairs={{0,2},{2,4},{4,6},{6,0},{1,3},{3,5},{5,7},{7,1},{8,10},{10,12},{12... | collective-permute-start | bytes 786440 | tf_op jit(solution)/shard_map/ppermute | solution.py:116
  298.3 12.4 %collective-permute-start.40 = (f32[2,32,1024]{2,1,0:T(8,128)S(1)}, f32[2,32,1024]{2,1,0:T(8,128)S(1)}, u32[]{:S(2)}, u32[]{:S(2)}) collective-permute-start(f32[2,32,1024]{2,1,0:T(8,128)S(1)} %collective-permute-done.39), channel_id=1, source_target_pairs={{0,6},{2,0},{4,2},{6,4},{1,7},{3,1},{5,3},{7,5},{8,14},{10,8},{12,... | collective-permute-start | bytes 786440 | tf_op jit(solution)/shard_map/ppermute | solution.py:116
  299.5 15.7 %collective-permute-start.51 = (f32[2,32,1024]{2,1,0:T(8,128)S(1)}, f32[2,32,1024]{2,1,0:T(8,128)S(1)}, u32[]{:S(2)}, u32[]{:S(2)}) collective-permute-start(f32[2,32,1024]{2,1,0:T(8,128)S(1)} %collective-permute-done.50), channel_id=1, source_target_pairs={{0,2},{2,4},{4,6},{6,0},{1,3},{3,5},{5,7},{7,1},{8,10},{10,12},{12... | collective-permute-start | bytes 786440 | tf_op jit(solution)/shard_map/ppermute | solution.py:116
  305.1 15.7 %collective-permute-start.65 = (f32[2,32,1024]{2,1,0:T(8,128)S(1)}, f32[2,32,1024]{2,1,0:T(8,128)S(1)}, u32[]{:S(2)}, u32[]{:S(2)}) collective-permute-start(f32[2,32,1024]{2,1,0:T(8,128)S(1)} %collective-permute-done.64), channel_id=1, source_target_pairs={{0,2},{2,4},{4,6},{6,0},{1,3},{3,5},{5,7},{7,1},{8,10},{10,12},{12... | collective-permute-start | bytes 786440 | tf_op jit(solution)/shard_map/ppermute | solution.py:116
  310.7 15.7 %collective-permute-start.79 = (f32[2,32,1024]{2,1,0:T(8,128)S(1)}, f32[2,32,1024]{2,1,0:T(8,128)S(1)}, u32[]{:S(2)}, u32[]{:S(2)}) collective-permute-start(f32[2,32,1024]{2,1,0:T(8,128)S(1)} %collective-permute-done.78), channel_id=1, source_target_pairs={{0,2},{2,4},{4,6},{6,0},{1,3},{3,5},{5,7},{7,1},{8,10},{10,12},{12... | collective-permute-start | bytes 786440 | tf_op jit(solution)/shard_map/ppermute | solution.py:116
  316.3 34.8 %collective-permute-start.38 = (f32[2,32,1024]{2,1,0:T(8,128)S(1)}, f32[2,32,1024]{2,1,0:T(8,128)S(1)}, u32[]{:S(2)}, u32[]{:S(2)}) collective-permute-start(f32[2,32,1024]{2,1,0:T(8,128)S(1)} %collective-permute-done.37), channel_id=1, source_target_pairs={{0,2},{2,4},{4,6},{6,0},{1,3},{3,5},{5,7},{7,1},{8,10},{10,12},{12... | collective-permute-start | bytes 786440 | tf_op jit(solution)/shard_map/ppermute | solution.py:116
  320.8 30.4 %collective-permute-start.41 = (f32[2,32,1024]{2,1,0:T(8,128)S(1)}, f32[2,32,1024]{2,1,0:T(8,128)S(1)}, u32[]{:S(2)}, u32[]{:S(2)}) collective-permute-start(f32[2,32,1024]{2,1,0:T(8,128)S(1)} %collective-permute-done.40), channel_id=1, source_target_pairs={{0,6},{2,0},{4,2},{6,4},{1,7},{3,1},{5,3},{7,5},{8,14},{10,8},{12,... | collective-permute-start | bytes 786440 | tf_op jit(solution)/shard_map/ppermute | solution.py:116
  321.7 29.7 %collective-permute-start.52 = (f32[2,32,1024]{2,1,0:T(8,128)S(1)}, f32[2,32,1024]{2,1,0:T(8,128)S(1)}, u32[]{:S(2)}, u32[]{:S(2)}) collective-permute-start(f32[2,32,1024]{2,1,0:T(8,128)S(1)} %collective-permute-done.51), channel_id=1, source_target_pairs={{0,2},{2,4},{4,6},{6,0},{1,3},{3,5},{5,7},{7,1},{8,10},{10,12},{12... | collective-permute-start | bytes 786440 | tf_op jit(solution)/shard_map/ppermute | solution.py:116
  326.4 12.8 %collective-permute-start.66 = (f32[2,32,1024]{2,1,0:T(8,128)S(1)}, f32[2,32,1024]{2,1,0:T(8,128)S(1)}, u32[]{:S(2)}, u32[]{:S(2)}) collective-permute-start(f32[2,32,1024]{2,1,0:T(8,128)S(1)} %collective-permute-done.65), channel_id=1, source_target_pairs={{0,2},{2,4},{4,6},{6,0},{1,3},{3,5},{5,7},{7,1},{8,10},{10,12},{12... | collective-permute-start | bytes 786440 | tf_op jit(solution)/shard_map/ppermute | solution.py:116
  421.2 15.6 %collective-permute-start.84 = (f32[2,64,1024]{2,1,0:T(8,128)S(1)}, f32[2,64,1024]{2,1,0:T(8,128)S(1)}, u32[]{:S(2)}, u32[]{:S(2)}) collective-permute-start(f32[2,64,1024]{2,1,0:T(8,128)S(1)} %dynamic-slice_bitcast_fusion.1), channel_id=1, source_target_pairs={{0,2},{2,4},{4,6},{6,0},{1,3},{3,5},{5,7},{7,1},{8,10},{10,12},{12... | collective-permute-start | bytes 1572872 | tf_op jit(solution)/shard_map/ppermute | solution.py:96
  423.6 19.4 %collective-permute-start.88 = (f32[2,64,1024]{2,1,0:T(8,128)}, f32[2,64,1024]{2,1,0:T(8,128)}, u32[]{:S(2)}, u32[]{:S(2)}) collective-permute-start(f32[2,64,1024]{2,1,0:T(8,128)} %bitcast_add_fusion.2), channel_id=1, source_target_pairs={{0,6},{2,0},{4,2},{6,4},{1,7},{3,1},{5,3},{7,5},{8,14},{10,8},{12,... | collective-permute-start | bytes 1572872 | tf_op jit(solution)/shard_map/ppermute | solution.py:96
  437.7 15.1 %collective-permute-start.85 = (f32[2,64,1024]{2,1,0:T(8,128)}, f32[2,64,1024]{2,1,0:T(8,128)}, u32[]{:S(2)}, u32[]{:S(2)}) collective-permute-start(f32[2,64,1024]{2,1,0:T(8,128)} %bitcast_add_fusion.5), channel_id=1, source_target_pairs={{0,2},{2,4},{4,6},{6,0},{1,3},{3,5},{5,7},{7,1},{8,10},{10,12},{12... | collective-permute-start | bytes 1572872 | tf_op jit(solution)/shard_map/ppermute | solution.py:96
  444.3 15.0 %collective-permute-start.89 = (f32[2,64,1024]{2,1,0:T(8,128)S(1)}, f32[2,64,1024]{2,1,0:T(8,128)S(1)}, u32[]{:S(2)}, u32[]{:S(2)}) collective-permute-start(f32[2,64,1024]{2,1,0:T(8,128)S(1)} %bitcast_add_fusion.1), channel_id=1, source_target_pairs={{0,6},{2,0},{4,2},{6,4},{1,7},{3,1},{5,3},{7,5},{8,14},{10,8},{12,... | collective-permute-start | bytes 1572872 | tf_op jit(solution)/shard_map/ppermute | solution.py:96
  453.8 13.9 %collective-permute-start.86 = (f32[2,64,1024]{2,1,0:T(8,128)S(1)}, f32[2,64,1024]{2,1,0:T(8,128)S(1)}, u32[]{:S(2)}, u32[]{:S(2)}) collective-permute-start(f32[2,64,1024]{2,1,0:T(8,128)S(1)} %bitcast_add_fusion.4), channel_id=1, source_target_pairs={{0,2},{2,4},{4,6},{6,0},{1,3},{3,5},{5,7},{7,1},{8,10},{10,12},{12... | collective-permute-start | bytes 1572872 | tf_op jit(solution)/shard_map/ppermute | solution.py:96
  454.0 14.6 %collective-permute-start.108 = (f32[64,1024]{1,0:T(8,128)S(1)}, f32[64,1024]{1,0:T(8,128)S(1)}, u32[]{:S(2)}, u32[]{:S(2)}) collective-permute-start(f32[64,1024]{1,0:T(8,128)S(1)} %bitcast.735), channel_id=1, source_target_pairs={{0,16},{16,32},{32,48},{48,0},{1,17},{17,33},{33,49},{49,1},{2,18}... | collective-permute-start | bytes 786440 | tf_op jit(solution)/shard_map/ppermute | solution.py:162
  454.1 14.6 %collective-permute-start.111 = (f32[64,1024]{1,0:T(8,128)S(1)}, f32[64,1024]{1,0:T(8,128)S(1)}, u32[]{:S(2)}, u32[]{:S(2)}) collective-permute-start(f32[64,1024]{1,0:T(8,128)S(1)} %bitcast.733), channel_id=1, source_target_pairs={{0,48},{16,0},{32,16},{48,32},{1,49},{17,1},{33,17},{49,33},{2,50}... | collective-permute-start | bytes 786440 | tf_op jit(solution)/shard_map/ppermute | solution.py:162
  467.9 13.3 %collective-permute-start.90 = (f32[2,64,1024]{2,1,0:T(8,128)S(1)}, f32[2,64,1024]{2,1,0:T(8,128)S(1)}, u32[]{:S(2)}, u32[]{:S(2)}) collective-permute-start(f32[2,64,1024]{2,1,0:T(8,128)S(1)} %fusion.34), channel_id=1, source_target_pairs={{0,1},{1,0},{2,3},{3,2},{4,5},{5,4},{6,7},{7,6},{8,9},{9,8},{10,11... | collective-permute-start | bytes 1572872 | tf_op jit(solution)/shard_map/ppermute | solution.py:106
  468.6 13.1 %collective-permute-start.109 = (f32[64,1024]{1,0:T(8,128)S(1)}, f32[64,1024]{1,0:T(8,128)S(1)}, u32[]{:S(2)}, u32[]{:S(2)}) collective-permute-start(f32[64,1024]{1,0:T(8,128)S(1)} %collective-permute-done.108), channel_id=1, source_target_pairs={{0,16},{16,32},{32,48},{48,0},{1,17},{17,33},{33,49},{49,1},{2,18}... | collective-permute-start | bytes 786440 | tf_op jit(solution)/shard_map/ppermute | solution.py:162
  468.7 13.0 %collective-permute-start.112 = (f32[64,1024]{1,0:T(8,128)S(1)}, f32[64,1024]{1,0:T(8,128)S(1)}, u32[]{:S(2)}, u32[]{:S(2)}) collective-permute-start(f32[64,1024]{1,0:T(8,128)S(1)} %collective-permute-done.111), channel_id=1, source_target_pairs={{0,48},{16,0},{32,16},{48,32},{1,49},{17,1},{33,17},{49,33},{2,50}... | collective-permute-start | bytes 786440 | tf_op jit(solution)/shard_map/ppermute | solution.py:162
  494.8 17.3 %collective-permute-start.92 = (f32[2,64,1024]{2,1,0:T(8,128)}, f32[2,64,1024]{2,1,0:T(8,128)}, u32[]{:S(2)}, u32[]{:S(2)}) collective-permute-start(f32[2,64,1024]{2,1,0:T(8,128)} %get-tuple-element.157), channel_id=1, source_target_pairs={{0,2},{2,4},{4,6},{6,0},{1,3},{3,5},{5,7},{7,1},{8,10},{10,12},{12... | collective-permute-start | bytes 1572872 | tf_op jit(solution)/shard_map/ppermute | solution.py:116
  512.1 13.2 %collective-permute-start.93 = (f32[2,64,1024]{2,1,0:T(8,128)}, f32[2,64,1024]{2,1,0:T(8,128)S(1)}, u32[]{:S(2)}, u32[]{:S(2)}) collective-permute-start(f32[2,64,1024]{2,1,0:T(8,128)} %collective-permute-done.92), channel_id=1, source_target_pairs={{0,2},{2,4},{4,6},{6,0},{1,3},{3,5},{5,7},{7,1},{8,10},{10,12},{12... | collective-permute-start | bytes 1572872 | tf_op jit(solution)/shard_map/ppermute | solution.py:116
  517.3 13.4 %collective-permute-start.96 = (f32[2,64,1024]{2,1,0:T(8,128)}, f32[2,64,1024]{2,1,0:T(8,128)S(1)}, u32[]{:S(2)}, u32[]{:S(2)}) collective-permute-start(f32[2,64,1024]{2,1,0:T(8,128)} %collective-permute-done.95), channel_id=1, source_target_pairs={{0,6},{2,0},{4,2},{6,4},{1,7},{3,1},{5,3},{7,5},{8,14},{10,8},{12,... | collective-permute-start | bytes 1572872 | tf_op jit(solution)/shard_map/ppermute | solution.py:116
  (161 other events, 1249.4 us)
Sparse Core Ops, SparseCore 0:
  181.7 160.6 all-reduce.4

commit v8 on v3

--- a/solution.py
+++ b/solution.py
@@ -243,7 +243,7 @@
     up_proj = jnp.dot(normed_two, w_up, preferred_element_type=jnp.float32)
     gate_sigmoid = jax.nn.sigmoid(gate_proj)
     hidden = (gate_proj * gate_sigmoid * up_proj).astype(jnp.bfloat16)
-    mlp_sum = split_tensor_sum(jnp.dot(hidden, w_down, preferred_element_type=jnp.float32))
+    mlp_sum = tensor_sum(jnp.dot(hidden, w_down, preferred_element_type=jnp.float32))
     output = (residual + mlp_sum).astype(jnp.bfloat16)
     down_grad = outer(hidden, cotangent)
     hidden_grad = inner(cotangent, w_down)

time: 550 us -> 527 us (0.958)
  waiting for transfers between devices: 187 us -> 167 us
    ppermute x8 -> x7, waiting for transfers between devices: 29.7 us -> 19.9 us  [tensor_sum(): got = lax.ppermute(send, 'tx', pairs)]
    ppermute x48 -> x42, waiting for transfers between devices: 40.9 us -> 31.5 us  [tensor_sum(): acc = lax.ppermute(acc, 'ty', ring(ny, shift))]
    ppermute x6, waiting for transfers between devices: 7.64 us -> 1.36 us  [ring_sum(): acc = lax.ppermute(acc, ring_axis, ring(size, shift))]
    ppermute x8 -> x7, waiting for transfers between devices: 10.5 us -> 16.2 us  [tensor_sum(): other = lax.ppermute(mine, 'tx', pairs)]
    ppermute x8 -> x7, starting transfers between devices: 21.5 us -> 16.7 us  [tensor_sum(): other = lax.ppermute(mine, 'tx', pairs)]
    ppermute x48 -> x42, starting transfers between devices: 55.3 us -> 59.9 us  [tensor_sum(): cur = lax.ppermute(cur, 'ty', ring(ny, shift))]
    ppermute x48 -> x42, starting transfers between devices: 64.6 us -> 61.5 us  [tensor_sum(): acc = lax.ppermute(acc, 'ty', ring(ny, shift))]
    ppermute x48 -> x42, waiting for transfers between devices: 78.8 us -> 76.6 us  [tensor_sum(): cur = lax.ppermute(cur, 'ty', ring(ny, shift))]
  transfers between devices with their start and end apart: 132 -> 118, of which waited for: 78 -> 62; matrix products, arithmetic and copies ran while one was open for 16% -> 17% of each run, Pallas kernels for 0% -> 0%
where the time goes in v8:
time: 527 us; the launch traced here: 517 us
  starting transfers between devices  175 us (33%)
  waiting for transfers between devices  167 us (32%)
  other arithmetic  57.7 us (11%)
  matrix products  50.2 us (10%)
  local copies, waits for them, and re-layouts  49.7 us (9%)
  between operations  17.2 us (3%)
    ppermute x42, waiting for transfers between devices, tensor_sum(): cur = lax.ppermute(cur, 'ty', ring(ny, shift))  76.6 us
    ppermute x42, starting transfers between devices, tensor_sum(): acc = lax.ppermute(acc, 'ty', ring(ny, shift))  61.5 us
    ppermute x42, starting transfers between devices, tensor_sum(): cur = lax.ppermute(cur, 'ty', ring(ny, shift))  59.9 us
    ppermute x42, waiting for transfers between devices, tensor_sum(): acc = lax.ppermute(acc, 'ty', ring(ny, shift))  31.5 us
    ppermute x7, waiting for transfers between devices, tensor_sum(): got = lax.ppermute(send, 'tx', pairs)  19.9 us
    unnamed x179, local copies, waits for them, and re-layouts  18.9 us
    ppermute x7, starting transfers between devices, tensor_sum(): other = lax.ppermute(mine, 'tx', pairs)  16.7 us
    ppermute x7, waiting for transfers between devices, tensor_sum(): other = lax.ppermute(mine, 'tx', pairs)  16.2 us
  transfers between devices with their start and end apart: 118, of which 62 were waited for; matrix products, arithmetic and copies ran while one was open for 17% of the time, Pallas kernels for 0%

profile of v8, /device:TPU:0, one launch (start us, length us, event | category | flops | bytes accessed | tf_op | source)
XLA Modules:
  0.0 517.0 jit_solution(14015090294944251337)
XLA Ops:
  46.8 3.4 collective-permute-start.17
  53.1 3.3 collective-permute-start.4
  58.7 3.3 collective-permute-start.18
  64.0 3.3 collective-permute-start.5
  68.3 3.8 collective-permute-start.19
  75.1 4.0 collective-permute-done.2
  91.3 3.7 collective-permute-done.20
  102.0 3.2 collective-permute-start.11
  106.0 3.3 collective-permute-start.25
  112.5 3.3 collective-permute-start.12
  118.1 3.3 collective-permute-start.26
  123.7 3.3 collective-permute-start.13
  129.3 3.7 collective-permute-start.27
  133.4 3.5 collective-permute-done.24
  146.7 3.9 fusion.122
  165.8 4.4 convolution_add_fusion
  176.2 3.2 collective-permute-start.59
  215.4 3.2 collective-permute-start.62
  219.8 3.4 collective-permute-done.48
  226.4 3.7 collective-permute-done.62
  236.4 3.5 collective-permute-start.53
  241.6 12.9 %collective-permute-done.50 = f32[2,32,1024]{2,1,0:T(8,128)S(1)} collective-permute-done((f32[2,32,1024]{2,1,0:T(8,128)S(1)}, f32[2,32,1024]{2,1,0:T(8,128)S(1)}, u32[]{:S(2)}, u32[]{:S(2)}) %collective-permute-start.50) | collective-permute-done | bytes 262176 | tf_op jit(solution)/shard_map/ppermute | solution.py:116
  256.7 3.5 collective-permute-done.64
  263.1 3.3 collective-permute-start.68
  267.3 3.3 collective-permute-start.55
  270.7 3.2 collective-permute-start.69
  274.0 4.7 collective-permute-done.34
  280.2 13.7 %collective-permute-done.35 = f32[2,64,1024]{2,1,0:T(8,128)S(1)} collective-permute-done((f32[2,64,1024]{2,1,0:T(8,128)S(1)}, f32[2,64,1024]{2,1,0:T(8,128)S(1)}, u32[]{:S(2)}, u32[]{:S(2)}) %collective-permute-start.35) | collective-permute-done | bytes 524320 | tf_op jit(solution)/shard_map/ppermute | solution.py:108
  294.2 3.2 collective-permute-start.39
  300.2 8.9 %collective-permute-done.36 = f32[2,64,1024]{2,1,0:T(8,128)S(1)} collective-permute-done((f32[2,64,1024]{2,1,0:T(8,128)S(1)}, f32[2,64,1024]{2,1,0:T(8,128)S(1)}, u32[]{:S(2)}, u32[]{:S(2)}) %collective-permute-start.36) | collective-permute-done | bytes 524320 | tf_op jit(solution)/shard_map/ppermute | solution.py:116
  309.4 3.4 collective-permute-start.40
  313.2 6.3 %collective-permute-done.37 = f32[2,64,1024]{2,1,0:T(8,128)S(1)} collective-permute-done((f32[2,64,1024]{2,1,0:T(8,128)S(1)}, f32[2,64,1024]{2,1,0:T(8,128)S(1)}, u32[]{:S(2)}, u32[]{:S(2)}) %collective-permute-start.37) | collective-permute-done | bytes 524320 | tf_op jit(solution)/shard_map/ppermute | solution.py:116
  319.6 4.0 collective-permute-start.41
  323.7 6.2 %collective-permute-done.38 = f32[2,64,1024]{2,1,0:T(8,128)S(1)} collective-permute-done((f32[2,64,1024]{2,1,0:T(8,128)S(1)}, f32[2,64,1024]{2,1,0:T(8,128)S(1)}, u32[]{:S(2)}, u32[]{:S(2)}) %collective-permute-start.38) | collective-permute-done | bytes 524320 | tf_op jit(solution)/shard_map/ppermute | solution.py:116
  330.7 4.5 multiply_add_fusion
  353.8 3.3 fusion.17
  369.2 3.2 collective-permute-start.101
  372.5 3.8 collective-permute-start.73
  376.4 3.3 collective-permute-start.87
  401.5 3.3 collective-permute-done.72
  411.8 3.8 collective-permute-done.76
  416.7 6.9 %collective-permute-done.105 = f32[2,16,1024]{2,1,0:T(8,128)S(1)} collective-permute-done((f32[2,16,1024]{2,1,0:T(8,128)S(1)}, f32[2,16,1024]{2,1,0:T(8,128)S(1)}, u32[]{:S(2)}, u32[]{:S(2)}) %collective-permute-start.105) | collective-permute-done | bytes 131104 | tf_op jit(solution)/shard_map/ppermute | solution.py:150
  426.3 4.7 collective-permute-done.106
  431.5 3.2 collective-permute-start.81
  451.7 3.3 collective-permute-done.79
  461.8 3.5 collective-permute-done.80
  476.4 4.2 collective-permute-done.110
  481.9 3.6 collective-permute-done.114
  (647 shorter events, 294.9 us)
Async XLA Ops:
  7.2 356.8 %all-reduce.5.cloned.1.call-start = ((), (), s32[]{:S(2)}) async-start(), calls=%async_computation | async-start | bytes 14155776 | tf_op jit(solution)/shard_map/psum | solution.py:259
  40.4 11.6 %collective-permute-start.3 = (f32[2,32,1024]{2,1,0:T(8,128)}, f32[2,32,1024]{2,1,0:T(8,128)}, u32[]{:S(2)}, u32[]{:S(2)}) collective-permute-start(f32[2,32,1024]{2,1,0:T(8,128)} %dynamic-slice_bitcast_fusion.14), channel_id=1, source_target_pairs={{0,6},{2,0},{4,2},{6,4},{1,7},{3,1},{5,3},{7,5},{8,14},{10,8},{12,... | collective-permute-start | bytes 786440 | tf_op jit(solution)/shard_map/ppermute | solution.py:96
  45.1 11.3 %collective-permute-start = (f32[2,32,1024]{2,1,0:T(8,128)}, f32[2,32,1024]{2,1,0:T(8,128)}, u32[]{:S(2)}, u32[]{:S(2)}) collective-permute-start(f32[2,32,1024]{2,1,0:T(8,128)} %dynamic-slice_bitcast_fusion.15), channel_id=1, source_target_pairs={{0,2},{2,4},{4,6},{6,0},{1,3},{3,5},{5,7},{7,1},{8,10},{10,12},{12... | collective-permute-start | bytes 786440 | tf_op jit(solution)/shard_map/ppermute | solution.py:96
  46.8 10.8 %collective-permute-start.17 = (f32[2,32,1024]{2,1,0:T(8,128)}, f32[2,32,1024]{2,1,0:T(8,128)}, u32[]{:S(2)}, u32[]{:S(2)}) collective-permute-start(f32[2,32,1024]{2,1,0:T(8,128)} %dynamic-slice_bitcast_fusion.12), channel_id=1, source_target_pairs={{0,6},{2,0},{4,2},{6,4},{1,7},{3,1},{5,3},{7,5},{8,14},{10,8},{12,... | collective-permute-start | bytes 786440 | tf_op jit(solution)/shard_map/ppermute | solution.py:96
  67.6 11.5 %collective-permute-start.2 = (f32[2,32,1024]{2,1,0:T(8,128)S(1)}, f32[2,32,1024]{2,1,0:T(8,128)S(1)}, u32[]{:S(2)}, u32[]{:S(2)}) collective-permute-start(f32[2,32,1024]{2,1,0:T(8,128)S(1)} %bitcast_add_fusion.47), channel_id=1, source_target_pairs={{0,2},{2,4},{4,6},{6,0},{1,3},{3,5},{5,7},{7,1},{8,10},{10,12},{12... | collective-permute-start | bytes 786440 | tf_op jit(solution)/shard_map/ppermute | solution.py:96
  68.3 13.9 %collective-permute-start.19 = (f32[2,32,1024]{2,1,0:T(8,128)S(1)}, f32[2,32,1024]{2,1,0:T(8,128)S(1)}, u32[]{:S(2)}, u32[]{:S(2)}) collective-permute-start(f32[2,32,1024]{2,1,0:T(8,128)S(1)} %bitcast_add_fusion.38), channel_id=1, source_target_pairs={{0,6},{2,0},{4,2},{6,4},{1,7},{3,1},{5,3},{7,5},{8,14},{10,8},{12,... | collective-permute-start | bytes 786440 | tf_op jit(solution)/shard_map/ppermute | solution.py:96
  83.9 11.1 %collective-permute-start.20 = (f32[2,32,1024]{2,1,0:T(8,128)}, f32[2,32,1024]{2,1,0:T(8,128)}, u32[]{:S(2)}, u32[]{:S(2)}) collective-permute-start(f32[2,32,1024]{2,1,0:T(8,128)} %fusion.67), channel_id=1, source_target_pairs={{0,1},{1,0},{2,3},{3,2},{4,5},{5,4},{6,7},{7,6},{8,9},{9,8},{10,11... | collective-permute-start | bytes 786440 | tf_op jit(solution)/shard_map/ppermute | solution.py:106
  88.3 12.3 %collective-permute-start.7 = (f32[2,32,1024]{2,1,0:T(8,128)}, f32[2,32,1024]{2,1,0:T(8,128)}, u32[]{:S(2)}, u32[]{:S(2)}) collective-permute-start(f32[2,32,1024]{2,1,0:T(8,128)} %fusion.75), channel_id=1, source_target_pairs={{0,1},{1,0},{2,3},{3,2},{4,5},{5,4},{6,7},{7,6},{8,9},{9,8},{10,11... | collective-permute-start | bytes 786440 | tf_op jit(solution)/shard_map/ppermute | solution.py:108
  105.8 12.3 %collective-permute-start.22 = (f32[2,32,1024]{2,1,0:T(8,128)S(1)}, f32[2,32,1024]{2,1,0:T(8,128)S(1)}, u32[]{:S(2)}, u32[]{:S(2)}) collective-permute-start(f32[2,32,1024]{2,1,0:T(8,128)S(1)} %get-tuple-element.174), channel_id=1, source_target_pairs={{0,2},{2,4},{4,6},{6,0},{1,3},{3,5},{5,7},{7,1},{8,10},{10,12},{12... | collective-permute-start | bytes 786440 | tf_op jit(solution)/shard_map/ppermute | solution.py:116
  106.0 12.1 %collective-permute-start.25 = (f32[2,32,1024]{2,1,0:T(8,128)S(1)}, f32[2,32,1024]{2,1,0:T(8,128)S(1)}, u32[]{:S(2)}, u32[]{:S(2)}) collective-permute-start(f32[2,32,1024]{2,1,0:T(8,128)S(1)} %get-tuple-element.175), channel_id=1, source_target_pairs={{0,6},{2,0},{4,2},{6,4},{1,7},{3,1},{5,3},{7,5},{8,14},{10,8},{12,... | collective-permute-start | bytes 786440 | tf_op jit(solution)/shard_map/ppermute | solution.py:116
  112.4 11.2 %collective-permute-start.9 = (f32[2,32,1024]{2,1,0:T(8,128)S(1)}, f32[2,32,1024]{2,1,0:T(8,128)S(1)}, u32[]{:S(2)}, u32[]{:S(2)}) collective-permute-start(f32[2,32,1024]{2,1,0:T(8,128)S(1)} %collective-permute-done.8), channel_id=1, source_target_pairs={{0,2},{2,4},{4,6},{6,0},{1,3},{3,5},{5,7},{7,1},{8,10},{10,12},{12... | collective-permute-start | bytes 786440 | tf_op jit(solution)/shard_map/ppermute | solution.py:116
  112.5 11.2 %collective-permute-start.12 = (f32[2,32,1024]{2,1,0:T(8,128)S(1)}, f32[2,32,1024]{2,1,0:T(8,128)S(1)}, u32[]{:S(2)}, u32[]{:S(2)}) collective-permute-start(f32[2,32,1024]{2,1,0:T(8,128)S(1)} %collective-permute-done.11), channel_id=1, source_target_pairs={{0,6},{2,0},{4,2},{6,4},{1,7},{3,1},{5,3},{7,5},{8,14},{10,8},{12,... | collective-permute-start | bytes 786440 | tf_op jit(solution)/shard_map/ppermute | solution.py:116
  118.0 11.2 %collective-permute-start.23 = (f32[2,32,1024]{2,1,0:T(8,128)S(1)}, f32[2,32,1024]{2,1,0:T(8,128)S(1)}, u32[]{:S(2)}, u32[]{:S(2)}) collective-permute-start(f32[2,32,1024]{2,1,0:T(8,128)S(1)} %collective-permute-done.22), channel_id=1, source_target_pairs={{0,2},{2,4},{4,6},{6,0},{1,3},{3,5},{5,7},{7,1},{8,10},{10,12},{12... | collective-permute-start | bytes 786440 | tf_op jit(solution)/shard_map/ppermute | solution.py:116
  118.1 11.2 %collective-permute-start.26 = (f32[2,32,1024]{2,1,0:T(8,128)S(1)}, f32[2,32,1024]{2,1,0:T(8,128)S(1)}, u32[]{:S(2)}, u32[]{:S(2)}) collective-permute-start(f32[2,32,1024]{2,1,0:T(8,128)S(1)} %collective-permute-done.25), channel_id=1, source_target_pairs={{0,6},{2,0},{4,2},{6,4},{1,7},{3,1},{5,3},{7,5},{8,14},{10,8},{12,... | collective-permute-start | bytes 786440 | tf_op jit(solution)/shard_map/ppermute | solution.py:116
  159.6 45.3 %collective-permute-start.31 = (f32[2,64,1024]{2,1,0:T(8,128)}, f32[2,64,1024]{2,1,0:T(8,128)}, u32[]{:S(2)}, u32[]{:S(2)}) collective-permute-start(f32[2,64,1024]{2,1,0:T(8,128)} %dynamic-slice_bitcast_fusion), channel_id=1, source_target_pairs={{0,6},{2,0},{4,2},{6,4},{1,7},{3,1},{5,3},{7,5},{8,14},{10,8},{12,... | collective-permute-start | bytes 1572872 | tf_op jit(solution)/shard_map/ppermute | solution.py:96
  162.7 55.9 %collective-permute-start.28 = (f32[2,64,1024]{2,1,0:T(8,128)}, f32[2,64,1024]{2,1,0:T(8,128)}, u32[]{:S(2)}, u32[]{:S(2)}) collective-permute-start(f32[2,64,1024]{2,1,0:T(8,128)} %dynamic-slice_bitcast_fusion.1), channel_id=1, source_target_pairs={{0,2},{2,4},{4,6},{6,0},{1,3},{3,5},{5,7},{7,1},{8,10},{10,12},{12... | collective-permute-start | bytes 1572872 | tf_op jit(solution)/shard_map/ppermute | solution.py:96
  206.3 26.8 %collective-permute-start.32 = (f32[2,64,1024]{2,1,0:T(8,128)S(1)}, f32[2,64,1024]{2,1,0:T(8,128)S(1)}, u32[]{:S(2)}, u32[]{:S(2)}) collective-permute-start(f32[2,64,1024]{2,1,0:T(8,128)S(1)} %bitcast_add_fusion.3), channel_id=1, source_target_pairs={{0,6},{2,0},{4,2},{6,4},{1,7},{3,1},{5,3},{7,5},{8,14},{10,8},{12,... | collective-permute-start | bytes 1572872 | tf_op jit(solution)/shard_map/ppermute | solution.py:96
  209.6 13.7 %collective-permute-start.48 = (f32[2,32,1024]{2,1,0:T(8,128)S(1)}, f32[2,32,1024]{2,1,0:T(8,128)S(1)}, u32[]{:S(2)}, u32[]{:S(2)}) collective-permute-start(f32[2,32,1024]{2,1,0:T(8,128)S(1)} %fusion.62), channel_id=1, source_target_pairs={{0,1},{1,0},{2,3},{3,2},{4,5},{5,4},{6,7},{7,6},{8,9},{9,8},{10,11... | collective-permute-start | bytes 786440 | tf_op jit(solution)/shard_map/ppermute | solution.py:106
  215.4 14.7 %collective-permute-start.62 = (f32[2,32,1024]{2,1,0:T(8,128)S(1)}, f32[2,32,1024]{2,1,0:T(8,128)S(1)}, u32[]{:S(2)}, u32[]{:S(2)}) collective-permute-start(f32[2,32,1024]{2,1,0:T(8,128)S(1)} %fusion.57), channel_id=1, source_target_pairs={{0,1},{1,0},{2,3},{3,2},{4,5},{5,4},{6,7},{7,6},{8,9},{9,8},{10,11... | collective-permute-start | bytes 786440 | tf_op jit(solution)/shard_map/ppermute | solution.py:106
  219.8 16.1 %collective-permute-start.29 = (f32[2,64,1024]{2,1,0:T(8,128)S(1)}, f32[2,64,1024]{2,1,0:T(8,128)S(1)}, u32[]{:S(2)}, u32[]{:S(2)}) collective-permute-start(f32[2,64,1024]{2,1,0:T(8,128)S(1)} %bitcast_add_fusion.6), channel_id=1, source_target_pairs={{0,2},{2,4},{4,6},{6,0},{1,3},{3,5},{5,7},{7,1},{8,10},{10,12},{12... | collective-permute-start | bytes 1572872 | tf_op jit(solution)/shard_map/ppermute | solution.py:96
  223.3 12.8 %collective-permute-start.49 = (f32[2,32,1024]{2,1,0:T(8,128)S(1)}, f32[2,32,1024]{2,1,0:T(8,128)S(1)}, u32[]{:S(2)}, u32[]{:S(2)}) collective-permute-start(f32[2,32,1024]{2,1,0:T(8,128)S(1)} %fusion.65), channel_id=1, source_target_pairs={{0,1},{1,0},{2,3},{3,2},{4,5},{5,4},{6,7},{7,6},{8,9},{9,8},{10,11... | collective-permute-start | bytes 786440 | tf_op jit(solution)/shard_map/ppermute | solution.py:108
  230.2 11.0 %collective-permute-start.63 = (f32[2,32,1024]{2,1,0:T(8,128)S(1)}, f32[2,32,1024]{2,1,0:T(8,128)S(1)}, u32[]{:S(2)}, u32[]{:S(2)}) collective-permute-start(f32[2,32,1024]{2,1,0:T(8,128)S(1)} %fusion.60), channel_id=1, source_target_pairs={{0,1},{1,0},{2,3},{3,2},{4,5},{5,4},{6,7},{7,6},{8,9},{9,8},{10,11... | collective-permute-start | bytes 786440 | tf_op jit(solution)/shard_map/ppermute | solution.py:108
  233.2 29.9 %collective-permute-start.33 = (f32[2,64,1024]{2,1,0:T(8,128)S(1)}, f32[2,64,1024]{2,1,0:T(8,128)S(1)}, u32[]{:S(2)}, u32[]{:S(2)}) collective-permute-start(f32[2,64,1024]{2,1,0:T(8,128)S(1)} %bitcast_add_fusion.2), channel_id=1, source_target_pairs={{0,6},{2,0},{4,2},{6,4},{1,7},{3,1},{5,3},{7,5},{8,14},{10,8},{12,... | collective-permute-start | bytes 1572872 | tf_op jit(solution)/shard_map/ppermute | solution.py:96
  236.0 30.5 %collective-permute-start.30 = (f32[2,64,1024]{2,1,0:T(8,128)S(1)}, f32[2,64,1024]{2,1,0:T(8,128)S(1)}, u32[]{:S(2)}, u32[]{:S(2)}) collective-permute-start(f32[2,64,1024]{2,1,0:T(8,128)S(1)} %bitcast_add_fusion.5), channel_id=1, source_target_pairs={{0,2},{2,4},{4,6},{6,0},{1,3},{3,5},{5,7},{7,1},{8,10},{10,12},{12... | collective-permute-start | bytes 1572872 | tf_op jit(solution)/shard_map/ppermute | solution.py:96
  236.3 18.2 %collective-permute-start.50 = (f32[2,32,1024]{2,1,0:T(8,128)S(1)}, f32[2,32,1024]{2,1,0:T(8,128)S(1)}, u32[]{:S(2)}, u32[]{:S(2)}) collective-permute-start(f32[2,32,1024]{2,1,0:T(8,128)S(1)} %get-tuple-element.168), channel_id=1, source_target_pairs={{0,2},{2,4},{4,6},{6,0},{1,3},{3,5},{5,7},{7,1},{8,10},{10,12},{12... | collective-permute-start | bytes 786440 | tf_op jit(solution)/shard_map/ppermute | solution.py:116
  236.4 18.2 %collective-permute-start.53 = (f32[2,32,1024]{2,1,0:T(8,128)S(1)}, f32[2,32,1024]{2,1,0:T(8,128)S(1)}, u32[]{:S(2)}, u32[]{:S(2)}) collective-permute-start(f32[2,32,1024]{2,1,0:T(8,128)S(1)} %get-tuple-element.169), channel_id=1, source_target_pairs={{0,6},{2,0},{4,2},{6,4},{1,7},{3,1},{5,3},{7,5},{8,14},{10,8},{12,... | collective-permute-start | bytes 786440 | tf_op jit(solution)/shard_map/ppermute | solution.py:116
  241.4 18.8 %collective-permute-start.64 = (f32[2,32,1024]{2,1,0:T(8,128)S(1)}, f32[2,32,1024]{2,1,0:T(8,128)S(1)}, u32[]{:S(2)}, u32[]{:S(2)}) collective-permute-start(f32[2,32,1024]{2,1,0:T(8,128)S(1)} %get-tuple-element.170), channel_id=1, source_target_pairs={{0,2},{2,4},{4,6},{6,0},{1,3},{3,5},{5,7},{7,1},{8,10},{10,12},{12... | collective-permute-start | bytes 786440 | tf_op jit(solution)/shard_map/ppermute | solution.py:116
  254.6 12.7 %collective-permute-start.51 = (f32[2,32,1024]{2,1,0:T(8,128)S(1)}, f32[2,32,1024]{2,1,0:T(8,128)S(1)}, u32[]{:S(2)}, u32[]{:S(2)}) collective-permute-start(f32[2,32,1024]{2,1,0:T(8,128)S(1)} %collective-permute-done.50), channel_id=1, source_target_pairs={{0,2},{2,4},{4,6},{6,0},{1,3},{3,5},{5,7},{7,1},{8,10},{10,12},{12... | collective-permute-start | bytes 786440 | tf_op jit(solution)/shard_map/ppermute | solution.py:116
  266.6 12.1 %collective-permute-start.34 = (f32[2,64,1024]{2,1,0:T(8,128)S(1)}, f32[2,64,1024]{2,1,0:T(8,128)S(1)}, u32[]{:S(2)}, u32[]{:S(2)}) collective-permute-start(f32[2,64,1024]{2,1,0:T(8,128)S(1)} %fusion.34), channel_id=1, source_target_pairs={{0,1},{1,0},{2,3},{3,2},{4,5},{5,4},{6,7},{7,6},{8,9},{9,8},{10,11... | collective-permute-start | bytes 1572872 | tf_op jit(solution)/shard_map/ppermute | solution.py:106
  267.3 12.4 %collective-permute-start.52 = (f32[2,32,1024]{2,1,0:T(8,128)S(1)}, f32[2,32,1024]{2,1,0:T(8,128)S(1)}, u32[]{:S(2)}, u32[]{:S(2)}) collective-permute-start(f32[2,32,1024]{2,1,0:T(8,128)S(1)} %collective-permute-done.51), channel_id=1, source_target_pairs={{0,2},{2,4},{4,6},{6,0},{1,3},{3,5},{5,7},{7,1},{8,10},{10,12},{12... | collective-permute-start | bytes 786440 | tf_op jit(solution)/shard_map/ppermute | solution.py:116
  267.3 12.4 %collective-permute-start.55 = (f32[2,32,1024]{2,1,0:T(8,128)S(1)}, f32[2,32,1024]{2,1,0:T(8,128)S(1)}, u32[]{:S(2)}, u32[]{:S(2)}) collective-permute-start(f32[2,32,1024]{2,1,0:T(8,128)S(1)} %collective-permute-done.54), channel_id=1, source_target_pairs={{0,6},{2,0},{4,2},{6,4},{1,7},{3,1},{5,3},{7,5},{8,14},{10,8},{12,... | collective-permute-start | bytes 786440 | tf_op jit(solution)/shard_map/ppermute | solution.py:116
  278.8 15.1 %collective-permute-start.35 = (f32[2,64,1024]{2,1,0:T(8,128)S(1)}, f32[2,64,1024]{2,1,0:T(8,128)S(1)}, u32[]{:S(2)}, u32[]{:S(2)}) collective-permute-start(f32[2,64,1024]{2,1,0:T(8,128)S(1)} %fusion.37), channel_id=1, source_target_pairs={{0,1},{1,0},{2,3},{3,2},{4,5},{5,4},{6,7},{7,6},{8,9},{9,8},{10,11... | collective-permute-start | bytes 1572872 | tf_op jit(solution)/shard_map/ppermute | solution.py:108
  294.1 15.0 %collective-permute-start.36 = (f32[2,64,1024]{2,1,0:T(8,128)S(1)}, f32[2,64,1024]{2,1,0:T(8,128)S(1)}, u32[]{:S(2)}, u32[]{:S(2)}) collective-permute-start(f32[2,64,1024]{2,1,0:T(8,128)S(1)} %get-tuple-element.157), channel_id=1, source_target_pairs={{0,2},{2,4},{4,6},{6,0},{1,3},{3,5},{5,7},{7,1},{8,10},{10,12},{12... | collective-permute-start | bytes 1572872 | tf_op jit(solution)/shard_map/ppermute | solution.py:116
  294.2 15.2 %collective-permute-start.39 = (f32[2,64,1024]{2,1,0:T(8,128)S(1)}, f32[2,64,1024]{2,1,0:T(8,128)S(1)}, u32[]{:S(2)}, u32[]{:S(2)}) collective-permute-start(f32[2,64,1024]{2,1,0:T(8,128)S(1)} %get-tuple-element.158), channel_id=1, source_target_pairs={{0,6},{2,0},{4,2},{6,4},{1,7},{3,1},{5,3},{7,5},{8,14},{10,8},{12,... | collective-permute-start | bytes 1572872 | tf_op jit(solution)/shard_map/ppermute | solution.py:116
  319.6 10.7 %collective-permute-start.41 = (f32[2,64,1024]{2,1,0:T(8,128)S(1)}, f32[2,64,1024]{2,1,0:T(8,128)S(1)}, u32[]{:S(2)}, u32[]{:S(2)}) collective-permute-start(f32[2,64,1024]{2,1,0:T(8,128)S(1)} %collective-permute-done.40), channel_id=1, source_target_pairs={{0,6},{2,0},{4,2},{6,4},{1,7},{3,1},{5,3},{7,5},{8,14},{10,8},{12,... | collective-permute-start | bytes 1572872 | tf_op jit(solution)/shard_map/ppermute | solution.py:116
  404.8 10.8 %collective-permute-start.76 = (f32[2,32,1024]{2,1,0:T(8,128)S(1)}, f32[2,32,1024]{2,1,0:T(8,128)S(1)}, u32[]{:S(2)}, u32[]{:S(2)}) collective-permute-start(f32[2,32,1024]{2,1,0:T(8,128)S(1)} %fusion.52), channel_id=1, source_target_pairs={{0,1},{1,0},{2,3},{3,2},{4,5},{5,4},{6,7},{7,6},{8,9},{9,8},{10,11... | collective-permute-start | bytes 786440 | tf_op jit(solution)/shard_map/ppermute | solution.py:106
  408.3 15.4 %collective-permute-start.90 = (f32[2,32,1024]{2,1,0:T(8,128)S(1)}, f32[2,32,1024]{2,1,0:T(8,128)S(1)}, u32[]{:S(2)}, u32[]{:S(2)}) collective-permute-start(f32[2,32,1024]{2,1,0:T(8,128)S(1)} %fusion.47), channel_id=1, source_target_pairs={{0,1},{1,0},{2,3},{3,2},{4,5},{5,4},{6,7},{7,6},{8,9},{9,8},{10,11... | collective-permute-start | bytes 786440 | tf_op jit(solution)/shard_map/ppermute | solution.py:106
  409.7 13.9 %collective-permute-start.105 = (f32[2,16,1024]{2,1,0:T(8,128)S(1)}, f32[2,16,1024]{2,1,0:T(8,128)S(1)}, u32[]{:S(2)}, u32[]{:S(2)}) collective-permute-start(f32[2,16,1024]{2,1,0:T(8,128)S(1)} %dynamic-slice_bitcast_fusion.16), channel_id=1, source_target_pairs={{0,64},{64,0},{1,65},{65,1},{2,66},{66,2},{3,67},{67,3},{4,68},{68... | collective-permute-start | bytes 393224 | tf_op jit(solution)/shard_map/ppermute | solution.py:150
  415.7 15.5 %collective-permute-start.77 = (f32[2,32,1024]{2,1,0:T(8,128)S(1)}, f32[2,32,1024]{2,1,0:T(8,128)S(1)}, u32[]{:S(2)}, u32[]{:S(2)}) collective-permute-start(f32[2,32,1024]{2,1,0:T(8,128)S(1)} %fusion.55), channel_id=1, source_target_pairs={{0,1},{1,0},{2,3},{3,2},{4,5},{5,4},{6,7},{7,6},{8,9},{9,8},{10,11... | collective-permute-start | bytes 786440 | tf_op jit(solution)/shard_map/ppermute | solution.py:108
  423.8 11.1 %collective-permute-start.91 = (f32[2,32,1024]{2,1,0:T(8,128)S(1)}, f32[2,32,1024]{2,1,0:T(8,128)S(1)}, u32[]{:S(2)}, u32[]{:S(2)}) collective-permute-start(f32[2,32,1024]{2,1,0:T(8,128)S(1)} %fusion.50), channel_id=1, source_target_pairs={{0,1},{1,0},{2,3},{3,2},{4,5},{5,4},{6,7},{7,6},{8,9},{9,8},{10,11... | collective-permute-start | bytes 786440 | tf_op jit(solution)/shard_map/ppermute | solution.py:108
  431.5 13.0 %collective-permute-start.81 = (f32[2,32,1024]{2,1,0:T(8,128)S(1)}, f32[2,32,1024]{2,1,0:T(8,128)S(1)}, u32[]{:S(2)}, u32[]{:S(2)}) collective-permute-start(f32[2,32,1024]{2,1,0:T(8,128)S(1)} %get-tuple-element.162), channel_id=1, source_target_pairs={{0,6},{2,0},{4,2},{6,4},{1,7},{3,1},{5,3},{7,5},{8,14},{10,8},{12,... | collective-permute-start | bytes 786440 | tf_op jit(solution)/shard_map/ppermute | solution.py:116
  435.1 11.9 %collective-permute-start.92 = (f32[2,32,1024]{2,1,0:T(8,128)S(1)}, f32[2,32,1024]{2,1,0:T(8,128)S(1)}, u32[]{:S(2)}, u32[]{:S(2)}) collective-permute-start(f32[2,32,1024]{2,1,0:T(8,128)S(1)} %get-tuple-element.163), channel_id=1, source_target_pairs={{0,2},{2,4},{4,6},{6,0},{1,3},{3,5},{5,7},{7,1},{8,10},{10,12},{12... | collective-permute-start | bytes 786440 | tf_op jit(solution)/shard_map/ppermute | solution.py:116
  435.2 12.7 %collective-permute-start.95 = (f32[2,32,1024]{2,1,0:T(8,128)S(1)}, f32[2,32,1024]{2,1,0:T(8,128)S(1)}, u32[]{:S(2)}, u32[]{:S(2)}) collective-permute-start(f32[2,32,1024]{2,1,0:T(8,128)S(1)} %get-tuple-element.164), channel_id=1, source_target_pairs={{0,6},{2,0},{4,2},{6,4},{1,7},{3,1},{5,3},{7,5},{8,14},{10,8},{12,... | collective-permute-start | bytes 786440 | tf_op jit(solution)/shard_map/ppermute | solution.py:116
  438.7 10.8 %collective-permute-start.108 = (f32[64,1024]{1,0:T(8,128)S(1)}, f32[64,1024]{1,0:T(8,128)S(1)}, u32[]{:S(2)}, u32[]{:S(2)}) collective-permute-start(f32[64,1024]{1,0:T(8,128)S(1)} %bitcast.737), channel_id=1, source_target_pairs={{0,16},{16,32},{32,48},{48,0},{1,17},{17,33},{33,49},{49,1},{2,18}... | collective-permute-start | bytes 786440 | tf_op jit(solution)/shard_map/ppermute | solution.py:162
  449.5 12.2 %collective-permute-start.96 = (f32[2,32,1024]{2,1,0:T(8,128)S(1)}, f32[2,32,1024]{2,1,0:T(8,128)S(1)}, u32[]{:S(2)}, u32[]{:S(2)}) collective-permute-start(f32[2,32,1024]{2,1,0:T(8,128)S(1)} %collective-permute-done.95), channel_id=1, source_target_pairs={{0,6},{2,0},{4,2},{6,4},{1,7},{3,1},{5,3},{7,5},{8,14},{10,8},{12,... | collective-permute-start | bytes 786440 | tf_op jit(solution)/shard_map/ppermute | solution.py:116
  451.6 21.4 %collective-permute-start.109 = (f32[64,1024]{1,0:T(8,128)S(1)}, f32[64,1024]{1,0:T(8,128)S(1)}, u32[]{:S(2)}, u32[]{:S(2)}) collective-permute-start(f32[64,1024]{1,0:T(8,128)S(1)} %collective-permute-done.108), channel_id=1, source_target_pairs={{0,16},{16,32},{32,48},{48,0},{1,17},{17,33},{33,49},{49,1},{2,18}... | collective-permute-start | bytes 786440 | tf_op jit(solution)/shard_map/ppermute | solution.py:162
  455.0 20.1 %collective-permute-start.112 = (f32[64,1024]{1,0:T(8,128)S(1)}, f32[64,1024]{1,0:T(8,128)S(1)}, u32[]{:S(2)}, u32[]{:S(2)}) collective-permute-start(f32[64,1024]{1,0:T(8,128)S(1)} %collective-permute-done.111), channel_id=1, source_target_pairs={{0,48},{16,0},{32,16},{48,32},{1,49},{17,1},{33,17},{49,33},{2,50}... | collective-permute-start | bytes 786440 | tf_op jit(solution)/shard_map/ppermute | solution.py:162
  490.8 11.2 %collective-permute-start.116 = (f32[2,1024]{1,0:T(2,128)S(1)}, f32[2,1024]{1,0:T(2,128)S(1)}, u32[]{:S(2)}, u32[]{:S(2)}) collective-permute-start(f32[2,1024]{1,0:T(2,128)S(1)} %add.790), channel_id=1, source_target_pairs={{0,1},{1,0},{2,3},{3,2},{4,5},{5,4},{6,7},{7,6},{8,9},{9,8},{10,11... | collective-permute-start | bytes 24584 | tf_op jit(solution)/shard_map/ppermute | solution.py:177
  (157 other events, 1164.8 us)
Sparse Core Ops, SparseCore 0:
  180.3 157.0 all-reduce.4

commit v9 on v8

--- a/solution.py
+++ b/solution.py
@@ -141,18 +141,8 @@
             acc = acc + lax.dynamic_index_in_dim(chunks, (here - shift * (1 + step)) % size, 0, keepdims=False)
         accs.append(acc)
     acc = jnp.stack(accs)
-    sides = []
     for axis in pair_axes:
-        side = lax.axis_index(axis)
-        halves = acc.reshape(2, 2, acc.shape[1] // 2, cols)
-        keep = lax.dynamic_index_in_dim(halves, side, 1, keepdims=False)
-        send = lax.dynamic_index_in_dim(halves, 1 - side, 1, keepdims=False)
-        acc = keep + lax.ppermute(send, axis, [(0, 1), (1, 0)])
-        sides.append(side)
-    for axis, side in zip(pair_axes[::-1], sides[::-1]):
-        other = lax.ppermute(acc, axis, [(0, 1), (1, 0)])
-        both = jnp.where(side == 0, jnp.stack([acc, other], 1), jnp.stack([other, acc], 1))
-        acc = both.reshape(2, 2 * acc.shape[1], cols)
+        acc = acc + lax.ppermute(acc, axis, [(0, 1), (1, 0)])
     outs = []
     for way, shift in ((0, 1), (1, -1)):
         cur = acc[way]

time: 527 us -> 528 us (level)
  the two profiles are of different devices: /device:TPU:0 before, /device:TPU:2 now
where the time goes in v9:
time: 528 us; the launch traced here: 519 us
  starting transfers between devices  175 us (33%)
  waiting for transfers between devices  171 us (32%)
  other arithmetic  58.4 us (11%)
  matrix products  50.2 us (10%)
  local copies, waits for them, and re-layouts  47.3 us (9%)
  between operations  17.2 us (3%)
    ppermute x42, waiting for transfers between devices, tensor_sum(): cur = lax.ppermute(cur, 'ty', ring(ny, shift))  72.2 us
    ppermute x42, starting transfers between devices, tensor_sum(): cur = lax.ppermute(cur, 'ty', ring(ny, shift))  62.5 us
    ppermute x42, starting transfers between devices, tensor_sum(): acc = lax.ppermute(acc, 'ty', ring(ny, shift))  61.4 us
    ppermute x42, waiting for transfers between devices, tensor_sum(): acc = lax.ppermute(acc, 'ty', ring(ny, shift))  33.6 us
    ppermute x7, waiting for transfers between devices, tensor_sum(): got = lax.ppermute(send, 'tx', pairs)  26.3 us
    ppermute x7, waiting for transfers between devices, tensor_sum(): other = lax.ppermute(mine, 'tx', pairs)  22.3 us
    unnamed x177, local copies, waits for them, and re-layouts  17.8 us
    dot_general x7, matrix products, inner(): lax.dot_general(first_op, second_op, (((1,), (1,)), ((), ())), preferred_...  16.2 us
  transfers between devices with their start and end apart: 116, of which 62 were waited for; matrix products, arithmetic and copies ran while one was open for 17% of the time, Pallas kernels for 0%

profile of v9, /device:TPU:2, one launch (start us, length us, event | category | flops | bytes accessed | tf_op | source)
XLA Modules:
  0.0 518.6 jit_solution(5577897270202727055)
XLA Ops:
  46.7 3.4 collective-permute-start.17
  53.1 3.3 collective-permute-start.4
  58.6 3.3 collective-permute-start.18
  68.2 3.8 collective-permute-start.19
  75.0 4.0 collective-permute-done.2
  90.3 4.6 collective-permute-done.20
  105.9 3.3 collective-permute-start.25
  112.3 3.3 collective-permute-start.12
  118.0 3.3 collective-permute-start.26
  123.6 3.3 collective-permute-start.13
  129.2 3.7 collective-permute-start.27
  133.3 3.4 collective-permute-done.24
  146.6 3.9 fusion.119
  165.6 4.4 convolution_add_fusion
  206.2 3.3 collective-permute-start.32
  211.8 3.5 collective-permute-done.58
  218.9 4.3 collective-permute-done.48
  225.5 4.4 collective-permute-done.62
  235.5 3.5 collective-permute-start.53
  240.9 13.0 %collective-permute-done.50 = f32[2,32,1024]{2,1,0:T(8,128)S(1)} collective-permute-done((f32[2,32,1024]{2,1,0:T(8,128)S(1)}, f32[2,32,1024]{2,1,0:T(8,128)S(1)}, u32[]{:S(2)}, u32[]{:S(2)}) %collective-permute-start.50) | collective-permute-done | bytes 262176 | tf_op jit(solution)/shard_map/ppermute | solution.py:116
  256.0 3.5 collective-permute-done.64
  262.5 3.3 collective-permute-start.68
  267.4 3.3 collective-permute-start.55
  274.1 4.0 collective-permute-done.34
  280.4 13.7 %collective-permute-done.35 = f32[2,64,1024]{2,1,0:T(8,128)S(1)} collective-permute-done((f32[2,64,1024]{2,1,0:T(8,128)S(1)}, f32[2,64,1024]{2,1,0:T(8,128)S(1)}, u32[]{:S(2)}, u32[]{:S(2)}) %collective-permute-start.35) | collective-permute-done | bytes 524320 | tf_op jit(solution)/shard_map/ppermute | solution.py:108
  300.3 8.6 %collective-permute-done.36 = f32[2,64,1024]{2,1,0:T(8,128)S(1)} collective-permute-done((f32[2,64,1024]{2,1,0:T(8,128)S(1)}, f32[2,64,1024]{2,1,0:T(8,128)S(1)}, u32[]{:S(2)}, u32[]{:S(2)}) %collective-permute-start.36) | collective-permute-done | bytes 524320 | tf_op jit(solution)/shard_map/ppermute | solution.py:116
  309.2 3.4 collective-permute-start.40
  313.0 6.3 %collective-permute-done.37 = f32[2,64,1024]{2,1,0:T(8,128)S(1)} collective-permute-done((f32[2,64,1024]{2,1,0:T(8,128)S(1)}, f32[2,64,1024]{2,1,0:T(8,128)S(1)}, u32[]{:S(2)}, u32[]{:S(2)}) %collective-permute-start.37) | collective-permute-done | bytes 524320 | tf_op jit(solution)/shard_map/ppermute | solution.py:116
  319.4 4.0 collective-permute-start.41
  323.5 6.2 %collective-permute-done.38 = f32[2,64,1024]{2,1,0:T(8,128)S(1)} collective-permute-done((f32[2,64,1024]{2,1,0:T(8,128)S(1)}, f32[2,64,1024]{2,1,0:T(8,128)S(1)}, u32[]{:S(2)}, u32[]{:S(2)}) %collective-permute-start.38) | collective-permute-done | bytes 524320 | tf_op jit(solution)/shard_map/ppermute | solution.py:116
  330.5 4.5 multiply_add_fusion
  353.6 3.3 fusion.17
  369.1 3.3 collective-permute-start.101
  372.4 3.8 collective-permute-start.73
  376.3 3.3 collective-permute-start.87
  400.9 3.8 collective-permute-done.72
  411.1 4.4 collective-permute-done.76
  432.9 3.3 collective-permute-start.95
  437.7 3.3 collective-permute-start.82
  443.2 3.4 collective-permute-start.96
  450.6 3.7 collective-permute-done.93
  462.5 3.5 collective-permute-done.97
  467.3 3.3 collective-permute-start.110
  470.6 6.9 %collective-permute-done.107 = f32[64,1024]{1,0:T(8,128)S(1)} collective-permute-done((f32[64,1024]{1,0:T(8,128)S(1)}, f32[64,1024]{1,0:T(8,128)S(1)}, u32[]{:S(2)}, u32[]{:S(2)}) %collective-permute-start.107) | collective-permute-done | bytes 262176 | tf_op jit(solution)/shard_map/ppermute | solution.py:152
  477.6 3.3 collective-permute-start.111
  480.9 4.2 collective-permute-done.108
  485.6 3.6 collective-permute-done.112
  503.9 3.5 copy.117
  (638 shorter events, 293.9 us)
Async XLA Ops:
  7.2 356.4 %all-reduce.5.cloned.1.call-start = ((), (), s32[]{:S(2)}) async-start(), calls=%async_computation | async-start | bytes 14155776 | tf_op jit(solution)/shard_map/psum | solution.py:249
  40.4 11.5 %collective-permute-start.3 = (f32[2,32,1024]{2,1,0:T(8,128)}, f32[2,32,1024]{2,1,0:T(8,128)}, u32[]{:S(2)}, u32[]{:S(2)}) collective-permute-start(f32[2,32,1024]{2,1,0:T(8,128)} %dynamic-slice_bitcast_fusion.14), channel_id=1, source_target_pairs={{0,6},{2,0},{4,2},{6,4},{1,7},{3,1},{5,3},{7,5},{8,14},{10,8},{12,... | collective-permute-start | bytes 786440 | tf_op jit(solution)/shard_map/ppermute | solution.py:96
  45.0 11.3 %collective-permute-start = (f32[2,32,1024]{2,1,0:T(8,128)}, f32[2,32,1024]{2,1,0:T(8,128)}, u32[]{:S(2)}, u32[]{:S(2)}) collective-permute-start(f32[2,32,1024]{2,1,0:T(8,128)} %dynamic-slice_bitcast_fusion.15), channel_id=1, source_target_pairs={{0,2},{2,4},{4,6},{6,0},{1,3},{3,5},{5,7},{7,1},{8,10},{10,12},{12... | collective-permute-start | bytes 786440 | tf_op jit(solution)/shard_map/ppermute | solution.py:96
  46.7 10.8 %collective-permute-start.17 = (f32[2,32,1024]{2,1,0:T(8,128)}, f32[2,32,1024]{2,1,0:T(8,128)}, u32[]{:S(2)}, u32[]{:S(2)}) collective-permute-start(f32[2,32,1024]{2,1,0:T(8,128)} %dynamic-slice_bitcast_fusion.12), channel_id=1, source_target_pairs={{0,6},{2,0},{4,2},{6,4},{1,7},{3,1},{5,3},{7,5},{8,14},{10,8},{12,... | collective-permute-start | bytes 786440 | tf_op jit(solution)/shard_map/ppermute | solution.py:96
  67.5 11.5 %collective-permute-start.2 = (f32[2,32,1024]{2,1,0:T(8,128)S(1)}, f32[2,32,1024]{2,1,0:T(8,128)S(1)}, u32[]{:S(2)}, u32[]{:S(2)}) collective-permute-start(f32[2,32,1024]{2,1,0:T(8,128)S(1)} %bitcast_add_fusion.47), channel_id=1, source_target_pairs={{0,2},{2,4},{4,6},{6,0},{1,3},{3,5},{5,7},{7,1},{8,10},{10,12},{12... | collective-permute-start | bytes 786440 | tf_op jit(solution)/shard_map/ppermute | solution.py:96
  68.2 13.0 %collective-permute-start.19 = (f32[2,32,1024]{2,1,0:T(8,128)S(1)}, f32[2,32,1024]{2,1,0:T(8,128)S(1)}, u32[]{:S(2)}, u32[]{:S(2)}) collective-permute-start(f32[2,32,1024]{2,1,0:T(8,128)S(1)} %bitcast_add_fusion.38), channel_id=1, source_target_pairs={{0,6},{2,0},{4,2},{6,4},{1,7},{3,1},{5,3},{7,5},{8,14},{10,8},{12,... | collective-permute-start | bytes 786440 | tf_op jit(solution)/shard_map/ppermute | solution.py:96
  83.8 11.1 %collective-permute-start.20 = (f32[2,32,1024]{2,1,0:T(8,128)}, f32[2,32,1024]{2,1,0:T(8,128)}, u32[]{:S(2)}, u32[]{:S(2)}) collective-permute-start(f32[2,32,1024]{2,1,0:T(8,128)} %fusion.62), channel_id=1, source_target_pairs={{0,1},{1,0},{2,3},{3,2},{4,5},{5,4},{6,7},{7,6},{8,9},{9,8},{10,11... | collective-permute-start | bytes 786440 | tf_op jit(solution)/shard_map/ppermute | solution.py:106
  88.2 12.3 %collective-permute-start.7 = (f32[2,32,1024]{2,1,0:T(8,128)}, f32[2,32,1024]{2,1,0:T(8,128)}, u32[]{:S(2)}, u32[]{:S(2)}) collective-permute-start(f32[2,32,1024]{2,1,0:T(8,128)} %fusion.70), channel_id=1, source_target_pairs={{0,1},{1,0},{2,3},{3,2},{4,5},{5,4},{6,7},{7,6},{8,9},{9,8},{10,11... | collective-permute-start | bytes 786440 | tf_op jit(solution)/shard_map/ppermute | solution.py:108
  105.7 12.3 %collective-permute-start.22 = (f32[2,32,1024]{2,1,0:T(8,128)S(1)}, f32[2,32,1024]{2,1,0:T(8,128)S(1)}, u32[]{:S(2)}, u32[]{:S(2)}) collective-permute-start(f32[2,32,1024]{2,1,0:T(8,128)S(1)} %get-tuple-element.161), channel_id=1, source_target_pairs={{0,2},{2,4},{4,6},{6,0},{1,3},{3,5},{5,7},{7,1},{8,10},{10,12},{12... | collective-permute-start | bytes 786440 | tf_op jit(solution)/shard_map/ppermute | solution.py:116
  105.9 12.1 %collective-permute-start.25 = (f32[2,32,1024]{2,1,0:T(8,128)S(1)}, f32[2,32,1024]{2,1,0:T(8,128)S(1)}, u32[]{:S(2)}, u32[]{:S(2)}) collective-permute-start(f32[2,32,1024]{2,1,0:T(8,128)S(1)} %get-tuple-element.162), channel_id=1, source_target_pairs={{0,6},{2,0},{4,2},{6,4},{1,7},{3,1},{5,3},{7,5},{8,14},{10,8},{12,... | collective-permute-start | bytes 786440 | tf_op jit(solution)/shard_map/ppermute | solution.py:116
  112.3 11.2 %collective-permute-start.9 = (f32[2,32,1024]{2,1,0:T(8,128)S(1)}, f32[2,32,1024]{2,1,0:T(8,128)S(1)}, u32[]{:S(2)}, u32[]{:S(2)}) collective-permute-start(f32[2,32,1024]{2,1,0:T(8,128)S(1)} %collective-permute-done.8), channel_id=1, source_target_pairs={{0,2},{2,4},{4,6},{6,0},{1,3},{3,5},{5,7},{7,1},{8,10},{10,12},{12... | collective-permute-start | bytes 786440 | tf_op jit(solution)/shard_map/ppermute | solution.py:116
  112.3 11.2 %collective-permute-start.12 = (f32[2,32,1024]{2,1,0:T(8,128)S(1)}, f32[2,32,1024]{2,1,0:T(8,128)S(1)}, u32[]{:S(2)}, u32[]{:S(2)}) collective-permute-start(f32[2,32,1024]{2,1,0:T(8,128)S(1)} %collective-permute-done.11), channel_id=1, source_target_pairs={{0,6},{2,0},{4,2},{6,4},{1,7},{3,1},{5,3},{7,5},{8,14},{10,8},{12,... | collective-permute-start | bytes 786440 | tf_op jit(solution)/shard_map/ppermute | solution.py:116
  117.9 11.2 %collective-permute-start.23 = (f32[2,32,1024]{2,1,0:T(8,128)S(1)}, f32[2,32,1024]{2,1,0:T(8,128)S(1)}, u32[]{:S(2)}, u32[]{:S(2)}) collective-permute-start(f32[2,32,1024]{2,1,0:T(8,128)S(1)} %collective-permute-done.22), channel_id=1, source_target_pairs={{0,2},{2,4},{4,6},{6,0},{1,3},{3,5},{5,7},{7,1},{8,10},{10,12},{12... | collective-permute-start | bytes 786440 | tf_op jit(solution)/shard_map/ppermute | solution.py:116
  118.0 11.2 %collective-permute-start.26 = (f32[2,32,1024]{2,1,0:T(8,128)S(1)}, f32[2,32,1024]{2,1,0:T(8,128)S(1)}, u32[]{:S(2)}, u32[]{:S(2)}) collective-permute-start(f32[2,32,1024]{2,1,0:T(8,128)S(1)} %collective-permute-done.25), channel_id=1, source_target_pairs={{0,6},{2,0},{4,2},{6,4},{1,7},{3,1},{5,3},{7,5},{8,14},{10,8},{12,... | collective-permute-start | bytes 786440 | tf_op jit(solution)/shard_map/ppermute | solution.py:116
  159.5 45.5 %collective-permute-start.31 = (f32[2,64,1024]{2,1,0:T(8,128)}, f32[2,64,1024]{2,1,0:T(8,128)}, u32[]{:S(2)}, u32[]{:S(2)}) collective-permute-start(f32[2,64,1024]{2,1,0:T(8,128)} %dynamic-slice_bitcast_fusion), channel_id=1, source_target_pairs={{0,6},{2,0},{4,2},{6,4},{1,7},{3,1},{5,3},{7,5},{8,14},{10,8},{12,... | collective-permute-start | bytes 1572872 | tf_op jit(solution)/shard_map/ppermute | solution.py:96
  162.6 55.1 %collective-permute-start.28 = (f32[2,64,1024]{2,1,0:T(8,128)}, f32[2,64,1024]{2,1,0:T(8,128)}, u32[]{:S(2)}, u32[]{:S(2)}) collective-permute-start(f32[2,64,1024]{2,1,0:T(8,128)} %dynamic-slice_bitcast_fusion.1), channel_id=1, source_target_pairs={{0,2},{2,4},{4,6},{6,0},{1,3},{3,5},{5,7},{7,1},{8,10},{10,12},{12... | collective-permute-start | bytes 1572872 | tf_op jit(solution)/shard_map/ppermute | solution.py:96
  206.2 26.2 %collective-permute-start.32 = (f32[2,64,1024]{2,1,0:T(8,128)S(1)}, f32[2,64,1024]{2,1,0:T(8,128)S(1)}, u32[]{:S(2)}, u32[]{:S(2)}) collective-permute-start(f32[2,64,1024]{2,1,0:T(8,128)S(1)} %bitcast_add_fusion.3), channel_id=1, source_target_pairs={{0,6},{2,0},{4,2},{6,4},{1,7},{3,1},{5,3},{7,5},{8,14},{10,8},{12,... | collective-permute-start | bytes 1572872 | tf_op jit(solution)/shard_map/ppermute | solution.py:96
  209.6 13.6 %collective-permute-start.48 = (f32[2,32,1024]{2,1,0:T(8,128)S(1)}, f32[2,32,1024]{2,1,0:T(8,128)S(1)}, u32[]{:S(2)}, u32[]{:S(2)}) collective-permute-start(f32[2,32,1024]{2,1,0:T(8,128)S(1)} %fusion.57), channel_id=1, source_target_pairs={{0,1},{1,0},{2,3},{3,2},{4,5},{5,4},{6,7},{7,6},{8,9},{9,8},{10,11... | collective-permute-start | bytes 786440 | tf_op jit(solution)/shard_map/ppermute | solution.py:106
  215.4 14.5 %collective-permute-start.62 = (f32[2,32,1024]{2,1,0:T(8,128)S(1)}, f32[2,32,1024]{2,1,0:T(8,128)S(1)}, u32[]{:S(2)}, u32[]{:S(2)}) collective-permute-start(f32[2,32,1024]{2,1,0:T(8,128)S(1)} %fusion.52), channel_id=1, source_target_pairs={{0,1},{1,0},{2,3},{3,2},{4,5},{5,4},{6,7},{7,6},{8,9},{9,8},{10,11... | collective-permute-start | bytes 786440 | tf_op jit(solution)/shard_map/ppermute | solution.py:106
  218.8 16.1 %collective-permute-start.29 = (f32[2,64,1024]{2,1,0:T(8,128)S(1)}, f32[2,64,1024]{2,1,0:T(8,128)S(1)}, u32[]{:S(2)}, u32[]{:S(2)}) collective-permute-start(f32[2,64,1024]{2,1,0:T(8,128)S(1)} %bitcast_add_fusion.6), channel_id=1, source_target_pairs={{0,2},{2,4},{4,6},{6,0},{1,3},{3,5},{5,7},{7,1},{8,10},{10,12},{12... | collective-permute-start | bytes 1572872 | tf_op jit(solution)/shard_map/ppermute | solution.py:96
  223.2 11.9 %collective-permute-start.49 = (f32[2,32,1024]{2,1,0:T(8,128)S(1)}, f32[2,32,1024]{2,1,0:T(8,128)S(1)}, u32[]{:S(2)}, u32[]{:S(2)}) collective-permute-start(f32[2,32,1024]{2,1,0:T(8,128)S(1)} %fusion.60), channel_id=1, source_target_pairs={{0,1},{1,0},{2,3},{3,2},{4,5},{5,4},{6,7},{7,6},{8,9},{9,8},{10,11... | collective-permute-start | bytes 786440 | tf_op jit(solution)/shard_map/ppermute | solution.py:108
  232.4 30.0 %collective-permute-start.33 = (f32[2,64,1024]{2,1,0:T(8,128)S(1)}, f32[2,64,1024]{2,1,0:T(8,128)S(1)}, u32[]{:S(2)}, u32[]{:S(2)}) collective-permute-start(f32[2,64,1024]{2,1,0:T(8,128)S(1)} %bitcast_add_fusion.2), channel_id=1, source_target_pairs={{0,6},{2,0},{4,2},{6,4},{1,7},{3,1},{5,3},{7,5},{8,14},{10,8},{12,... | collective-permute-start | bytes 1572872 | tf_op jit(solution)/shard_map/ppermute | solution.py:96
  235.0 30.8 %collective-permute-start.30 = (f32[2,64,1024]{2,1,0:T(8,128)S(1)}, f32[2,64,1024]{2,1,0:T(8,128)S(1)}, u32[]{:S(2)}, u32[]{:S(2)}) collective-permute-start(f32[2,64,1024]{2,1,0:T(8,128)S(1)} %bitcast_add_fusion.5), channel_id=1, source_target_pairs={{0,2},{2,4},{4,6},{6,0},{1,3},{3,5},{5,7},{7,1},{8,10},{10,12},{12... | collective-permute-start | bytes 1572872 | tf_op jit(solution)/shard_map/ppermute | solution.py:96
  235.4 18.5 %collective-permute-start.50 = (f32[2,32,1024]{2,1,0:T(8,128)S(1)}, f32[2,32,1024]{2,1,0:T(8,128)S(1)}, u32[]{:S(2)}, u32[]{:S(2)}) collective-permute-start(f32[2,32,1024]{2,1,0:T(8,128)S(1)} %get-tuple-element.155), channel_id=1, source_target_pairs={{0,2},{2,4},{4,6},{6,0},{1,3},{3,5},{5,7},{7,1},{8,10},{10,12},{12... | collective-permute-start | bytes 786440 | tf_op jit(solution)/shard_map/ppermute | solution.py:116
  235.5 18.4 %collective-permute-start.53 = (f32[2,32,1024]{2,1,0:T(8,128)S(1)}, f32[2,32,1024]{2,1,0:T(8,128)S(1)}, u32[]{:S(2)}, u32[]{:S(2)}) collective-permute-start(f32[2,32,1024]{2,1,0:T(8,128)S(1)} %get-tuple-element.156), channel_id=1, source_target_pairs={{0,6},{2,0},{4,2},{6,4},{1,7},{3,1},{5,3},{7,5},{8,14},{10,8},{12,... | collective-permute-start | bytes 786440 | tf_op jit(solution)/shard_map/ppermute | solution.py:116
  240.7 18.8 %collective-permute-start.64 = (f32[2,32,1024]{2,1,0:T(8,128)S(1)}, f32[2,32,1024]{2,1,0:T(8,128)S(1)}, u32[]{:S(2)}, u32[]{:S(2)}) collective-permute-start(f32[2,32,1024]{2,1,0:T(8,128)S(1)} %get-tuple-element.157), channel_id=1, source_target_pairs={{0,2},{2,4},{4,6},{6,0},{1,3},{3,5},{5,7},{7,1},{8,10},{10,12},{12... | collective-permute-start | bytes 786440 | tf_op jit(solution)/shard_map/ppermute | solution.py:116
  253.9 13.5 %collective-permute-start.51 = (f32[2,32,1024]{2,1,0:T(8,128)S(1)}, f32[2,32,1024]{2,1,0:T(8,128)S(1)}, u32[]{:S(2)}, u32[]{:S(2)}) collective-permute-start(f32[2,32,1024]{2,1,0:T(8,128)S(1)} %collective-permute-done.50), channel_id=1, source_target_pairs={{0,2},{2,4},{4,6},{6,0},{1,3},{3,5},{5,7},{7,1},{8,10},{10,12},{12... | collective-permute-start | bytes 786440 | tf_op jit(solution)/shard_map/ppermute | solution.py:116
  266.0 12.1 %collective-permute-start.34 = (f32[2,64,1024]{2,1,0:T(8,128)S(1)}, f32[2,64,1024]{2,1,0:T(8,128)S(1)}, u32[]{:S(2)}, u32[]{:S(2)}) collective-permute-start(f32[2,64,1024]{2,1,0:T(8,128)S(1)} %fusion.34), channel_id=1, source_target_pairs={{0,1},{1,0},{2,3},{3,2},{4,5},{5,4},{6,7},{7,6},{8,9},{9,8},{10,11... | collective-permute-start | bytes 1572872 | tf_op jit(solution)/shard_map/ppermute | solution.py:106
  267.4 12.4 %collective-permute-start.52 = (f32[2,32,1024]{2,1,0:T(8,128)S(1)}, f32[2,32,1024]{2,1,0:T(8,128)S(1)}, u32[]{:S(2)}, u32[]{:S(2)}) collective-permute-start(f32[2,32,1024]{2,1,0:T(8,128)S(1)} %collective-permute-done.51), channel_id=1, source_target_pairs={{0,2},{2,4},{4,6},{6,0},{1,3},{3,5},{5,7},{7,1},{8,10},{10,12},{12... | collective-permute-start | bytes 786440 | tf_op jit(solution)/shard_map/ppermute | solution.py:116
  267.4 12.4 %collective-permute-start.55 = (f32[2,32,1024]{2,1,0:T(8,128)S(1)}, f32[2,32,1024]{2,1,0:T(8,128)S(1)}, u32[]{:S(2)}, u32[]{:S(2)}) collective-permute-start(f32[2,32,1024]{2,1,0:T(8,128)S(1)} %collective-permute-done.54), channel_id=1, source_target_pairs={{0,6},{2,0},{4,2},{6,4},{1,7},{3,1},{5,3},{7,5},{8,14},{10,8},{12,... | collective-permute-start | bytes 786440 | tf_op jit(solution)/shard_map/ppermute | solution.py:116
  278.2 15.8 %collective-permute-start.35 = (f32[2,64,1024]{2,1,0:T(8,128)S(1)}, f32[2,64,1024]{2,1,0:T(8,128)S(1)}, u32[]{:S(2)}, u32[]{:S(2)}) collective-permute-start(f32[2,64,1024]{2,1,0:T(8,128)S(1)} %fusion.37), channel_id=1, source_target_pairs={{0,1},{1,0},{2,3},{3,2},{4,5},{5,4},{6,7},{7,6},{8,9},{9,8},{10,11... | collective-permute-start | bytes 1572872 | tf_op jit(solution)/shard_map/ppermute | solution.py:108
  294.2 14.7 %collective-permute-start.36 = (f32[2,64,1024]{2,1,0:T(8,128)S(1)}, f32[2,64,1024]{2,1,0:T(8,128)S(1)}, u32[]{:S(2)}, u32[]{:S(2)}) collective-permute-start(f32[2,64,1024]{2,1,0:T(8,128)S(1)} %get-tuple-element.144), channel_id=1, source_target_pairs={{0,2},{2,4},{4,6},{6,0},{1,3},{3,5},{5,7},{7,1},{8,10},{10,12},{12... | collective-permute-start | bytes 1572872 | tf_op jit(solution)/shard_map/ppermute | solution.py:116
  294.3 15.0 %collective-permute-start.39 = (f32[2,64,1024]{2,1,0:T(8,128)S(1)}, f32[2,64,1024]{2,1,0:T(8,128)S(1)}, u32[]{:S(2)}, u32[]{:S(2)}) collective-permute-start(f32[2,64,1024]{2,1,0:T(8,128)S(1)} %get-tuple-element.145), channel_id=1, source_target_pairs={{0,6},{2,0},{4,2},{6,4},{1,7},{3,1},{5,3},{7,5},{8,14},{10,8},{12,... | collective-permute-start | bytes 1572872 | tf_op jit(solution)/shard_map/ppermute | solution.py:116
  319.4 10.7 %collective-permute-start.41 = (f32[2,64,1024]{2,1,0:T(8,128)S(1)}, f32[2,64,1024]{2,1,0:T(8,128)S(1)}, u32[]{:S(2)}, u32[]{:S(2)}) collective-permute-start(f32[2,64,1024]{2,1,0:T(8,128)S(1)} %collective-permute-done.40), channel_id=1, source_target_pairs={{0,6},{2,0},{4,2},{6,4},{1,7},{3,1},{5,3},{7,5},{8,14},{10,8},{12,... | collective-permute-start | bytes 1572872 | tf_op jit(solution)/shard_map/ppermute | solution.py:116
  365.8 13.8 %collective-permute-start.98 = (f32[64,1024]{1,0:T(8,128)S(1)}, f32[64,1024]{1,0:T(8,128)S(1)}, u32[]{:S(2)}, u32[]{:S(2)}) collective-permute-start(f32[64,1024]{1,0:T(8,128)S(1)} %dynamic-slice_bitcast_fusion.3), channel_id=1, source_target_pairs={{0,16},{16,32},{32,48},{48,0},{1,17},{17,33},{33,49},{49,1},{2,18}... | collective-permute-start | bytes 786440 | tf_op jit(solution)/shard_map/ppermute | solution.py:140
  400.7 22.8 %collective-permute-start.104 = (f32[2,64,1024]{2,1,0:T(8,128)S(1)}, f32[2,64,1024]{2,1,0:T(8,128)S(1)}, u32[]{:S(2)}, u32[]{:S(2)}) collective-permute-start(f32[2,64,1024]{2,1,0:T(8,128)S(1)} %pad_maximum_fusion.12), channel_id=1, source_target_pairs={{0,8},{8,0},{1,9},{9,1},{2,10},{10,2},{3,11},{11,3},{4,12},{12,4},... | collective-permute-start | bytes 1572872 | tf_op jit(solution)/shard_map/ppermute | solution.py:145
  404.7 10.8 %collective-permute-start.76 = (f32[2,32,1024]{2,1,0:T(8,128)S(1)}, f32[2,32,1024]{2,1,0:T(8,128)S(1)}, u32[]{:S(2)}, u32[]{:S(2)}) collective-permute-start(f32[2,32,1024]{2,1,0:T(8,128)S(1)} %fusion.47), channel_id=1, source_target_pairs={{0,1},{1,0},{2,3},{3,2},{4,5},{5,4},{6,7},{7,6},{8,9},{9,8},{10,11... | collective-permute-start | bytes 786440 | tf_op jit(solution)/shard_map/ppermute | solution.py:106
  408.9 12.3 %collective-permute-start.90 = (f32[2,32,1024]{2,1,0:T(8,128)}, f32[2,32,1024]{2,1,0:T(8,128)S(1)}, u32[]{:S(2)}, u32[]{:S(2)}) collective-permute-start(f32[2,32,1024]{2,1,0:T(8,128)} %fusion.42), channel_id=1, source_target_pairs={{0,1},{1,0},{2,3},{3,2},{4,5},{5,4},{6,7},{7,6},{8,9},{9,8},{10,11... | collective-permute-start | bytes 786440 | tf_op jit(solution)/shard_map/ppermute | solution.py:106
  415.6 11.2 %collective-permute-start.77 = (f32[2,32,1024]{2,1,0:T(8,128)S(1)}, f32[2,32,1024]{2,1,0:T(8,128)S(1)}, u32[]{:S(2)}, u32[]{:S(2)}) collective-permute-start(f32[2,32,1024]{2,1,0:T(8,128)S(1)} %fusion.50), channel_id=1, source_target_pairs={{0,1},{1,0},{2,3},{3,2},{4,5},{5,4},{6,7},{7,6},{8,9},{9,8},{10,11... | collective-permute-start | bytes 786440 | tf_op jit(solution)/shard_map/ppermute | solution.py:108
  421.2 11.2 %collective-permute-start.91 = (f32[2,32,1024]{2,1,0:T(8,128)S(1)}, f32[2,32,1024]{2,1,0:T(8,128)S(1)}, u32[]{:S(2)}, u32[]{:S(2)}) collective-permute-start(f32[2,32,1024]{2,1,0:T(8,128)S(1)} %fusion.45), channel_id=1, source_target_pairs={{0,1},{1,0},{2,3},{3,2},{4,5},{5,4},{6,7},{7,6},{8,9},{9,8},{10,11... | collective-permute-start | bytes 786440 | tf_op jit(solution)/shard_map/ppermute | solution.py:108
  423.6 23.1 %collective-permute-start.105 = (f32[2,64,1024]{2,1,0:T(8,128)S(1)}, f32[2,64,1024]{2,1,0:T(8,128)S(1)}, u32[]{:S(2)}, u32[]{:S(2)}) collective-permute-start(f32[2,64,1024]{2,1,0:T(8,128)S(1)} %fusion.103), channel_id=1, source_target_pairs={{0,64},{64,0},{1,65},{65,1},{2,66},{66,2},{3,67},{67,3},{4,68},{68... | collective-permute-start | bytes 1572872 | tf_op jit(solution)/shard_map/ppermute | solution.py:145
  427.1 10.7 %collective-permute-start.81 = (f32[2,32,1024]{2,1,0:T(8,128)S(1)}, f32[2,32,1024]{2,1,0:T(8,128)S(1)}, u32[]{:S(2)}, u32[]{:S(2)}) collective-permute-start(f32[2,32,1024]{2,1,0:T(8,128)S(1)} %get-tuple-element.149), channel_id=1, source_target_pairs={{0,6},{2,0},{4,2},{6,4},{1,7},{3,1},{5,3},{7,5},{8,14},{10,8},{12,... | collective-permute-start | bytes 786440 | tf_op jit(solution)/shard_map/ppermute | solution.py:116
  437.5 11.3 %collective-permute-start.79 = (f32[2,32,1024]{2,1,0:T(8,128)S(1)}, f32[2,32,1024]{2,1,0:T(8,128)S(1)}, u32[]{:S(2)}, u32[]{:S(2)}) collective-permute-start(f32[2,32,1024]{2,1,0:T(8,128)S(1)} %collective-permute-done.78), channel_id=1, source_target_pairs={{0,2},{2,4},{4,6},{6,0},{1,3},{3,5},{5,7},{7,1},{8,10},{10,12},{12... | collective-permute-start | bytes 786440 | tf_op jit(solution)/shard_map/ppermute | solution.py:116
  437.7 12.8 %collective-permute-start.82 = (f32[2,32,1024]{2,1,0:T(8,128)S(1)}, f32[2,32,1024]{2,1,0:T(8,128)S(1)}, u32[]{:S(2)}, u32[]{:S(2)}) collective-permute-start(f32[2,32,1024]{2,1,0:T(8,128)S(1)} %collective-permute-done.81), channel_id=1, source_target_pairs={{0,6},{2,0},{4,2},{6,4},{1,7},{3,1},{5,3},{7,5},{8,14},{10,8},{12,... | collective-permute-start | bytes 786440 | tf_op jit(solution)/shard_map/ppermute | solution.py:116
  443.1 11.2 %collective-permute-start.93 = (f32[2,32,1024]{2,1,0:T(8,128)S(1)}, f32[2,32,1024]{2,1,0:T(8,128)S(1)}, u32[]{:S(2)}, u32[]{:S(2)}) collective-permute-start(f32[2,32,1024]{2,1,0:T(8,128)S(1)} %collective-permute-done.92), channel_id=1, source_target_pairs={{0,2},{2,4},{4,6},{6,0},{1,3},{3,5},{5,7},{7,1},{8,10},{10,12},{12... | collective-permute-start | bytes 786440 | tf_op jit(solution)/shard_map/ppermute | solution.py:116
  443.2 11.3 %collective-permute-start.96 = (f32[2,32,1024]{2,1,0:T(8,128)S(1)}, f32[2,32,1024]{2,1,0:T(8,128)S(1)}, u32[]{:S(2)}, u32[]{:S(2)}) collective-permute-start(f32[2,32,1024]{2,1,0:T(8,128)S(1)} %collective-permute-done.95), channel_id=1, source_target_pairs={{0,6},{2,0},{4,2},{6,4},{1,7},{3,1},{5,3},{7,5},{8,14},{10,8},{12,... | collective-permute-start | bytes 786440 | tf_op jit(solution)/shard_map/ppermute | solution.py:116
  446.8 20.4 %collective-permute-start.106 = (f32[64,1024]{1,0:T(8,128)S(1)}, f32[64,1024]{1,0:T(8,128)S(1)}, u32[]{:S(2)}, u32[]{:S(2)}) collective-permute-start(f32[64,1024]{1,0:T(8,128)S(1)} %get-tuple-element.146), channel_id=1, source_target_pairs={{0,16},{16,32},{32,48},{48,0},{1,17},{17,33},{33,49},{49,1},{2,18}... | collective-permute-start | bytes 786440 | tf_op jit(solution)/shard_map/ppermute | solution.py:152
  448.8 18.6 %collective-permute-start.109 = (f32[64,1024]{1,0:T(8,128)S(1)}, f32[64,1024]{1,0:T(8,128)S(1)}, u32[]{:S(2)}, u32[]{:S(2)}) collective-permute-start(f32[64,1024]{1,0:T(8,128)S(1)} %get-tuple-element.147), channel_id=1, source_target_pairs={{0,48},{16,0},{32,16},{48,32},{1,49},{17,1},{33,17},{49,33},{2,50}... | collective-permute-start | bytes 786440 | tf_op jit(solution)/shard_map/ppermute | solution.py:152
  (154 other events, 1147.7 us)
Sparse Core Ops, SparseCore 0:
  180.2 156.3 all-reduce.4

commit v10 on v8

--- a/solution.py
+++ b/solution.py
@@ -257,7 +257,7 @@
         ((down_grad, gate_w_grad, up_w_grad), inner(gate_grad, w_gate) + inner(up_grad, w_up))
     )
     ffn_w_grads = lax.psum(ffn_w_grads, DP)
-    normed_two_grad = split_tensor_sum(two_partial)
+    normed_two_grad = tensor_sum(two_partial)
     ffn_grad = jnp.sum(normed_two_grad * residual * scale_two, axis=0)
     residual_grad = cotangent.astype(jnp.float32) + rms_back(
         normed_two_grad, residual, scale_two, ffn_gain

time: 527 us -> 554 us (1.051)
  waiting for transfers between devices: 167 us -> 213 us
  starting transfers between devices: 175 us -> 159 us
    ppermute x42 -> x36, waiting for transfers between devices: 31.5 us -> 62.1 us  [tensor_sum(): acc = lax.ppermute(acc, 'ty', ring(ny, shift))]
    psum x1, waiting for transfers between devices: 0.02 us -> 17.9 us  [per_device(): ffn_w_grads = lax.psum(ffn_w_grads, DP)]
    ppermute x42 -> x36, starting transfers between devices: 59.9 us -> 52 us  [tensor_sum(): cur = lax.ppermute(cur, 'ty', ring(ny, shift))]
    ppermute x42 -> x36, starting transfers between devices: 61.5 us -> 55 us  [tensor_sum(): acc = lax.ppermute(acc, 'ty', ring(ny, shift))]
    add x28 -> x24, other arithmetic: 11.7 us -> 8.39 us  [tensor_sum(): acc + lax.dynamic_index_in_dim(chunks, (y - shift * (1 + step)) % ny, 0,...]
    squeeze x14 -> x12, local copies, waits for them, and re-layouts: 11.5 us -> 8.58 us  [tensor_sum(): acc = lax.dynamic_index_in_dim(chunks, (y - shift) % ny, 0, keepdims=False)]
    ppermute x7 -> x6, waiting for transfers between devices: 19.9 us -> 22.2 us  [tensor_sum(): got = lax.ppermute(send, 'tx', pairs)]
    ppermute x7 -> x6, starting transfers between devices: 15.4 us -> 17.4 us  [tensor_sum(): got = lax.ppermute(send, 'tx', pairs)]
  transfers between devices with their start and end apart: 118 -> 104, of which waited for: 62 -> 58; matrix products, arithmetic and copies ran while one was open for 17% -> 15% of each run, Pallas kernels for 0% -> 0%
where the time goes in v10:
time: 554 us; the launch traced here: 544 us
  waiting for transfers between devices  213 us (38%)
  starting transfers between devices  159 us (29%)
  other arithmetic  58.5 us (11%)
  matrix products  50.3 us (9%)
  local copies, waits for them, and re-layouts  46.2 us (8%)
  between operations  16.9 us (3%)
    ppermute x36, waiting for transfers between devices, tensor_sum(): cur = lax.ppermute(cur, 'ty', ring(ny, shift))  75.2 us
    ppermute x36, waiting for transfers between devices, tensor_sum(): acc = lax.ppermute(acc, 'ty', ring(ny, shift))  62.1 us
    ppermute x36, starting transfers between devices, tensor_sum(): acc = lax.ppermute(acc, 'ty', ring(ny, shift))  55 us
    ppermute x36, starting transfers between devices, tensor_sum(): cur = lax.ppermute(cur, 'ty', ring(ny, shift))  52 us
    ppermute x6, waiting for transfers between devices, tensor_sum(): got = lax.ppermute(send, 'tx', pairs)  22.2 us
    unnamed x163, local copies, waits for them, and re-layouts  20.2 us
    psum x1, waiting for transfers between devices, per_device(): ffn_w_grads = lax.psum(ffn_w_grads, DP)  17.9 us
    ppermute x6, waiting for transfers between devices, tensor_sum(): other = lax.ppermute(mine, 'tx', pairs)  17.8 us
  transfers between devices with their start and end apart: 104, of which 58 were waited for; matrix products, arithmetic and copies ran while one was open for 15% of the time, Pallas kernels for 0%

profile of v10, /device:TPU:0, one launch (start us, length us, event | category | flops | bytes accessed | tf_op | source)
XLA Modules:
  0.0 544.1 jit_solution(12913458285852658534)
XLA Ops:
  46.7 3.4 collective-permute-start.17
  53.1 3.3 collective-permute-start.4
  68.2 3.8 collective-permute-start.19
  75.0 4.0 collective-permute-done.2
  91.3 3.5 collective-permute-done.20
  105.8 3.3 collective-permute-start.25
  112.3 3.3 collective-permute-start.12
  117.9 3.3 collective-permute-start.26
  123.5 3.3 collective-permute-start.13
  129.2 3.7 collective-permute-start.27
  133.4 3.3 collective-permute-done.24
  146.6 3.9 fusion.117
  165.6 4.4 convolution_add_fusion
  179.7 6.6 %collective-permute-done.45 = f32[2,64,1024]{2,1,0:T(8,128)S(1)} collective-permute-done((f32[2,64,1024]{2,1,0:T(8,128)S(1)}, f32[2,64,1024]{2,1,0:T(8,128)S(1)}, u32[]{:S(2)}, u32[]{:S(2)}) %collective-permute-start.45) | collective-permute-done | bytes 524320 | tf_op jit(solution)/shard_map/ppermute | solution.py:96
  186.4 3.8 collective-permute-start.46
  190.3 7.2 %collective-permute-done.32 = f32[2,64,1024]{2,1,0:T(8,128)S(1)} collective-permute-done((f32[2,64,1024]{2,1,0:T(8,128)S(1)}, f32[2,64,1024]{2,1,0:T(8,128)S(1)}, u32[]{:S(2)}, u32[]{:S(2)}) %collective-permute-start.32) | collective-permute-done | bytes 524320 | tf_op jit(solution)/shard_map/ppermute | solution.py:96
  197.6 3.8 collective-permute-start.33
  201.6 7.2 %collective-permute-done.46 = f32[2,64,1024]{2,1,0:T(8,128)S(1)} collective-permute-done((f32[2,64,1024]{2,1,0:T(8,128)S(1)}, f32[2,64,1024]{2,1,0:T(8,128)S(1)}, u32[]{:S(2)}, u32[]{:S(2)}) %collective-permute-start.46) | collective-permute-done | bytes 524320 | tf_op jit(solution)/shard_map/ppermute | solution.py:96
  208.9 3.8 collective-permute-start.47
  212.8 6.5 %collective-permute-done.33 = f32[2,64,1024]{2,1,0:T(8,128)S(1)} collective-permute-done((f32[2,64,1024]{2,1,0:T(8,128)S(1)}, f32[2,64,1024]{2,1,0:T(8,128)S(1)}, u32[]{:S(2)}, u32[]{:S(2)}) %collective-permute-start.33) | collective-permute-done | bytes 524320 | tf_op jit(solution)/shard_map/ppermute | solution.py:96
  219.4 4.5 collective-permute-done.30
  233.5 6.6 %collective-permute-done.34 = f32[2,64,1024]{2,1,0:T(8,128)S(1)} collective-permute-done((f32[2,64,1024]{2,1,0:T(8,128)S(1)}, f32[2,64,1024]{2,1,0:T(8,128)S(1)}, u32[]{:S(2)}, u32[]{:S(2)}) %collective-permute-start.34) | collective-permute-done | bytes 524320 | tf_op jit(solution)/shard_map/ppermute | solution.py:106
  244.0 7.4 %collective-permute-done.48 = f32[2,64,1024]{2,1,0:T(8,128)} collective-permute-done((f32[2,64,1024]{2,1,0:T(8,128)}, f32[2,64,1024]{2,1,0:T(8,128)}, u32[]{:S(2)}, u32[]{:S(2)}) %collective-permute-start.48) | collective-permute-done | bytes 524320 | tf_op jit(solution)/shard_map/ppermute | solution.py:106
  255.7 11.3 %collective-permute-done.35 = f32[2,64,1024]{2,1,0:T(8,128)} collective-permute-done((f32[2,64,1024]{2,1,0:T(8,128)}, f32[2,64,1024]{2,1,0:T(8,128)}, u32[]{:S(2)}, u32[]{:S(2)}) %collective-permute-start.35) | collective-permute-done | bytes 524320 | tf_op jit(solution)/shard_map/ppermute | solution.py:108
  272.5 3.7 collective-permute-done.49
  276.8 3.3 collective-permute-start.53
  280.7 4.3 collective-permute-done.36
  288.5 7.8 %collective-permute-done.50 = f32[2,64,1024]{2,1,0:T(8,128)S(1)} collective-permute-done((f32[2,64,1024]{2,1,0:T(8,128)S(1)}, f32[2,64,1024]{2,1,0:T(8,128)S(1)}, u32[]{:S(2)}, u32[]{:S(2)}) %collective-permute-start.50) | collective-permute-done | bytes 524320 | tf_op jit(solution)/shard_map/ppermute | solution.py:116
  296.4 3.3 collective-permute-start.54
  299.8 7.7 %collective-permute-done.37 = f32[2,64,1024]{2,1,0:T(8,128)S(1)} collective-permute-done((f32[2,64,1024]{2,1,0:T(8,128)S(1)}, f32[2,64,1024]{2,1,0:T(8,128)S(1)}, u32[]{:S(2)}, u32[]{:S(2)}) %collective-permute-start.37) | collective-permute-done | bytes 524320 | tf_op jit(solution)/shard_map/ppermute | solution.py:116
  310.8 8.0 %collective-permute-done.51 = f32[2,64,1024]{2,1,0:T(8,128)S(1)} collective-permute-done((f32[2,64,1024]{2,1,0:T(8,128)S(1)}, f32[2,64,1024]{2,1,0:T(8,128)S(1)}, u32[]{:S(2)}, u32[]{:S(2)}) %collective-permute-start.51) | collective-permute-done | bytes 524320 | tf_op jit(solution)/shard_map/ppermute | solution.py:116
  318.9 3.3 collective-permute-start.55
  322.3 11.3 %collective-permute-done.52 = f32[2,64,1024]{2,1,0:T(8,128)S(1)} collective-permute-done((f32[2,64,1024]{2,1,0:T(8,128)S(1)}, f32[2,64,1024]{2,1,0:T(8,128)S(1)}, u32[]{:S(2)}, u32[]{:S(2)}) %collective-permute-start.52) | collective-permute-done | bytes 524320 | tf_op jit(solution)/shard_map/ppermute | solution.py:116
  347.3 3.3 fusion.18
  361.5 3.3 fusion.17
  371.8 17.9 %all-reduce.5.cloned.1.call-done = (f32[576,1024]{1,0:T(8,128)}, f32[1024,576]{0,1:T(8,128)}, f32[1024,576]{0,1:T(8,128)}) async-done(((f32[576,1024]{1,0:T(8,128)}, f32[1024,576]{0,1:T(8,128)}, f32[1024,576]{0,1:T(8,128)}), (f32[576,1024]{1,0:T(8,128)}, f32[1024,576]{0,1:T(8,128)}, f32[1024,576]{0,1:T(8,128)})) %all-reduce.5.cloned.1.call-update) | async-done | bytes 7077904 | tf_op jit(solution)/shard_map/psum | solution.py:259
  406.8 3.7 collective-permute-done.56
  419.6 3.6 collective-permute-done.57
  431.5 4.0 collective-permute-done.58
  442.4 3.9 collective-permute-done.62
  447.3 5.0 collective-permute-done.91
  457.0 3.8 collective-permute-done.92
  473.4 3.7 collective-permute-done.78
  491.2 4.2 collective-permute-done.66
  503.1 3.3 collective-permute-start.99
  506.4 4.2 collective-permute-done.96
  511.1 3.6 collective-permute-done.100
  529.5 3.5 copy.117
  (580 shorter events, 288.4 us)
Async XLA Ops:
  7.2 382.5 %all-reduce.5.cloned.1.call-start = ((), (), s32[]{:S(2)}) async-start(), calls=%async_computation | async-start | bytes 14155776 | tf_op jit(solution)/shard_map/psum | solution.py:259
  40.3 11.6 %collective-permute-start.3 = (f32[2,32,1024]{2,1,0:T(8,128)}, f32[2,32,1024]{2,1,0:T(8,128)}, u32[]{:S(2)}, u32[]{:S(2)}) collective-permute-start(f32[2,32,1024]{2,1,0:T(8,128)} %dynamic-slice_bitcast_fusion.12), channel_id=1, source_target_pairs={{0,6},{2,0},{4,2},{6,4},{1,7},{3,1},{5,3},{7,5},{8,14},{10,8},{12,... | collective-permute-start | bytes 786440 | tf_op jit(solution)/shard_map/ppermute | solution.py:96
  67.5 11.5 %collective-permute-start.2 = (f32[2,32,1024]{2,1,0:T(8,128)S(1)}, f32[2,32,1024]{2,1,0:T(8,128)S(1)}, u32[]{:S(2)}, u32[]{:S(2)}) collective-permute-start(f32[2,32,1024]{2,1,0:T(8,128)S(1)} %bitcast_add_fusion.41), channel_id=1, source_target_pairs={{0,2},{2,4},{4,6},{6,0},{1,3},{3,5},{5,7},{7,1},{8,10},{10,12},{12... | collective-permute-start | bytes 786440 | tf_op jit(solution)/shard_map/ppermute | solution.py:96
  68.2 13.9 %collective-permute-start.19 = (f32[2,32,1024]{2,1,0:T(8,128)S(1)}, f32[2,32,1024]{2,1,0:T(8,128)S(1)}, u32[]{:S(2)}, u32[]{:S(2)}) collective-permute-start(f32[2,32,1024]{2,1,0:T(8,128)S(1)} %bitcast_add_fusion.32), channel_id=1, source_target_pairs={{0,6},{2,0},{4,2},{6,4},{1,7},{3,1},{5,3},{7,5},{8,14},{10,8},{12,... | collective-permute-start | bytes 786440 | tf_op jit(solution)/shard_map/ppermute | solution.py:96
  88.2 12.2 %collective-permute-start.7 = (f32[2,32,1024]{2,1,0:T(8,128)}, f32[2,32,1024]{2,1,0:T(8,128)}, u32[]{:S(2)}, u32[]{:S(2)}) collective-permute-start(f32[2,32,1024]{2,1,0:T(8,128)} %fusion.74), channel_id=1, source_target_pairs={{0,1},{1,0},{2,3},{3,2},{4,5},{5,4},{6,7},{7,6},{8,9},{9,8},{10,11... | collective-permute-start | bytes 786440 | tf_op jit(solution)/shard_map/ppermute | solution.py:108
  105.6 12.3 %collective-permute-start.22 = (f32[2,32,1024]{2,1,0:T(8,128)S(1)}, f32[2,32,1024]{2,1,0:T(8,128)S(1)}, u32[]{:S(2)}, u32[]{:S(2)}) collective-permute-start(f32[2,32,1024]{2,1,0:T(8,128)S(1)} %get-tuple-element.170), channel_id=1, source_target_pairs={{0,2},{2,4},{4,6},{6,0},{1,3},{3,5},{5,7},{7,1},{8,10},{10,12},{12... | collective-permute-start | bytes 786440 | tf_op jit(solution)/shard_map/ppermute | solution.py:116
  105.8 12.1 %collective-permute-start.25 = (f32[2,32,1024]{2,1,0:T(8,128)S(1)}, f32[2,32,1024]{2,1,0:T(8,128)S(1)}, u32[]{:S(2)}, u32[]{:S(2)}) collective-permute-start(f32[2,32,1024]{2,1,0:T(8,128)S(1)} %get-tuple-element.171), channel_id=1, source_target_pairs={{0,6},{2,0},{4,2},{6,4},{1,7},{3,1},{5,3},{7,5},{8,14},{10,8},{12,... | collective-permute-start | bytes 786440 | tf_op jit(solution)/shard_map/ppermute | solution.py:116
  159.4 14.7 %collective-permute-start.31 = (f32[2,64,1024]{2,1,0:T(8,128)}, f32[2,64,1024]{2,1,0:T(8,128)}, u32[]{:S(2)}, u32[]{:S(2)}) collective-permute-start(f32[2,64,1024]{2,1,0:T(8,128)} %dynamic-slice_bitcast_fusion.2), channel_id=1, source_target_pairs={{0,6},{2,0},{4,2},{6,4},{1,7},{3,1},{5,3},{7,5},{8,14},{10,8},{12,... | collective-permute-start | bytes 1572872 | tf_op jit(solution)/shard_map/ppermute | solution.py:96
  162.6 15.9 %collective-permute-start.28 = (f32[2,64,1024]{2,1,0:T(8,128)}, f32[2,64,1024]{2,1,0:T(8,128)}, u32[]{:S(2)}, u32[]{:S(2)}) collective-permute-start(f32[2,64,1024]{2,1,0:T(8,128)} %dynamic-slice_bitcast_fusion.3), channel_id=1, source_target_pairs={{0,2},{2,4},{4,6},{6,0},{1,3},{3,5},{5,7},{7,1},{8,10},{10,12},{12... | collective-permute-start | bytes 1572872 | tf_op jit(solution)/shard_map/ppermute | solution.py:96
  170.7 15.7 %collective-permute-start.45 = (f32[2,64,1024]{2,1,0:T(8,128)S(1)}, f32[2,64,1024]{2,1,0:T(8,128)S(1)}, u32[]{:S(2)}, u32[]{:S(2)}) collective-permute-start(f32[2,64,1024]{2,1,0:T(8,128)S(1)} %dynamic-slice_bitcast_fusion), channel_id=1, source_target_pairs={{0,6},{2,0},{4,2},{6,4},{1,7},{3,1},{5,3},{7,5},{8,14},{10,8},{12,... | collective-permute-start | bytes 1572872 | tf_op jit(solution)/shard_map/ppermute | solution.py:96
  174.0 16.2 %collective-permute-start.42 = (f32[2,64,1024]{2,1,0:T(8,128)S(1)}, f32[2,64,1024]{2,1,0:T(8,128)S(1)}, u32[]{:S(2)}, u32[]{:S(2)}) collective-permute-start(f32[2,64,1024]{2,1,0:T(8,128)S(1)} %dynamic-slice_bitcast_fusion.1), channel_id=1, source_target_pairs={{0,2},{2,4},{4,6},{6,0},{1,3},{3,5},{5,7},{7,1},{8,10},{10,12},{12... | collective-permute-start | bytes 1572872 | tf_op jit(solution)/shard_map/ppermute | solution.py:96
  175.2 22.4 %collective-permute-start.32 = (f32[2,64,1024]{2,1,0:T(8,128)S(1)}, f32[2,64,1024]{2,1,0:T(8,128)S(1)}, u32[]{:S(2)}, u32[]{:S(2)}) collective-permute-start(f32[2,64,1024]{2,1,0:T(8,128)S(1)} %bitcast_add_fusion.9), channel_id=1, source_target_pairs={{0,6},{2,0},{4,2},{6,4},{1,7},{3,1},{5,3},{7,5},{8,14},{10,8},{12,... | collective-permute-start | bytes 1572872 | tf_op jit(solution)/shard_map/ppermute | solution.py:96
  179.6 21.8 %collective-permute-start.29 = (f32[2,64,1024]{2,1,0:T(8,128)S(1)}, f32[2,64,1024]{2,1,0:T(8,128)S(1)}, u32[]{:S(2)}, u32[]{:S(2)}) collective-permute-start(f32[2,64,1024]{2,1,0:T(8,128)S(1)} %bitcast_add_fusion.12), channel_id=1, source_target_pairs={{0,2},{2,4},{4,6},{6,0},{1,3},{3,5},{5,7},{7,1},{8,10},{10,12},{12... | collective-permute-start | bytes 1572872 | tf_op jit(solution)/shard_map/ppermute | solution.py:96
  186.4 22.4 %collective-permute-start.46 = (f32[2,64,1024]{2,1,0:T(8,128)S(1)}, f32[2,64,1024]{2,1,0:T(8,128)S(1)}, u32[]{:S(2)}, u32[]{:S(2)}) collective-permute-start(f32[2,64,1024]{2,1,0:T(8,128)S(1)} %bitcast_add_fusion.3), channel_id=1, source_target_pairs={{0,6},{2,0},{4,2},{6,4},{1,7},{3,1},{5,3},{7,5},{8,14},{10,8},{12,... | collective-permute-start | bytes 1572872 | tf_op jit(solution)/shard_map/ppermute | solution.py:96
  190.2 22.4 %collective-permute-start.43 = (f32[2,64,1024]{2,1,0:T(8,128)S(1)}, f32[2,64,1024]{2,1,0:T(8,128)S(1)}, u32[]{:S(2)}, u32[]{:S(2)}) collective-permute-start(f32[2,64,1024]{2,1,0:T(8,128)S(1)} %bitcast_add_fusion.6), channel_id=1, source_target_pairs={{0,2},{2,4},{4,6},{6,0},{1,3},{3,5},{5,7},{7,1},{8,10},{10,12},{12... | collective-permute-start | bytes 1572872 | tf_op jit(solution)/shard_map/ppermute | solution.py:96
  197.6 21.7 %collective-permute-start.33 = (f32[2,64,1024]{2,1,0:T(8,128)S(1)}, f32[2,64,1024]{2,1,0:T(8,128)S(1)}, u32[]{:S(2)}, u32[]{:S(2)}) collective-permute-start(f32[2,64,1024]{2,1,0:T(8,128)S(1)} %bitcast_add_fusion.8), channel_id=1, source_target_pairs={{0,6},{2,0},{4,2},{6,4},{1,7},{3,1},{5,3},{7,5},{8,14},{10,8},{12,... | collective-permute-start | bytes 1572872 | tf_op jit(solution)/shard_map/ppermute | solution.py:96
  201.5 22.4 %collective-permute-start.30 = (f32[2,64,1024]{2,1,0:T(8,128)S(1)}, f32[2,64,1024]{2,1,0:T(8,128)S(1)}, u32[]{:S(2)}, u32[]{:S(2)}) collective-permute-start(f32[2,64,1024]{2,1,0:T(8,128)S(1)} %bitcast_add_fusion.11), channel_id=1, source_target_pairs={{0,2},{2,4},{4,6},{6,0},{1,3},{3,5},{5,7},{7,1},{8,10},{10,12},{12... | collective-permute-start | bytes 1572872 | tf_op jit(solution)/shard_map/ppermute | solution.py:96
  208.9 18.2 %collective-permute-start.47 = (f32[2,64,1024]{2,1,0:T(8,128)S(1)}, f32[2,64,1024]{2,1,0:T(8,128)S(1)}, u32[]{:S(2)}, u32[]{:S(2)}) collective-permute-start(f32[2,64,1024]{2,1,0:T(8,128)S(1)} %bitcast_add_fusion.2), channel_id=1, source_target_pairs={{0,6},{2,0},{4,2},{6,4},{1,7},{3,1},{5,3},{7,5},{8,14},{10,8},{12,... | collective-permute-start | bytes 1572872 | tf_op jit(solution)/shard_map/ppermute | solution.py:96
  212.7 16.8 %collective-permute-start.44 = (f32[2,64,1024]{2,1,0:T(8,128)S(1)}, f32[2,64,1024]{2,1,0:T(8,128)S(1)}, u32[]{:S(2)}, u32[]{:S(2)}) collective-permute-start(f32[2,64,1024]{2,1,0:T(8,128)S(1)} %bitcast_add_fusion.5), channel_id=1, source_target_pairs={{0,2},{2,4},{4,6},{6,0},{1,3},{3,5},{5,7},{7,1},{8,10},{10,12},{12... | collective-permute-start | bytes 1572872 | tf_op jit(solution)/shard_map/ppermute | solution.py:96
  224.0 16.1 %collective-permute-start.34 = (f32[2,64,1024]{2,1,0:T(8,128)S(1)}, f32[2,64,1024]{2,1,0:T(8,128)S(1)}, u32[]{:S(2)}, u32[]{:S(2)}) collective-permute-start(f32[2,64,1024]{2,1,0:T(8,128)S(1)} %fusion.41), channel_id=1, source_target_pairs={{0,1},{1,0},{2,3},{3,2},{4,5},{5,4},{6,7},{7,6},{8,9},{9,8},{10,11... | collective-permute-start | bytes 1572872 | tf_op jit(solution)/shard_map/ppermute | solution.py:106
  230.5 21.0 %collective-permute-start.48 = (f32[2,64,1024]{2,1,0:T(8,128)}, f32[2,64,1024]{2,1,0:T(8,128)}, u32[]{:S(2)}, u32[]{:S(2)}) collective-permute-start(f32[2,64,1024]{2,1,0:T(8,128)} %fusion.36), channel_id=1, source_target_pairs={{0,1},{1,0},{2,3},{3,2},{4,5},{5,4},{6,7},{7,6},{8,9},{9,8},{10,11... | collective-permute-start | bytes 1572872 | tf_op jit(solution)/shard_map/ppermute | solution.py:106
  241.0 26.0 %collective-permute-start.35 = (f32[2,64,1024]{2,1,0:T(8,128)}, f32[2,64,1024]{2,1,0:T(8,128)}, u32[]{:S(2)}, u32[]{:S(2)}) collective-permute-start(f32[2,64,1024]{2,1,0:T(8,128)} %fusion.44), channel_id=1, source_target_pairs={{0,1},{1,0},{2,3},{3,2},{4,5},{5,4},{6,7},{7,6},{8,9},{9,8},{10,11... | collective-permute-start | bytes 1572872 | tf_op jit(solution)/shard_map/ppermute | solution.py:108
  252.6 23.6 %collective-permute-start.49 = (f32[2,64,1024]{2,1,0:T(8,128)S(1)}, f32[2,64,1024]{2,1,0:T(8,128)S(1)}, u32[]{:S(2)}, u32[]{:S(2)}) collective-permute-start(f32[2,64,1024]{2,1,0:T(8,128)S(1)} %fusion.39), channel_id=1, source_target_pairs={{0,1},{1,0},{2,3},{3,2},{4,5},{5,4},{6,7},{7,6},{8,9},{9,8},{10,11... | collective-permute-start | bytes 1572872 | tf_op jit(solution)/shard_map/ppermute | solution.py:108
  268.9 16.1 %collective-permute-start.36 = (f32[2,64,1024]{2,1,0:T(8,128)S(1)}, f32[2,64,1024]{2,1,0:T(8,128)S(1)}, u32[]{:S(2)}, u32[]{:S(2)}) collective-permute-start(f32[2,64,1024]{2,1,0:T(8,128)S(1)} %get-tuple-element.157), channel_id=1, source_target_pairs={{0,2},{2,4},{4,6},{6,0},{1,3},{3,5},{5,7},{7,1},{8,10},{10,12},{12... | collective-permute-start | bytes 1572872 | tf_op jit(solution)/shard_map/ppermute | solution.py:116
  269.0 16.3 %collective-permute-start.39 = (f32[2,64,1024]{2,1,0:T(8,128)S(1)}, f32[2,64,1024]{2,1,0:T(8,128)S(1)}, u32[]{:S(2)}, u32[]{:S(2)}) collective-permute-start(f32[2,64,1024]{2,1,0:T(8,128)S(1)} %get-tuple-element.158), channel_id=1, source_target_pairs={{0,6},{2,0},{4,2},{6,4},{1,7},{3,1},{5,3},{7,5},{8,14},{10,8},{12,... | collective-permute-start | bytes 1572872 | tf_op jit(solution)/shard_map/ppermute | solution.py:116
  276.4 19.9 %collective-permute-start.50 = (f32[2,64,1024]{2,1,0:T(8,128)S(1)}, f32[2,64,1024]{2,1,0:T(8,128)S(1)}, u32[]{:S(2)}, u32[]{:S(2)}) collective-permute-start(f32[2,64,1024]{2,1,0:T(8,128)S(1)} %get-tuple-element.155), channel_id=1, source_target_pairs={{0,2},{2,4},{4,6},{6,0},{1,3},{3,5},{5,7},{7,1},{8,10},{10,12},{12... | collective-permute-start | bytes 1572872 | tf_op jit(solution)/shard_map/ppermute | solution.py:116
  276.8 19.6 %collective-permute-start.53 = (f32[2,64,1024]{2,1,0:T(8,128)S(1)}, f32[2,64,1024]{2,1,0:T(8,128)S(1)}, u32[]{:S(2)}, u32[]{:S(2)}) collective-permute-start(f32[2,64,1024]{2,1,0:T(8,128)S(1)} %get-tuple-element.156), channel_id=1, source_target_pairs={{0,6},{2,0},{4,2},{6,4},{1,7},{3,1},{5,3},{7,5},{8,14},{10,8},{12,... | collective-permute-start | bytes 1572872 | tf_op jit(solution)/shard_map/ppermute | solution.py:116
  285.0 22.5 %collective-permute-start.37 = (f32[2,64,1024]{2,1,0:T(8,128)S(1)}, f32[2,64,1024]{2,1,0:T(8,128)S(1)}, u32[]{:S(2)}, u32[]{:S(2)}) collective-permute-start(f32[2,64,1024]{2,1,0:T(8,128)S(1)} %collective-permute-done.36), channel_id=1, source_target_pairs={{0,2},{2,4},{4,6},{6,0},{1,3},{3,5},{5,7},{7,1},{8,10},{10,12},{12... | collective-permute-start | bytes 1572872 | tf_op jit(solution)/shard_map/ppermute | solution.py:116
  285.3 22.3 %collective-permute-start.40 = (f32[2,64,1024]{2,1,0:T(8,128)S(1)}, f32[2,64,1024]{2,1,0:T(8,128)S(1)}, u32[]{:S(2)}, u32[]{:S(2)}) collective-permute-start(f32[2,64,1024]{2,1,0:T(8,128)S(1)} %collective-permute-done.39), channel_id=1, source_target_pairs={{0,6},{2,0},{4,2},{6,4},{1,7},{3,1},{5,3},{7,5},{8,14},{10,8},{12,... | collective-permute-start | bytes 1572872 | tf_op jit(solution)/shard_map/ppermute | solution.py:116
  296.3 22.5 %collective-permute-start.51 = (f32[2,64,1024]{2,1,0:T(8,128)S(1)}, f32[2,64,1024]{2,1,0:T(8,128)S(1)}, u32[]{:S(2)}, u32[]{:S(2)}) collective-permute-start(f32[2,64,1024]{2,1,0:T(8,128)S(1)} %collective-permute-done.50), channel_id=1, source_target_pairs={{0,2},{2,4},{4,6},{6,0},{1,3},{3,5},{5,7},{7,1},{8,10},{10,12},{12... | collective-permute-start | bytes 1572872 | tf_op jit(solution)/shard_map/ppermute | solution.py:116
  296.4 22.5 %collective-permute-start.54 = (f32[2,64,1024]{2,1,0:T(8,128)S(1)}, f32[2,64,1024]{2,1,0:T(8,128)S(1)}, u32[]{:S(2)}, u32[]{:S(2)}) collective-permute-start(f32[2,64,1024]{2,1,0:T(8,128)S(1)} %collective-permute-done.53), channel_id=1, source_target_pairs={{0,6},{2,0},{4,2},{6,4},{1,7},{3,1},{5,3},{7,5},{8,14},{10,8},{12,... | collective-permute-start | bytes 1572872 | tf_op jit(solution)/shard_map/ppermute | solution.py:116
  307.5 29.7 %collective-permute-start.38 = (f32[2,64,1024]{2,1,0:T(8,128)S(1)}, f32[2,64,1024]{2,1,0:T(8,128)S(1)}, u32[]{:S(2)}, u32[]{:S(2)}) collective-permute-start(f32[2,64,1024]{2,1,0:T(8,128)S(1)} %collective-permute-done.37), channel_id=1, source_target_pairs={{0,2},{2,4},{4,6},{6,0},{1,3},{3,5},{5,7},{7,1},{8,10},{10,12},{12... | collective-permute-start | bytes 1572872 | tf_op jit(solution)/shard_map/ppermute | solution.py:116
  307.5 29.8 %collective-permute-start.41 = (f32[2,64,1024]{2,1,0:T(8,128)S(1)}, f32[2,64,1024]{2,1,0:T(8,128)S(1)}, u32[]{:S(2)}, u32[]{:S(2)}) collective-permute-start(f32[2,64,1024]{2,1,0:T(8,128)S(1)} %collective-permute-done.40), channel_id=1, source_target_pairs={{0,6},{2,0},{4,2},{6,4},{1,7},{3,1},{5,3},{7,5},{8,14},{10,8},{12,... | collective-permute-start | bytes 1572872 | tf_op jit(solution)/shard_map/ppermute | solution.py:116
  318.8 14.8 %collective-permute-start.52 = (f32[2,64,1024]{2,1,0:T(8,128)S(1)}, f32[2,64,1024]{2,1,0:T(8,128)S(1)}, u32[]{:S(2)}, u32[]{:S(2)}) collective-permute-start(f32[2,64,1024]{2,1,0:T(8,128)S(1)} %collective-permute-done.51), channel_id=1, source_target_pairs={{0,2},{2,4},{4,6},{6,0},{1,3},{3,5},{5,7},{7,1},{8,10},{10,12},{12... | collective-permute-start | bytes 1572872 | tf_op jit(solution)/shard_map/ppermute | solution.py:116
  318.9 14.7 %collective-permute-start.55 = (f32[2,64,1024]{2,1,0:T(8,128)S(1)}, f32[2,64,1024]{2,1,0:T(8,128)S(1)}, u32[]{:S(2)}, u32[]{:S(2)}) collective-permute-start(f32[2,64,1024]{2,1,0:T(8,128)S(1)} %collective-permute-done.54), channel_id=1, source_target_pairs={{0,6},{2,0},{4,2},{6,4},{1,7},{3,1},{5,3},{7,5},{8,14},{10,8},{12,... | collective-permute-start | bytes 1572872 | tf_op jit(solution)/shard_map/ppermute | solution.py:116
  400.1 12.1 %collective-permute-start.73 = (f32[2,32,1024]{2,1,0:T(8,128)S(1)}, f32[2,32,1024]{2,1,0:T(8,128)S(1)}, u32[]{:S(2)}, u32[]{:S(2)}) collective-permute-start(f32[2,32,1024]{2,1,0:T(8,128)S(1)} %dynamic-slice_bitcast_fusion.6), channel_id=1, source_target_pairs={{0,6},{2,0},{4,2},{6,4},{1,7},{3,1},{5,3},{7,5},{8,14},{10,8},{12,... | collective-permute-start | bytes 786440 | tf_op jit(solution)/shard_map/ppermute | solution.py:96
  403.4 11.7 %collective-permute-start.70 = (f32[2,32,1024]{2,1,0:T(8,128)S(1)}, f32[2,32,1024]{2,1,0:T(8,128)S(1)}, u32[]{:S(2)}, u32[]{:S(2)}) collective-permute-start(f32[2,32,1024]{2,1,0:T(8,128)S(1)} %dynamic-slice_bitcast_fusion.7), channel_id=1, source_target_pairs={{0,2},{2,4},{4,6},{6,0},{1,3},{3,5},{5,7},{7,1},{8,10},{10,12},{12... | collective-permute-start | bytes 786440 | tf_op jit(solution)/shard_map/ppermute | solution.py:96
  404.1 12.0 %collective-permute-start.88 = (f32[64,1024]{1,0:T(8,128)S(1)}, f32[64,1024]{1,0:T(8,128)S(1)}, u32[]{:S(2)}, u32[]{:S(2)}) collective-permute-start(f32[64,1024]{1,0:T(8,128)S(1)} %bitcast_add_fusion.15), channel_id=1, source_target_pairs={{0,48},{16,0},{32,16},{48,32},{1,49},{17,1},{33,17},{49,33},{2,50}... | collective-permute-start | bytes 786440 | tf_op jit(solution)/shard_map/ppermute | solution.py:140
  417.3 11.4 %collective-permute-start.89 = (f32[64,1024]{1,0:T(8,128)S(1)}, f32[64,1024]{1,0:T(8,128)S(1)}, u32[]{:S(2)}, u32[]{:S(2)}) collective-permute-start(f32[64,1024]{1,0:T(8,128)S(1)} %bitcast_add_fusion.14), channel_id=1, source_target_pairs={{0,48},{16,0},{32,16},{48,32},{1,49},{17,1},{33,17},{49,33},{2,50}... | collective-permute-start | bytes 786440 | tf_op jit(solution)/shard_map/ppermute | solution.py:140
  429.2 12.4 %collective-permute-start.90 = (f32[2,32,1024]{2,1,0:T(8,128)S(1)}, f32[2,32,1024]{2,1,0:T(8,128)S(1)}, u32[]{:S(2)}, u32[]{:S(2)}) collective-permute-start(f32[2,32,1024]{2,1,0:T(8,128)S(1)} %fusion.51), channel_id=1, source_target_pairs={{0,8},{8,0},{1,9},{9,1},{2,10},{10,2},{3,11},{11,3},{4,12},{12,4},... | collective-permute-start | bytes 786440 | tf_op jit(solution)/shard_map/ppermute | solution.py:150
  438.6 15.6 %collective-permute-start.76 = (f32[2,32,1024]{2,1,0:T(8,128)S(1)}, f32[2,32,1024]{2,1,0:T(8,128)S(1)}, u32[]{:S(2)}, u32[]{:S(2)}) collective-permute-start(f32[2,32,1024]{2,1,0:T(8,128)S(1)} %fusion.56), channel_id=1, source_target_pairs={{0,1},{1,0},{2,3},{3,2},{4,5},{5,4},{6,7},{7,6},{8,9},{9,8},{10,11... | collective-permute-start | bytes 786440 | tf_op jit(solution)/shard_map/ppermute | solution.py:106
  446.3 14.5 %collective-permute-start.63 = (f32[2,32,1024]{2,1,0:T(8,128)S(1)}, f32[2,32,1024]{2,1,0:T(8,128)S(1)}, u32[]{:S(2)}, u32[]{:S(2)}) collective-permute-start(f32[2,32,1024]{2,1,0:T(8,128)S(1)} %fusion.64), channel_id=1, source_target_pairs={{0,1},{1,0},{2,3},{3,2},{4,5},{5,4},{6,7},{7,6},{8,9},{9,8},{10,11... | collective-permute-start | bytes 786440 | tf_op jit(solution)/shard_map/ppermute | solution.py:108
  454.2 11.7 %collective-permute-start.77 = (f32[2,32,1024]{2,1,0:T(8,128)S(1)}, f32[2,32,1024]{2,1,0:T(8,128)S(1)}, u32[]{:S(2)}, u32[]{:S(2)}) collective-permute-start(f32[2,32,1024]{2,1,0:T(8,128)S(1)} %fusion.59), channel_id=1, source_target_pairs={{0,1},{1,0},{2,3},{3,2},{4,5},{5,4},{6,7},{7,6},{8,9},{9,8},{10,11... | collective-permute-start | bytes 786440 | tf_op jit(solution)/shard_map/ppermute | solution.py:108
  461.2 12.1 %collective-permute-start.67 = (f32[2,32,1024]{2,1,0:T(8,128)S(1)}, f32[2,32,1024]{2,1,0:T(8,128)S(1)}, u32[]{:S(2)}, u32[]{:S(2)}) collective-permute-start(f32[2,32,1024]{2,1,0:T(8,128)S(1)} %get-tuple-element.162), channel_id=1, source_target_pairs={{0,6},{2,0},{4,2},{6,4},{1,7},{3,1},{5,3},{7,5},{8,14},{10,8},{12,... | collective-permute-start | bytes 786440 | tf_op jit(solution)/shard_map/ppermute | solution.py:116
  466.3 11.4 %collective-permute-start.81 = (f32[2,32,1024]{2,1,0:T(8,128)S(1)}, f32[2,32,1024]{2,1,0:T(8,128)S(1)}, u32[]{:S(2)}, u32[]{:S(2)}) collective-permute-start(f32[2,32,1024]{2,1,0:T(8,128)S(1)} %get-tuple-element.164), channel_id=1, source_target_pairs={{0,6},{2,0},{4,2},{6,4},{1,7},{3,1},{5,3},{7,5},{8,14},{10,8},{12,... | collective-permute-start | bytes 786440 | tf_op jit(solution)/shard_map/ppermute | solution.py:116
  479.6 11.6 %collective-permute-start.82 = (f32[2,32,1024]{2,1,0:T(8,128)S(1)}, f32[2,32,1024]{2,1,0:T(8,128)S(1)}, u32[]{:S(2)}, u32[]{:S(2)}) collective-permute-start(f32[2,32,1024]{2,1,0:T(8,128)S(1)} %collective-permute-done.81), channel_id=1, source_target_pairs={{0,6},{2,0},{4,2},{6,4},{1,7},{3,1},{5,3},{7,5},{8,14},{10,8},{12,... | collective-permute-start | bytes 786440 | tf_op jit(solution)/shard_map/ppermute | solution.py:116
  481.4 21.6 %collective-permute-start.95 = (f32[64,1024]{1,0:T(8,128)S(1)}, f32[64,1024]{1,0:T(8,128)S(1)}, u32[]{:S(2)}, u32[]{:S(2)}) collective-permute-start(f32[64,1024]{1,0:T(8,128)S(1)} %collective-permute-done.94), channel_id=1, source_target_pairs={{0,16},{16,32},{32,48},{48,0},{1,17},{17,33},{33,49},{49,1},{2,18}... | collective-permute-start | bytes 786440 | tf_op jit(solution)/shard_map/ppermute | solution.py:162
  483.7 19.4 %collective-permute-start.98 = (f32[64,1024]{1,0:T(8,128)S(1)}, f32[64,1024]{1,0:T(8,128)S(1)}, u32[]{:S(2)}, u32[]{:S(2)}) collective-permute-start(f32[64,1024]{1,0:T(8,128)S(1)} %collective-permute-done.97), channel_id=1, source_target_pairs={{0,48},{16,0},{32,16},{48,32},{1,49},{17,1},{33,17},{49,33},{2,50}... | collective-permute-start | bytes 786440 | tf_op jit(solution)/shard_map/ppermute | solution.py:162
  (135 other events, 935.4 us)
Sparse Core Ops, SparseCore 0:
  244.1 145.5 all-reduce.4
